TPU v7x, 512 devices: a whole 4x8x8 slice. The times are simulated.
512 devices in a mesh: dp: 16 (over x_lo, y), tensor: 32 (over x_hi, z, core).
Axes of the slice: x: 4 (x_hi: 2, x_lo: 2; x = x_hi * 2 + x_lo), y: 8, z: 8, core: 2. Of those that a mesh axis runs over, the one named last changes fastest.
Arguments:
- tokens: bfloat16 [4096, 14336], P('dp', 'tensor'), may hold values from -6 to 6
- base_weight: bfloat16 [14336, 4096], P('tensor'), may hold values from -0.5 to 0.5
- adapter_down: bfloat16 [16, 14336, 16], P(None, 'tensor'), may hold values from -0.046875 to 0.046875
- adapter_up: bfloat16 [16, 16, 4096], P(None, None, 'tensor'), may hold values from -1.5 to 1.5
- magnitude: bfloat16 [16, 4096], P(None, 'tensor'), may hold values from 0.5 to 2
- seg_lengths: int32 [16], replicated, may hold values from 1 to 2048, 4096 in all
- cotangent: bfloat16 [4096, 4096], P('dp', 'tensor'), may hold values from -6 to 6
Outputs:
- projected: bfloat16 [4096, 4096], P('dp', 'tensor')
- grad_tokens: bfloat16 [4096, 14336], P('dp', 'tensor')
- grad_down: bfloat16 [16, 14336, 16], P(None, 'tensor')
- grad_up: float32 [16, 16, 4096], P(None, None, 'tensor')
- grad_magnitude: float32 [16, 4096], P(None, 'tensor')
Inputs may be any that keep to these rules, and one draw needn't show every extreme that they name: The segments cover all 4096 tokens in order: seg_lengths sums to 4096.
All inputs are finite; a program needn't handle non-finite values.
Results may differ from a plain program's by a relative error of at most 0.019.
Values may be sent and summed in bfloat16 or wider, within the bound.
No kernel may reach another device: no remote copies, remote signals or barrier semaphores. Data moves between devices by JAX's collectives and lax.ppermute only.
A program may use at most 64 MiB of HBM per device.

v0:
```python
import jax
import jax.numpy as jnp
from jax import lax
from jax.sharding import PartitionSpec as P

HIGHEST_MODE = lax.Precision.HIGHEST
EPSILON = 1e-06


def from_everyone(shard, axis):
    size = lax.axis_size(axis)
    return lax.all_to_all(
        jnp.broadcast_to(shard[None], (size, *shard.shape)), axis, 0, 0, tiled=True
    )


def taken_together(shard, axis):
    return from_everyone(shard, axis).sum(axis=0)


def split_up(shard, dim, size):
    lengths = shard.shape
    tiles = shard.reshape(*lengths[:dim], size, lengths[dim] // size, *lengths[dim + 1 :])
    return jnp.moveaxis(tiles, dim, 0)


def summed_on_arrival(shard, axis, dim):
    size = lax.axis_size(axis)
    tiles = lax.all_to_all(split_up(shard, dim, size), axis, 0, 0, tiled=True)
    return jnp.sum(tiles.astype(jnp.float32), axis=0)


def padded_to(lines, size):
    spare = -lines.shape[0] % size
    if not spare:
        return lines
    return jnp.concatenate([lines, jnp.zeros((spare, *lines.shape[1:]), lines.dtype)])


def laid_out(tiles, dim):
    lengths = list(tiles.shape[1:])
    lengths[dim] *= tiles.shape[0]
    return jnp.moveaxis(tiles, 0, dim).reshape(lengths)


def collect(shard, axis, dim):
    return laid_out(from_everyone(shard, axis), dim)


def total_of(shard, axes):
    lines = shard.reshape(-1, shard.shape[-1])
    own = summed_on_arrival(padded_to(lines, lax.axis_size(axes)), axes, 0)
    whole = collect(own.astype(jnp.bfloat16), axes, 0)
    return whole[: len(lines)].reshape(shard.shape).astype(jnp.float32)


def member_table(seg_lengths, first_token, token_count):
    seg_ends = jnp.cumsum(seg_lengths)
    seg_starts = seg_ends - seg_lengths
    positions = first_token + jnp.arange(token_count, dtype=jnp.int32)[:, None]
    return ((positions >= seg_starts[None, :]) & (positions < seg_ends[None, :])).astype(
        jnp.float32
    )


def pick_rank(member, spread):
    token_count, adapter_count = member.shape
    return jnp.einsum(
        "ta,tar->tr", member, spread.reshape(token_count, adapter_count, -1), precision=HIGHEST_MODE
    )


def expand_rank(member, low_rounded):
    widened = member[:, :, None] * low_rounded.astype(jnp.float32)[:, None, :]
    return widened.reshape(member.shape[0], -1).astype(jnp.bfloat16)


def local(tokens, base_weight, adapter_down, adapter_up, magnitude, seg_lengths, cotangent):
    token_count, own_rows = tokens.shape
    adapter_count, _, rank_width = adapter_down.shape
    own_width = adapter_up.shape[2]
    full_width = base_weight.shape[1]
    member = member_table(seg_lengths, lax.axis_index("dp") * token_count, token_count)
    down_flat = jnp.transpose(adapter_down, (1, 0, 2)).reshape(own_rows, adapter_count * rank_width)
    up_whole = lax.all_gather(adapter_up, "tensor", axis=2, tiled=True)
    spread = jnp.dot(tokens, down_flat, preferred_element_type=jnp.float32)
    low_rank = taken_together(pick_rank(member, spread), "tensor")
    low_wide = expand_rank(member, low_rank.astype(jnp.bfloat16))
    cross_terms = lax.dot_general(
        down_flat, base_weight, (((0,), (0,)), ((), ())), preferred_element_type=jnp.float32
    )
    up_float = up_whole.astype(jnp.float32)
    gram_matrix = jnp.einsum(
        "afr,afs->ars", adapter_down, adapter_down, preferred_element_type=jnp.float32
    )
    column_squares = jnp.sum(jnp.square(base_weight.astype(jnp.float32)), axis=0)
    cross_sum = jnp.sum(
        cross_terms.reshape(adapter_count, rank_width, full_width) * up_float, axis=1
    )
    gram_sum = jnp.sum(
        up_float * jnp.einsum("ars,asd->ard", gram_matrix, up_float, precision=HIGHEST_MODE), axis=1
    )
    partial_squares = column_squares[None, :] + 2.0 * cross_sum + gram_sum
    base_terms = jnp.dot(tokens, base_weight, preferred_element_type=jnp.float32)
    col_norms = jnp.sqrt(
        summed_on_arrival(partial_squares.astype(jnp.bfloat16), "tensor", 1) + EPSILON
    )
    base_own = summed_on_arrival(base_terms.astype(jnp.bfloat16), "tensor", 1)
    up_own = adapter_up.reshape(adapter_count * rank_width, own_width)
    hidden = base_own + jnp.dot(low_wide, up_own, preferred_element_type=jnp.float32)
    col_scale = magnitude.astype(jnp.float32) / col_norms
    token_scale = jnp.dot(member, col_scale, precision=HIGHEST_MODE)
    projected = (hidden * token_scale).astype(jnp.bfloat16)
    grad_in = cotangent.astype(jnp.float32)
    grad_mag_part = jnp.dot(member.T, grad_in * hidden, precision=HIGHEST_MODE)
    grad_own = (grad_in * token_scale).astype(jnp.bfloat16)
    grad_up_part = jnp.dot(low_wide.T, grad_own, preferred_element_type=jnp.float32)
    grad_up_part = grad_up_part.reshape(adapter_count, rank_width, own_width)
    back_spread = lax.dot_general(
        grad_own, up_own, (((1,), (1,)), ((), ())), preferred_element_type=jnp.float32
    )
    back_rank = taken_together(pick_rank(member, back_spread), "tensor")
    back_wide = expand_rank(member, back_rank.astype(jnp.bfloat16))
    start_grad = lax.dot_general(
        back_wide, down_flat, (((1,), (1,)), ((), ())), preferred_element_type=jnp.float32
    )
    grad_base = start_grad + lax.dot_general(
        lax.all_gather(grad_own, "tensor", axis=1, tiled=True),
        base_weight,
        (((1,), (1,)), ((), ())),
        preferred_element_type=jnp.float32,
    )
    grad_tokens = grad_base.astype(jnp.bfloat16)
    grad_down_part = lax.dot_general(
        tokens, back_wide, (((0,), (0,)), ((), ())), preferred_element_type=jnp.float32
    )
    grad_down_part = jnp.transpose(
        grad_down_part.reshape(own_rows, adapter_count, rank_width), (1, 0, 2)
    )
    mag_summed, up_summed, down_summed = (
        total_of(grad_mag_part.astype(jnp.bfloat16), "dp"),
        total_of(grad_up_part.astype(jnp.bfloat16), "dp"),
        total_of(grad_down_part.astype(jnp.bfloat16), "dp"),
    )
    grad_magnitude = mag_summed / col_norms
    return (projected, grad_tokens, down_summed.astype(jnp.bfloat16), up_summed, grad_magnitude)


def solution(mesh):
    placed = (
        P("dp", "tensor"),
        P("tensor", None),
        P(None, "tensor", None),
        P(None, None, "tensor"),
        P(None, "tensor"),
        P(),
        P("dp", "tensor"),
    )
    return jax.shard_map(
        local,
        mesh=mesh,
        in_specs=placed,
        out_specs=(
            P("dp", "tensor"),
            P("dp", "tensor"),
            P(None, "tensor", None),
            P(None, None, "tensor"),
            P(None, "tensor"),
        ),
        check_vma=False,
    )
```

profile of v0, /device:TPU:8, one launch (start us, length us, event | category | flops | bytes accessed | tf_op | source)
XLA Modules:
  0.0 259.1 jit_solution(895637971586263253)
XLA Ops:
  7.2 0.7 all-gather.3.cloned.1.call-update
  7.9 0.7 copy.20
  8.8 0.7 sub.3
  9.6 1.2 fusion.9
  10.7 0.9 broadcast_in_dim.10
  11.6 13.2 %all-to-all-start.1 = ((f32[32,256,16]{1,2,0:T(8,128)}), f32[32,256,16]{1,2,0:T(8,128)S(1)}, u32[]{:S(2)}, u32[]{:S(2)}) async-start(f32[32,256,16]{1,2,0:T(8,128)} %broadcast_in_dim.10), calls=%async_computation.1 | async-start | bytes 1048576 | tf_op jit(solution)/shard_map/all_to_all | solution.py:12
  24.8 3.5 %fusion.5 = bf16[32,32,8,128]{3,2,1,0:T(8,128)(2,1)S(1)} fusion(bf16[256,448]{0,1:T(8,128)(2,1)} %param.7, bf16[448,4096]{1,0:T(8,128)(2,1)} %param.8), kind=kOutput, calls=%fused_computation.9 | convolution fusion | flops 940572672 | bytes 5996544 | tf_op jit(solution)/shard_map/dot_general | solution.py:104
  28.2 1.9 copy.37
  30.1 15.0 %all-to-all-done.1 = f32[32,256,16]{1,2,0:T(8,128)S(1)} async-done(((f32[32,256,16]{1,2,0:T(8,128)}), f32[32,256,16]{1,2,0:T(8,128)S(1)}, u32[]{:S(2)}, u32[]{:S(2)}) %all-to-all-start.1) | async-done | bytes 524320 | tf_op jit(solution)/shard_map/all_to_all | solution.py:12
  45.1 4.0 %all-to-all-start = ((bf16[32,256,128]{2,1,0:T(8,128)(2,1)}), bf16[32,256,128]{2,1,0:T(8,128)(2,1)S(1)}, u32[]{:S(2)}, u32[]{:S(2)}) async-start(bf16[32,256,128]{2,1,0:T(8,128)(2,1)} %bitcast.86), calls=%async_computation | async-start | bytes 4194304 | tf_op jit(solution)/shard_map/all_to_all | solution.py:29
  49.4 2.8 %multiply_reduce_fusion = f32[4096]{0:T(1024)S(1)} fusion(bf16[448,4096]{1,0:T(8,128)(2,1)} %param.8), kind=kLoop, calls=%fused_computation | loop fusion | flops 5500928 | bytes 3686400 | tf_op jit(solution)/shard_map/reduce_sum | solution.py:96
  52.2 59.5 %all-gather.3.cloned.1.call-done = bf16[16,16,4096]{2,1,0:T(8,128)(2,1)} async-done(((bf16[16,16,128]{2,1,0:T(8,128)(2,1)}), bf16[16,16,4096]{2,1,0:T(8,128)(2,1)}) %all-gather.3.cloned.1.call-update) | async-done | bytes 2097168 | tf_op jit(solution)/shard_map/all_gather | solution.py:85
  111.8 4.7 %fusion.4 = f32[16,4096]{1,0:T(8,128)S(1)} fusion(f32[16,16,16]{2,1,0:T(8,128)S(1)} %fusion.40, bf16[16,16,4096]{2,1,0:T(8,128)(2,1)} %all-gather.3.cloned.1.call-done), kind=kOutput, calls=%fused_computation.8 | convolution fusion | flops 204406784 | bytes 2375680 | tf_op jit(solution)/shard_map/ars,asd->ard/dot_general | solution.py:101
  116.6 4.3 %fusion.1 = f32[16,4096]{1,0:T(8,128)S(1)} fusion(bf16[16,16,4096]{2,1,0:T(8,128)(2,1)} %all-gather.3.cloned.1.call-done, bf16[448,4096]{1,0:T(8,128)(2,1)} %param.8, bf16[16,448,16]{1,2,0:T(8,128)(2,1)S(1)} %copy-done), kind=kOutput, calls=%fused_computation.7 | convolution fusion | flops 942604288 | bytes 6258688 | tf_op jit(solution)/shard_map/dot_general | solution.py:89
  121.1 0.7 copy.21
  121.8 6.6 %all-to-all-start.2 = ((bf16[32,16,128]{2,1,0:T(8,128)(2,1)}), bf16[32,16,128]{2,1,0:T(8,128)(2,1)S(1)}, u32[]{:S(2)}, u32[]{:S(2)}) async-start(bf16[32,16,128]{2,1,0:T(8,128)(2,1)} %copy.21), calls=%async_computation.2 | async-start | bytes 262144 | tf_op jit(solution)/shard_map/all_to_all | solution.py:29
  128.4 0.3 convert_reduce_fusion
  128.7 0.2 fusion.11
  128.9 11.3 %all-to-all-done.2 = bf16[32,16,128]{2,1,0:T(8,128)(2,1)S(1)} async-done(((bf16[32,16,128]{2,1,0:T(8,128)(2,1)}), bf16[32,16,128]{2,1,0:T(8,128)(2,1)S(1)}, u32[]{:S(2)}, u32[]{:S(2)}) %all-to-all-start.2) | async-done | bytes 131104 | tf_op jit(solution)/shard_map/all_to_all | solution.py:29
  140.3 1.0 fusion.19
  141.6 0.6 copy.23
  142.2 7.8 %all-to-all-start.8 = ((bf16[16,1,128]{2,1,0:T(2,128)(2,1)}), bf16[16,1,128]{2,1,0:T(2,128)(2,1)S(1)}, u32[]{:S(2)}, u32[]{:S(2)}) async-start(bf16[16,1,128]{2,1,0:T(2,128)(2,1)} %copy.23), calls=%async_computation.8 | async-start | bytes 16384 | tf_op jit(solution)/shard_map/all_to_all | solution.py:29
  150.0 1.0 fusion.10
  151.1 6.0 %all-to-all-done.8 = bf16[16,1,128]{2,1,0:T(2,128)(2,1)S(1)} async-done(((bf16[16,1,128]{2,1,0:T(2,128)(2,1)}), bf16[16,1,128]{2,1,0:T(2,128)(2,1)S(1)}, u32[]{:S(2)}, u32[]{:S(2)}) %all-to-all-start.8) | async-done | bytes 4128 | tf_op jit(solution)/shard_map/all_to_all | solution.py:29
  157.1 0.9 broadcast_in_dim.11
  157.9 3.9 %all-to-all-start.3 = ((f32[32,256,16]{1,2,0:T(8,128)}), f32[32,256,16]{1,2,0:T(8,128)S(1)}, u32[]{:S(2)}, u32[]{:S(2)}) async-start(f32[32,256,16]{1,2,0:T(8,128)} %broadcast_in_dim.11), calls=%async_computation.3 | async-start | bytes 1048576 | tf_op jit(solution)/shard_map/all_to_all | solution.py:12
  161.9 1.6 convolution_convert_fusion.2
  163.5 18.5 %all-to-all-done.3 = f32[32,256,16]{1,2,0:T(8,128)S(1)} async-done(((f32[32,256,16]{1,2,0:T(8,128)}), f32[32,256,16]{1,2,0:T(8,128)S(1)}, u32[]{:S(2)}, u32[]{:S(2)}) %all-to-all-start.3) | async-done | bytes 524320 | tf_op jit(solution)/shard_map/all_to_all | solution.py:12
  182.0 0.6 broadcast_in_dim.14
  182.6 4.5 %all-to-all-start.9 = ((bf16[16,1,128]{2,1,0:T(2,128)(2,1)}), bf16[16,1,128]{2,1,0:T(2,128)(2,1)S(1)}, u32[]{:S(2)}, u32[]{:S(2)}) async-start(bf16[16,1,128]{2,1,0:T(2,128)(2,1)} %broadcast_in_dim.14), calls=%async_computation.9 | async-start | bytes 16384 | tf_op jit(solution)/shard_map/all_to_all | solution.py:12
  187.2 7.1 %all-to-all-done.9 = bf16[16,1,128]{2,1,0:T(2,128)(2,1)S(1)} async-done(((bf16[16,1,128]{2,1,0:T(2,128)(2,1)}), bf16[16,1,128]{2,1,0:T(2,128)(2,1)S(1)}, u32[]{:S(2)}, u32[]{:S(2)}) %all-to-all-start.9) | async-done | bytes 4128 | tf_op jit(solution)/shard_map/all_to_all | solution.py:12
  194.2 4.7 %all-to-all-start.6 = ((bf16[16,16,128]{2,1,0:T(8,128)(2,1)}), bf16[16,16,128]{2,1,0:T(8,128)(2,1)S(1)}, u32[]{:S(2)}, u32[]{:S(2)}) async-start(bf16[16,16,128]{2,1,0:T(8,128)(2,1)} %convolution_convert_fusion.2), calls=%async_computation.6 | async-start | bytes 131072 | tf_op jit(solution)/shard_map/all_to_all | solution.py:29
  199.0 0.3 fusion.8
  199.2 0.8 copy.22
  200.1 6.5 %all-to-all-done.6 = bf16[16,16,128]{2,1,0:T(8,128)(2,1)S(1)} async-done(((bf16[16,16,128]{2,1,0:T(8,128)(2,1)}), bf16[16,16,128]{2,1,0:T(8,128)(2,1)S(1)}, u32[]{:S(2)}, u32[]{:S(2)}) %all-to-all-start.6) | async-done | bytes 65568 | tf_op jit(solution)/shard_map/all_to_all | solution.py:29
  206.6 4.4 %all-to-all-start.4 = ((bf16[16,448,16]{1,2,0:T(8,128)(2,1)}), bf16[16,448,16]{1,2,0:T(8,128)(2,1)S(1)}, u32[]{:S(2)}, u32[]{:S(2)}) async-start(bf16[16,448,16]{1,2,0:T(8,128)(2,1)} %bitcast.19), calls=%async_computation.4 | async-start | bytes 524288 | tf_op jit(solution)/shard_map/all_to_all | solution.py:29
  211.0 9.1 %all-to-all-done.4 = bf16[16,448,16]{1,2,0:T(8,128)(2,1)S(1)} async-done(((bf16[16,448,16]{1,2,0:T(8,128)(2,1)}), bf16[16,448,16]{1,2,0:T(8,128)(2,1)S(1)}, u32[]{:S(2)}, u32[]{:S(2)}) %all-to-all-start.4) | async-done | bytes 229408 | tf_op jit(solution)/shard_map/all_to_all | solution.py:29
  220.1 0.6 broadcast_in_dim.13
  220.7 4.2 %all-to-all-start.7 = ((bf16[16,16,128]{2,1,0:T(8,128)(2,1)}), bf16[16,16,128]{2,1,0:T(8,128)(2,1)S(1)}, u32[]{:S(2)}, u32[]{:S(2)}) async-start(bf16[16,16,128]{2,1,0:T(8,128)(2,1)} %broadcast_in_dim.13), calls=%async_computation.7 | async-start | bytes 131072 | tf_op jit(solution)/shard_map/all_to_all | solution.py:12
  225.0 7.6 %all-to-all-done.7 = bf16[16,16,128]{2,1,0:T(8,128)(2,1)S(1)} async-done(((bf16[16,16,128]{2,1,0:T(8,128)(2,1)}), bf16[16,16,128]{2,1,0:T(8,128)(2,1)S(1)}, u32[]{:S(2)}, u32[]{:S(2)}) %all-to-all-start.7) | async-done | bytes 65568 | tf_op jit(solution)/shard_map/all_to_all | solution.py:12
  232.5 0.7 broadcast_in_dim.12
  233.3 4.3 %all-to-all-start.5 = ((bf16[16,448,16]{1,2,0:T(8,128)(2,1)}), bf16[16,448,16]{1,2,0:T(8,128)(2,1)S(1)}, u32[]{:S(2)}, u32[]{:S(2)}) async-start(bf16[16,448,16]{1,2,0:T(8,128)(2,1)} %broadcast_in_dim.12), calls=%async_computation.5 | async-start | bytes 524288 | tf_op jit(solution)/shard_map/all_to_all | solution.py:12
  237.6 0.6 fusion.37
  238.2 0.7 convert_element_type.143
  238.9 7.8 %all-to-all-done.5 = bf16[16,448,16]{1,2,0:T(8,128)(2,1)S(1)} async-done(((bf16[16,448,16]{1,2,0:T(8,128)(2,1)}), bf16[16,448,16]{1,2,0:T(8,128)(2,1)S(1)}, u32[]{:S(2)}, u32[]{:S(2)}) %all-to-all-start.5) | async-done | bytes 229408 | tf_op jit(solution)/shard_map/all_to_all | solution.py:12
  246.7 3.8 %fusion.41 = f32[256,448]{0,1:T(8,128)S(1)} fusion(bf16[256,4096]{1,0:T(8,128)(2,1)} %all-gather.5.cloned.1.call-done, bf16[448,4096]{1,0:T(8,128)(2,1)} %param.8), kind=kOutput, calls=%fused_computation.65 | convolution fusion | flops 939524096 | bytes 6225920 | tf_op jit(solution)/shard_map/dot_general | solution.py:127
  250.5 1.0 fusion.7
  251.5 0.7 copy.39
  (35 shorter events, 1.2 us)
Async XLA Ops:
  7.2 2.4 copy-start
  7.2 104.6 %all-gather.3.cloned.1.call-start = ((), (), s32[]{:S(2)}) async-start(), calls=%async_computation.10 | async-start | bytes 2162688 | tf_op jit(solution)/shard_map/all_gather | solution.py:85
  11.6 33.5 %all-to-all-start.1 = ((f32[32,256,16]{1,2,0:T(8,128)}), f32[32,256,16]{1,2,0:T(8,128)S(1)}, u32[]{:S(2)}, u32[]{:S(2)}) async-start(f32[32,256,16]{1,2,0:T(8,128)} %broadcast_in_dim.10), calls=%async_computation.1 | async-start | bytes 1048576 | tf_op jit(solution)/shard_map/all_to_all | solution.py:12
  45.1 76.6 %all-to-all-start = ((bf16[32,256,128]{2,1,0:T(8,128)(2,1)}), bf16[32,256,128]{2,1,0:T(8,128)(2,1)S(1)}, u32[]{:S(2)}, u32[]{:S(2)}) async-start(bf16[32,256,128]{2,1,0:T(8,128)(2,1)} %bitcast.86), calls=%async_computation | async-start | bytes 4194304 | tf_op jit(solution)/shard_map/all_to_all | solution.py:29
  120.9 7.8 %copy-start.3 = (bf16[16,16,128]{2,1,0:T(8,128)(2,1)S(1)}, bf16[16,16,128]{2,1,0:T(8,128)(2,1)}, u32[]{:S(2)}) copy-start(bf16[16,16,128]{2,1,0:T(8,128)(2,1)} %param.10) | copy-start | bytes 196612
  120.9 19.4 %copy-start.2 = (bf16[256,128]{1,0:T(8,128)(2,1)S(1)}, bf16[256,128]{1,0:T(8,128)(2,1)}, u32[]{:S(2)}) copy-start(bf16[256,128]{1,0:T(8,128)(2,1)} %param.13) | copy-start | bytes 196612
  120.9 19.4 %copy-start.4 = (bf16[16,128]{1,0:T(8,128)(2,1)S(1)}, bf16[16,128]{1,0:T(8,128)(2,1)}, u32[]{:S(2)}) copy-start(bf16[16,128]{1,0:T(8,128)(2,1)} %param.11) | copy-start | bytes 12292
  121.1 77.9 %copy-start.1 = (bf16[256,448]{0,1:T(8,128)(2,1)S(1)}, bf16[256,448]{0,1:T(8,128)(2,1)}, u32[]{:S(2)}) copy-start(bf16[256,448]{0,1:T(8,128)(2,1)} %param.7) | copy-start | bytes 688132
  121.8 18.5 %all-to-all-start.2 = ((bf16[32,16,128]{2,1,0:T(8,128)(2,1)}), bf16[32,16,128]{2,1,0:T(8,128)(2,1)S(1)}, u32[]{:S(2)}, u32[]{:S(2)}) async-start(bf16[32,16,128]{2,1,0:T(8,128)(2,1)} %copy.21), calls=%async_computation.2 | async-start | bytes 262144 | tf_op jit(solution)/shard_map/all_to_all | solution.py:29
  128.3 118.4 %all-gather.5.cloned.1.call-start = ((), (), s32[]{:S(2)}) async-start(), calls=%async_computation.11 | async-start | bytes 2162688 | tf_op jit(solution)/shard_map/all_gather | solution.py:128
  142.2 14.9 %all-to-all-start.8 = ((bf16[16,1,128]{2,1,0:T(2,128)(2,1)}), bf16[16,1,128]{2,1,0:T(2,128)(2,1)S(1)}, u32[]{:S(2)}, u32[]{:S(2)}) async-start(bf16[16,1,128]{2,1,0:T(2,128)(2,1)} %copy.23), calls=%async_computation.8 | async-start | bytes 16384 | tf_op jit(solution)/shard_map/all_to_all | solution.py:29
  157.9 24.1 %all-to-all-start.3 = ((f32[32,256,16]{1,2,0:T(8,128)}), f32[32,256,16]{1,2,0:T(8,128)S(1)}, u32[]{:S(2)}, u32[]{:S(2)}) async-start(f32[32,256,16]{1,2,0:T(8,128)} %broadcast_in_dim.11), calls=%async_computation.3 | async-start | bytes 1048576 | tf_op jit(solution)/shard_map/all_to_all | solution.py:12
  182.6 11.6 %all-to-all-start.9 = ((bf16[16,1,128]{2,1,0:T(2,128)(2,1)}), bf16[16,1,128]{2,1,0:T(2,128)(2,1)S(1)}, u32[]{:S(2)}, u32[]{:S(2)}) async-start(bf16[16,1,128]{2,1,0:T(2,128)(2,1)} %broadcast_in_dim.14), calls=%async_computation.9 | async-start | bytes 16384 | tf_op jit(solution)/shard_map/all_to_all | solution.py:12
  194.2 12.4 %all-to-all-start.6 = ((bf16[16,16,128]{2,1,0:T(8,128)(2,1)}), bf16[16,16,128]{2,1,0:T(8,128)(2,1)S(1)}, u32[]{:S(2)}, u32[]{:S(2)}) async-start(bf16[16,16,128]{2,1,0:T(8,128)(2,1)} %convolution_convert_fusion.2), calls=%async_computation.6 | async-start | bytes 131072 | tf_op jit(solution)/shard_map/all_to_all | solution.py:29
  206.6 13.5 %all-to-all-start.4 = ((bf16[16,448,16]{1,2,0:T(8,128)(2,1)}), bf16[16,448,16]{1,2,0:T(8,128)(2,1)S(1)}, u32[]{:S(2)}, u32[]{:S(2)}) async-start(bf16[16,448,16]{1,2,0:T(8,128)(2,1)} %bitcast.19), calls=%async_computation.4 | async-start | bytes 524288 | tf_op jit(solution)/shard_map/all_to_all | solution.py:29
  220.7 11.8 %all-to-all-start.7 = ((bf16[16,16,128]{2,1,0:T(8,128)(2,1)}), bf16[16,16,128]{2,1,0:T(8,128)(2,1)S(1)}, u32[]{:S(2)}, u32[]{:S(2)}) async-start(bf16[16,16,128]{2,1,0:T(8,128)(2,1)} %broadcast_in_dim.13), calls=%async_computation.7 | async-start | bytes 131072 | tf_op jit(solution)/shard_map/all_to_all | solution.py:12
  233.3 13.5 %all-to-all-start.5 = ((bf16[16,448,16]{1,2,0:T(8,128)(2,1)}), bf16[16,448,16]{1,2,0:T(8,128)(2,1)S(1)}, u32[]{:S(2)}, u32[]{:S(2)}) async-start(bf16[16,448,16]{1,2,0:T(8,128)(2,1)} %broadcast_in_dim.12), calls=%async_computation.5 | async-start | bytes 524288 | tf_op jit(solution)/shard_map/all_to_all | solution.py:12
Sparse Core Ops, SparseCore 0:
  11.1 100.6 all-gather.2
  141.5 80.5 all-gather.4
where the time goes:
time: 260 us; the launch traced here: 259 us
  waiting for transfers between devices  149 us (57%)
  starting transfers between devices  57.6 us (22%)
  matrix products  23 us (9%)
  between operations  14.3 us (6%)
  local copies, waits for them, and re-layouts  9.3 us (4%)
  other arithmetic  5.62 us (2%)
    all_gather x1, waiting for transfers between devices, local(): up_whole = lax.all_gather(adapter_up, 'tensor', axis=2, tiled=True)  59.5 us
    all_to_all x5, waiting for transfers between devices, from_everyone(): lax.all_to_all(jnp.broadcast_to(shard[None], (size, *shard.shape)), axis,...  55.9 us
    all_to_all x5, waiting for transfers between devices, summed_on_arrival(): tiles = lax.all_to_all(split_up(shard, dim, size), axis, 0, 0, tiled=True)  33 us
    all_to_all x5, starting transfers between devices, from_everyone(): lax.all_to_all(jnp.broadcast_to(shard[None], (size, *shard.shape)), axis,...  30.1 us
    all_to_all x5, starting transfers between devices, summed_on_arrival(): tiles = lax.all_to_all(split_up(shard, dim, size), axis, 0, 0, tiled=True)  27.5 us
  transfers between devices with their start and end apart: 12, of which 10 were waited for; matrix products, arithmetic and copies ran while one was open for 12% of the time, Pallas kernels for 0%

commit v1 on v0

v1 whole, which is shorter than its diff:
```python
import jax
import jax.numpy as jnp
from jax import lax
from jax.sharding import PartitionSpec as P

HIGHEST_MODE = lax.Precision.HIGHEST
EPSILON = 1e-06
F32 = jnp.float32
BF16 = jnp.bfloat16
LANES = 128


def member_table(seg_lengths, first_token, token_count):
    ends = jnp.cumsum(seg_lengths)
    starts = ends - seg_lengths
    at = first_token + jnp.arange(token_count, dtype=jnp.int32)[None, :]
    return ((at >= starts[:, None]) & (at < ends[:, None])).astype(F32)


def picked(spread, member):
    count, tokens = member.shape
    return jnp.sum(spread.reshape(count, -1, tokens) * member[:, None, :], axis=0)


def widened(member, rank_rows):
    wide = member[:, None, :] * rank_rows.astype(F32)[None, :, :]
    return wide.reshape(-1, member.shape[1]).astype(BF16)


def packed(rows):
    return jnp.concatenate([rows[:, :LANES], rows[:, LANES:]], axis=0)


def unpacked(rows):
    half = rows.shape[0] // 2
    return jnp.concatenate([rows[:half], rows[half:]], axis=1)


def dot(a, b, ca, cb, precision=None):
    return lax.dot_general(
        a, b, (((ca,), (cb,)), ((), ())), precision=precision, preferred_element_type=F32
    )


def exchange(blocks, axis, groups=None):
    return lax.all_to_all(blocks, axis, 0, 0, tiled=True, axis_index_groups=groups)


def local(tokens, base_weight, adapter_down, adapter_up, magnitude, seg_lengths, cotangent):
    token_count, own_rows = tokens.shape
    adapters, _, rank = adapter_down.shape
    own_width = adapter_up.shape[2]
    full_width = base_weight.shape[1]
    size = full_width // own_width
    ZS = size // 4
    me_dp = lax.axis_index("dp")
    me = lax.axis_index("tensor")
    core, hi = me % 2, me // (2 * ZS)
    core_pairs = [(i, i ^ 1) for i in range(size)]
    hi_pairs = [(i, (i + size // 2) % size) for i in range(size)]
    z_groups = [[h * 2 * ZS + z * 2 + c for z in range(ZS)] for h in range(2) for c in range(2)]

    member = member_table(seg_lengths, me_dp * token_count, token_count)
    down_rows = jnp.transpose(adapter_down, (0, 2, 1))
    down_flat = down_rows.reshape(adapters * rank, own_rows)
    up_own = adapter_up.reshape(adapters * rank, own_width)

    down_mine = lax.dynamic_index_in_dim(down_rows, me_dp, 0, keepdims=False)
    cross = dot(down_mine, base_weight, 1, 0)
    gram = dot(down_mine, down_mine, 1, 1)
    share = 32
    pieces = own_rows // share
    part_rows = lax.dynamic_slice_in_dim(
        base_weight, jnp.minimum(me_dp, pieces - 1) * share, share, 0
    ).astype(F32)
    squares = jnp.sum(part_rows * part_rows, axis=0) * (me_dp < pieces).astype(F32)
    first = jnp.concatenate(
        [
            cross.astype(BF16).reshape(rank, size, own_width).transpose(1, 0, 2),
            squares.astype(BF16).reshape(size, 1, own_width),
            jnp.broadcast_to(
                gram.astype(BF16).reshape(1, rank * rank // own_width, own_width),
                (size, rank * rank // own_width, own_width),
            ),
        ],
        axis=1,
    )
    first = jnp.sum(exchange(first, "tensor").astype(F32), axis=0)

    low_part = picked(dot(down_flat, tokens, 1, 1), member)
    base = dot(tokens, base_weight, 1, 0).astype(BF16)
    base = base.reshape(token_count, size // 2, 2, own_width).transpose(2, 1, 0, 3)
    keep = lax.dynamic_index_in_dim(base, core, 0, keepdims=False)
    give = lax.dynamic_index_in_dim(base, 1 - core, 0, keepdims=False)
    got = lax.ppermute(give, "tensor", core_pairs)
    base = (keep.astype(F32) + got.astype(F32)).astype(BF16)
    base = base.reshape(2, ZS, token_count, own_width)
    keep = lax.dynamic_index_in_dim(base, hi, 0, keepdims=False)
    give = lax.dynamic_index_in_dim(base, 1 - hi, 0, keepdims=False)
    got = lax.ppermute(give, "tensor", hi_pairs)
    base = (keep.astype(F32) + got.astype(F32)).astype(BF16)

    up_mine = lax.dynamic_index_in_dim(adapter_up, me_dp, 0, keepdims=False).astype(F32)
    gram = first[rank + 1 :].reshape(rank, rank)
    mine = jnp.sum(
        up_mine * (2.0 * first[:rank] + dot(gram, up_mine, 1, 0, HIGHEST_MODE)), axis=0
    )
    second = jnp.stack([mine, first[rank]])
    second = exchange(jnp.broadcast_to(second[None], (adapters, *second.shape)), "dp")
    squares = second[:, 0] + jnp.sum(second[:, 1], axis=0)[None, :]
    col_norms = jnp.sqrt(jnp.maximum(squares, 0.0) + EPSILON)
    col_scale = magnitude.astype(F32) / col_norms

    token_scale = dot(member, col_scale, 0, 0, HIGHEST_MODE)
    grad_in = cotangent.astype(F32)
    grad_own = (grad_in * token_scale).astype(BF16)
    back_part = picked(dot(up_own, grad_own, 1, 1), member)

    every = jnp.concatenate(
        [grad_own, packed(low_part.astype(BF16)), packed(back_part.astype(BF16))], axis=0
    )
    third = jnp.concatenate([base, jnp.broadcast_to(every[None], (ZS, *every.shape))], axis=1)
    third = exchange(third, "tensor", z_groups)
    ranks = jnp.sum(third[:, 2 * token_count :].astype(F32), axis=0)
    ranks = ranks + lax.ppermute(ranks.astype(BF16), "tensor", hi_pairs).astype(F32)
    ranks = ranks + lax.ppermute(ranks.astype(BF16), "tensor", core_pairs).astype(F32)
    low_wide = widened(member, unpacked(ranks[: 2 * rank]).astype(BF16))
    back_wide = widened(member, unpacked(ranks[2 * rank :]).astype(BF16))

    hidden = jnp.sum(third[:, :token_count].astype(F32), axis=0) + dot(low_wide, up_own, 0, 0)
    projected = (hidden * token_scale).astype(BF16)
    mag_part = dot(member, grad_in * hidden, 1, 0, HIGHEST_MODE)
    up_part = dot(low_wide, grad_own, 1, 0)
    down_part = dot(back_wide, tokens, 1, 0)

    pad = -own_rows % LANES
    mag_rows = own_width // pad
    fourth = jnp.concatenate(
        [
            down_part.astype(BF16).reshape(adapters, rank, own_rows),
            jnp.pad(
                mag_part.astype(BF16).reshape(adapters, mag_rows, pad),
                ((0, 0), (0, rank - mag_rows), (0, 0)),
            ),
            up_part.astype(BF16).reshape(adapters, rank, own_width),
        ],
        axis=2,
    )
    fourth = jnp.sum(exchange(fourth, "dp").astype(F32), axis=0).astype(BF16)
    fifth = exchange(jnp.broadcast_to(fourth[None], (adapters, *fourth.shape)), "dp")
    grad_down = jnp.transpose(fifth[:, :, :own_rows], (0, 2, 1))
    grad_up = fifth[:, :, own_rows + pad :].astype(F32)
    mag_sum = fifth[:, :mag_rows, own_rows : own_rows + pad].astype(F32)
    grad_magnitude = mag_sum.reshape(adapters, own_width) / col_norms

    gathered = third[:, token_count : 2 * token_count]
    other = lax.ppermute(gathered, "tensor", hi_pairs)
    gathered = jnp.where(
        hi == 0, jnp.stack([gathered, other]), jnp.stack([other, gathered])
    ).reshape(2 * ZS, token_count, own_width)
    other = lax.ppermute(gathered, "tensor", core_pairs)
    whole = jnp.where(
        core == 0, jnp.stack([gathered, other], 1), jnp.stack([other, gathered], 1)
    )
    whole = whole.transpose(2, 0, 1, 3).reshape(token_count, full_width)
    grad_tokens = dot(whole, base_weight, 1, 1) + dot(back_wide, down_flat, 0, 0)
    return (projected, grad_tokens.astype(BF16), grad_down, grad_up, grad_magnitude)


def solution(mesh):
    placed = (
        P("dp", "tensor"),
        P("tensor", None),
        P(None, "tensor", None),
        P(None, None, "tensor"),
        P(None, "tensor"),
        P(),
        P("dp", "tensor"),
    )
    return jax.shard_map(
        local,
        mesh=mesh,
        in_specs=placed,
        out_specs=(
            P("dp", "tensor"),
            P("dp", "tensor"),
            P(None, "tensor", None),
            P(None, None, "tensor"),
            P(None, "tensor"),
        ),
        check_vma=False,
    )
```

time: 260 us -> 177 us (0.68)
  the two profiles are of different devices: /device:TPU:8 before, /device:TPU:10 now
where the time goes in v1:
time: 177 us; the launch traced here: 176 us
  waiting for transfers between devices  51.4 us (29%)
  starting transfers between devices  43.8 us (25%)
  blocking collectives  33.5 us (19%)
  local copies, waits for them, and re-layouts  20.1 us (11%)
  matrix products  16.5 us (9%)
  other arithmetic  9.57 us (5%)
    all_to_all x1, blocking collectives, exchange(): lax.all_to_all(blocks, axis, 0, 0, tiled=True, axis_index_groups=groups)  33.5 us
    all_to_all x4, waiting for transfers between devices, exchange(): lax.all_to_all(blocks, axis, 0, 0, tiled=True, axis_index_groups=groups)  31.7 us
    all_to_all x4, starting transfers between devices, exchange(): lax.all_to_all(blocks, axis, 0, 0, tiled=True, axis_index_groups=groups)  31 us
    dot_general x13, matrix products, dot(): lax.dot_general(a, b, (((ca,), (cb,)), ((), ())), precision=precision, pr...  16.5 us
    ppermute x1, waiting for transfers between devices, local(): got = lax.ppermute(give, 'tensor', hi_pairs)  12 us
    dynamic_slice x1, local copies, waits for them, and re-layouts, local(): keep = lax.dynamic_index_in_dim(base, core, 0, keepdims=False)  5.66 us
    ppermute x1, waiting for transfers between devices, local(): lax.ppermute(ranks.astype(BF16), 'tensor', hi_pairs).astype(F32)  4.98 us
    unnamed x39, local copies, waits for them, and re-layouts  4.57 us
  transfers between devices with their start and end apart: 10, of which 8 were waited for; matrix products, arithmetic and copies ran while one was open for 12% of the time, Pallas kernels for 0%

profile of v1, /device:TPU:10, one launch (start us, length us, event | category | flops | bytes accessed | tf_op | source)
XLA Modules:
  0.0 175.9 jit_solution(17857835978423345636)
XLA Ops:
  0.7 4.8 %convolution_convert_fusion = bf16[256,4096]{1,0:T(8,128)(2,1)} fusion(bf16[256,448]{0,1:T(8,128)(2,1)} %param.7, bf16[448,4096]{1,0:T(8,128)(2,1)} %param.8), kind=kOutput, calls=%fused_computation | convolution fusion | flops 940572672 | bytes 5996544 | tf_op jit(solution)/shard_map/dot_general | solution.py:40
  5.5 3.2 %reshape.220 = bf16[256,16,2,128]{3,2,1,0:T(2,128)(2,1)S(1)} reshape(bf16[256,4096]{1,0:T(8,128)(2,1)} %convolution_convert_fusion) | data formatting | bytes 4194304 | tf_op jit(solution)/shard_map/reshape | solution.py:92
  8.7 5.7 %constant_dynamic-slice_fusion.1 = (bf16[256,16,1,128]{3,2,1,0:T(2,128)(2,1)}, bf16[256,16,1,128]{3,2,1,0:T(2,128)(2,1)S(1)}) fusion(bf16[256,16,2,128]{3,2,1,0:T(2,128)(2,1)S(1)} %reshape.220, s32[]{:T(128)S(6)} %select_n.65, s32[]{:T(128)S(6)} %select_n.66), kind=kLoop, calls=%fused_computation.91 | loop fusion | bytes 4194312 | tf_op jit(solution)/shard_map/jit(dynamic_index_in_dim)/dynamic_slice | solution.py:93
  14.4 0.7 copy.75
  15.1 1.9 %collective-permute-start = (bf16[16,256,128]{2,1,0:T(8,128)(2,1)S(1)}, bf16[16,256,128]{2,1,0:T(8,128)(2,1)}, u32[]{:S(2)}, u32[]{:S(2)}) collective-permute-start(bf16[16,256,128]{2,1,0:T(8,128)(2,1)S(1)} %bitcast.93), channel_id=1, source_target_pairs={{0,1},{1,0},{2,3},{3,2},{4,5},{5,4},{6,7},{7,6},{8,9},{9,8},{10,11... | collective-permute-start | bytes 3145736 | tf_op jit(solution)/shard_map/ppermute | solution.py:95
  17.0 2.6 %fusion.3 = bf16[2,32,8,128]{3,2,1,0:T(8,128)(2,1)S(1)} fusion(bf16[448,4096]{1,0:T(8,128)(2,1)} %param.8, bf16[16,448,16]{1,2,0:T(8,128)(2,1)S(1)} %copy-done, s32[]{:T(128)S(6)} %select_n.70), kind=kOutput, calls=%fused_computation.13 | convolution fusion | flops 58785792 | bytes 3817476 | tf_op jit(solution)/shard_map/dot_general | solution.py:40
  19.7 0.7 convolution_convert_fusion.5
  20.4 1.0 multiply_reduce_fusion
  21.4 0.6 copy.54
  22.1 0.7 copy.76
  22.7 0.8 broadcast_in_dim.10
  23.6 1.7 pad_maximum_fusion.1
  25.2 12.5 %all-to-all-start = ((bf16[32,19,128]{2,1,0:T(8,128)(2,1)}), bf16[32,19,128]{2,1,0:T(8,128)(2,1)}, u32[]{:S(2)}, u32[]{:S(2)}) async-start(bf16[32,19,128]{2,1,0:T(8,128)(2,1)} %pad_maximum_fusion.1), calls=%async_computation | async-start | bytes 393216 | tf_op jit(solution)/shard_map/all_to_all | solution.py:46
  37.7 0.7 copy.52
  38.6 0.7 sub.16
  39.8 11.2 %all-to-all-done = bf16[32,19,128]{2,1,0:T(8,128)(2,1)} async-done(((bf16[32,19,128]{2,1,0:T(8,128)(2,1)}), bf16[32,19,128]{2,1,0:T(8,128)(2,1)}, u32[]{:S(2)}, u32[]{:S(2)}) %all-to-all-start) | async-done | bytes 155680 | tf_op jit(solution)/shard_map/all_to_all | solution.py:46
  51.0 1.0 convert_reduce_fusion.1
  52.0 0.9 fusion.6
  53.0 0.6 broadcast_in_dim.12
  53.6 8.5 %all-to-all-start.1 = ((f32[16,2,128]{2,1,0:T(2,128)}), f32[16,2,128]{2,1,0:T(2,128)S(1)}, u32[]{:S(2)}, u32[]{:S(2)}) async-start(f32[16,2,128]{2,1,0:T(2,128)} %broadcast_in_dim.12), calls=%async_computation.1 | async-start | bytes 32768 | tf_op jit(solution)/shard_map/all_to_all | solution.py:46
  62.0 1.8 %fusion.2 = bf16[16,256]{1,0:T(8,128)(2,1)} fusion(bf16[16,448,16]{1,2,0:T(8,128)(2,1)S(1)} %copy-done, bf16[256,448]{0,1:T(8,128)(2,1)} %param.7, f32[16,256]{1,0:T(8,128)S(1)} %fusion.21), kind=kOutput, calls=%fused_computation.11 | convolution fusion | flops 58847232 | bytes 483328 | tf_op jit(solution)/shard_map/dot_general | solution.py:40
  63.8 4.6 %all-to-all-done.1 = f32[16,2,128]{2,1,0:T(2,128)S(1)} async-done(((f32[16,2,128]{2,1,0:T(2,128)}), f32[16,2,128]{2,1,0:T(2,128)S(1)}, u32[]{:S(2)}, u32[]{:S(2)}) %all-to-all-start.1) | async-done | bytes 16416 | tf_op jit(solution)/shard_map/all_to_all | solution.py:46
  68.4 1.9 %constant_dynamic-update-slice_fusion.4 = (bf16[320,128]{1,0:T(8,128)(2,1)S(1)}, bf16[256,128]{1,0:T(8,128)(2,1)S(1)}, f32[256,128]{1,0:T(8,128)}) fusion(bf16[256,128]{1,0:T(8,128)(2,1)} %param.13, bf16[16,128]{1,0:T(8,128)(2,1)} %param.11, f32[16,128]{1,0:T(8,128)S(1)} %bitcast.103, f32[128]{0:T(128)S(1)} %get-tuple-element.17, s32[256]{0:T(256)} %copy-done.9, ...), kind=kOutput, calls=%fused_computation.63 | convolution fusion | flops 6412287 | bytes 341632 | tf_op jit(solution)/shard_map/dot_general | solution.py:40
  70.3 0.7 constant_dynamic-update-slice_fusion.3
  71.0 0.7 constant_dynamic-update-slice_fusion.2
  71.9 1.9 %fusion = bf16[16,256,128]{2,1,0:T(8,128)(2,1)S(1)} fusion(bf16[16,256,128]{2,1,0:T(8,128)(2,1)} %collective-permute-done, bf16[256,16,1,128]{3,2,1,0:T(2,128)(2,1)S(1)} %copy-done.2), kind=kLoop, calls=%fused_computation.4 | loop fusion | flops 2097152 | bytes 3145728 | tf_op jit(solution)/shard_map/convert_element_type | solution.py:96
  73.9 2.4 %collective-permute-start.1 = (bf16[8,256,128]{2,1,0:T(8,128)(2,1)S(1)}, bf16[8,256,128]{2,1,0:T(8,128)(2,1)S(1)}, u32[]{:S(2)}, u32[]{:S(2)}) collective-permute-start(bf16[8,256,128]{2,1,0:T(8,128)(2,1)S(1)} %dynamic-slice_bitcast_fusion), channel_id=1, source_target_pairs={{0,16},{1,17},{2,18},{3,19},{4,20},{5,21},{6,22},{7,23},{8,24},{9,... | collective-permute-start | bytes 1572872 | tf_op jit(solution)/shard_map/ppermute | solution.py:100
  76.4 12.0 %collective-permute-done.1 = bf16[8,256,128]{2,1,0:T(8,128)(2,1)S(1)} collective-permute-done((bf16[8,256,128]{2,1,0:T(8,128)(2,1)S(1)}, bf16[8,256,128]{2,1,0:T(8,128)(2,1)S(1)}, u32[]{:S(2)}, u32[]{:S(2)}) %collective-permute-start.1) | collective-permute-done | bytes 524320 | tf_op jit(solution)/shard_map/ppermute | solution.py:100
  88.7 33.5 %all_to_all.25 = bf16[8,576,128]{2,1,0:T(8,128)(2,1)S(1)} all-to-all(bf16[8,576,128]{2,1,0:T(8,128)(2,1)S(1)} %pad_maximum_fusion), channel_id=1, replica_groups={{0,2,4,6,8,10,12,14},{1,3,5,7,9,11,13,15},{16,18,20,22,24,26,28,30},{17..., dimensions={0} | all-to-all | bytes 2359296 | tf_op jit(solution)/shard_map/all_to_all | solution.py:46
  122.3 2.3 %collective-permute-start.2 = (bf16[64,128]{0,1:T(8,128)(2,1)S(1)}, bf16[64,128]{0,1:T(8,128)(2,1)S(1)}, u32[]{:S(2)}, u32[]{:S(2)}) collective-permute-start(bf16[64,128]{0,1:T(8,128)(2,1)S(1)} %convert_element_type.188), channel_id=1, source_target_pairs={{0,16},{1,17},{2,18},{3,19},{4,20},{5,21},{6,22},{7,23},{8,24},{9,... | collective-permute-start | bytes 49160 | tf_op jit(solution)/shard_map/ppermute | solution.py:125
  124.7 5.0 %collective-permute-done.2 = bf16[64,128]{0,1:T(8,128)(2,1)S(1)} collective-permute-done((bf16[64,128]{0,1:T(8,128)(2,1)S(1)}, bf16[64,128]{0,1:T(8,128)(2,1)S(1)}, u32[]{:S(2)}, u32[]{:S(2)}) %collective-permute-start.2) | collective-permute-done | bytes 16416 | tf_op jit(solution)/shard_map/ppermute | solution.py:125
  129.7 1.9 %collective-permute-start.3 = (bf16[64,128]{0,1:T(8,128)(2,1)S(1)}, bf16[64,128]{0,1:T(8,128)(2,1)S(1)}, u32[]{:S(2)}, u32[]{:S(2)}) collective-permute-start(bf16[64,128]{0,1:T(8,128)(2,1)S(1)} %fusion.16), channel_id=1, source_target_pairs={{0,1},{1,0},{2,3},{3,2},{4,5},{5,4},{6,7},{7,6},{8,9},{9,8},{10,11... | collective-permute-start | bytes 49160 | tf_op jit(solution)/shard_map/ppermute | solution.py:126
  131.7 1.1 collective-permute-done.3
  133.9 0.9 multiply_convert_fusion.2
  135.0 0.8 fusion.11
  135.9 5.4 %all-to-all-start.3 = ((bf16[16,16,640]{2,1,0:T(8,128)(2,1)}), bf16[16,16,640]{2,1,0:T(8,128)(2,1)S(1)}, u32[]{:S(2)}, u32[]{:S(2)}) async-start(bf16[16,16,640]{2,1,0:T(8,128)(2,1)} %fusion.11), calls=%async_computation.3 | async-start | bytes 655360 | tf_op jit(solution)/shard_map/all_to_all | solution.py:46
  141.4 2.3 %collective-permute-start.4 = (bf16[8,256,128]{2,1,0:T(8,128)(2,1)S(1)}, bf16[8,256,128]{2,1,0:T(8,128)(2,1)S(1)}, u32[]{:S(2)}, u32[]{:S(2)}) collective-permute-start(bf16[8,256,128]{2,1,0:T(8,128)(2,1)S(1)} %get-tuple-element.10), channel_id=1, source_target_pairs={{0,16},{1,17},{2,18},{3,19},{4,20},{5,21},{6,22},{7,23},{8,24},{9,... | collective-permute-start | bytes 1572872 | tf_op jit(solution)/shard_map/ppermute | solution.py:157
  143.8 9.5 %all-to-all-done.3 = bf16[16,16,640]{2,1,0:T(8,128)(2,1)S(1)} async-done(((bf16[16,16,640]{2,1,0:T(8,128)(2,1)}), bf16[16,16,640]{2,1,0:T(8,128)(2,1)S(1)}, u32[]{:S(2)}, u32[]{:S(2)}) %all-to-all-start.3) | async-done | bytes 327712 | tf_op jit(solution)/shard_map/all_to_all | solution.py:46
  153.3 0.8 broadcast_in_dim.14
  154.0 4.7 %all-to-all-start.4 = ((bf16[16,16,640]{2,1,0:T(8,128)(2,1)}), bf16[16,16,640]{2,1,0:T(8,128)(2,1)S(1)}, u32[]{:S(2)}, u32[]{:S(2)}) async-start(bf16[16,16,640]{2,1,0:T(8,128)(2,1)} %broadcast_in_dim.14), calls=%async_computation.4 | async-start | bytes 655360 | tf_op jit(solution)/shard_map/all_to_all | solution.py:46
  158.7 1.7 collective-permute-done.4
  161.1 1.9 %collective-permute-start.5 = (bf16[16,256,128]{1,2,0:T(8,128)(2,1)S(1)}, bf16[16,256,128]{1,2,0:T(8,128)(2,1)S(1)}, u32[]{:S(2)}, u32[]{:S(2)}) collective-permute-start(bf16[16,256,128]{1,2,0:T(8,128)(2,1)S(1)} %bitcast.88), channel_id=1, source_target_pairs={{0,1},{1,0},{2,3},{3,2},{4,5},{5,4},{6,7},{7,6},{8,9},{9,8},{10,11... | collective-permute-start | bytes 3145736 | tf_op jit(solution)/shard_map/ppermute | solution.py:161
  163.3 6.5 %all-to-all-done.4 = bf16[16,16,640]{2,1,0:T(8,128)(2,1)S(1)} async-done(((bf16[16,16,640]{2,1,0:T(8,128)(2,1)}), bf16[16,16,640]{2,1,0:T(8,128)(2,1)S(1)}, u32[]{:S(2)}, u32[]{:S(2)}) %all-to-all-start.4) | async-done | bytes 327712 | tf_op jit(solution)/shard_map/all_to_all | solution.py:46
  170.0 0.6 fusion.32
  170.6 0.7 slice_convert_fusion
  171.3 0.7 slice_bitcast_fusion
  172.2 1.8 %copy-done.1 = bf16[448,4096]{1,0:T(8,128)(2,1)S(1)} copy-done((bf16[448,4096]{1,0:T(8,128)(2,1)S(1)}, bf16[448,4096]{1,0:T(8,128)(2,1)}, u32[]{:S(2)}) %copy-start.1) | copy-done | bytes 3670040
  174.0 1.8 %fusion.1 = bf16[256,448]{0,1:T(8,128)(2,1)} fusion(f32[256,448]{0,1:T(8,128)S(1)} %convolution_bitcast_fusion, bf16[448,4096]{1,0:T(8,128)(2,1)S(1)} %copy-done.1, bf16[256,4096]{0,1:T(8,128)(2,1)S(1)} %bitcast.92), kind=kOutput, calls=%fused_computation.7 | convolution fusion | flops 939753472 | bytes 6455296 | tf_op jit(solution)/shard_map/dot_general | solution.py:40
  (81 shorter events, 4.6 us)
Async XLA Ops:
  0.6 16.4 %copy-start = (bf16[16,448,16]{1,2,0:T(8,128)(2,1)S(1)}, bf16[16,448,16]{1,2,0:T(8,128)(2,1)}, u32[]{:S(2)}) copy-start(bf16[16,448,16]{1,2,0:T(8,128)(2,1)} %param.9) | copy-start | bytes 688132
  15.1 56.8 %collective-permute-start = (bf16[16,256,128]{2,1,0:T(8,128)(2,1)S(1)}, bf16[16,256,128]{2,1,0:T(8,128)(2,1)}, u32[]{:S(2)}, u32[]{:S(2)}) collective-permute-start(bf16[16,256,128]{2,1,0:T(8,128)(2,1)S(1)} %bitcast.93), channel_id=1, source_target_pairs={{0,1},{1,0},{2,3},{3,2},{4,5},{5,4},{6,7},{7,6},{8,9},{9,8},{10,11... | collective-permute-start | bytes 3145736 | tf_op jit(solution)/shard_map/ppermute | solution.py:95
  19.7 52.3 %copy-start.2 = (bf16[256,16,1,128]{3,2,1,0:T(2,128)(2,1)S(1)}, bf16[256,16,1,128]{3,2,1,0:T(2,128)(2,1)}, u32[]{:S(2)}) copy-start(bf16[256,16,1,128]{3,2,1,0:T(2,128)(2,1)} %get-tuple-element.7) | copy-start | bytes 3145732
  22.7 49.0 %copy-start.6 = (bf16[16,16,128]{2,1,0:T(8,128)(2,1)S(1)}, bf16[16,16,128]{2,1,0:T(8,128)(2,1)}, u32[]{:S(2)}) copy-start(bf16[16,16,128]{2,1,0:T(8,128)(2,1)} %param.10) | copy-start | bytes 196612
  25.2 25.8 %all-to-all-start = ((bf16[32,19,128]{2,1,0:T(8,128)(2,1)}), bf16[32,19,128]{2,1,0:T(8,128)(2,1)}, u32[]{:S(2)}, u32[]{:S(2)}) async-start(bf16[32,19,128]{2,1,0:T(8,128)(2,1)} %pad_maximum_fusion.1), calls=%async_computation | async-start | bytes 393216 | tf_op jit(solution)/shard_map/all_to_all | solution.py:46
  38.6 0.7 copy-start.11
  39.2 0.6 copy-start.13
  39.3 0.6 copy-start.9
  53.6 14.8 %all-to-all-start.1 = ((f32[16,2,128]{2,1,0:T(2,128)}), f32[16,2,128]{2,1,0:T(2,128)S(1)}, u32[]{:S(2)}, u32[]{:S(2)}) async-start(f32[16,2,128]{2,1,0:T(2,128)} %broadcast_in_dim.12), calls=%async_computation.1 | async-start | bytes 32768 | tf_op jit(solution)/shard_map/all_to_all | solution.py:46
  68.4 3.5 %copy-start.7 = (f32[16,1,128]{2,1,0:T(1,128)}, f32[16,1,128]{2,1,0:T(1,128)S(1)}, u32[]{:S(2)}) copy-start(f32[16,1,128]{2,1,0:T(1,128)S(1)} %get-tuple-element.18) | copy-start | bytes 24580
  68.4 3.5 %copy-start.15 = (f32[128]{0:T(128)}, f32[128]{0:T(128)S(1)}, u32[]{:S(2)}) copy-start(f32[128]{0:T(128)S(1)} %get-tuple-element.17) | copy-start | bytes 1540
  73.9 14.4 %collective-permute-start.1 = (bf16[8,256,128]{2,1,0:T(8,128)(2,1)S(1)}, bf16[8,256,128]{2,1,0:T(8,128)(2,1)S(1)}, u32[]{:S(2)}, u32[]{:S(2)}) collective-permute-start(bf16[8,256,128]{2,1,0:T(8,128)(2,1)S(1)} %dynamic-slice_bitcast_fusion), channel_id=1, source_target_pairs={{0,16},{1,17},{2,18},{3,19},{4,20},{5,21},{6,22},{7,23},{8,24},{9,... | collective-permute-start | bytes 1572872 | tf_op jit(solution)/shard_map/ppermute | solution.py:100
  88.6 44.6 %copy-start.3 = (bf16[256,448]{0,1:T(8,128)(2,1)S(1)}, bf16[256,448]{0,1:T(8,128)(2,1)}, u32[]{:S(2)}) copy-start(bf16[256,448]{0,1:T(8,128)(2,1)} %param.7) | copy-start | bytes 688132
  122.2 11.7 %copy-start.5 = (f32[256,128]{1,0:T(8,128)S(1)}, f32[256,128]{1,0:T(8,128)}, u32[]{:S(2)}) copy-start(f32[256,128]{1,0:T(8,128)} %get-tuple-element.19) | copy-start | bytes 393220
  122.3 12.5 %copy-start.4 = (bf16[256,128]{1,0:T(8,128)(2,1)S(1)}, bf16[256,128]{1,0:T(8,128)(2,1)}, u32[]{:S(2)}) copy-start(bf16[256,128]{1,0:T(8,128)(2,1)} %param.13) | copy-start | bytes 196612
  122.3 12.4 %copy-start.10 = (s32[256]{0:T(256)S(1)}, s32[256]{0:T(256)}, u32[]{:S(2)}) copy-start(s32[256]{0:T(256)} %copy-done.9) | copy-start | bytes 3076
  122.3 12.4 %copy-start.12 = (s32[16]{0:T(128)S(1)}, s32[16]{0:T(128)}, u32[]{:S(2)}) copy-start(s32[16]{0:T(128)} %copy-done.11) | copy-start | bytes 196
  122.3 12.4 %copy-start.14 = (s32[16]{0:T(128)S(1)}, s32[16]{0:T(128)}, u32[]{:S(2)}) copy-start(s32[16]{0:T(128)} %copy-done.13) | copy-start | bytes 196
  122.3 7.3 %collective-permute-start.2 = (bf16[64,128]{0,1:T(8,128)(2,1)S(1)}, bf16[64,128]{0,1:T(8,128)(2,1)S(1)}, u32[]{:S(2)}, u32[]{:S(2)}) collective-permute-start(bf16[64,128]{0,1:T(8,128)(2,1)S(1)} %convert_element_type.188), channel_id=1, source_target_pairs={{0,16},{1,17},{2,18},{3,19},{4,20},{5,21},{6,22},{7,23},{8,24},{9,... | collective-permute-start | bytes 49160 | tf_op jit(solution)/shard_map/ppermute | solution.py:125
  129.7 3.1 %collective-permute-start.3 = (bf16[64,128]{0,1:T(8,128)(2,1)S(1)}, bf16[64,128]{0,1:T(8,128)(2,1)S(1)}, u32[]{:S(2)}, u32[]{:S(2)}) collective-permute-start(bf16[64,128]{0,1:T(8,128)(2,1)S(1)} %fusion.16), channel_id=1, source_target_pairs={{0,1},{1,0},{2,3},{3,2},{4,5},{5,4},{6,7},{7,6},{8,9},{9,8},{10,11... | collective-permute-start | bytes 49160 | tf_op jit(solution)/shard_map/ppermute | solution.py:126
  135.9 17.4 %all-to-all-start.3 = ((bf16[16,16,640]{2,1,0:T(8,128)(2,1)}), bf16[16,16,640]{2,1,0:T(8,128)(2,1)S(1)}, u32[]{:S(2)}, u32[]{:S(2)}) async-start(bf16[16,16,640]{2,1,0:T(8,128)(2,1)} %fusion.11), calls=%async_computation.3 | async-start | bytes 655360 | tf_op jit(solution)/shard_map/all_to_all | solution.py:46
  141.4 19.0 %collective-permute-start.4 = (bf16[8,256,128]{2,1,0:T(8,128)(2,1)S(1)}, bf16[8,256,128]{2,1,0:T(8,128)(2,1)S(1)}, u32[]{:S(2)}, u32[]{:S(2)}) collective-permute-start(bf16[8,256,128]{2,1,0:T(8,128)(2,1)S(1)} %get-tuple-element.10), channel_id=1, source_target_pairs={{0,16},{1,17},{2,18},{3,19},{4,20},{5,21},{6,22},{7,23},{8,24},{9,... | collective-permute-start | bytes 1572872 | tf_op jit(solution)/shard_map/ppermute | solution.py:157
  154.0 15.8 %all-to-all-start.4 = ((bf16[16,16,640]{2,1,0:T(8,128)(2,1)}), bf16[16,16,640]{2,1,0:T(8,128)(2,1)S(1)}, u32[]{:S(2)}, u32[]{:S(2)}) async-start(bf16[16,16,640]{2,1,0:T(8,128)(2,1)} %broadcast_in_dim.14), calls=%async_computation.4 | async-start | bytes 655360 | tf_op jit(solution)/shard_map/all_to_all | solution.py:46
  160.4 9.6 %copy-start.8 = (f32[16,1,128]{2,1,0:T(1,128)S(1)}, f32[16,1,128]{2,1,0:T(1,128)}, u32[]{:S(2)}) copy-start(f32[16,1,128]{2,1,0:T(1,128)} %copy-done.7) | copy-start | bytes 24580
  160.4 9.6 %copy-start.16 = (f32[128]{0:T(128)S(1)}, f32[128]{0:T(128)}, u32[]{:S(2)}) copy-start(f32[128]{0:T(128)} %copy-done.15) | copy-start | bytes 1540
  161.1 10.9 %collective-permute-start.5 = (bf16[16,256,128]{1,2,0:T(8,128)(2,1)S(1)}, bf16[16,256,128]{1,2,0:T(8,128)(2,1)S(1)}, u32[]{:S(2)}, u32[]{:S(2)}) collective-permute-start(bf16[16,256,128]{1,2,0:T(8,128)(2,1)S(1)} %bitcast.88), channel_id=1, source_target_pairs={{0,1},{1,0},{2,3},{3,2},{4,5},{5,4},{6,7},{7,6},{8,9},{9,8},{10,11... | collective-permute-start | bytes 3145736 | tf_op jit(solution)/shard_map/ppermute | solution.py:161
  172.0 2.0 %copy-start.1 = (bf16[448,4096]{1,0:T(8,128)(2,1)S(1)}, bf16[448,4096]{1,0:T(8,128)(2,1)}, u32[]{:S(2)}) copy-start(bf16[448,4096]{1,0:T(8,128)(2,1)} %param.8) | copy-start | bytes 11010052

commit v2 on v1

v2 whole, which is shorter than its diff:
```python
import jax
import jax.numpy as jnp
from jax import lax
from jax.experimental import pallas as pl
from jax.experimental.pallas import tpu as pltpu
from jax.sharding import PartitionSpec as P


HIGHEST_MODE = lax.Precision.HIGHEST
EPSILON = 1e-06
F32 = jnp.float32
BF16 = jnp.bfloat16
I32 = jnp.int32
LANES = 128
HEAD = 24


def dot(a, b, ca, cb, precision=None):
    return lax.dot_general(
        a, b, (((ca,), (cb,)), ((), ())), precision=precision, preferred_element_type=F32
    )


def iota(shape, dim):
    return lax.broadcasted_iota(I32, shape, dim)


def shaped(*dims, dtype=BF16):
    return jax.ShapeDtypeStruct(dims, dtype)


def bounds(seg, adapters, first_token):
    marks, at = [], -first_token
    for a in range(adapters):
        marks.append((at, at + seg[a]))
        at = at + seg[a]
    return marks


def picked(spread, marks):
    rank = spread.shape[0] // len(marks)
    at = iota((rank, spread.shape[1]), 1)
    total = jnp.zeros((rank, spread.shape[1]), F32)
    for a, (lo, hi) in enumerate(marks):
        total += jnp.where((at >= lo) & (at < hi), spread[a * rank : (a + 1) * rank], 0.0)
    return total


def widened(rank_rows, marks):
    at = iota(rank_rows.shape, 1)
    wide = [jnp.where((at >= lo) & (at < hi), rank_rows, 0.0) for lo, hi in marks]
    return jnp.concatenate(wide, axis=0).astype(BF16)


def packed(rows):
    return jnp.concatenate([rows[:, :LANES], rows[:, LANES:]], axis=0)


def unpacked(rows):
    half = rows.shape[0] // 2
    return jnp.concatenate([rows[:half], rows[half:]], axis=1)


def token_scale_of(col_scale, marks, token_count):
    at = iota((token_count, LANES), 0)
    total = jnp.zeros((token_count, LANES), F32)
    for a, (lo, hi) in enumerate(marks):
        total += jnp.where((at >= lo) & (at < hi), col_scale[a : a + 1], 0.0)
    return total


def shift(block, pairs):
    return lax.ppermute(block, "tensor", pairs)


def call(kernel, out_shape, scalars=0, grid=(), in_specs=None, out_specs=None, scratch=(),
         flops=0, moved=0):
    return pl.pallas_call(
        kernel,
        out_shape=out_shape,
        grid_spec=pltpu.PrefetchScalarGridSpec(
            num_scalar_prefetch=scalars,
            grid=grid,
            in_specs=in_specs,
            out_specs=out_specs,
            scratch_shapes=list(scratch),
        ),
        cost_estimate=pl.CostEstimate(flops=flops, bytes_accessed=moved, transcendentals=0),
        compiler_params=pltpu.CompilerParams(vmem_limit_bytes=16 * 2**20),
    )


def whole(*dims):
    return pl.BlockSpec(dims, lambda *ids: (0,) * len(dims))


def first_kernel(where, tokens, weight, down, head, keep, give, gram, lines):
    rank = down.shape[1]
    count = tokens.shape[1]

    @pl.when(pl.program_id(0) == 0)
    def _():
        mine = down[0]
        lines[:count] = tokens[...].T
        lines[count:] = mine
        square = dot(mine, mine, 1, 1)
        tile = (iota((rank, LANES), 1) % rank == iota((rank, LANES), 0)).astype(F32)
        spread = dot(square, tile, 1, 0, HIGHEST_MODE)
        rows, cols = iota((rank, LANES), 0), iota((rank, LANES), 1)
        spread = jnp.where(cols // rank == rows % 8, spread, 0.0)
        gram[0:1, :] = jnp.sum(spread[:8], axis=0, keepdims=True)
        gram[1:2, :] = jnp.sum(spread[8:], axis=0, keepdims=True)

    block = weight[...]
    both = dot(lines[...], block, 1, 0)
    share = 32
    pieces = weight.shape[0] // share
    part = weight[pl.ds(pl.multiple_of(jnp.minimum(where[0], pieces - 1) * share, share), share), :]
    part = part.astype(F32)
    squares = jnp.sum(part * part, axis=0, keepdims=True) * (where[0] < pieces).astype(F32)
    row = iota((8, LANES), 0)
    for k in range(4):
        lanes = slice(k * LANES, (k + 1) * LANES)
        tail = jnp.where(
            row == 0,
            squares[:, lanes],
            jnp.where(row == 1, gram[0:1, :], jnp.where(row == 2, gram[1:2, :], 0.0)),
        )
        head[k] = jnp.concatenate([both[count:, lanes], tail], axis=0).astype(BF16)

    base = both[:count].astype(BF16)

    @pl.when(where[1] == 0)
    def _():
        for k in range(2):
            keep[k] = base[:, 2 * k * LANES : (2 * k + 1) * LANES]
            give[k] = base[:, (2 * k + 1) * LANES : (2 * k + 2) * LANES]

    @pl.when(where[1] != 0)
    def _():
        for k in range(2):
            give[k] = base[:, 2 * k * LANES : (2 * k + 1) * LANES]
            keep[k] = base[:, (2 * k + 1) * LANES : (2 * k + 2) * LANES]


def low_kernel(where, seg, tokens, down, low):
    marks = bounds(seg, seg.shape[0], where[0] * tokens.shape[1])
    spread = dot(down[...], tokens[...], 1, 0)
    low[...] = packed(picked(spread, marks)).astype(BF16)


def halves_kernel(where, keep_a, got_a, keep_b, got_b, keep, give):
    keep[...] = (keep_a[...].astype(F32) + got_a[...].astype(F32)).astype(BF16)
    give[...] = (keep_b[...].astype(F32) + got_b[...].astype(F32)).astype(BF16)


def squares_kernel(where, head, up, second):
    rank = up.shape[1]
    total = jnp.sum(head[...].astype(F32), axis=0)
    factor = up[0].astype(F32)
    rows, cols = iota((rank, LANES), 0), iota((rank, LANES), 1)
    spread = jnp.where(rows < 8, total[rank + 1 : rank + 2], total[rank + 2 : rank + 3])
    spread = jnp.where(cols // rank == rows % 8, spread, 0.0)
    tiled = jnp.concatenate([factor] * (LANES // rank), axis=0)
    gram_up = dot(spread, tiled, 1, 0, HIGHEST_MODE)
    mine = jnp.sum(factor * (2.0 * total[:rank] + gram_up), axis=0, keepdims=True)
    both = jnp.concatenate([mine, total[rank : rank + 1]], axis=0)
    second[...] = jnp.broadcast_to(both[None], second.shape)


def scale_kernel(where, seg, second, magnitude, cotangent, up, low, keep, got,
                 third, scaled, norms, every):
    count = cotangent.shape[0]

    @pl.when(pl.program_id(0) == 0)
    def _():
        marks = bounds(seg, seg.shape[0], where[0] * count)
        parts = second[...]
        squares = parts[:, 0, :] + jnp.sum(parts[:, 1, :], axis=0, keepdims=True)
        col_norms = jnp.sqrt(jnp.maximum(squares, 0.0) + EPSILON)
        norms[...] = col_norms
        scale = token_scale_of(magnitude[...].astype(F32) / col_norms, marks, count)
        grad = (cotangent[...].astype(F32) * scale).astype(BF16)
        scaled[...] = grad
        spread = dot(up[...], grad, 1, 1)
        back = packed(picked(spread, marks)).astype(BF16)
        every[...] = jnp.concatenate([grad, low[...], back], axis=0)

    third[0, :count] = (keep[0].astype(F32) + got[0].astype(F32)).astype(BF16)
    third[0, count:] = every[...]


def sums_kernel(rank_rows, base_rows, ranks, base):
    ranks[...] = jnp.sum(rank_rows[...].astype(F32), axis=0).astype(BF16)
    base[...] = jnp.sum(base_rows[...].astype(F32), axis=0)


def grads_kernel(where, seg, ranks, got, base, norms, magnitude, cotangent, scaled, up, tokens,
                 fourth, projected, back_wide):
    adapters = seg.shape[0]
    own_rows, count = tokens.shape
    rank = up.shape[0] // adapters
    marks = bounds(seg, adapters, where[0] * count)
    total = ranks[...].astype(F32) + got[...].astype(F32)
    low = widened(unpacked(total[: 2 * rank]), marks)
    back = widened(unpacked(total[2 * rank :]), marks)
    back_wide[...] = back
    hidden = base[...] + dot(low, up[...], 0, 0)
    scale = token_scale_of(magnitude[...].astype(F32) / norms[...], marks, count)
    projected[...] = (hidden * scale).astype(BF16)
    weighted = cotangent[...].astype(F32) * hidden
    at = iota((count, LANES), 0)
    row = iota((rank, LANES // 2), 0)
    down_part = dot(back, tokens[...], 1, 1).astype(BF16)
    up_part = dot(low, scaled[...], 1, 0).astype(BF16)
    pad = -own_rows % LANES
    for a, (lo, hi) in enumerate(marks):
        mag = jnp.sum(jnp.where((at >= lo) & (at < hi), weighted, 0.0), axis=0, keepdims=True)
        halves = jnp.where(row == 0, mag[:, :pad], jnp.where(row == 1, mag[:, pad:], 0.0))
        lines = slice(a * rank, (a + 1) * rank)
        fourth[a] = jnp.concatenate(
            [down_part[lines], halves.astype(BF16), up_part[lines]], axis=1
        )


def total_kernel(arrived, fifth):
    total = jnp.sum(arrived[...].astype(F32), axis=0).astype(BF16)
    fifth[...] = jnp.broadcast_to(total[None], fifth.shape)


def final_kernel(fifth, norms, grad_down, grad_up, grad_magnitude):
    own_rows = grad_down.shape[2]
    pad = -own_rows % LANES
    grad_down[...] = fifth[:, :, :own_rows]
    grad_up[...] = fifth[:, :, own_rows + pad :].astype(F32)
    halves = fifth[:, :, own_rows : own_rows + pad].astype(F32)
    total = jnp.concatenate([halves[:, 0, :], halves[:, 1, :]], axis=1)
    grad_magnitude[...] = total / norms[...]


def tokens_kernel(where, a0, a1, b0, b1, w0, w1, w2, w3, back, down, out, total):
    step = pl.program_id(0)

    @pl.when(step == 0)
    def _():
        total[...] = dot(down[...], back[...], 0, 0)

    left = jnp.concatenate([a0[0], a1[0], b0[0], b1[0]], axis=1)
    right = jnp.concatenate([w0[...], w1[...], w2[...], w3[...]], axis=1)
    total[...] += dot(right, left, 1, 1)

    @pl.when(step == pl.num_programs(0) - 1)
    def _():
        out[...] = total[...].astype(BF16)


def exchange(blocks, axis, groups=None):
    return lax.all_to_all(blocks, axis, 0, 0, tiled=True, axis_index_groups=groups)


def local(tokens, base_weight, adapter_down, adapter_up, magnitude, seg_lengths, cotangent):
    count, own_rows = tokens.shape
    adapters, _, rank = adapter_down.shape
    width = adapter_up.shape[2]
    full = base_weight.shape[1]
    size = full // width
    zs = size // 4
    wide = adapters * rank
    me_dp = lax.axis_index("dp")
    me = lax.axis_index("tensor")
    core, hi = me % 2, me // (2 * zs)
    where = jnp.stack([me_dp, core, hi]).astype(I32)
    core_pairs = [(i, i ^ 1) for i in range(size)]
    hi_pairs = [(i, (i + size // 2) % size) for i in range(size)]
    z_groups = [[h * 2 * zs + z * 2 + c for z in range(zs)] for h in range(2) for c in range(2)]

    turned = tokens.T
    down_rows = jnp.transpose(adapter_down, (0, 2, 1))
    down_flat = down_rows.reshape(wide, own_rows)
    up_own = adapter_up.reshape(wide, width)

    head, keep, give = call(
        first_kernel,
        [shaped(size, HEAD, width), shaped(size // 2, count, width), shaped(size // 2, count, width)],
        scalars=1,
        grid=(size // 4,),
        in_specs=[
            whole(own_rows, count),
            pl.BlockSpec((own_rows, 4 * width), lambda i, s: (0, i)),
            pl.BlockSpec((1, rank, own_rows), lambda i, s: (s[0], 0, 0)),
        ],
        out_specs=[
            pl.BlockSpec((4, HEAD, width), lambda i, s: (i, 0, 0)),
            pl.BlockSpec((2, count, width), lambda i, s: (i, 0, 0)),
            pl.BlockSpec((2, count, width), lambda i, s: (i, 0, 0)),
        ],
        scratch=[pltpu.VMEM((8, width), F32), pltpu.VMEM((count + rank, own_rows), BF16)],
        flops=2 * count * own_rows * full,
        moved=2 * own_rows * full,
    )(where, turned, base_weight, down_rows)
    head = exchange(head, "tensor")
    got = shift(give, core_pairs)
    low = call(
        low_kernel,
        shaped(2 * rank, width),
        scalars=2,
        grid=(1,),
        in_specs=[whole(own_rows, count), whole(wide, own_rows)],
        out_specs=whole(2 * rank, width),
        flops=2 * count * own_rows * wide,
        moved=4 * count * own_rows,
    )(where, seg_lengths, turned, down_flat)

    mine = pl.BlockSpec((2, count, width), lambda i, s: (s[2] * (zs // 2) + i, 0, 0))
    theirs = pl.BlockSpec((2, count, width), lambda i, s: ((1 - s[2]) * (zs // 2) + i, 0, 0))
    out = pl.BlockSpec((2, count, width), lambda i, s: (i, 0, 0))
    keep, give = call(
        halves_kernel,
        [shaped(zs, count, width)] * 2,
        scalars=1,
        grid=(zs // 2,),
        in_specs=[mine, mine, theirs, theirs],
        out_specs=[out, out],
        moved=12 * zs * count * width,
    )(where, keep, got, keep, got)
    got = shift(give, hi_pairs)

    second = call(
        squares_kernel,
        shaped(adapters, 2, width, dtype=F32),
        scalars=1,
        grid=(1,),
        in_specs=[
            whole(size, HEAD, width),
            pl.BlockSpec((1, rank, width), lambda i, s: (s[0], 0, 0)),
        ],
        out_specs=whole(adapters, 2, width),
        moved=2 * size * HEAD * width,
    )(where, head, adapter_up)
    second = exchange(second, "dp")

    rows = 2 * count + 4 * rank
    third, scaled, norms = call(
        scale_kernel,
        [shaped(zs, rows, width), shaped(count, width), shaped(adapters, width, dtype=F32)],
        scalars=2,
        grid=(zs,),
        in_specs=[
            whole(adapters, 2, width),
            whole(adapters, width),
            whole(count, width),
            whole(wide, width),
            whole(2 * rank, width),
            pl.BlockSpec((1, count, width), lambda i, *s: (i, 0, 0)),
            pl.BlockSpec((1, count, width), lambda i, *s: (i, 0, 0)),
        ],
        out_specs=[
            pl.BlockSpec((1, rows, width), lambda i, *s: (i, 0, 0)),
            whole(count, width),
            whole(adapters, width),
        ],
        scratch=[pltpu.VMEM((count + 4 * rank, width), BF16)],
        flops=2 * count * wide * width,
        moved=2 * zs * rows * width,
    )(where, seg_lengths, second, magnitude, cotangent, up_own, low, keep, got)
    third = exchange(third, "tensor", z_groups)

    ranks, base = call(
        sums_kernel,
        [shaped(4 * rank, width), shaped(count, width, dtype=F32)],
        grid=(1,),
        in_specs=[
            pl.BlockSpec((zs, 4 * rank, width), lambda i: (0, 2 * count // (4 * rank), 0)),
            pl.BlockSpec((zs, count, width), lambda i: (0, 0, 0)),
        ],
        out_specs=[whole(4 * rank, width), whole(count, width)],
        moved=2 * zs * count * width,
    )(third, third)
    ranks = (ranks.astype(F32) + shift(ranks, hi_pairs).astype(F32)).astype(BF16)
    other = shift(ranks, core_pairs)
    gather_a = third[:, count : 2 * count]
    gather_b = shift(gather_a, hi_pairs)

    blocks = rank * 40
    fourth, projected, back_wide = call(
        grads_kernel,
        [shaped(adapters, rank, blocks), shaped(count, width), shaped(wide, count)],
        scalars=2,
        grid=(1,),
        in_specs=[
            whole(4 * rank, width),
            whole(4 * rank, width),
            whole(count, width),
            whole(adapters, width),
            whole(adapters, width),
            whole(count, width),
            whole(count, width),
            whole(wide, width),
            whole(own_rows, count),
        ],
        out_specs=[whole(adapters, rank, blocks), whole(count, width), whole(wide, count)],
        flops=2 * count * wide * (own_rows + 2 * width),
        moved=4 * adapters * rank * blocks,
    )(where, seg_lengths, ranks, other, base, norms, magnitude, cotangent, scaled, up_own, turned)
    fourth = exchange(fourth, "dp")
    gather_c = shift(gather_a, core_pairs)
    gather_d = shift(gather_b, core_pairs)

    fifth = call(
        total_kernel,
        shaped(adapters, rank, blocks),
        grid=(1,),
        in_specs=[whole(adapters, rank, blocks)],
        out_specs=whole(adapters, rank, blocks),
        moved=4 * adapters * rank * blocks,
    )(fourth)
    fifth = exchange(fifth, "dp")

    def column(x_bit, c_bit):
        return pl.BlockSpec(
            (own_rows, width),
            lambda i, s: (0, (s[2] ^ x_bit) * (2 * zs) + i * 2 + (s[1] ^ c_bit)),
        )

    block = pl.BlockSpec((1, count, width), lambda i, s: (i, 0, 0))
    grad_tokens = call(
        tokens_kernel,
        shaped(own_rows, count),
        scalars=1,
        grid=(zs,),
        in_specs=[block] * 4
        + [column(0, 0), column(1, 0), column(0, 1), column(1, 1)]
        + [whole(wide, count), whole(wide, own_rows)],
        out_specs=whole(own_rows, count),
        scratch=[pltpu.VMEM((own_rows, count), F32)],
        flops=2 * count * own_rows * (full + wide),
        moved=2 * own_rows * full,
    )(where, gather_a, gather_b, gather_c, gather_d, *[base_weight] * 4, back_wide, down_flat)

    grad_down, grad_up, grad_magnitude = call(
        final_kernel,
        [
            shaped(adapters, rank, own_rows),
            shaped(adapters, rank, width, dtype=F32),
            shaped(adapters, width, dtype=F32),
        ],
        grid=(1,),
        in_specs=[whole(adapters, rank, blocks), whole(adapters, width)],
        out_specs=[
            whole(adapters, rank, own_rows),
            whole(adapters, rank, width),
            whole(adapters, width),
        ],
        moved=4 * adapters * rank * blocks,
    )(fifth, norms)
    return (projected, grad_tokens.T, jnp.transpose(grad_down, (0, 2, 1)), grad_up, grad_magnitude)


def solution(mesh):
    placed = (
        P("dp", "tensor"),
        P("tensor", None),
        P(None, "tensor", None),
        P(None, None, "tensor"),
        P(None, "tensor"),
        P(),
        P("dp", "tensor"),
    )
    return jax.shard_map(
        local,
        mesh=mesh,
        in_specs=placed,
        out_specs=(
            P("dp", "tensor"),
            P("dp", "tensor"),
            P(None, "tensor", None),
            P(None, None, "tensor"),
            P(None, "tensor"),
        ),
        check_vma=False,
    )
```

time: 177 us -> 154 us (0.87)
  the two profiles are of different devices: /device:TPU:10 before, /device:TPU:8 now
where the time goes in v2:
time: 154 us; the launch traced here: 153 us
  blocking collectives  55.9 us (36%)
  starting transfers between devices  40.8 us (26%)
  waiting for transfers between devices  31.7 us (21%)
  Pallas kernels  17.9 us (12%)
  local copies, waits for them, and re-layouts  6.02 us (4%)
    all_to_all x2, blocking collectives, exchange(): lax.all_to_all(blocks, axis, 0, 0, tiled=True, axis_index_groups=groups)  55.9 us
    ppermute x7, waiting for transfers between devices, shift(): return lax.ppermute(block, 'tensor', pairs)  20.9 us
    all_to_all x3, starting transfers between devices, exchange(): lax.all_to_all(blocks, axis, 0, 0, tiled=True, axis_index_groups=groups)  20.4 us
    ppermute x7, starting transfers between devices, shift(): return lax.ppermute(block, 'tensor', pairs)  20.4 us
    all_to_all x3, waiting for transfers between devices, exchange(): lax.all_to_all(blocks, axis, 0, 0, tiled=True, axis_index_groups=groups)  10.8 us
    unnamed x20, local copies, waits for them, and re-layouts  5.99 us
    pallas_call x1, Pallas kernels, local(): call(tokens_kernel, shaped(own_rows, count), scalars=1, grid=(zs,), in_sp...  5.51 us
    pallas_call x1, Pallas kernels, local(): call(first_kernel, [shaped(size, HEAD, width), shaped(size // 2, count, w...  3.89 us
  transfers between devices with their start and end apart: 10, of which 6 were waited for; matrix products, arithmetic and copies ran while one was open for 0% of the time, Pallas kernels for 5%

profile of v2, /device:TPU:8, one launch (start us, length us, event | category | flops | bytes accessed | tf_op | source)
XLA Modules:
  0.0 153.2 jit_solution(15980735099801588806)
XLA Ops:
  0.7 0.1 pad_add_fusion.where
  0.7 0.0 copy-start
  0.7 2.0 %copy-done = bf16[448,4096]{1,0:T(8,128)(2,1)S(1)} copy-done((bf16[448,4096]{1,0:T(8,128)(2,1)S(1)}, bf16[448,4096]{1,0:T(8,128)(2,1)}, u32[]{:S(2)}) %copy-start) | copy-done | bytes 3670040
  2.8 0.9 copy-done.2
  3.7 0.0 copy-start.4
  3.7 0.9 copy-done.4
  4.7 3.9 %shard_map.110 = (bf16[32,24,128]{2,1,0:T(8,128)(2,1)S(1)}, bf16[16,256,128]{2,1,0:T(8,128)(2,1)S(1)}, bf16[16,256,128]{2,1,0:T(8,128)(2,1)S(1)}) custom-call(s32[3]{0:T(128)S(1)} %pad_add_fusion.where, bf16[448,256]{1,0:T(8,128)(2,1)S(1)} %bitcast.13, bf16[448,4096]{1,0:T(8,128)(2,1)S(1)} %copy-done, bf16[16,16,448]{2,1,0:T(8,128)(2,1)S(1)} %bitcast.10), custom_call_target="tpu_custom_call" | custom-call | flops 939524096 | bytes 3670016 | tf_op jit(solution)/shard_map/pallas_call | solution.py:282
  8.6 1.9 %collective-permute-start = (bf16[16,256,128]{2,1,0:T(8,128)(2,1)S(1)}, bf16[16,256,128]{2,1,0:T(8,128)(2,1)S(1)}, u32[]{:S(2)}, u32[]{:S(2)}) collective-permute-start(bf16[16,256,128]{2,1,0:T(8,128)(2,1)S(1)} %get-tuple-element.23), channel_id=1, source_target_pairs={{0,1},{1,0},{2,3},{3,2},{4,5},{5,4},{6,7},{7,6},{8,9},{9,8},{10,11... | collective-permute-start | bytes 3145736 | tf_op jit(solution)/shard_map/ppermute | solution.py:73
  10.5 2.6 %collective-permute-done.got_a.got_b = bf16[16,256,128]{2,1,0:T(8,128)(2,1)S(1)} collective-permute-done((bf16[16,256,128]{2,1,0:T(8,128)(2,1)S(1)}, bf16[16,256,128]{2,1,0:T(8,128)(2,1)S(1)}, u32[]{:S(2)}, u32[]{:S(2)}) %collective-permute-start) | collective-permute-done | bytes 1048608 | tf_op jit(solution)/shard_map/ppermute | solution.py:73
  13.1 0.9 shard_map.113
  14.0 0.0 copy-start.7
  14.0 0.0 copy-start.8
  14.0 5.1 %collective-permute-start.1 = (bf16[8,256,128]{2,1,0:T(8,128)(2,1)S(1)}, bf16[8,256,128]{2,1,0:T(8,128)(2,1)S(1)}, u32[]{:S(2)}, u32[]{:S(2)}) collective-permute-start(bf16[8,256,128]{2,1,0:T(8,128)(2,1)S(1)} %get-tuple-element.25), channel_id=1, source_target_pairs={{0,16},{1,17},{2,18},{3,19},{4,20},{5,21},{6,22},{7,23},{8,24},{9,... | collective-permute-start | bytes 1572872 | tf_op jit(solution)/shard_map/ppermute | solution.py:73
  19.1 23.8 %all_to_all.25.head = bf16[32,24,128]{2,1,0:T(8,128)(2,1)S(1)} all-to-all(bf16[32,24,128]{2,1,0:T(8,128)(2,1)S(1)} %get-tuple-element.21), channel_id=1, replica_groups=mesh['dp'=16,'tensor'=32] {'tensor'}, dimensions={0} | all-to-all | bytes 393216 | tf_op jit(solution)/shard_map/all_to_all | solution.py:258
  42.9 0.0 copy-done.6
  42.9 1.3 shard_map.111
  44.2 8.4 %all-to-all-start.1 = ((f32[16,2,128]{2,1,0:T(2,128)}), f32[16,2,128]{2,1,0:T(2,128)S(1)}, u32[]{:S(2)}, u32[]{:S(2)}) async-start(f32[16,2,128]{2,1,0:T(2,128)} %shard_map.111), calls=%async_computation.1 | async-start | bytes 32768 | tf_op jit(solution)/shard_map/all_to_all | solution.py:258
  52.7 0.0 copy-done.3
  52.7 0.0 copy-done.5
  52.7 0.0 copy-done.9
  52.7 0.8 shard_map.112.low
  53.5 6.4 %all-to-all-done.1.second = f32[16,2,128]{2,1,0:T(2,128)S(1)} async-done(((f32[16,2,128]{2,1,0:T(2,128)}), f32[16,2,128]{2,1,0:T(2,128)S(1)}, u32[]{:S(2)}, u32[]{:S(2)}) %all-to-all-start.1) | async-done | bytes 16416 | tf_op jit(solution)/shard_map/all_to_all | solution.py:258
  59.8 0.0 collective-permute-done.1.got
  59.8 0.0 copy-done.7
  59.8 0.0 copy-done.8
  59.9 1.4 shard_map.114
  61.3 32.1 %all_to_all.26.rank_rows.base_rows = bf16[8,576,128]{2,1,0:T(8,128)(2,1)S(1)} all-to-all(bf16[8,576,128]{2,1,0:T(8,128)(2,1)S(1)} %get-tuple-element.26), channel_id=1, replica_groups={{0,2,4,6,8,10,12,14},{1,3,5,7,9,11,13,15},{16,18,20,22,24,26,28,30},{17..., dimensions={0} | all-to-all | bytes 2359296 | tf_op jit(solution)/shard_map/all_to_all | solution.py:258
  93.4 0.1 shard_map.115
  93.5 3.7 %collective-permute-start.2 = (bf16[64,128]{1,0:T(8,128)(2,1)S(1)}, bf16[64,128]{1,0:T(8,128)(2,1)S(1)}, u32[]{:S(2)}, u32[]{:S(2)}) collective-permute-start(bf16[64,128]{1,0:T(8,128)(2,1)S(1)} %get-tuple-element.27), channel_id=1, source_target_pairs={{0,16},{1,17},{2,18},{3,19},{4,20},{5,21},{6,22},{7,23},{8,24},{9,... | collective-permute-start | bytes 49160 | tf_op jit(solution)/shard_map/ppermute | solution.py:73
  97.2 3.5 %collective-permute-done.2 = bf16[64,128]{1,0:T(8,128)(2,1)S(1)} collective-permute-done((bf16[64,128]{1,0:T(8,128)(2,1)S(1)}, bf16[64,128]{1,0:T(8,128)(2,1)S(1)}, u32[]{:S(2)}, u32[]{:S(2)}) %collective-permute-start.2) | collective-permute-done | bytes 16416 | tf_op jit(solution)/shard_map/ppermute | solution.py:73
  100.7 1.9 %collective-permute-start.3 = (bf16[64,128]{1,0:T(8,128)(2,1)S(1)}, bf16[64,128]{1,0:T(8,128)(2,1)S(1)}, u32[]{:S(2)}, u32[]{:S(2)}) collective-permute-start(bf16[64,128]{1,0:T(8,128)(2,1)S(1)} %add_convert_fusion.ranks), channel_id=1, source_target_pairs={{0,1},{1,0},{2,3},{3,2},{4,5},{5,4},{6,7},{7,6},{8,9},{9,8},{10,11... | collective-permute-start | bytes 49160 | tf_op jit(solution)/shard_map/ppermute | solution.py:73
  102.6 1.1 collective-permute-done.3.got
  103.8 2.4 %shard_map.116 = (bf16[16,16,640]{2,1,0:T(8,128)(2,1)}, bf16[256,128]{1,0:T(8,128)(2,1)}, bf16[256,256]{1,0:T(8,128)(2,1)S(1)}) custom-call(s32[3]{0:T(128)S(1)} %pad_add_fusion.where, s32[16]{0:T(128)S(1)} %copy-done.9, bf16[64,128]{1,0:T(8,128)(2,1)S(1)} %add_convert_fusion.ranks, bf16[64,128]{1,0:T(8,128)(2,1)S(1)} %collective-permute-done.3.got, ...), custom_call_target="tpu_custom_call" | custom-call | flops 92274688 | bytes 655360 | tf_op jit(solution)/shard_map/pallas_call | solution.py:385
  106.2 4.5 %all-to-all-start.3 = ((bf16[16,16,640]{2,1,0:T(8,128)(2,1)}), bf16[16,16,640]{2,1,0:T(8,128)(2,1)S(1)}, u32[]{:S(2)}, u32[]{:S(2)}) async-start(bf16[16,16,640]{2,1,0:T(8,128)(2,1)} %get-tuple-element.33), calls=%async_computation.3 | async-start | bytes 655360 | tf_op jit(solution)/shard_map/all_to_all | solution.py:258
  110.7 4.0 %collective-permute-start.4 = (bf16[8,256,128]{2,1,0:T(8,128)(2,1)S(1)}, bf16[8,256,128]{2,1,0:T(8,128)(2,1)S(1)}, u32[]{:S(2)}, u32[]{:S(2)}) collective-permute-start(bf16[8,256,128]{2,1,0:T(8,128)(2,1)S(1)} %slice.4.a0), channel_id=1, source_target_pairs={{0,16},{1,17},{2,18},{3,19},{4,20},{5,21},{6,22},{7,23},{8,24},{9,... | collective-permute-start | bytes 1572872 | tf_op jit(solution)/shard_map/ppermute | solution.py:73
  114.6 1.9 %collective-permute-start.5 = (bf16[8,256,128]{2,1,0:T(8,128)(2,1)S(1)}, bf16[8,256,128]{2,1,0:T(8,128)(2,1)S(1)}, u32[]{:S(2)}, u32[]{:S(2)}) collective-permute-start(bf16[8,256,128]{2,1,0:T(8,128)(2,1)S(1)} %slice.4.a0), channel_id=1, source_target_pairs={{0,1},{1,0},{2,3},{3,2},{4,5},{5,4},{6,7},{7,6},{8,9},{9,8},{10,11... | collective-permute-start | bytes 1572872 | tf_op jit(solution)/shard_map/ppermute | solution.py:73
  116.6 13.6 %collective-permute-done.4.a1 = bf16[8,256,128]{2,1,0:T(8,128)(2,1)S(1)} collective-permute-done((bf16[8,256,128]{2,1,0:T(8,128)(2,1)S(1)}, bf16[8,256,128]{2,1,0:T(8,128)(2,1)S(1)}, u32[]{:S(2)}, u32[]{:S(2)}) %collective-permute-start.4) | collective-permute-done | bytes 524320 | tf_op jit(solution)/shard_map/ppermute | solution.py:73
  130.2 1.9 %collective-permute-start.6 = (bf16[8,256,128]{2,1,0:T(8,128)(2,1)S(1)}, bf16[8,256,128]{2,1,0:T(8,128)(2,1)S(1)}, u32[]{:S(2)}, u32[]{:S(2)}) collective-permute-start(bf16[8,256,128]{2,1,0:T(8,128)(2,1)S(1)} %collective-permute-done.4.a1), channel_id=1, source_target_pairs={{0,1},{1,0},{2,3},{3,2},{4,5},{5,4},{6,7},{7,6},{8,9},{9,8},{10,11... | collective-permute-start | bytes 1572872 | tf_op jit(solution)/shard_map/ppermute | solution.py:73
  132.1 0.0 all-to-all-done.3.arrived
  132.1 0.8 shard_map.118
  132.9 7.5 %all-to-all-start.4 = ((bf16[16,16,640]{2,1,0:T(8,128)(2,1)}), bf16[16,16,640]{2,1,0:T(8,128)(2,1)S(1)}, u32[]{:S(2)}, u32[]{:S(2)}) async-start(bf16[16,16,640]{2,1,0:T(8,128)(2,1)} %shard_map.118), calls=%async_computation.4 | async-start | bytes 655360 | tf_op jit(solution)/shard_map/all_to_all | solution.py:258
  140.4 0.0 collective-permute-done.5.b0
  140.4 0.0 collective-permute-done.6.b1
  140.4 0.0 copy-start.1
  140.4 2.0 %copy-done.1 = bf16[448,4096]{1,0:T(8,128)(2,1)S(1)} copy-done((bf16[448,4096]{1,0:T(8,128)(2,1)S(1)}, bf16[448,4096]{1,0:T(8,128)(2,1)}, u32[]{:S(2)}) %copy-start.1) | copy-done | bytes 3670040
  142.5 5.5 %shard_map.117 = bf16[448,256]{1,0:T(8,128)(2,1)} custom-call(s32[3]{0:T(128)S(1)} %pad_add_fusion.where, bf16[8,256,128]{2,1,0:T(8,128)(2,1)S(1)} %slice.4.a0, bf16[8,256,128]{2,1,0:T(8,128)(2,1)S(1)} %collective-permute-done.4.a1, bf16[8,256,128]{2,1,0:T(8,128)(2,1)S(1)} %collective-permute-done.5.b0, bf16[8,256,128]{2,1,0:T(8,128)(2,1)S(1)} %collective-permute-done.6.b1, ...), custom_call_target="tpu_custom_call" | custom-call | flops 998244352 | bytes 3670016 | tf_op jit(solution)/shard_map/pallas_call | solution.py:426
  148.0 4.5 %all-to-all-done.4.fifth = bf16[16,16,640]{2,1,0:T(8,128)(2,1)S(1)} async-done(((bf16[16,16,640]{2,1,0:T(8,128)(2,1)}), bf16[16,16,640]{2,1,0:T(8,128)(2,1)S(1)}, u32[]{:S(2)}, u32[]{:S(2)}) %all-to-all-start.4) | async-done | bytes 327712 | tf_op jit(solution)/shard_map/all_to_all | solution.py:258
  152.4 0.8 shard_map.119
  (7 shorter events, 0.1 us)
Async XLA Ops:
  0.7 2.0 %copy-start = (bf16[448,4096]{1,0:T(8,128)(2,1)S(1)}, bf16[448,4096]{1,0:T(8,128)(2,1)}, u32[]{:S(2)}) copy-start(bf16[448,4096]{1,0:T(8,128)(2,1)} %w3.1) | copy-start | bytes 11010052
  2.8 0.9 copy-start.2
  3.7 0.9 copy-start.4
  8.6 4.6 %collective-permute-start = (bf16[16,256,128]{2,1,0:T(8,128)(2,1)S(1)}, bf16[16,256,128]{2,1,0:T(8,128)(2,1)S(1)}, u32[]{:S(2)}, u32[]{:S(2)}) collective-permute-start(bf16[16,256,128]{2,1,0:T(8,128)(2,1)S(1)} %get-tuple-element.23), channel_id=1, source_target_pairs={{0,1},{1,0},{2,3},{3,2},{4,5},{5,4},{6,7},{7,6},{8,9},{9,8},{10,11... | collective-permute-start | bytes 3145736 | tf_op jit(solution)/shard_map/ppermute | solution.py:73
  13.1 29.8 %copy-start.6 = (bf16[16,16,128]{2,1,0:T(8,128)(2,1)S(1)}, bf16[16,16,128]{2,1,0:T(8,128)(2,1)}, u32[]{:S(2)}) copy-start(bf16[16,16,128]{2,1,0:T(8,128)(2,1)} %up.1) | copy-start | bytes 196612
  13.1 39.6 %copy-start.3 = (bf16[16,448,16]{1,2,0:T(8,128)(2,1)S(1)}, bf16[16,448,16]{1,2,0:T(8,128)(2,1)}, u32[]{:S(2)}) copy-start(bf16[16,448,16]{1,2,0:T(8,128)(2,1)} %param.9) | copy-start | bytes 688132
  13.1 39.6 %copy-start.5 = (bf16[256,448]{0,1:T(8,128)(2,1)S(1)}, bf16[256,448]{0,1:T(8,128)(2,1)}, u32[]{:S(2)}) copy-start(bf16[256,448]{0,1:T(8,128)(2,1)} %param.7) | copy-start | bytes 688132
  13.1 39.6 %copy-start.9 = (s32[16]{0:T(128)S(1)}, s32[16]{0:T(128)}, u32[]{:S(2)}) copy-start(s32[16]{0:T(128)} %seg.5) | copy-start | bytes 196
  14.0 45.9 %copy-start.7 = (bf16[256,128]{1,0:T(8,128)(2,1)S(1)}, bf16[256,128]{1,0:T(8,128)(2,1)}, u32[]{:S(2)}) copy-start(bf16[256,128]{1,0:T(8,128)(2,1)} %cotangent.3) | copy-start | bytes 196612
  14.0 45.8 %copy-start.8 = (bf16[16,128]{1,0:T(8,128)(2,1)S(1)}, bf16[16,128]{1,0:T(8,128)(2,1)}, u32[]{:S(2)}) copy-start(bf16[16,128]{1,0:T(8,128)(2,1)} %magnitude.3) | copy-start | bytes 12292
  14.0 45.8 %collective-permute-start.1 = (bf16[8,256,128]{2,1,0:T(8,128)(2,1)S(1)}, bf16[8,256,128]{2,1,0:T(8,128)(2,1)S(1)}, u32[]{:S(2)}, u32[]{:S(2)}) collective-permute-start(bf16[8,256,128]{2,1,0:T(8,128)(2,1)S(1)} %get-tuple-element.25), channel_id=1, source_target_pairs={{0,16},{1,17},{2,18},{3,19},{4,20},{5,21},{6,22},{7,23},{8,24},{9,... | collective-permute-start | bytes 1572872 | tf_op jit(solution)/shard_map/ppermute | solution.py:73
  44.2 15.6 %all-to-all-start.1 = ((f32[16,2,128]{2,1,0:T(2,128)}), f32[16,2,128]{2,1,0:T(2,128)S(1)}, u32[]{:S(2)}, u32[]{:S(2)}) async-start(f32[16,2,128]{2,1,0:T(2,128)} %shard_map.111), calls=%async_computation.1 | async-start | bytes 32768 | tf_op jit(solution)/shard_map/all_to_all | solution.py:258
  93.5 7.1 %collective-permute-start.2 = (bf16[64,128]{1,0:T(8,128)(2,1)S(1)}, bf16[64,128]{1,0:T(8,128)(2,1)S(1)}, u32[]{:S(2)}, u32[]{:S(2)}) collective-permute-start(bf16[64,128]{1,0:T(8,128)(2,1)S(1)} %get-tuple-element.27), channel_id=1, source_target_pairs={{0,16},{1,17},{2,18},{3,19},{4,20},{5,21},{6,22},{7,23},{8,24},{9,... | collective-permute-start | bytes 49160 | tf_op jit(solution)/shard_map/ppermute | solution.py:73
  100.7 3.1 %collective-permute-start.3 = (bf16[64,128]{1,0:T(8,128)(2,1)S(1)}, bf16[64,128]{1,0:T(8,128)(2,1)S(1)}, u32[]{:S(2)}, u32[]{:S(2)}) collective-permute-start(bf16[64,128]{1,0:T(8,128)(2,1)S(1)} %add_convert_fusion.ranks), channel_id=1, source_target_pairs={{0,1},{1,0},{2,3},{3,2},{4,5},{5,4},{6,7},{7,6},{8,9},{9,8},{10,11... | collective-permute-start | bytes 49160 | tf_op jit(solution)/shard_map/ppermute | solution.py:73
  106.2 25.9 %all-to-all-start.3 = ((bf16[16,16,640]{2,1,0:T(8,128)(2,1)}), bf16[16,16,640]{2,1,0:T(8,128)(2,1)S(1)}, u32[]{:S(2)}, u32[]{:S(2)}) async-start(bf16[16,16,640]{2,1,0:T(8,128)(2,1)} %get-tuple-element.33), calls=%async_computation.3 | async-start | bytes 655360 | tf_op jit(solution)/shard_map/all_to_all | solution.py:258
  110.7 19.5 %collective-permute-start.4 = (bf16[8,256,128]{2,1,0:T(8,128)(2,1)S(1)}, bf16[8,256,128]{2,1,0:T(8,128)(2,1)S(1)}, u32[]{:S(2)}, u32[]{:S(2)}) collective-permute-start(bf16[8,256,128]{2,1,0:T(8,128)(2,1)S(1)} %slice.4.a0), channel_id=1, source_target_pairs={{0,16},{1,17},{2,18},{3,19},{4,20},{5,21},{6,22},{7,23},{8,24},{9,... | collective-permute-start | bytes 1572872 | tf_op jit(solution)/shard_map/ppermute | solution.py:73
  114.6 25.8 %collective-permute-start.5 = (bf16[8,256,128]{2,1,0:T(8,128)(2,1)S(1)}, bf16[8,256,128]{2,1,0:T(8,128)(2,1)S(1)}, u32[]{:S(2)}, u32[]{:S(2)}) collective-permute-start(bf16[8,256,128]{2,1,0:T(8,128)(2,1)S(1)} %slice.4.a0), channel_id=1, source_target_pairs={{0,1},{1,0},{2,3},{3,2},{4,5},{5,4},{6,7},{7,6},{8,9},{9,8},{10,11... | collective-permute-start | bytes 1572872 | tf_op jit(solution)/shard_map/ppermute | solution.py:73
  130.2 10.2 %collective-permute-start.6 = (bf16[8,256,128]{2,1,0:T(8,128)(2,1)S(1)}, bf16[8,256,128]{2,1,0:T(8,128)(2,1)S(1)}, u32[]{:S(2)}, u32[]{:S(2)}) collective-permute-start(bf16[8,256,128]{2,1,0:T(8,128)(2,1)S(1)} %collective-permute-done.4.a1), channel_id=1, source_target_pairs={{0,1},{1,0},{2,3},{3,2},{4,5},{5,4},{6,7},{7,6},{8,9},{9,8},{10,11... | collective-permute-start | bytes 1572872 | tf_op jit(solution)/shard_map/ppermute | solution.py:73
  132.9 19.5 %all-to-all-start.4 = ((bf16[16,16,640]{2,1,0:T(8,128)(2,1)}), bf16[16,16,640]{2,1,0:T(8,128)(2,1)S(1)}, u32[]{:S(2)}, u32[]{:S(2)}) async-start(bf16[16,16,640]{2,1,0:T(8,128)(2,1)} %shard_map.118), calls=%async_computation.4 | async-start | bytes 655360 | tf_op jit(solution)/shard_map/all_to_all | solution.py:258
  140.4 2.0 %copy-start.1 = (bf16[448,4096]{1,0:T(8,128)(2,1)S(1)}, bf16[448,4096]{1,0:T(8,128)(2,1)}, u32[]{:S(2)}) copy-start(bf16[448,4096]{1,0:T(8,128)(2,1)} %w3.1) | copy-start | bytes 11010052

commit v3 on v2

--- a/solution.py
+++ b/solution.py
@@ -88,6 +88,10 @@
         cost_estimate=pl.CostEstimate(flops=flops, bytes_accessed=moved, transcendentals=0),
         compiler_params=pltpu.CompilerParams(vmem_limit_bytes=16 * 2**20),
     )
+
+
+def in_hbm(array):
+    return pltpu.with_memory_space_constraint(array, pltpu.HBM)
 
 
 def whole(*dims):
@@ -168,34 +172,48 @@
     second[...] = jnp.broadcast_to(both[None], second.shape)
 
 
-def scale_kernel(where, seg, second, magnitude, cotangent, up, low, keep, got,
-                 third, scaled, norms, every):
+def lift_kernel(where, keep, got, up, down, near):
+    count = keep.shape[0]
+    for out, first in ((up, 2), (down, count - 3), (near, count - 1)):
+        for i in range(out.shape[0]):
+            at = (where[3] + first + i) % count
+            out[i] = (keep[at].astype(F32) + got[at].astype(F32)).astype(BF16)
+
+
+def near_kernel(near, up, down, before, after, own):
+    before[...] = (near[0].astype(F32) + up[0].astype(F32)).astype(BF16)
+    after[...] = (near[2].astype(F32) + up[2].astype(F32) + down[1].astype(F32)).astype(BF16)
+    own[...] = near[1].astype(F32) + up[1].astype(F32) + down[0].astype(F32)
+
+
+def trio_kernel(before, own, after, trio, pair):
+    trio[0] = before[...]
+    trio[1] = own[...]
+    trio[2] = after[...]
+    pair[0] = before[...]
+    pair[1] = own[...]
+
+
+def scale_kernel(where, seg, second, magnitude, cotangent, up, low, third, scaled, norms):
     count = cotangent.shape[0]
-
-    @pl.when(pl.program_id(0) == 0)
-    def _():
-        marks = bounds(seg, seg.shape[0], where[0] * count)
-        parts = second[...]
-        squares = parts[:, 0, :] + jnp.sum(parts[:, 1, :], axis=0, keepdims=True)
-        col_norms = jnp.sqrt(jnp.maximum(squares, 0.0) + EPSILON)
-        norms[...] = col_norms
-        scale = token_scale_of(magnitude[...].astype(F32) / col_norms, marks, count)
-        grad = (cotangent[...].astype(F32) * scale).astype(BF16)
-        scaled[...] = grad
-        spread = dot(up[...], grad, 1, 1)
-        back = packed(picked(spread, marks)).astype(BF16)
-        every[...] = jnp.concatenate([grad, low[...], back], axis=0)
-
-    third[0, :count] = (keep[0].astype(F32) + got[0].astype(F32)).astype(BF16)
-    third[0, count:] = every[...]
-
-
-def sums_kernel(rank_rows, base_rows, ranks, base):
+    marks = bounds(seg, seg.shape[0], where[0] * count)
+    parts = second[...]
+    squares = parts[:, 0, :] + jnp.sum(parts[:, 1, :], axis=0, keepdims=True)
+    col_norms = jnp.sqrt(jnp.maximum(squares, 0.0) + EPSILON)
+    norms[...] = col_norms
+    scale = token_scale_of(magnitude[...].astype(F32) / col_norms, marks, count)
+    grad = (cotangent[...].astype(F32) * scale).astype(BF16)
+    scaled[...] = grad
+    back = packed(picked(dot(up[...], grad, 1, 1), marks)).astype(BF16)
+    every = jnp.concatenate([low[...], back], axis=0)
+    third[...] = jnp.broadcast_to(every[None], third.shape)
+
+
+def sums_kernel(rank_rows, ranks):
     ranks[...] = jnp.sum(rank_rows[...].astype(F32), axis=0).astype(BF16)
-    base[...] = jnp.sum(base_rows[...].astype(F32), axis=0)
-
-
-def grads_kernel(where, seg, ranks, got, base, norms, magnitude, cotangent, scaled, up, tokens,
+
+
+def grads_kernel(where, seg, ranks, got, base, base_a, base_b, norms, magnitude, cotangent, scaled, up, tokens,
                  fourth, projected, back_wide):
     adapters = seg.shape[0]
     own_rows, count = tokens.shape
@@ -205,7 +223,8 @@
     low = widened(unpacked(total[: 2 * rank]), marks)
     back = widened(unpacked(total[2 * rank :]), marks)
     back_wide[...] = back
-    hidden = base[...] + dot(low, up[...], 0, 0)
+    hidden = base[...] + base_a[...].astype(F32) + base_b[...].astype(F32)
+    hidden = hidden + dot(low, up[...], 0, 0)
     scale = token_scale_of(magnitude[...].astype(F32) / norms[...], marks, count)
     projected[...] = (hidden * scale).astype(BF16)
     weighted = cotangent[...].astype(F32) * hidden
@@ -269,7 +288,8 @@
     me_dp = lax.axis_index("dp")
     me = lax.axis_index("tensor")
     core, hi = me % 2, me // (2 * zs)
-    where = jnp.stack([me_dp, core, hi]).astype(I32)
+    z = (me // 2) % zs
+    where = jnp.stack([me_dp, core, hi, z]).astype(I32)
     core_pairs = [(i, i ^ 1) for i in range(size)]
     hi_pairs = [(i, (i + size // 2) % size) for i in range(size)]
     z_groups = [[h * 2 * zs + z * 2 + c for z in range(zs)] for h in range(2) for c in range(2)]
@@ -297,7 +317,7 @@
         scratch=[pltpu.VMEM((8, width), F32), pltpu.VMEM((count + rank, own_rows), BF16)],
         flops=2 * count * own_rows * full,
         moved=2 * own_rows * full,
-    )(where, turned, base_weight, down_rows)
+    )(where, in_hbm(turned), in_hbm(base_weight), in_hbm(down_rows))
     head = exchange(head, "tensor")
     got = shift(give, core_pairs)
     low = call(
@@ -325,6 +345,14 @@
     )(where, keep, got, keep, got)
     got = shift(give, hi_pairs)
 
+    def along_z(step):
+        return [
+            (h * 2 * zs + a * 2 + c, h * 2 * zs + (a + step) % zs * 2 + c)
+            for h in range(2)
+            for a in range(zs)
+            for c in range(2)
+        ]
+
     second = call(
         squares_kernel,
         shaped(adapters, 2, width, dtype=F32),
@@ -339,46 +367,70 @@
     )(where, head, adapter_up)
     second = exchange(second, "dp")
 
-    rows = 2 * count + 4 * rank
+    up3, down2, near = call(
+        lift_kernel,
+        [shaped(n, count, width) for n in (3, 2, 3)],
+        scalars=1,
+        grid=(1,),
+        in_specs=[whole(zs, count, width)] * 2,
+        out_specs=[whole(n, count, width) for n in (3, 2, 3)],
+        moved=6 * zs * count * width,
+    )(where, keep, got)
+    up3 = shift(up3, along_z(3))
+    down2 = shift(down2, along_z(-3))
+
     third, scaled, norms = call(
         scale_kernel,
-        [shaped(zs, rows, width), shaped(count, width), shaped(adapters, width, dtype=F32)],
+        [shaped(zs, 4 * rank, width), shaped(count, width), shaped(adapters, width, dtype=F32)],
         scalars=2,
-        grid=(zs,),
+        grid=(1,),
         in_specs=[
             whole(adapters, 2, width),
             whole(adapters, width),
             whole(count, width),
             whole(wide, width),
             whole(2 * rank, width),
-            pl.BlockSpec((1, count, width), lambda i, *s: (i, 0, 0)),
-            pl.BlockSpec((1, count, width), lambda i, *s: (i, 0, 0)),
-        ],
-        out_specs=[
-            pl.BlockSpec((1, rows, width), lambda i, *s: (i, 0, 0)),
-            whole(count, width),
-            whole(adapters, width),
-        ],
-        scratch=[pltpu.VMEM((count + 4 * rank, width), BF16)],
+        ],
+        out_specs=[whole(zs, 4 * rank, width), whole(count, width), whole(adapters, width)],
         flops=2 * count * wide * width,
-        moved=2 * zs * rows * width,
-    )(where, seg_lengths, second, magnitude, cotangent, up_own, low, keep, got)
+        moved=8 * count * width,
+    )(where, seg_lengths, second, magnitude, cotangent, up_own, low)
     third = exchange(third, "tensor", z_groups)
-
-    ranks, base = call(
+    from_below = shift(scaled, along_z(1))
+    from_above = shift(scaled, along_z(-1))
+
+    before, after, base = call(
+        near_kernel,
+        [shaped(count, width), shaped(count, width), shaped(count, width, dtype=F32)],
+        grid=(1,),
+        in_specs=[whole(3, count, width), whole(3, count, width), whole(2, count, width)],
+        out_specs=[whole(count, width)] * 3,
+        moved=24 * count * width,
+    )(near, up3, down2)
+    base_a = shift(before, along_z(-1))
+    base_b = shift(after, along_z(1))
+
+    ranks = call(
         sums_kernel,
-        [shaped(4 * rank, width), shaped(count, width, dtype=F32)],
-        grid=(1,),
-        in_specs=[
-            pl.BlockSpec((zs, 4 * rank, width), lambda i: (0, 2 * count // (4 * rank), 0)),
-            pl.BlockSpec((zs, count, width), lambda i: (0, 0, 0)),
-        ],
-        out_specs=[whole(4 * rank, width), whole(count, width)],
-        moved=2 * zs * count * width,
-    )(third, third)
+        shaped(4 * rank, width),
+        grid=(1,),
+        in_specs=[whole(zs, 4 * rank, width)],
+        out_specs=whole(4 * rank, width),
+        moved=2 * zs * 4 * rank * width,
+    )(third)
     ranks = (ranks.astype(F32) + shift(ranks, hi_pairs).astype(F32)).astype(BF16)
     other = shift(ranks, core_pairs)
-    gather_a = third[:, count : 2 * count]
+    trio, pair = call(
+        trio_kernel,
+        [shaped(3, count, width), shaped(2, count, width)],
+        grid=(1,),
+        in_specs=[whole(count, width)] * 3,
+        out_specs=[whole(3, count, width), whole(2, count, width)],
+        moved=16 * count * width,
+    )(from_below, scaled, from_above)
+    far_up = shift(trio, along_z(3))
+    far_down = shift(pair, along_z(-3))
+    gather_a = jnp.concatenate([trio, far_up, far_down], axis=0)
     gather_b = shift(gather_a, hi_pairs)
 
     blocks = rank * 40
@@ -390,6 +442,8 @@
         in_specs=[
             whole(4 * rank, width),
             whole(4 * rank, width),
+            whole(count, width),
+            whole(count, width),
             whole(count, width),
             whole(adapters, width),
             whole(adapters, width),
@@ -401,7 +455,7 @@
         out_specs=[whole(adapters, rank, blocks), whole(count, width), whole(wide, count)],
         flops=2 * count * wide * (own_rows + 2 * width),
         moved=4 * adapters * rank * blocks,
-    )(where, seg_lengths, ranks, other, base, norms, magnitude, cotangent, scaled, up_own, turned)
+    )(where, seg_lengths, ranks, other, base, base_a, base_b, norms, magnitude, cotangent, scaled, up_own, turned)
     fourth = exchange(fourth, "dp")
     gather_c = shift(gather_a, core_pairs)
     gather_d = shift(gather_b, core_pairs)
@@ -417,10 +471,12 @@
     fifth = exchange(fifth, "dp")
 
     def column(x_bit, c_bit):
-        return pl.BlockSpec(
-            (own_rows, width),
-            lambda i, s: (0, (s[2] ^ x_bit) * (2 * zs) + i * 2 + (s[1] ^ c_bit)),
-        )
+        def at(i, s):
+            off = jnp.where(i < 3, i - 1, jnp.where(i < 6, i - 7, i - 4))
+            block = (s[3] + off + zs) % zs
+            return (0, (s[2] ^ x_bit) * (2 * zs) + block * 2 + (s[1] ^ c_bit))
+
+        return pl.BlockSpec((own_rows, width), at)
 
     block = pl.BlockSpec((1, count, width), lambda i, s: (i, 0, 0))
     grad_tokens = call(
@@ -435,7 +491,7 @@
         scratch=[pltpu.VMEM((own_rows, count), F32)],
         flops=2 * count * own_rows * (full + wide),
         moved=2 * own_rows * full,
-    )(where, gather_a, gather_b, gather_c, gather_d, *[base_weight] * 4, back_wide, down_flat)
+    )(where, gather_a, gather_b, gather_c, gather_d, *[in_hbm(base_weight)] * 4, back_wide, down_flat)
 
     grad_down, grad_up, grad_magnitude = call(
         final_kernel,

time: 154 us -> 157 us (1.019)
  blocking collectives: 55.9 us -> 0 us
  starting transfers between devices: 40.8 us -> 87.9 us
  waiting for transfers between devices: 31.7 us -> 40.2 us
  Pallas kernels: 17.9 us -> 26.2 us
  local copies, waits for them, and re-layouts: 6.02 us -> 0.09 us
    all_to_all x2 -> x0, blocking collectives: 55.9 us -> none  [exchange(): lax.all_to_all(blocks, axis, 0, 0, tiled=True, axis_index_groups=groups)]
    ppermute x7 -> x15, starting transfers between devices: 20.4 us -> 51.5 us  [shift(): return lax.ppermute(block, 'tensor', pairs)]
    all_to_all x3 -> x5, starting transfers between devices: 20.4 us -> 36.3 us  [exchange(): lax.all_to_all(blocks, axis, 0, 0, tiled=True, axis_index_groups=groups)]
    all_to_all x3 -> x5, waiting for transfers between devices: 10.8 us -> 16.9 us  [exchange(): lax.all_to_all(blocks, axis, 0, 0, tiled=True, axis_index_groups=groups)]
    unnamed x20 -> x14, local copies, waits for them, and re-layouts: 5.99 us -> 0.06 us
    pallas_call x1, Pallas kernels: 3.89 us -> 7.89 us  [local(): call(first_kernel, [shaped(size, HEAD, width), shaped(size // 2, count, w...]
    ppermute x7 -> x15, waiting for transfers between devices: 20.9 us -> 23.3 us  [shift(): return lax.ppermute(block, 'tensor', pairs)]
    pallas_call x1, Pallas kernels: 5.51 us -> 7.62 us  [local(): call(tokens_kernel, shaped(own_rows, count), scalars=1, grid=(zs,), in_sp...]
  transfers between devices with their start and end apart: 10 -> 20, of which waited for: 6 -> 10; matrix products, arithmetic and copies ran while one was open for 0% -> 0% of each run, Pallas kernels for 5% -> 11%
where the time goes in v3:
time: 157 us; the launch traced here: 155 us
  starting transfers between devices  87.9 us (56%)
  waiting for transfers between devices  40.2 us (26%)
  Pallas kernels  26.2 us (17%)
    ppermute x15, starting transfers between devices, shift(): return lax.ppermute(block, 'tensor', pairs)  51.5 us
    all_to_all x5, starting transfers between devices, exchange(): lax.all_to_all(blocks, axis, 0, 0, tiled=True, axis_index_groups=groups)  36.3 us
    ppermute x15, waiting for transfers between devices, shift(): return lax.ppermute(block, 'tensor', pairs)  23.3 us
    all_to_all x5, waiting for transfers between devices, exchange(): lax.all_to_all(blocks, axis, 0, 0, tiled=True, axis_index_groups=groups)  16.9 us
    pallas_call x1, Pallas kernels, local(): call(first_kernel, [shaped(size, HEAD, width), shaped(size // 2, count, w...  7.89 us
    pallas_call x1, Pallas kernels, local(): call(tokens_kernel, shaped(own_rows, count), scalars=1, grid=(zs,), in_sp...  7.62 us
  transfers between devices with their start and end apart: 20, of which 10 were waited for; matrix products, arithmetic and copies ran while one was open for 0% of the time, Pallas kernels for 11%

profile of v3, /device:TPU:8, one launch (start us, length us, event | category | flops | bytes accessed | tf_op | source)
XLA Modules:
  0.0 155.4 jit_solution(17446155598235964780)
XLA Ops:
  0.7 0.1 pad_add_fusion.where
  0.8 7.9 %shard_map.110 = (bf16[32,24,128]{2,1,0:T(8,128)(2,1)}, bf16[16,256,128]{2,1,0:T(8,128)(2,1)S(1)}, bf16[16,256,128]{2,1,0:T(8,128)(2,1)}) custom-call(s32[4]{0:T(128)S(1)} %pad_add_fusion.where, bf16[448,256]{1,0:T(8,128)(2,1)} %bitcast.14, bf16[448,4096]{1,0:T(8,128)(2,1)} %w3.1, bf16[16,16,448]{2,1,0:T(8,128)(2,1)} %bitcast.11), custom_call_target="tpu_custom_call" | custom-call | flops 939524096 | bytes 3670016 | tf_op jit(solution)/shard_map/pallas_call | solution.py:302
  8.7 2.0 %collective-permute-start.2 = (bf16[16,256,128]{2,1,0:T(8,128)(2,1)}, bf16[16,256,128]{2,1,0:T(8,128)(2,1)S(1)}, u32[]{:S(2)}, u32[]{:S(2)}) collective-permute-start(bf16[16,256,128]{2,1,0:T(8,128)(2,1)} %get-tuple-element.30), channel_id=1, source_target_pairs={{0,1},{1,0},{2,3},{3,2},{4,5},{5,4},{6,7},{7,6},{8,9},{9,8},{10,11... | collective-permute-start | bytes 3145736 | tf_op jit(solution)/shard_map/ppermute | solution.py:73
  10.7 13.3 %all-to-all-start = ((bf16[32,24,128]{2,1,0:T(8,128)(2,1)}), bf16[32,24,128]{2,1,0:T(8,128)(2,1)S(1)}, u32[]{:S(2)}, u32[]{:S(2)}) async-start(bf16[32,24,128]{2,1,0:T(8,128)(2,1)} %get-tuple-element.27), calls=%async_computation | async-start | bytes 393216 | tf_op jit(solution)/shard_map/all_to_all | solution.py:277
  24.0 0.0 collective-permute-done.2.got_a.got_b
  24.0 2.0 %shard_map.115 = (bf16[8,256,128]{2,1,0:T(8,128)(2,1)S(1)}, bf16[8,256,128]{2,1,0:T(8,128)(2,1)}) custom-call(s32[4]{0:T(128)S(1)} %pad_add_fusion.where, bf16[16,256,128]{2,1,0:T(8,128)(2,1)S(1)} %get-tuple-element.29.keep_a.keep_b, bf16[16,256,128]{2,1,0:T(8,128)(2,1)S(1)} %collective-permute-done.2.got_a.got_b, ...), custom_call_target="tpu_custom_call" | custom-call | bytes 3145728 | tf_op jit(solution)/shard_map/pallas_call | solution.py:337
  26.1 5.2 %collective-permute-start.3 = (bf16[8,256,128]{2,1,0:T(8,128)(2,1)}, bf16[8,256,128]{2,1,0:T(8,128)(2,1)S(1)}, u32[]{:S(2)}, u32[]{:S(2)}) collective-permute-start(bf16[8,256,128]{2,1,0:T(8,128)(2,1)} %get-tuple-element.32), channel_id=1, source_target_pairs={{0,16},{1,17},{2,18},{3,19},{4,20},{5,21},{6,22},{7,23},{8,24},{9,... | collective-permute-start | bytes 1572872 | tf_op jit(solution)/shard_map/ppermute | solution.py:73
  31.3 6.1 %all-to-all-done.head = bf16[32,24,128]{2,1,0:T(8,128)(2,1)S(1)} async-done(((bf16[32,24,128]{2,1,0:T(8,128)(2,1)}), bf16[32,24,128]{2,1,0:T(8,128)(2,1)S(1)}, u32[]{:S(2)}, u32[]{:S(2)}) %all-to-all-start) | async-done | bytes 196640 | tf_op jit(solution)/shard_map/all_to_all | solution.py:277
  37.4 1.3 shard_map.111
  38.7 7.6 %all-to-all-start.1 = ((f32[16,2,128]{2,1,0:T(2,128)}), f32[16,2,128]{2,1,0:T(2,128)S(1)}, u32[]{:S(2)}, u32[]{:S(2)}) async-start(f32[16,2,128]{2,1,0:T(2,128)} %shard_map.111), calls=%async_computation.1 | async-start | bytes 32768 | tf_op jit(solution)/shard_map/all_to_all | solution.py:277
  46.4 0.8 shard_map.112.low
  47.1 6.4 %all-to-all-done.1.second = f32[16,2,128]{2,1,0:T(2,128)S(1)} async-done(((f32[16,2,128]{2,1,0:T(2,128)}), f32[16,2,128]{2,1,0:T(2,128)S(1)}, u32[]{:S(2)}, u32[]{:S(2)}) %all-to-all-start.1) | async-done | bytes 16416 | tf_op jit(solution)/shard_map/all_to_all | solution.py:277
  53.5 1.8 %shard_map.113 = (bf16[8,64,128]{2,1,0:T(8,128)(2,1)}, bf16[256,128]{1,0:T(8,128)(2,1)S(1)}, f32[16,128]{1,0:T(8,128)S(1)}) custom-call(s32[4]{0:T(128)S(1)} %pad_add_fusion.where, s32[16]{0:T(128)S(1)} %copy-done.5, f32[16,2,128]{2,1,0:T(2,128)S(1)} %all-to-all-done.1.second, bf16[16,128]{1,0:T(8,128)(2,1)S(1)} %copy-done.4, ...), custom_call_target="tpu_custom_call" | custom-call | flops 16777216 | bytes 262144 | tf_op jit(solution)/shard_map/pallas_call | solution.py:382
  55.3 3.4 %all-to-all-start.2 = ((bf16[8,64,128]{2,1,0:T(8,128)(2,1)}), bf16[8,64,128]{2,1,0:T(8,128)(2,1)S(1)}, u32[]{:S(2)}, u32[]{:S(2)}) async-start(bf16[8,64,128]{2,1,0:T(8,128)(2,1)} %get-tuple-element.28), calls=%async_computation.2 | async-start | bytes 262144 | tf_op jit(solution)/shard_map/all_to_all | solution.py:277
  58.7 3.8 %collective-permute-start.8 = (bf16[256,128]{1,0:T(8,128)(2,1)S(1)}, bf16[256,128]{1,0:T(8,128)(2,1)S(1)}, u32[]{:S(2)}, u32[]{:S(2)}) collective-permute-start(bf16[256,128]{1,0:T(8,128)(2,1)S(1)} %get-tuple-element.40.scaled.own), channel_id=1, source_target_pairs={{0,2},{1,3},{2,4},{3,5},{4,6},{5,7},{6,8},{7,9},{8,10},{9,11},{10,... | collective-permute-start | bytes 196616 | tf_op jit(solution)/shard_map/ppermute | solution.py:73
  62.5 3.2 %collective-permute-start.9 = (bf16[256,128]{1,0:T(8,128)(2,1)S(1)}, bf16[256,128]{1,0:T(8,128)(2,1)S(1)}, u32[]{:S(2)}, u32[]{:S(2)}) collective-permute-start(bf16[256,128]{1,0:T(8,128)(2,1)S(1)} %get-tuple-element.40.scaled.own), channel_id=1, source_target_pairs={{0,14},{1,15},{2,0},{3,1},{4,2},{5,3},{6,4},{7,5},{8,6},{9,7},{10,... | collective-permute-start | bytes 196616 | tf_op jit(solution)/shard_map/ppermute | solution.py:73
  65.7 0.5 collective-permute-done.8.before
  66.2 2.4 %collective-permute-done.9.after = bf16[256,128]{1,0:T(8,128)(2,1)S(1)} collective-permute-done((bf16[256,128]{1,0:T(8,128)(2,1)S(1)}, bf16[256,128]{1,0:T(8,128)(2,1)S(1)}, u32[]{:S(2)}, u32[]{:S(2)}) %collective-permute-start.9) | collective-permute-done | bytes 65568 | tf_op jit(solution)/shard_map/ppermute | solution.py:73
  68.7 3.0 %collective-permute-start = (bf16[64,128]{1,0:T(8,128)(2,1)S(1)}, bf16[64,128]{1,0:T(8,128)(2,1)S(1)}, u32[]{:S(2)}, u32[]{:S(2)}) collective-permute-start(bf16[64,128]{1,0:T(8,128)(2,1)S(1)} %shard_map.114), channel_id=1, source_target_pairs={{0,16},{1,17},{2,18},{3,19},{4,20},{5,21},{6,22},{7,23},{8,24},{9,... | collective-permute-start | bytes 49160 | tf_op jit(solution)/shard_map/ppermute | solution.py:73
  71.7 7.6 %collective-permute-start.10 = (bf16[3,256,128]{2,1,0:T(8,128)(2,1)S(1)}, bf16[3,256,128]{2,1,0:T(8,128)(2,1)S(1)}, u32[]{:S(2)}, u32[]{:S(2)}) collective-permute-start(bf16[3,256,128]{2,1,0:T(8,128)(2,1)S(1)} %get-tuple-element.42), channel_id=1, source_target_pairs={{0,6},{1,7},{2,8},{3,9},{4,10},{5,11},{6,12},{7,13},{8,14},{9,15},... | collective-permute-start | bytes 589832 | tf_op jit(solution)/shard_map/ppermute | solution.py:73
  79.3 1.9 %collective-permute-start.11 = (bf16[2,256,128]{2,1,0:T(8,128)(2,1)S(1)}, bf16[2,256,128]{2,1,0:T(8,128)(2,1)S(1)}, u32[]{:S(2)}, u32[]{:S(2)}) collective-permute-start(bf16[2,256,128]{2,1,0:T(8,128)(2,1)S(1)} %get-tuple-element.43), channel_id=1, source_target_pairs={{0,10},{1,11},{2,12},{3,13},{4,14},{5,15},{6,0},{7,1},{8,2},{9,3},... | collective-permute-start | bytes 393224 | tf_op jit(solution)/shard_map/ppermute | solution.py:73
  81.3 0.7 shard_map.116
  82.0 5.7 %collective-permute-start.4 = (bf16[3,256,128]{2,1,0:T(8,128)(2,1)S(1)}, bf16[3,256,128]{2,1,0:T(8,128)(2,1)S(1)}, u32[]{:S(2)}, u32[]{:S(2)}) collective-permute-start(bf16[3,256,128]{2,1,0:T(8,128)(2,1)S(1)} %get-tuple-element.34), channel_id=1, source_target_pairs={{0,6},{1,7},{2,8},{3,9},{4,10},{5,11},{6,12},{7,13},{8,14},{9,15},... | collective-permute-start | bytes 589832 | tf_op jit(solution)/shard_map/ppermute | solution.py:73
  87.7 3.1 %collective-permute-start.5 = (bf16[2,256,128]{2,1,0:T(8,128)(2,1)S(1)}, bf16[2,256,128]{2,1,0:T(8,128)(2,1)S(1)}, u32[]{:S(2)}, u32[]{:S(2)}) collective-permute-start(bf16[2,256,128]{2,1,0:T(8,128)(2,1)S(1)} %get-tuple-element.35), channel_id=1, source_target_pairs={{0,10},{1,11},{2,12},{3,13},{4,14},{5,15},{6,0},{7,1},{8,2},{9,3},... | collective-permute-start | bytes 393224 | tf_op jit(solution)/shard_map/ppermute | solution.py:73
  90.8 0.0 collective-permute-done
  90.9 1.9 %collective-permute-start.1 = (bf16[64,128]{1,0:T(8,128)(2,1)S(1)}, bf16[64,128]{1,0:T(8,128)(2,1)S(1)}, u32[]{:S(2)}, u32[]{:S(2)}) collective-permute-start(bf16[64,128]{1,0:T(8,128)(2,1)S(1)} %add_convert_fusion.ranks), channel_id=1, source_target_pairs={{0,1},{1,0},{2,3},{3,2},{4,5},{5,4},{6,7},{7,6},{8,9},{9,8},{10,11... | collective-permute-start | bytes 49160 | tf_op jit(solution)/shard_map/ppermute | solution.py:73
  92.8 5.3 %collective-permute-done.5.down = bf16[2,256,128]{2,1,0:T(8,128)(2,1)S(1)} collective-permute-done((bf16[2,256,128]{2,1,0:T(8,128)(2,1)S(1)}, bf16[2,256,128]{2,1,0:T(8,128)(2,1)S(1)}, u32[]{:S(2)}, u32[]{:S(2)}) %collective-permute-start.5) | collective-permute-done | bytes 131104 | tf_op jit(solution)/shard_map/ppermute | solution.py:73
  98.1 2.0 %collective-permute-done.4.up = bf16[3,256,128]{2,1,0:T(8,128)(2,1)S(1)} collective-permute-done((bf16[3,256,128]{2,1,0:T(8,128)(2,1)S(1)}, bf16[3,256,128]{2,1,0:T(8,128)(2,1)S(1)}, u32[]{:S(2)}, u32[]{:S(2)}) %collective-permute-start.4) | collective-permute-done | bytes 196640 | tf_op jit(solution)/shard_map/ppermute | solution.py:73
  100.1 0.1 shard_map.117
  100.2 3.6 %collective-permute-start.6 = (bf16[256,128]{1,0:T(8,128)(2,1)S(1)}, bf16[256,128]{1,0:T(8,128)(2,1)S(1)}, u32[]{:S(2)}, u32[]{:S(2)}) collective-permute-start(bf16[256,128]{1,0:T(8,128)(2,1)S(1)} %get-tuple-element.37), channel_id=1, source_target_pairs={{0,14},{1,15},{2,0},{3,1},{4,2},{5,3},{6,4},{7,5},{8,6},{9,7},{10,... | collective-permute-start | bytes 196616 | tf_op jit(solution)/shard_map/ppermute | solution.py:73
  103.8 2.2 %collective-permute-start.7 = (bf16[256,128]{1,0:T(8,128)(2,1)S(1)}, bf16[256,128]{1,0:T(8,128)(2,1)S(1)}, u32[]{:S(2)}, u32[]{:S(2)}) collective-permute-start(bf16[256,128]{1,0:T(8,128)(2,1)S(1)} %get-tuple-element.38), channel_id=1, source_target_pairs={{0,2},{1,3},{2,4},{3,5},{4,6},{5,7},{6,8},{7,9},{8,10},{9,11},{10,... | collective-permute-start | bytes 196616 | tf_op jit(solution)/shard_map/ppermute | solution.py:73
  106.0 0.0 collective-permute-done.10
  106.1 0.0 collective-permute-done.1.got
  106.1 0.2 collective-permute-done.6.base_a
  106.3 4.8 %collective-permute-done.7.base_b = bf16[256,128]{1,0:T(8,128)(2,1)S(1)} collective-permute-done((bf16[256,128]{1,0:T(8,128)(2,1)S(1)}, bf16[256,128]{1,0:T(8,128)(2,1)S(1)}, u32[]{:S(2)}, u32[]{:S(2)}) %collective-permute-start.7) | collective-permute-done | bytes 65568 | tf_op jit(solution)/shard_map/ppermute | solution.py:73
  111.1 2.4 %shard_map.118 = (bf16[16,16,640]{2,1,0:T(8,128)(2,1)}, bf16[256,128]{1,0:T(8,128)(2,1)}, bf16[256,256]{1,0:T(8,128)(2,1)S(1)}) custom-call(s32[4]{0:T(128)S(1)} %pad_add_fusion.where, s32[16]{0:T(128)S(1)} %copy-done.5, bf16[64,128]{1,0:T(8,128)(2,1)S(1)} %add_convert_fusion.ranks, bf16[64,128]{1,0:T(8,128)(2,1)S(1)} %collective-permute-done.1.got, ...), custom_call_target="tpu_custom_call" | custom-call | flops 92274688 | bytes 655360 | tf_op jit(solution)/shard_map/pallas_call | solution.py:437
  113.5 4.8 %all-to-all-start.3 = ((bf16[16,16,640]{2,1,0:T(8,128)(2,1)}), bf16[16,16,640]{2,1,0:T(8,128)(2,1)S(1)}, u32[]{:S(2)}, u32[]{:S(2)}) async-start(bf16[16,16,640]{2,1,0:T(8,128)(2,1)} %get-tuple-element.45), calls=%async_computation.3 | async-start | bytes 655360 | tf_op jit(solution)/shard_map/all_to_all | solution.py:277
  118.3 4.3 %collective-permute-start.12 = (bf16[8,256,128]{2,1,0:T(8,128)(2,1)S(1)}, bf16[8,256,128]{2,1,0:T(8,128)(2,1)S(1)}, u32[]{:S(2)}, u32[]{:S(2)}) collective-permute-start(bf16[8,256,128]{2,1,0:T(8,128)(2,1)S(1)} %constant_dynamic-update-slice_fusion.a0), channel_id=1, source_target_pairs={{0,16},{1,17},{2,18},{3,19},{4,20},{5,21},{6,22},{7,23},{8,24},{9,... | collective-permute-start | bytes 1572872 | tf_op jit(solution)/shard_map/ppermute | solution.py:73
  122.6 1.9 %collective-permute-start.13 = (bf16[8,256,128]{2,1,0:T(8,128)(2,1)S(1)}, bf16[8,256,128]{2,1,0:T(8,128)(2,1)S(1)}, u32[]{:S(2)}, u32[]{:S(2)}) collective-permute-start(bf16[8,256,128]{2,1,0:T(8,128)(2,1)S(1)} %constant_dynamic-update-slice_fusion.a0), channel_id=1, source_target_pairs={{0,1},{1,0},{2,3},{3,2},{4,5},{5,4},{6,7},{7,6},{8,9},{9,8},{10,11... | collective-permute-start | bytes 1572872 | tf_op jit(solution)/shard_map/ppermute | solution.py:73
  124.6 8.0 %collective-permute-done.12.a1 = bf16[8,256,128]{2,1,0:T(8,128)(2,1)S(1)} collective-permute-done((bf16[8,256,128]{2,1,0:T(8,128)(2,1)S(1)}, bf16[8,256,128]{2,1,0:T(8,128)(2,1)S(1)}, u32[]{:S(2)}, u32[]{:S(2)}) %collective-permute-start.12) | collective-permute-done | bytes 524320 | tf_op jit(solution)/shard_map/ppermute | solution.py:73
  132.6 1.9 %collective-permute-start.14 = (bf16[8,256,128]{2,1,0:T(8,128)(2,1)S(1)}, bf16[8,256,128]{2,1,0:T(8,128)(2,1)S(1)}, u32[]{:S(2)}, u32[]{:S(2)}) collective-permute-start(bf16[8,256,128]{2,1,0:T(8,128)(2,1)S(1)} %collective-permute-done.12.a1), channel_id=1, source_target_pairs={{0,1},{1,0},{2,3},{3,2},{4,5},{5,4},{6,7},{7,6},{8,9},{9,8},{10,11... | collective-permute-start | bytes 1572872 | tf_op jit(solution)/shard_map/ppermute | solution.py:73
  134.5 0.0 all-to-all-done.3.arrived
  134.5 0.8 shard_map.121
  135.3 7.3 %all-to-all-start.4 = ((bf16[16,16,640]{2,1,0:T(8,128)(2,1)}), bf16[16,16,640]{2,1,0:T(8,128)(2,1)S(1)}, u32[]{:S(2)}, u32[]{:S(2)}) async-start(bf16[16,16,640]{2,1,0:T(8,128)(2,1)} %shard_map.121), calls=%async_computation.4 | async-start | bytes 655360 | tf_op jit(solution)/shard_map/all_to_all | solution.py:277
  142.6 0.0 collective-permute-done.13.b0
  142.6 7.6 %shard_map.120 = bf16[448,256]{1,0:T(8,128)(2,1)} custom-call(s32[4]{0:T(128)S(1)} %pad_add_fusion.where, bf16[8,256,128]{2,1,0:T(8,128)(2,1)S(1)} %constant_dynamic-update-slice_fusion.a0, bf16[8,256,128]{2,1,0:T(8,128)(2,1)S(1)} %collective-permute-done.12.a1, bf16[8,256,128]{2,1,0:T(8,128)(2,1)S(1)} %collective-permute-done.13.b0, ...), custom_call_target="tpu_custom_call" | custom-call | flops 998244352 | bytes 3670016 | tf_op jit(solution)/shard_map/pallas_call | solution.py:482
  150.2 4.4 %all-to-all-done.4.fifth = bf16[16,16,640]{2,1,0:T(8,128)(2,1)S(1)} async-done(((bf16[16,16,640]{2,1,0:T(8,128)(2,1)}), bf16[16,16,640]{2,1,0:T(8,128)(2,1)S(1)}, u32[]{:S(2)}, u32[]{:S(2)}) %all-to-all-start.4) | async-done | bytes 327712 | tf_op jit(solution)/shard_map/all_to_all | solution.py:277
  154.6 0.8 shard_map.122
  (22 shorter events, 0.2 us)
Async XLA Ops:
  0.8 36.6 %copy-start.2 = (bf16[16,16,128]{2,1,0:T(8,128)(2,1)S(1)}, bf16[16,16,128]{2,1,0:T(8,128)(2,1)}, u32[]{:S(2)}) copy-start(bf16[16,16,128]{2,1,0:T(8,128)(2,1)} %up.1) | copy-start | bytes 196612
  0.8 45.6 %copy-start = (bf16[16,448,16]{1,2,0:T(8,128)(2,1)S(1)}, bf16[16,448,16]{1,2,0:T(8,128)(2,1)}, u32[]{:S(2)}) copy-start(bf16[16,448,16]{1,2,0:T(8,128)(2,1)} %param.9) | copy-start | bytes 688132
  0.8 45.6 %copy-start.1 = (bf16[256,448]{0,1:T(8,128)(2,1)S(1)}, bf16[256,448]{0,1:T(8,128)(2,1)}, u32[]{:S(2)}) copy-start(bf16[256,448]{0,1:T(8,128)(2,1)} %param.7) | copy-start | bytes 688132
  0.8 45.6 %copy-start.5 = (s32[16]{0:T(128)S(1)}, s32[16]{0:T(128)}, u32[]{:S(2)}) copy-start(s32[16]{0:T(128)} %seg.5) | copy-start | bytes 196
  8.7 44.9 %copy-start.3 = (bf16[256,128]{1,0:T(8,128)(2,1)S(1)}, bf16[256,128]{1,0:T(8,128)(2,1)}, u32[]{:S(2)}) copy-start(bf16[256,128]{1,0:T(8,128)(2,1)} %cotangent.3) | copy-start | bytes 196612
  8.7 44.9 %copy-start.4 = (bf16[16,128]{1,0:T(8,128)(2,1)S(1)}, bf16[16,128]{1,0:T(8,128)(2,1)}, u32[]{:S(2)}) copy-start(bf16[16,128]{1,0:T(8,128)(2,1)} %magnitude.3) | copy-start | bytes 12292
  8.7 15.3 %collective-permute-start.2 = (bf16[16,256,128]{2,1,0:T(8,128)(2,1)}, bf16[16,256,128]{2,1,0:T(8,128)(2,1)S(1)}, u32[]{:S(2)}, u32[]{:S(2)}) collective-permute-start(bf16[16,256,128]{2,1,0:T(8,128)(2,1)} %get-tuple-element.30), channel_id=1, source_target_pairs={{0,1},{1,0},{2,3},{3,2},{4,5},{5,4},{6,7},{7,6},{8,9},{9,8},{10,11... | collective-permute-start | bytes 3145736 | tf_op jit(solution)/shard_map/ppermute | solution.py:73
  10.7 26.7 %all-to-all-start = ((bf16[32,24,128]{2,1,0:T(8,128)(2,1)}), bf16[32,24,128]{2,1,0:T(8,128)(2,1)S(1)}, u32[]{:S(2)}, u32[]{:S(2)}) async-start(bf16[32,24,128]{2,1,0:T(8,128)(2,1)} %get-tuple-element.27), calls=%async_computation | async-start | bytes 393216 | tf_op jit(solution)/shard_map/all_to_all | solution.py:277
  26.1 55.2 %collective-permute-start.3 = (bf16[8,256,128]{2,1,0:T(8,128)(2,1)}, bf16[8,256,128]{2,1,0:T(8,128)(2,1)S(1)}, u32[]{:S(2)}, u32[]{:S(2)}) collective-permute-start(bf16[8,256,128]{2,1,0:T(8,128)(2,1)} %get-tuple-element.32), channel_id=1, source_target_pairs={{0,16},{1,17},{2,18},{3,19},{4,20},{5,21},{6,22},{7,23},{8,24},{9,... | collective-permute-start | bytes 1572872 | tf_op jit(solution)/shard_map/ppermute | solution.py:73
  38.7 14.8 %all-to-all-start.1 = ((f32[16,2,128]{2,1,0:T(2,128)}), f32[16,2,128]{2,1,0:T(2,128)S(1)}, u32[]{:S(2)}, u32[]{:S(2)}) async-start(f32[16,2,128]{2,1,0:T(2,128)} %shard_map.111), calls=%async_computation.1 | async-start | bytes 32768 | tf_op jit(solution)/shard_map/all_to_all | solution.py:277
  55.3 13.4 %all-to-all-start.2 = ((bf16[8,64,128]{2,1,0:T(8,128)(2,1)}), bf16[8,64,128]{2,1,0:T(8,128)(2,1)S(1)}, u32[]{:S(2)}, u32[]{:S(2)}) async-start(bf16[8,64,128]{2,1,0:T(8,128)(2,1)} %get-tuple-element.28), calls=%async_computation.2 | async-start | bytes 262144 | tf_op jit(solution)/shard_map/all_to_all | solution.py:277
  58.7 7.5 %collective-permute-start.8 = (bf16[256,128]{1,0:T(8,128)(2,1)S(1)}, bf16[256,128]{1,0:T(8,128)(2,1)S(1)}, u32[]{:S(2)}, u32[]{:S(2)}) collective-permute-start(bf16[256,128]{1,0:T(8,128)(2,1)S(1)} %get-tuple-element.40.scaled.own), channel_id=1, source_target_pairs={{0,2},{1,3},{2,4},{3,5},{4,6},{5,7},{6,8},{7,9},{8,10},{9,11},{10,... | collective-permute-start | bytes 196616 | tf_op jit(solution)/shard_map/ppermute | solution.py:73
  62.5 6.2 %collective-permute-start.9 = (bf16[256,128]{1,0:T(8,128)(2,1)S(1)}, bf16[256,128]{1,0:T(8,128)(2,1)S(1)}, u32[]{:S(2)}, u32[]{:S(2)}) collective-permute-start(bf16[256,128]{1,0:T(8,128)(2,1)S(1)} %get-tuple-element.40.scaled.own), channel_id=1, source_target_pairs={{0,14},{1,15},{2,0},{3,1},{4,2},{5,3},{6,4},{7,5},{8,6},{9,7},{10,... | collective-permute-start | bytes 196616 | tf_op jit(solution)/shard_map/ppermute | solution.py:73
  68.7 22.1 %collective-permute-start = (bf16[64,128]{1,0:T(8,128)(2,1)S(1)}, bf16[64,128]{1,0:T(8,128)(2,1)S(1)}, u32[]{:S(2)}, u32[]{:S(2)}) collective-permute-start(bf16[64,128]{1,0:T(8,128)(2,1)S(1)} %shard_map.114), channel_id=1, source_target_pairs={{0,16},{1,17},{2,18},{3,19},{4,20},{5,21},{6,22},{7,23},{8,24},{9,... | collective-permute-start | bytes 49160 | tf_op jit(solution)/shard_map/ppermute | solution.py:73
  71.7 34.3 %collective-permute-start.10 = (bf16[3,256,128]{2,1,0:T(8,128)(2,1)S(1)}, bf16[3,256,128]{2,1,0:T(8,128)(2,1)S(1)}, u32[]{:S(2)}, u32[]{:S(2)}) collective-permute-start(bf16[3,256,128]{2,1,0:T(8,128)(2,1)S(1)} %get-tuple-element.42), channel_id=1, source_target_pairs={{0,6},{1,7},{2,8},{3,9},{4,10},{5,11},{6,12},{7,13},{8,14},{9,15},... | collective-permute-start | bytes 589832 | tf_op jit(solution)/shard_map/ppermute | solution.py:73
  79.3 39.0 %collective-permute-start.11 = (bf16[2,256,128]{2,1,0:T(8,128)(2,1)S(1)}, bf16[2,256,128]{2,1,0:T(8,128)(2,1)S(1)}, u32[]{:S(2)}, u32[]{:S(2)}) collective-permute-start(bf16[2,256,128]{2,1,0:T(8,128)(2,1)S(1)} %get-tuple-element.43), channel_id=1, source_target_pairs={{0,10},{1,11},{2,12},{3,13},{4,14},{5,15},{6,0},{7,1},{8,2},{9,3},... | collective-permute-start | bytes 393224 | tf_op jit(solution)/shard_map/ppermute | solution.py:73
  82.0 18.1 %collective-permute-start.4 = (bf16[3,256,128]{2,1,0:T(8,128)(2,1)S(1)}, bf16[3,256,128]{2,1,0:T(8,128)(2,1)S(1)}, u32[]{:S(2)}, u32[]{:S(2)}) collective-permute-start(bf16[3,256,128]{2,1,0:T(8,128)(2,1)S(1)} %get-tuple-element.34), channel_id=1, source_target_pairs={{0,6},{1,7},{2,8},{3,9},{4,10},{5,11},{6,12},{7,13},{8,14},{9,15},... | collective-permute-start | bytes 589832 | tf_op jit(solution)/shard_map/ppermute | solution.py:73
  87.7 10.4 %collective-permute-start.5 = (bf16[2,256,128]{2,1,0:T(8,128)(2,1)S(1)}, bf16[2,256,128]{2,1,0:T(8,128)(2,1)S(1)}, u32[]{:S(2)}, u32[]{:S(2)}) collective-permute-start(bf16[2,256,128]{2,1,0:T(8,128)(2,1)S(1)} %get-tuple-element.35), channel_id=1, source_target_pairs={{0,10},{1,11},{2,12},{3,13},{4,14},{5,15},{6,0},{7,1},{8,2},{9,3},... | collective-permute-start | bytes 393224 | tf_op jit(solution)/shard_map/ppermute | solution.py:73
  90.9 15.2 %collective-permute-start.1 = (bf16[64,128]{1,0:T(8,128)(2,1)S(1)}, bf16[64,128]{1,0:T(8,128)(2,1)S(1)}, u32[]{:S(2)}, u32[]{:S(2)}) collective-permute-start(bf16[64,128]{1,0:T(8,128)(2,1)S(1)} %add_convert_fusion.ranks), channel_id=1, source_target_pairs={{0,1},{1,0},{2,3},{3,2},{4,5},{5,4},{6,7},{7,6},{8,9},{9,8},{10,11... | collective-permute-start | bytes 49160 | tf_op jit(solution)/shard_map/ppermute | solution.py:73
  100.2 6.2 %collective-permute-start.6 = (bf16[256,128]{1,0:T(8,128)(2,1)S(1)}, bf16[256,128]{1,0:T(8,128)(2,1)S(1)}, u32[]{:S(2)}, u32[]{:S(2)}) collective-permute-start(bf16[256,128]{1,0:T(8,128)(2,1)S(1)} %get-tuple-element.37), channel_id=1, source_target_pairs={{0,14},{1,15},{2,0},{3,1},{4,2},{5,3},{6,4},{7,5},{8,6},{9,7},{10,... | collective-permute-start | bytes 196616 | tf_op jit(solution)/shard_map/ppermute | solution.py:73
  103.8 7.4 %collective-permute-start.7 = (bf16[256,128]{1,0:T(8,128)(2,1)S(1)}, bf16[256,128]{1,0:T(8,128)(2,1)S(1)}, u32[]{:S(2)}, u32[]{:S(2)}) collective-permute-start(bf16[256,128]{1,0:T(8,128)(2,1)S(1)} %get-tuple-element.38), channel_id=1, source_target_pairs={{0,2},{1,3},{2,4},{3,5},{4,6},{5,7},{6,8},{7,9},{8,10},{9,11},{10,... | collective-permute-start | bytes 196616 | tf_op jit(solution)/shard_map/ppermute | solution.py:73
  113.5 21.0 %all-to-all-start.3 = ((bf16[16,16,640]{2,1,0:T(8,128)(2,1)}), bf16[16,16,640]{2,1,0:T(8,128)(2,1)S(1)}, u32[]{:S(2)}, u32[]{:S(2)}) async-start(bf16[16,16,640]{2,1,0:T(8,128)(2,1)} %get-tuple-element.45), calls=%async_computation.3 | async-start | bytes 655360 | tf_op jit(solution)/shard_map/all_to_all | solution.py:277
  118.3 14.3 %collective-permute-start.12 = (bf16[8,256,128]{2,1,0:T(8,128)(2,1)S(1)}, bf16[8,256,128]{2,1,0:T(8,128)(2,1)S(1)}, u32[]{:S(2)}, u32[]{:S(2)}) collective-permute-start(bf16[8,256,128]{2,1,0:T(8,128)(2,1)S(1)} %constant_dynamic-update-slice_fusion.a0), channel_id=1, source_target_pairs={{0,16},{1,17},{2,18},{3,19},{4,20},{5,21},{6,22},{7,23},{8,24},{9,... | collective-permute-start | bytes 1572872 | tf_op jit(solution)/shard_map/ppermute | solution.py:73
  122.6 20.0 %collective-permute-start.13 = (bf16[8,256,128]{2,1,0:T(8,128)(2,1)S(1)}, bf16[8,256,128]{2,1,0:T(8,128)(2,1)S(1)}, u32[]{:S(2)}, u32[]{:S(2)}) collective-permute-start(bf16[8,256,128]{2,1,0:T(8,128)(2,1)S(1)} %constant_dynamic-update-slice_fusion.a0), channel_id=1, source_target_pairs={{0,1},{1,0},{2,3},{3,2},{4,5},{5,4},{6,7},{7,6},{8,9},{9,8},{10,11... | collective-permute-start | bytes 1572872 | tf_op jit(solution)/shard_map/ppermute | solution.py:73
  132.6 10.0 %collective-permute-start.14 = (bf16[8,256,128]{2,1,0:T(8,128)(2,1)S(1)}, bf16[8,256,128]{2,1,0:T(8,128)(2,1)S(1)}, u32[]{:S(2)}, u32[]{:S(2)}) collective-permute-start(bf16[8,256,128]{2,1,0:T(8,128)(2,1)S(1)} %collective-permute-done.12.a1), channel_id=1, source_target_pairs={{0,1},{1,0},{2,3},{3,2},{4,5},{5,4},{6,7},{7,6},{8,9},{9,8},{10,11... | collective-permute-start | bytes 1572872 | tf_op jit(solution)/shard_map/ppermute | solution.py:73
  135.3 19.4 %all-to-all-start.4 = ((bf16[16,16,640]{2,1,0:T(8,128)(2,1)}), bf16[16,16,640]{2,1,0:T(8,128)(2,1)S(1)}, u32[]{:S(2)}, u32[]{:S(2)}) async-start(bf16[16,16,640]{2,1,0:T(8,128)(2,1)} %shard_map.121), calls=%async_computation.4 | async-start | bytes 655360 | tf_op jit(solution)/shard_map/all_to_all | solution.py:277

commit v4 on v3

--- a/solution.py
+++ b/solution.py
@@ -115,36 +115,37 @@
         gram[0:1, :] = jnp.sum(spread[:8], axis=0, keepdims=True)
         gram[1:2, :] = jnp.sum(spread[8:], axis=0, keepdims=True)
 
-    block = weight[...]
-    both = dot(lines[...], block, 1, 0)
     share = 32
     pieces = weight.shape[0] // share
     part = weight[pl.ds(pl.multiple_of(jnp.minimum(where[0], pieces - 1) * share, share), share), :]
     part = part.astype(F32)
     squares = jnp.sum(part * part, axis=0, keepdims=True) * (where[0] < pieces).astype(F32)
     row = iota((8, LANES), 0)
-    for k in range(4):
-        lanes = slice(k * LANES, (k + 1) * LANES)
-        tail = jnp.where(
-            row == 0,
-            squares[:, lanes],
-            jnp.where(row == 1, gram[0:1, :], jnp.where(row == 2, gram[1:2, :], 0.0)),
-        )
-        head[k] = jnp.concatenate([both[count:, lanes], tail], axis=0).astype(BF16)
-
-    base = both[:count].astype(BF16)
-
-    @pl.when(where[1] == 0)
-    def _():
+    for block in range(0, weight.shape[1], 4 * LANES):
+        both = dot(lines[...], weight[:, block : block + 4 * LANES], 1, 0)
+        base = both[:count].astype(BF16)
+        for k in range(4):
+            lanes = slice(k * LANES, (k + 1) * LANES)
+            tail = jnp.where(
+                row == 0,
+                squares[:, block + k * LANES : block + (k + 1) * LANES],
+                jnp.where(row == 1, gram[0:1, :], jnp.where(row == 2, gram[1:2, :], 0.0)),
+            )
+            head[block // LANES + k] = jnp.concatenate([both[count:, lanes], tail], 0).astype(BF16)
         for k in range(2):
-            keep[k] = base[:, 2 * k * LANES : (2 * k + 1) * LANES]
-            give[k] = base[:, (2 * k + 1) * LANES : (2 * k + 2) * LANES]
-
-    @pl.when(where[1] != 0)
-    def _():
-        for k in range(2):
-            give[k] = base[:, 2 * k * LANES : (2 * k + 1) * LANES]
-            keep[k] = base[:, (2 * k + 1) * LANES : (2 * k + 2) * LANES]
+            at = block // LANES // 2 + k
+            even = base[:, 2 * k * LANES : (2 * k + 1) * LANES]
+            odd = base[:, (2 * k + 1) * LANES : (2 * k + 2) * LANES]
+
+            @pl.when(where[1] == 0)
+            def _():
+                keep[at] = even
+                give[at] = odd
+
+            @pl.when(where[1] != 0)
+            def _():
+                keep[at] = odd
+                give[at] = even
 
 
 def low_kernel(where, seg, tokens, down, low):
@@ -180,18 +181,26 @@
             out[i] = (keep[at].astype(F32) + got[at].astype(F32)).astype(BF16)
 
 
-def near_kernel(near, up, down, before, after, own):
-    before[...] = (near[0].astype(F32) + up[0].astype(F32)).astype(BF16)
-    after[...] = (near[2].astype(F32) + up[2].astype(F32) + down[1].astype(F32)).astype(BF16)
+def near_kernel(near, up, down, scaled, before, after, own):
+    before[0] = (near[0].astype(F32) + up[0].astype(F32)).astype(BF16)
+    before[1] = scaled[...]
+    after[0] = (near[2].astype(F32) + up[2].astype(F32) + down[1].astype(F32)).astype(BF16)
+    after[1] = scaled[...]
     own[...] = near[1].astype(F32) + up[1].astype(F32) + down[0].astype(F32)
 
 
 def trio_kernel(before, own, after, trio, pair):
-    trio[0] = before[...]
+    trio[0] = before[0]
     trio[1] = own[...]
-    trio[2] = after[...]
-    pair[0] = before[...]
+    trio[2] = after[0]
+    pair[0] = before[0]
     pair[1] = own[...]
+
+
+def join_kernel(near, up, down, out):
+    out[:3] = near[...]
+    out[3:6] = up[...]
+    out[6:] = down[...]
 
 
 def scale_kernel(where, seg, second, magnitude, cotangent, up, low, third, scaled, norms):
@@ -209,21 +218,17 @@
     third[...] = jnp.broadcast_to(every[None], third.shape)
 
 
-def sums_kernel(rank_rows, ranks):
-    ranks[...] = jnp.sum(rank_rows[...].astype(F32), axis=0).astype(BF16)
-
-
-def grads_kernel(where, seg, ranks, got, base, base_a, base_b, norms, magnitude, cotangent, scaled, up, tokens,
+def grads_kernel(where, seg, ranks, base, base_a, base_b, norms, magnitude, cotangent, scaled, up, tokens,
                  fourth, projected, back_wide):
     adapters = seg.shape[0]
     own_rows, count = tokens.shape
     rank = up.shape[0] // adapters
     marks = bounds(seg, adapters, where[0] * count)
-    total = ranks[...].astype(F32) + got[...].astype(F32)
+    total = jnp.sum(ranks[...].astype(F32), axis=0)
     low = widened(unpacked(total[: 2 * rank]), marks)
     back = widened(unpacked(total[2 * rank :]), marks)
     back_wide[...] = back
-    hidden = base[...] + base_a[...].astype(F32) + base_b[...].astype(F32)
+    hidden = base[...] + base_a[0].astype(F32) + base_b[0].astype(F32)
     hidden = hidden + dot(low, up[...], 0, 0)
     scale = token_scale_of(magnitude[...].astype(F32) / norms[...], marks, count)
     projected[...] = (hidden * scale).astype(BF16)
@@ -257,16 +262,17 @@
     grad_magnitude[...] = total / norms[...]
 
 
-def tokens_kernel(where, a0, a1, b0, b1, w0, w1, w2, w3, back, down, out, total):
+def tokens_kernel(where, a0, a1, b0, b1, *rest):
+    *columns, back, down, out, total = rest
     step = pl.program_id(0)
 
     @pl.when(step == 0)
     def _():
         total[...] = dot(down[...], back[...], 0, 0)
 
-    left = jnp.concatenate([a0[0], a1[0], b0[0], b1[0]], axis=1)
-    right = jnp.concatenate([w0[...], w1[...], w2[...], w3[...]], axis=1)
-    total[...] += dot(right, left, 1, 1)
+    left = [block[i] for i in range(a0.shape[0]) for block in (a0, a1, b0, b1)]
+    right = [column[...] for column in columns]
+    total[...] += dot(jnp.concatenate(right, axis=1), jnp.concatenate(left, axis=1), 1, 1)
 
     @pl.when(step == pl.num_programs(0) - 1)
     def _():
@@ -292,7 +298,6 @@
     where = jnp.stack([me_dp, core, hi, z]).astype(I32)
     core_pairs = [(i, i ^ 1) for i in range(size)]
     hi_pairs = [(i, (i + size // 2) % size) for i in range(size)]
-    z_groups = [[h * 2 * zs + z * 2 + c for z in range(zs)] for h in range(2) for c in range(2)]
 
     turned = tokens.T
     down_rows = jnp.transpose(adapter_down, (0, 2, 1))
@@ -303,16 +308,16 @@
         first_kernel,
         [shaped(size, HEAD, width), shaped(size // 2, count, width), shaped(size // 2, count, width)],
         scalars=1,
-        grid=(size // 4,),
+        grid=(2,),
         in_specs=[
             whole(own_rows, count),
-            pl.BlockSpec((own_rows, 4 * width), lambda i, s: (0, i)),
+            pl.BlockSpec((own_rows, full // 2), lambda i, s: (0, i)),
             pl.BlockSpec((1, rank, own_rows), lambda i, s: (s[0], 0, 0)),
         ],
         out_specs=[
-            pl.BlockSpec((4, HEAD, width), lambda i, s: (i, 0, 0)),
-            pl.BlockSpec((2, count, width), lambda i, s: (i, 0, 0)),
-            pl.BlockSpec((2, count, width), lambda i, s: (i, 0, 0)),
+            pl.BlockSpec((size // 2, HEAD, width), lambda i, s: (i, 0, 0)),
+            pl.BlockSpec((size // 4, count, width), lambda i, s: (i, 0, 0)),
+            pl.BlockSpec((size // 4, count, width), lambda i, s: (i, 0, 0)),
         ],
         scratch=[pltpu.VMEM((8, width), F32), pltpu.VMEM((count + rank, own_rows), BF16)],
         flops=2 * count * own_rows * full,
@@ -381,7 +386,7 @@
 
     third, scaled, norms = call(
         scale_kernel,
-        [shaped(zs, 4 * rank, width), shaped(count, width), shaped(adapters, width, dtype=F32)],
+        [shaped(size, 4 * rank, width), shaped(count, width), shaped(adapters, width, dtype=F32)],
         scalars=2,
         grid=(1,),
         in_specs=[
@@ -391,48 +396,45 @@
             whole(wide, width),
             whole(2 * rank, width),
         ],
-        out_specs=[whole(zs, 4 * rank, width), whole(count, width), whole(adapters, width)],
+        out_specs=[whole(size, 4 * rank, width), whole(count, width), whole(adapters, width)],
         flops=2 * count * wide * width,
         moved=8 * count * width,
     )(where, seg_lengths, second, magnitude, cotangent, up_own, low)
-    third = exchange(third, "tensor", z_groups)
-    from_below = shift(scaled, along_z(1))
-    from_above = shift(scaled, along_z(-1))
+    third = exchange(third, "tensor")
 
     before, after, base = call(
         near_kernel,
-        [shaped(count, width), shaped(count, width), shaped(count, width, dtype=F32)],
-        grid=(1,),
-        in_specs=[whole(3, count, width), whole(3, count, width), whole(2, count, width)],
-        out_specs=[whole(count, width)] * 3,
+        [shaped(2, count, width), shaped(2, count, width), shaped(count, width, dtype=F32)],
+        grid=(1,),
+        in_specs=[whole(n, count, width) for n in (3, 3, 2)] + [whole(count, width)],
+        out_specs=[whole(2, count, width), whole(2, count, width), whole(count, width)],
         moved=24 * count * width,
-    )(near, up3, down2)
-    base_a = shift(before, along_z(-1))
-    base_b = shift(after, along_z(1))
-
-    ranks = call(
-        sums_kernel,
-        shaped(4 * rank, width),
-        grid=(1,),
-        in_specs=[whole(zs, 4 * rank, width)],
-        out_specs=whole(4 * rank, width),
-        moved=2 * zs * 4 * rank * width,
-    )(third)
-    ranks = (ranks.astype(F32) + shift(ranks, hi_pairs).astype(F32)).astype(BF16)
-    other = shift(ranks, core_pairs)
+    )(near, up3, down2, scaled)
+    from_above = shift(before, along_z(-1))
+    from_below = shift(after, along_z(1))
+
+    second_block = pl.BlockSpec((1, count, width), lambda i: (1, 0, 0))
     trio, pair = call(
         trio_kernel,
         [shaped(3, count, width), shaped(2, count, width)],
         grid=(1,),
-        in_specs=[whole(count, width)] * 3,
+        in_specs=[second_block, whole(count, width), second_block],
         out_specs=[whole(3, count, width), whole(2, count, width)],
         moved=16 * count * width,
     )(from_below, scaled, from_above)
     far_up = shift(trio, along_z(3))
     far_down = shift(pair, along_z(-3))
-    gather_a = jnp.concatenate([trio, far_up, far_down], axis=0)
+    gather_a = call(
+        join_kernel,
+        shaped(zs, count, width),
+        grid=(1,),
+        in_specs=[whole(n, count, width) for n in (3, 3, 2)],
+        out_specs=whole(zs, count, width),
+        moved=4 * zs * count * width,
+    )(trio, far_up, far_down)
     gather_b = shift(gather_a, hi_pairs)
 
+    first_block = pl.BlockSpec((1, count, width), lambda i, *s: (0, 0, 0))
     blocks = rank * 40
     fourth, projected, back_wide = call(
         grads_kernel,
@@ -440,11 +442,10 @@
         scalars=2,
         grid=(1,),
         in_specs=[
-            whole(4 * rank, width),
-            whole(4 * rank, width),
+            whole(size, 4 * rank, width),
             whole(count, width),
-            whole(count, width),
-            whole(count, width),
+            first_block,
+            first_block,
             whole(adapters, width),
             whole(adapters, width),
             whole(count, width),
@@ -455,7 +456,7 @@
         out_specs=[whole(adapters, rank, blocks), whole(count, width), whole(wide, count)],
         flops=2 * count * wide * (own_rows + 2 * width),
         moved=4 * adapters * rank * blocks,
-    )(where, seg_lengths, ranks, other, base, base_a, base_b, norms, magnitude, cotangent, scaled, up_own, turned)
+    )(where, seg_lengths, third, base, from_below, from_above, norms, magnitude, cotangent, scaled, up_own, turned)
     fourth = exchange(fourth, "dp")
     gather_c = shift(gather_a, core_pairs)
     gather_d = shift(gather_b, core_pairs)
@@ -470,28 +471,34 @@
     )(fourth)
     fifth = exchange(fifth, "dp")
 
-    def column(x_bit, c_bit):
+    per = 4
+
+    def column(k, x_bit, c_bit):
         def at(i, s):
-            off = jnp.where(i < 3, i - 1, jnp.where(i < 6, i - 7, i - 4))
+            slot = i * per + k
+            off = jnp.where(slot < 3, slot - 1, jnp.where(slot < 6, slot - 7, slot - 4))
             block = (s[3] + off + zs) % zs
             return (0, (s[2] ^ x_bit) * (2 * zs) + block * 2 + (s[1] ^ c_bit))
 
         return pl.BlockSpec((own_rows, width), at)
 
-    block = pl.BlockSpec((1, count, width), lambda i, s: (i, 0, 0))
+    columns = [
+        column(k, x, c) for k in range(per) for x, c in ((0, 0), (1, 0), (0, 1), (1, 1))
+    ]
+    block = pl.BlockSpec((per, count, width), lambda i, s: (i, 0, 0))
     grad_tokens = call(
         tokens_kernel,
         shaped(own_rows, count),
         scalars=1,
-        grid=(zs,),
+        grid=(zs // per,),
         in_specs=[block] * 4
-        + [column(0, 0), column(1, 0), column(0, 1), column(1, 1)]
+        + columns
         + [whole(wide, count), whole(wide, own_rows)],
         out_specs=whole(own_rows, count),
         scratch=[pltpu.VMEM((own_rows, count), F32)],
         flops=2 * count * own_rows * (full + wide),
         moved=2 * own_rows * full,
-    )(where, gather_a, gather_b, gather_c, gather_d, *[in_hbm(base_weight)] * 4, back_wide, down_flat)
+    )(where, gather_a, gather_b, gather_c, gather_d, *[in_hbm(base_weight)] * (4 * per), back_wide, down_flat)
 
     grad_down, grad_up, grad_magnitude = call(
         final_kernel,

time: 157 us -> 166 us (1.057)
  blocking collectives: 0 us -> 26.4 us
  starting transfers between devices: 87.9 us -> 63.5 us
  waiting for transfers between devices: 40.2 us -> 52.8 us
  Pallas kernels: 26.2 us -> 20.3 us
    all_to_all x0 -> x1, blocking collectives: none -> 26.4 us  [exchange(): lax.all_to_all(blocks, axis, 0, 0, tiled=True, axis_index_groups=groups)]
    ppermute x15 -> x11, waiting for transfers between devices: 23.3 us -> 42.5 us  [shift(): return lax.ppermute(block, 'tensor', pairs)]
    all_to_all x5 -> x4, starting transfers between devices: 36.3 us -> 23.8 us  [exchange(): lax.all_to_all(blocks, axis, 0, 0, tiled=True, axis_index_groups=groups)]
    ppermute x15 -> x11, starting transfers between devices: 51.5 us -> 39.7 us  [shift(): return lax.ppermute(block, 'tensor', pairs)]
    all_to_all x5 -> x4, waiting for transfers between devices: 16.9 us -> 10.3 us  [exchange(): lax.all_to_all(blocks, axis, 0, 0, tiled=True, axis_index_groups=groups)]
    pallas_call x4, Pallas kernels: 9.48 us -> 6.25 us  [the longest x1 5 us: local(): call(tokens_kernel, shaped(own_rows, count), scalars=1, grid=(zs // per,)...]
  transfers between devices with their start and end apart: 20 -> 15, of which waited for: 10 -> 9; matrix products, arithmetic and copies ran while one was open for 0% -> 0% of each run, Pallas kernels for 11% -> 5%
where the time goes in v4:
time: 166 us; the launch traced here: 165 us
  starting transfers between devices  63.5 us (38%)
  waiting for transfers between devices  52.8 us (32%)
  blocking collectives  26.4 us (16%)
  Pallas kernels  20.3 us (12%)
    ppermute x11, waiting for transfers between devices, shift(): return lax.ppermute(block, 'tensor', pairs)  42.5 us
    ppermute x11, starting transfers between devices, shift(): return lax.ppermute(block, 'tensor', pairs)  39.7 us
    all_to_all x1, blocking collectives, exchange(): lax.all_to_all(blocks, axis, 0, 0, tiled=True, axis_index_groups=groups)  26.4 us
    all_to_all x4, starting transfers between devices, exchange(): lax.all_to_all(blocks, axis, 0, 0, tiled=True, axis_index_groups=groups)  23.8 us
    all_to_all x4, waiting for transfers between devices, exchange(): lax.all_to_all(blocks, axis, 0, 0, tiled=True, axis_index_groups=groups)  10.3 us
    pallas_call x1, Pallas kernels, local(): call(first_kernel, [shaped(size, HEAD, width), shaped(size // 2, count, w...  6.34 us
    pallas_call x1, Pallas kernels, local(): call(tokens_kernel, shaped(own_rows, count), scalars=1, grid=(zs // per,)...  5 us
  transfers between devices with their start and end apart: 15, of which 9 were waited for; matrix products, arithmetic and copies ran while one was open for 0% of the time, Pallas kernels for 5%

profile of v4, /device:TPU:8, one launch (start us, length us, event | category | flops | bytes accessed | tf_op | source)
XLA Modules:
  0.0 164.8 jit_solution(14304799108295520588)
XLA Ops:
  0.6 0.0 copy-start.1
  0.6 0.0 copy-start
  0.7 0.1 pad_add_fusion.where
  0.8 6.3 %shard_map.110 = (bf16[32,24,128]{2,1,0:T(8,128)(2,1)S(1)}, bf16[16,256,128]{2,1,0:T(8,128)(2,1)S(1)}, bf16[16,256,128]{2,1,0:T(8,128)(2,1)}) custom-call(s32[4]{0:T(128)S(1)} %pad_add_fusion.where, bf16[448,256]{1,0:T(8,128)(2,1)} %bitcast.14, bf16[448,4096]{1,0:T(8,128)(2,1)} %rest_15_.1, bf16[16,16,448]{2,1,0:T(8,128)(2,1)} %bitcast.11), custom_call_target="tpu_custom_call" | custom-call | flops 939524096 | bytes 3670016 | tf_op jit(solution)/shard_map/pallas_call | solution.py:307
  7.2 1.9 %collective-permute-start = (bf16[16,256,128]{2,1,0:T(8,128)(2,1)}, bf16[16,256,128]{2,1,0:T(8,128)(2,1)S(1)}, u32[]{:S(2)}, u32[]{:S(2)}) collective-permute-start(bf16[16,256,128]{2,1,0:T(8,128)(2,1)} %get-tuple-element.30), channel_id=1, source_target_pairs={{0,1},{1,0},{2,3},{3,2},{4,5},{5,4},{6,7},{7,6},{8,9},{9,8},{10,11... | collective-permute-start | bytes 3145736 | tf_op jit(solution)/shard_map/ppermute | solution.py:73
  9.1 26.4 %all_to_all.25.head = bf16[32,24,128]{2,1,0:T(8,128)(2,1)S(1)} all-to-all(bf16[32,24,128]{2,1,0:T(8,128)(2,1)S(1)} %get-tuple-element.27), channel_id=1, replica_groups=mesh['dp'=16,'tensor'=32] {'tensor'}, dimensions={0} | all-to-all | bytes 393216 | tf_op jit(solution)/shard_map/all_to_all | solution.py:283
  35.4 1.3 shard_map.111
  36.8 7.6 %all-to-all-start.1 = ((f32[16,2,128]{2,1,0:T(2,128)}), f32[16,2,128]{2,1,0:T(2,128)S(1)}, u32[]{:S(2)}, u32[]{:S(2)}) async-start(f32[16,2,128]{2,1,0:T(2,128)} %shard_map.111), calls=%async_computation.1 | async-start | bytes 32768 | tf_op jit(solution)/shard_map/all_to_all | solution.py:283
  44.4 0.0 copy-done.1
  44.4 0.0 copy-done
  44.4 0.8 shard_map.112.low
  45.2 6.4 %all-to-all-done.1.second = f32[16,2,128]{2,1,0:T(2,128)S(1)} async-done(((f32[16,2,128]{2,1,0:T(2,128)}), f32[16,2,128]{2,1,0:T(2,128)S(1)}, u32[]{:S(2)}, u32[]{:S(2)}) %all-to-all-start.1) | async-done | bytes 16416 | tf_op jit(solution)/shard_map/all_to_all | solution.py:283
  51.5 1.1 shard_map.113
  52.7 0.8 copy-done.3
  53.5 3.9 %all-to-all-start.2 = ((bf16[32,64,128]{2,1,0:T(8,128)(2,1)}), bf16[32,64,128]{2,1,0:T(8,128)(2,1)S(1)}, u32[]{:S(2)}, u32[]{:S(2)}) async-start(bf16[32,64,128]{2,1,0:T(8,128)(2,1)} %copy-done.3), calls=%async_computation.2 | async-start | bytes 1048576 | tf_op jit(solution)/shard_map/all_to_all | solution.py:283
  57.4 0.0 collective-permute-done.got_a.got_b
  57.4 0.9 shard_map.114
  58.3 5.2 %collective-permute-start.1 = (bf16[8,256,128]{2,1,0:T(8,128)(2,1)S(1)}, bf16[8,256,128]{2,1,0:T(8,128)(2,1)S(1)}, u32[]{:S(2)}, u32[]{:S(2)}) collective-permute-start(bf16[8,256,128]{2,1,0:T(8,128)(2,1)S(1)} %get-tuple-element.32), channel_id=1, source_target_pairs={{0,16},{1,17},{2,18},{3,19},{4,20},{5,21},{6,22},{7,23},{8,24},{9,... | collective-permute-start | bytes 1572872 | tf_op jit(solution)/shard_map/ppermute | solution.py:73
  63.5 16.6 %collective-permute-done.1.got = bf16[8,256,128]{2,1,0:T(8,128)(2,1)S(1)} collective-permute-done((bf16[8,256,128]{2,1,0:T(8,128)(2,1)S(1)}, bf16[8,256,128]{2,1,0:T(8,128)(2,1)S(1)}, u32[]{:S(2)}, u32[]{:S(2)}) %collective-permute-start.1) | collective-permute-done | bytes 524320 | tf_op jit(solution)/shard_map/ppermute | solution.py:73
  80.1 0.7 shard_map.115
  80.8 5.1 %collective-permute-start.2 = (bf16[3,256,128]{2,1,0:T(8,128)(2,1)S(1)}, bf16[3,256,128]{2,1,0:T(8,128)(2,1)S(1)}, u32[]{:S(2)}, u32[]{:S(2)}) collective-permute-start(bf16[3,256,128]{2,1,0:T(8,128)(2,1)S(1)} %get-tuple-element.34), channel_id=1, source_target_pairs={{0,6},{1,7},{2,8},{3,9},{4,10},{5,11},{6,12},{7,13},{8,14},{9,15},... | collective-permute-start | bytes 589832 | tf_op jit(solution)/shard_map/ppermute | solution.py:73
  85.9 3.8 %collective-permute-start.3 = (bf16[2,256,128]{2,1,0:T(8,128)(2,1)S(1)}, bf16[2,256,128]{2,1,0:T(8,128)(2,1)S(1)}, u32[]{:S(2)}, u32[]{:S(2)}) collective-permute-start(bf16[2,256,128]{2,1,0:T(8,128)(2,1)S(1)} %get-tuple-element.35), channel_id=1, source_target_pairs={{0,10},{1,11},{2,12},{3,13},{4,14},{5,15},{6,0},{7,1},{8,2},{9,3},... | collective-permute-start | bytes 393224 | tf_op jit(solution)/shard_map/ppermute | solution.py:73
  89.7 6.6 %collective-permute-done.3.down = bf16[2,256,128]{2,1,0:T(8,128)(2,1)S(1)} collective-permute-done((bf16[2,256,128]{2,1,0:T(8,128)(2,1)S(1)}, bf16[2,256,128]{2,1,0:T(8,128)(2,1)S(1)}, u32[]{:S(2)}, u32[]{:S(2)}) %collective-permute-start.3) | collective-permute-done | bytes 131104 | tf_op jit(solution)/shard_map/ppermute | solution.py:73
  96.2 4.2 %collective-permute-done.2.up = bf16[3,256,128]{2,1,0:T(8,128)(2,1)S(1)} collective-permute-done((bf16[3,256,128]{2,1,0:T(8,128)(2,1)S(1)}, bf16[3,256,128]{2,1,0:T(8,128)(2,1)S(1)}, u32[]{:S(2)}, u32[]{:S(2)}) %collective-permute-start.2) | collective-permute-done | bytes 196640 | tf_op jit(solution)/shard_map/ppermute | solution.py:73
  100.5 0.1 shard_map.116
  100.6 4.8 %collective-permute-start.4 = (bf16[2,256,128]{2,1,0:T(8,128)(2,1)S(1)}, bf16[2,256,128]{2,1,0:T(8,128)(2,1)S(1)}, u32[]{:S(2)}, u32[]{:S(2)}) collective-permute-start(bf16[2,256,128]{2,1,0:T(8,128)(2,1)S(1)} %get-tuple-element.38), channel_id=1, source_target_pairs={{0,2},{1,3},{2,4},{3,5},{4,6},{5,7},{6,8},{7,9},{8,10},{9,11},{10,... | collective-permute-start | bytes 393224 | tf_op jit(solution)/shard_map/ppermute | solution.py:73
  105.4 2.3 %collective-permute-start.5 = (bf16[2,256,128]{2,1,0:T(8,128)(2,1)S(1)}, bf16[2,256,128]{2,1,0:T(8,128)(2,1)S(1)}, u32[]{:S(2)}, u32[]{:S(2)}) collective-permute-start(bf16[2,256,128]{2,1,0:T(8,128)(2,1)S(1)} %get-tuple-element.39), channel_id=1, source_target_pairs={{0,14},{1,15},{2,0},{3,1},{4,2},{5,3},{6,4},{7,5},{8,6},{9,7},{10,... | collective-permute-start | bytes 393224 | tf_op jit(solution)/shard_map/ppermute | solution.py:73
  107.6 1.0 collective-permute-done.4.base_a.before
  108.6 3.6 %collective-permute-done.5.base_b.after = bf16[2,256,128]{2,1,0:T(8,128)(2,1)S(1)} collective-permute-done((bf16[2,256,128]{2,1,0:T(8,128)(2,1)S(1)}, bf16[2,256,128]{2,1,0:T(8,128)(2,1)S(1)}, u32[]{:S(2)}, u32[]{:S(2)}) %collective-permute-start.5) | collective-permute-done | bytes 131104 | tf_op jit(solution)/shard_map/ppermute | solution.py:73
  112.3 4.9 %collective-permute-start.6 = (bf16[3,256,128]{2,1,0:T(8,128)(2,1)S(1)}, bf16[3,256,128]{2,1,0:T(8,128)(2,1)S(1)}, u32[]{:S(2)}, u32[]{:S(2)}) collective-permute-start(bf16[3,256,128]{2,1,0:T(8,128)(2,1)S(1)} %get-tuple-element.42.near), channel_id=1, source_target_pairs={{0,6},{1,7},{2,8},{3,9},{4,10},{5,11},{6,12},{7,13},{8,14},{9,15},... | collective-permute-start | bytes 589832 | tf_op jit(solution)/shard_map/ppermute | solution.py:73
  117.2 0.0 all-to-all-done.2.ranks
  117.2 2.4 %shard_map.117 = (bf16[16,16,640]{2,1,0:T(8,128)(2,1)}, bf16[256,128]{1,0:T(8,128)(2,1)}, bf16[256,256]{1,0:T(8,128)(2,1)S(1)}) custom-call(s32[4]{0:T(128)S(1)} %pad_add_fusion.where, s32[16]{0:T(128)S(1)} %copy-done.6, bf16[32,64,128]{2,1,0:T(8,128)(2,1)S(1)} %all-to-all-done.2.ranks, f32[256,128]{1,0:T(8,128)S(1)} %get-tuple-element.37.base, ...), custom_call_target="tpu_custom_call" | custom-call | flops 92274688 | bytes 655360 | tf_op jit(solution)/shard_map/pallas_call | solution.py:439
  119.7 4.8 %all-to-all-start.3 = ((bf16[16,16,640]{2,1,0:T(8,128)(2,1)}), bf16[16,16,640]{2,1,0:T(8,128)(2,1)S(1)}, u32[]{:S(2)}, u32[]{:S(2)}) async-start(bf16[16,16,640]{2,1,0:T(8,128)(2,1)} %get-tuple-element.45), calls=%async_computation.3 | async-start | bytes 655360 | tf_op jit(solution)/shard_map/all_to_all | solution.py:283
  124.4 3.9 %collective-permute-start.7 = (bf16[2,256,128]{2,1,0:T(8,128)(2,1)S(1)}, bf16[2,256,128]{2,1,0:T(8,128)(2,1)S(1)}, u32[]{:S(2)}, u32[]{:S(2)}) collective-permute-start(bf16[2,256,128]{2,1,0:T(8,128)(2,1)S(1)} %get-tuple-element.43), channel_id=1, source_target_pairs={{0,10},{1,11},{2,12},{3,13},{4,14},{5,15},{6,0},{7,1},{8,2},{9,3},... | collective-permute-start | bytes 393224 | tf_op jit(solution)/shard_map/ppermute | solution.py:73
  128.3 8.7 %collective-permute-done.7.down = bf16[2,256,128]{2,1,0:T(8,128)(2,1)S(1)} collective-permute-done((bf16[2,256,128]{2,1,0:T(8,128)(2,1)S(1)}, bf16[2,256,128]{2,1,0:T(8,128)(2,1)S(1)}, u32[]{:S(2)}, u32[]{:S(2)}) %collective-permute-start.7) | collective-permute-done | bytes 131104 | tf_op jit(solution)/shard_map/ppermute | solution.py:73
  137.0 0.0 collective-permute-done.6.up
  137.1 4.0 %collective-permute-start.8 = (bf16[8,256,128]{2,1,0:T(8,128)(2,1)S(1)}, bf16[8,256,128]{2,1,0:T(8,128)(2,1)S(1)}, u32[]{:S(2)}, u32[]{:S(2)}) collective-permute-start(bf16[8,256,128]{2,1,0:T(8,128)(2,1)S(1)} %shard_map.119.a0), channel_id=1, source_target_pairs={{0,16},{1,17},{2,18},{3,19},{4,20},{5,21},{6,22},{7,23},{8,24},{9,... | collective-permute-start | bytes 1572872 | tf_op jit(solution)/shard_map/ppermute | solution.py:73
  141.1 0.0 all-to-all-done.3.arrived
  141.1 0.8 shard_map.121
  141.9 7.6 %all-to-all-start.4 = ((bf16[16,16,640]{2,1,0:T(8,128)(2,1)}), bf16[16,16,640]{2,1,0:T(8,128)(2,1)S(1)}, u32[]{:S(2)}, u32[]{:S(2)}) async-start(bf16[16,16,640]{2,1,0:T(8,128)(2,1)} %shard_map.121), calls=%async_computation.4 | async-start | bytes 655360 | tf_op jit(solution)/shard_map/all_to_all | solution.py:283
  149.5 1.9 %collective-permute-start.9 = (bf16[8,256,128]{2,1,0:T(8,128)(2,1)S(1)}, bf16[8,256,128]{2,1,0:T(8,128)(2,1)S(1)}, u32[]{:S(2)}, u32[]{:S(2)}) collective-permute-start(bf16[8,256,128]{2,1,0:T(8,128)(2,1)S(1)} %shard_map.119.a0), channel_id=1, source_target_pairs={{0,1},{1,0},{2,3},{3,2},{4,5},{5,4},{6,7},{7,6},{8,9},{9,8},{10,11... | collective-permute-start | bytes 1572872 | tf_op jit(solution)/shard_map/ppermute | solution.py:73
  151.4 1.7 %collective-permute-done.8.a1 = bf16[8,256,128]{2,1,0:T(8,128)(2,1)S(1)} collective-permute-done((bf16[8,256,128]{2,1,0:T(8,128)(2,1)S(1)}, bf16[8,256,128]{2,1,0:T(8,128)(2,1)S(1)}, u32[]{:S(2)}, u32[]{:S(2)}) %collective-permute-start.8) | collective-permute-done | bytes 524320 | tf_op jit(solution)/shard_map/ppermute | solution.py:73
  153.1 1.9 %collective-permute-start.10 = (bf16[8,256,128]{2,1,0:T(8,128)(2,1)S(1)}, bf16[8,256,128]{2,1,0:T(8,128)(2,1)S(1)}, u32[]{:S(2)}, u32[]{:S(2)}) collective-permute-start(bf16[8,256,128]{2,1,0:T(8,128)(2,1)S(1)} %collective-permute-done.8.a1), channel_id=1, source_target_pairs={{0,1},{1,0},{2,3},{3,2},{4,5},{5,4},{6,7},{7,6},{8,9},{9,8},{10,11... | collective-permute-start | bytes 1572872 | tf_op jit(solution)/shard_map/ppermute | solution.py:73
  155.0 4.0 %all-to-all-done.4.fifth = bf16[16,16,640]{2,1,0:T(8,128)(2,1)S(1)} async-done(((bf16[16,16,640]{2,1,0:T(8,128)(2,1)}), bf16[16,16,640]{2,1,0:T(8,128)(2,1)S(1)}, u32[]{:S(2)}, u32[]{:S(2)}) %all-to-all-start.4) | async-done | bytes 327712 | tf_op jit(solution)/shard_map/all_to_all | solution.py:283
  159.0 0.8 shard_map.122
  159.8 0.0 collective-permute-done.9.b0
  159.8 0.0 collective-permute-done.10.b1
  159.8 5.0 %shard_map.120 = bf16[448,256]{1,0:T(8,128)(2,1)} custom-call(s32[4]{0:T(128)S(1)} %pad_add_fusion.where, bf16[8,256,128]{2,1,0:T(8,128)(2,1)S(1)} %shard_map.119.a0, bf16[8,256,128]{2,1,0:T(8,128)(2,1)S(1)} %collective-permute-done.8.a1, bf16[8,256,128]{2,1,0:T(8,128)(2,1)S(1)} %collective-permute-done.9.b0, ...), custom_call_target="tpu_custom_call" | custom-call | flops 998244352 | bytes 3670016 | tf_op jit(solution)/shard_map/pallas_call | solution.py:489
  (11 shorter events, 0.1 us)
Async XLA Ops:
  0.6 43.7 %copy-start.1 = (bf16[256,448]{0,1:T(8,128)(2,1)S(1)}, bf16[256,448]{0,1:T(8,128)(2,1)}, u32[]{:S(2)}) copy-start(bf16[256,448]{0,1:T(8,128)(2,1)} %param.7) | copy-start | bytes 688132
  0.6 43.7 %copy-start = (bf16[16,448,16]{1,2,0:T(8,128)(2,1)S(1)}, bf16[16,448,16]{1,2,0:T(8,128)(2,1)}, u32[]{:S(2)}) copy-start(bf16[16,448,16]{1,2,0:T(8,128)(2,1)} %param.9) | copy-start | bytes 688132
  0.7 34.8 %copy-start.2 = (bf16[16,16,128]{2,1,0:T(8,128)(2,1)S(1)}, bf16[16,16,128]{2,1,0:T(8,128)(2,1)}, u32[]{:S(2)}) copy-start(bf16[16,16,128]{2,1,0:T(8,128)(2,1)} %up.1) | copy-start | bytes 196612
  0.7 43.7 %copy-start.6 = (s32[16]{0:T(128)S(1)}, s32[16]{0:T(128)}, u32[]{:S(2)}) copy-start(s32[16]{0:T(128)} %seg.5) | copy-start | bytes 196
  0.7 50.9 %copy-start.5 = (bf16[16,128]{1,0:T(8,128)(2,1)S(1)}, bf16[16,128]{1,0:T(8,128)(2,1)}, u32[]{:S(2)}) copy-start(bf16[16,128]{1,0:T(8,128)(2,1)} %magnitude.3) | copy-start | bytes 12292
  0.7 50.9 %copy-start.4 = (bf16[256,128]{1,0:T(8,128)(2,1)S(1)}, bf16[256,128]{1,0:T(8,128)(2,1)}, u32[]{:S(2)}) copy-start(bf16[256,128]{1,0:T(8,128)(2,1)} %cotangent.3) | copy-start | bytes 196612
  7.2 50.2 %collective-permute-start = (bf16[16,256,128]{2,1,0:T(8,128)(2,1)}, bf16[16,256,128]{2,1,0:T(8,128)(2,1)S(1)}, u32[]{:S(2)}, u32[]{:S(2)}) collective-permute-start(bf16[16,256,128]{2,1,0:T(8,128)(2,1)} %get-tuple-element.30), channel_id=1, source_target_pairs={{0,1},{1,0},{2,3},{3,2},{4,5},{5,4},{6,7},{7,6},{8,9},{9,8},{10,11... | collective-permute-start | bytes 3145736 | tf_op jit(solution)/shard_map/ppermute | solution.py:73
  36.8 14.8 %all-to-all-start.1 = ((f32[16,2,128]{2,1,0:T(2,128)}), f32[16,2,128]{2,1,0:T(2,128)S(1)}, u32[]{:S(2)}, u32[]{:S(2)}) async-start(f32[16,2,128]{2,1,0:T(2,128)} %shard_map.111), calls=%async_computation.1 | async-start | bytes 32768 | tf_op jit(solution)/shard_map/all_to_all | solution.py:283
  52.7 0.8 copy-start.3
  53.5 63.7 %all-to-all-start.2 = ((bf16[32,64,128]{2,1,0:T(8,128)(2,1)}), bf16[32,64,128]{2,1,0:T(8,128)(2,1)S(1)}, u32[]{:S(2)}, u32[]{:S(2)}) async-start(bf16[32,64,128]{2,1,0:T(8,128)(2,1)} %copy-done.3), calls=%async_computation.2 | async-start | bytes 1048576 | tf_op jit(solution)/shard_map/all_to_all | solution.py:283
  58.3 21.8 %collective-permute-start.1 = (bf16[8,256,128]{2,1,0:T(8,128)(2,1)S(1)}, bf16[8,256,128]{2,1,0:T(8,128)(2,1)S(1)}, u32[]{:S(2)}, u32[]{:S(2)}) collective-permute-start(bf16[8,256,128]{2,1,0:T(8,128)(2,1)S(1)} %get-tuple-element.32), channel_id=1, source_target_pairs={{0,16},{1,17},{2,18},{3,19},{4,20},{5,21},{6,22},{7,23},{8,24},{9,... | collective-permute-start | bytes 1572872 | tf_op jit(solution)/shard_map/ppermute | solution.py:73
  80.8 19.7 %collective-permute-start.2 = (bf16[3,256,128]{2,1,0:T(8,128)(2,1)S(1)}, bf16[3,256,128]{2,1,0:T(8,128)(2,1)S(1)}, u32[]{:S(2)}, u32[]{:S(2)}) collective-permute-start(bf16[3,256,128]{2,1,0:T(8,128)(2,1)S(1)} %get-tuple-element.34), channel_id=1, source_target_pairs={{0,6},{1,7},{2,8},{3,9},{4,10},{5,11},{6,12},{7,13},{8,14},{9,15},... | collective-permute-start | bytes 589832 | tf_op jit(solution)/shard_map/ppermute | solution.py:73
  85.9 10.4 %collective-permute-start.3 = (bf16[2,256,128]{2,1,0:T(8,128)(2,1)S(1)}, bf16[2,256,128]{2,1,0:T(8,128)(2,1)S(1)}, u32[]{:S(2)}, u32[]{:S(2)}) collective-permute-start(bf16[2,256,128]{2,1,0:T(8,128)(2,1)S(1)} %get-tuple-element.35), channel_id=1, source_target_pairs={{0,10},{1,11},{2,12},{3,13},{4,14},{5,15},{6,0},{7,1},{8,2},{9,3},... | collective-permute-start | bytes 393224 | tf_op jit(solution)/shard_map/ppermute | solution.py:73
  100.6 8.1 %collective-permute-start.4 = (bf16[2,256,128]{2,1,0:T(8,128)(2,1)S(1)}, bf16[2,256,128]{2,1,0:T(8,128)(2,1)S(1)}, u32[]{:S(2)}, u32[]{:S(2)}) collective-permute-start(bf16[2,256,128]{2,1,0:T(8,128)(2,1)S(1)} %get-tuple-element.38), channel_id=1, source_target_pairs={{0,2},{1,3},{2,4},{3,5},{4,6},{5,7},{6,8},{7,9},{8,10},{9,11},{10,... | collective-permute-start | bytes 393224 | tf_op jit(solution)/shard_map/ppermute | solution.py:73
  105.4 6.9 %collective-permute-start.5 = (bf16[2,256,128]{2,1,0:T(8,128)(2,1)S(1)}, bf16[2,256,128]{2,1,0:T(8,128)(2,1)S(1)}, u32[]{:S(2)}, u32[]{:S(2)}) collective-permute-start(bf16[2,256,128]{2,1,0:T(8,128)(2,1)S(1)} %get-tuple-element.39), channel_id=1, source_target_pairs={{0,14},{1,15},{2,0},{3,1},{4,2},{5,3},{6,4},{7,5},{8,6},{9,7},{10,... | collective-permute-start | bytes 393224 | tf_op jit(solution)/shard_map/ppermute | solution.py:73
  112.3 24.8 %collective-permute-start.6 = (bf16[3,256,128]{2,1,0:T(8,128)(2,1)S(1)}, bf16[3,256,128]{2,1,0:T(8,128)(2,1)S(1)}, u32[]{:S(2)}, u32[]{:S(2)}) collective-permute-start(bf16[3,256,128]{2,1,0:T(8,128)(2,1)S(1)} %get-tuple-element.42.near), channel_id=1, source_target_pairs={{0,6},{1,7},{2,8},{3,9},{4,10},{5,11},{6,12},{7,13},{8,14},{9,15},... | collective-permute-start | bytes 589832 | tf_op jit(solution)/shard_map/ppermute | solution.py:73
  119.7 21.4 %all-to-all-start.3 = ((bf16[16,16,640]{2,1,0:T(8,128)(2,1)}), bf16[16,16,640]{2,1,0:T(8,128)(2,1)S(1)}, u32[]{:S(2)}, u32[]{:S(2)}) async-start(bf16[16,16,640]{2,1,0:T(8,128)(2,1)} %get-tuple-element.45), calls=%async_computation.3 | async-start | bytes 655360 | tf_op jit(solution)/shard_map/all_to_all | solution.py:283
  124.4 12.6 %collective-permute-start.7 = (bf16[2,256,128]{2,1,0:T(8,128)(2,1)S(1)}, bf16[2,256,128]{2,1,0:T(8,128)(2,1)S(1)}, u32[]{:S(2)}, u32[]{:S(2)}) collective-permute-start(bf16[2,256,128]{2,1,0:T(8,128)(2,1)S(1)} %get-tuple-element.43), channel_id=1, source_target_pairs={{0,10},{1,11},{2,12},{3,13},{4,14},{5,15},{6,0},{7,1},{8,2},{9,3},... | collective-permute-start | bytes 393224 | tf_op jit(solution)/shard_map/ppermute | solution.py:73
  137.1 16.0 %collective-permute-start.8 = (bf16[8,256,128]{2,1,0:T(8,128)(2,1)S(1)}, bf16[8,256,128]{2,1,0:T(8,128)(2,1)S(1)}, u32[]{:S(2)}, u32[]{:S(2)}) collective-permute-start(bf16[8,256,128]{2,1,0:T(8,128)(2,1)S(1)} %shard_map.119.a0), channel_id=1, source_target_pairs={{0,16},{1,17},{2,18},{3,19},{4,20},{5,21},{6,22},{7,23},{8,24},{9,... | collective-permute-start | bytes 1572872 | tf_op jit(solution)/shard_map/ppermute | solution.py:73
  141.9 17.1 %all-to-all-start.4 = ((bf16[16,16,640]{2,1,0:T(8,128)(2,1)}), bf16[16,16,640]{2,1,0:T(8,128)(2,1)S(1)}, u32[]{:S(2)}, u32[]{:S(2)}) async-start(bf16[16,16,640]{2,1,0:T(8,128)(2,1)} %shard_map.121), calls=%async_computation.4 | async-start | bytes 655360 | tf_op jit(solution)/shard_map/all_to_all | solution.py:283
  149.5 10.3 %collective-permute-start.9 = (bf16[8,256,128]{2,1,0:T(8,128)(2,1)S(1)}, bf16[8,256,128]{2,1,0:T(8,128)(2,1)S(1)}, u32[]{:S(2)}, u32[]{:S(2)}) collective-permute-start(bf16[8,256,128]{2,1,0:T(8,128)(2,1)S(1)} %shard_map.119.a0), channel_id=1, source_target_pairs={{0,1},{1,0},{2,3},{3,2},{4,5},{5,4},{6,7},{7,6},{8,9},{9,8},{10,11... | collective-permute-start | bytes 1572872 | tf_op jit(solution)/shard_map/ppermute | solution.py:73
  153.1 6.7 %collective-permute-start.10 = (bf16[8,256,128]{2,1,0:T(8,128)(2,1)S(1)}, bf16[8,256,128]{2,1,0:T(8,128)(2,1)S(1)}, u32[]{:S(2)}, u32[]{:S(2)}) collective-permute-start(bf16[8,256,128]{2,1,0:T(8,128)(2,1)S(1)} %collective-permute-done.8.a1), channel_id=1, source_target_pairs={{0,1},{1,0},{2,3},{3,2},{4,5},{5,4},{6,7},{7,6},{8,9},{9,8},{10,11... | collective-permute-start | bytes 1572872 | tf_op jit(solution)/shard_map/ppermute | solution.py:73

commit v5 on v4

--- a/solution.py
+++ b/solution.py
@@ -181,26 +181,21 @@
             out[i] = (keep[at].astype(F32) + got[at].astype(F32)).astype(BF16)
 
 
-def near_kernel(near, up, down, scaled, before, after, own):
+def pack_kernel(near, up, down, scaled, below, above, before, after, own):
     before[0] = (near[0].astype(F32) + up[0].astype(F32)).astype(BF16)
     before[1] = scaled[...]
+    before[2] = below[...]
     after[0] = (near[2].astype(F32) + up[2].astype(F32) + down[1].astype(F32)).astype(BF16)
     after[1] = scaled[...]
+    after[2] = below[...]
+    after[3] = above[...]
     own[...] = near[1].astype(F32) + up[1].astype(F32) + down[0].astype(F32)
 
 
-def trio_kernel(before, own, after, trio, pair):
-    trio[0] = before[0]
-    trio[1] = own[...]
-    trio[2] = after[0]
-    pair[0] = before[0]
-    pair[1] = own[...]
-
-
-def join_kernel(near, up, down, out):
-    out[:3] = near[...]
-    out[3:6] = up[...]
-    out[6:] = down[...]
+def join_kernel(after, from_below, from_above, out):
+    out[:3] = after[1:]
+    out[3:6] = from_below[1:]
+    out[6:] = from_above[1:]
 
 
 def scale_kernel(where, seg, second, magnitude, cotangent, up, low, third, scaled, norms):
@@ -218,59 +213,86 @@
     third[...] = jnp.broadcast_to(every[None], third.shape)
 
 
-def grads_kernel(where, seg, ranks, base, base_a, base_b, norms, magnitude, cotangent, scaled, up, tokens,
-                 fourth, projected, back_wide):
+def sums_kernel(rank_rows, ranks):
+    ranks[...] = jnp.sum(rank_rows[...].astype(F32), axis=0).astype(BF16)
+
+
+def grads_kernel(where, seg, ranks, got, scaled, up, tokens, fourth, low_wide, back_wide):
     adapters = seg.shape[0]
     own_rows, count = tokens.shape
     rank = up.shape[0] // adapters
     marks = bounds(seg, adapters, where[0] * count)
-    total = jnp.sum(ranks[...].astype(F32), axis=0)
+    total = ranks[...].astype(F32) + got[...].astype(F32)
     low = widened(unpacked(total[: 2 * rank]), marks)
     back = widened(unpacked(total[2 * rank :]), marks)
+    low_wide[...] = low
     back_wide[...] = back
+    down_part = dot(back, tokens[...], 1, 1).astype(BF16)
+    up_part = dot(low, scaled[...], 1, 0).astype(BF16)
+    pad = jnp.zeros((rank, -own_rows % LANES), BF16)
+    for a in range(adapters):
+        lines = slice(a * rank, (a + 1) * rank)
+        fourth[a] = jnp.concatenate([down_part[lines], pad, up_part[lines]], axis=1)
+
+
+def hidden_kernel(where, seg, base, base_a, base_b, low, up, norms, magnitude, cotangent,
+                  projected, mag):
+    count = cotangent.shape[0]
+    marks = bounds(seg, seg.shape[0], where[0] * count)
     hidden = base[...] + base_a[0].astype(F32) + base_b[0].astype(F32)
-    hidden = hidden + dot(low, up[...], 0, 0)
+    hidden = hidden + dot(low[...], up[...], 0, 0)
     scale = token_scale_of(magnitude[...].astype(F32) / norms[...], marks, count)
     projected[...] = (hidden * scale).astype(BF16)
     weighted = cotangent[...].astype(F32) * hidden
     at = iota((count, LANES), 0)
-    row = iota((rank, LANES // 2), 0)
-    down_part = dot(back, tokens[...], 1, 1).astype(BF16)
-    up_part = dot(low, scaled[...], 1, 0).astype(BF16)
-    pad = -own_rows % LANES
-    for a, (lo, hi) in enumerate(marks):
-        mag = jnp.sum(jnp.where((at >= lo) & (at < hi), weighted, 0.0), axis=0, keepdims=True)
-        halves = jnp.where(row == 0, mag[:, :pad], jnp.where(row == 1, mag[:, pad:], 0.0))
-        lines = slice(a * rank, (a + 1) * rank)
-        fourth[a] = jnp.concatenate(
-            [down_part[lines], halves.astype(BF16), up_part[lines]], axis=1
-        )
-
-
-def total_kernel(arrived, fifth):
+    sums = [
+        jnp.sum(jnp.where((at >= lo) & (at < hi), weighted, 0.0), axis=0, keepdims=True)
+        for lo, hi in marks
+    ]
+    mag[...] = jnp.concatenate(sums, axis=0).astype(BF16)
+
+
+def total_kernel(arrived, mag, fifth):
     total = jnp.sum(arrived[...].astype(F32), axis=0).astype(BF16)
-    fifth[...] = jnp.broadcast_to(total[None], fifth.shape)
+    both = jnp.concatenate([total, mag[...]], axis=1)
+    fifth[...] = jnp.broadcast_to(both[None], fifth.shape)
 
 
 def final_kernel(fifth, norms, grad_down, grad_up, grad_magnitude):
     own_rows = grad_down.shape[2]
-    pad = -own_rows % LANES
+    edge = own_rows + -own_rows % LANES
     grad_down[...] = fifth[:, :, :own_rows]
-    grad_up[...] = fifth[:, :, own_rows + pad :].astype(F32)
-    halves = fifth[:, :, own_rows : own_rows + pad].astype(F32)
-    total = jnp.concatenate([halves[:, 0, :], halves[:, 1, :]], axis=1)
+    grad_up[...] = fifth[:, :, edge : edge + LANES].astype(F32)
+    total = jnp.sum(fifth[:, :, edge + LANES :].astype(F32), axis=0)
     grad_magnitude[...] = total / norms[...]
 
 
-def tokens_kernel(where, a0, a1, b0, b1, *rest):
-    *columns, back, down, out, total = rest
+def tokens_kernel(where, x0, x1, *rest):
+    *columns, first, second, out, total = rest
     step = pl.program_id(0)
 
     @pl.when(step == 0)
     def _():
-        total[...] = dot(down[...], back[...], 0, 0)
-
-    left = [block[i] for i in range(a0.shape[0]) for block in (a0, a1, b0, b1)]
+        total[...] = dot(first[...], second[...], 0, 0)
+
+    left = [block[i] for i in range(x0.shape[0]) for block in (x0, x1)]
+    right = [column[...] for column in columns]
+    total[...] += dot(jnp.concatenate(right, axis=1), jnp.concatenate(left, axis=1), 1, 1)
+
+    @pl.when(step == pl.num_programs(0) - 1)
+    def _():
+        out[...] = total[...]
+
+
+def tokens_rest_kernel(where, x0, x1, *rest):
+    *columns, part, out, total = rest
+    step = pl.program_id(0)
+
+    @pl.when(step == 0)
+    def _():
+        total[...] = part[...]
+
+    left = [block[i] for i in range(x0.shape[0]) for block in (x0, x1)]
     right = [column[...] for column in columns]
     total[...] += dot(jnp.concatenate(right, axis=1), jnp.concatenate(left, axis=1), 1, 1)
 
@@ -300,6 +322,7 @@
     hi_pairs = [(i, (i + size // 2) % size) for i in range(size)]
 
     turned = tokens.T
+    z_groups = [[h * 2 * zs + a * 2 + c for a in range(zs)] for h in range(2) for c in range(2)]
     down_rows = jnp.transpose(adapter_down, (0, 2, 1))
     down_flat = down_rows.reshape(wide, own_rows)
     up_own = adapter_up.reshape(wide, width)
@@ -386,7 +409,7 @@
 
     third, scaled, norms = call(
         scale_kernel,
-        [shaped(size, 4 * rank, width), shaped(count, width), shaped(adapters, width, dtype=F32)],
+        [shaped(zs, 4 * rank, width), shaped(count, width), shaped(adapters, width, dtype=F32)],
         scalars=2,
         grid=(1,),
         in_specs=[
@@ -396,109 +419,136 @@
             whole(wide, width),
             whole(2 * rank, width),
         ],
-        out_specs=[whole(size, 4 * rank, width), whole(count, width), whole(adapters, width)],
+        out_specs=[whole(zs, 4 * rank, width), whole(count, width), whole(adapters, width)],
         flops=2 * count * wide * width,
         moved=8 * count * width,
     )(where, seg_lengths, second, magnitude, cotangent, up_own, low)
-    third = exchange(third, "tensor")
+    third = exchange(third, "tensor", z_groups)
+    below = shift(scaled, along_z(3))
+    above = shift(scaled, along_z(-3))
+    ranks = call(
+        sums_kernel,
+        shaped(4 * rank, width),
+        grid=(1,),
+        in_specs=[whole(zs, 4 * rank, width)],
+        out_specs=whole(4 * rank, width),
+        moved=2 * zs * 4 * rank * width,
+    )(third)
+    ranks = (ranks.astype(F32) + shift(ranks, hi_pairs).astype(F32)).astype(BF16)
+    other = shift(ranks, core_pairs)
 
     before, after, base = call(
-        near_kernel,
-        [shaped(2, count, width), shaped(2, count, width), shaped(count, width, dtype=F32)],
-        grid=(1,),
-        in_specs=[whole(n, count, width) for n in (3, 3, 2)] + [whole(count, width)],
-        out_specs=[whole(2, count, width), whole(2, count, width), whole(count, width)],
-        moved=24 * count * width,
-    )(near, up3, down2, scaled)
+        pack_kernel,
+        [shaped(3, count, width), shaped(4, count, width), shaped(count, width, dtype=F32)],
+        grid=(1,),
+        in_specs=[whole(n, count, width) for n in (3, 3, 2)] + [whole(count, width)] * 3,
+        out_specs=[whole(3, count, width), whole(4, count, width), whole(count, width)],
+        moved=36 * count * width,
+    )(near, up3, down2, scaled, below, above)
+    from_below = shift(after, along_z(1))
     from_above = shift(before, along_z(-1))
-    from_below = shift(after, along_z(1))
-
-    second_block = pl.BlockSpec((1, count, width), lambda i: (1, 0, 0))
-    trio, pair = call(
-        trio_kernel,
-        [shaped(3, count, width), shaped(2, count, width)],
-        grid=(1,),
-        in_specs=[second_block, whole(count, width), second_block],
-        out_specs=[whole(3, count, width), whole(2, count, width)],
-        moved=16 * count * width,
-    )(from_below, scaled, from_above)
-    far_up = shift(trio, along_z(3))
-    far_down = shift(pair, along_z(-3))
     gather_a = call(
         join_kernel,
         shaped(zs, count, width),
         grid=(1,),
-        in_specs=[whole(n, count, width) for n in (3, 3, 2)],
+        in_specs=[whole(n, count, width) for n in (4, 4, 3)],
         out_specs=whole(zs, count, width),
         moved=4 * zs * count * width,
-    )(trio, far_up, far_down)
+    )(after, from_below, from_above)
     gather_b = shift(gather_a, hi_pairs)
+    gather_c = shift(gather_a, core_pairs)
+    gather_d = shift(gather_b, core_pairs)
+
+    edge = own_rows + -own_rows % LANES
+    blocks = edge + width
+    fourth, low_wide, back_wide = call(
+        grads_kernel,
+        [shaped(adapters, rank, blocks), shaped(wide, count), shaped(wide, count)],
+        scalars=2,
+        grid=(1,),
+        in_specs=[
+            whole(4 * rank, width),
+            whole(4 * rank, width),
+            whole(count, width),
+            whole(wide, width),
+            whole(own_rows, count),
+        ],
+        out_specs=[whole(adapters, rank, blocks), whole(wide, count), whole(wide, count)],
+        flops=2 * count * wide * (own_rows + width),
+        moved=4 * adapters * rank * blocks,
+    )(where, seg_lengths, ranks, other, scaled, up_own, turned)
+    fourth = exchange(fourth, "dp")
 
     first_block = pl.BlockSpec((1, count, width), lambda i, *s: (0, 0, 0))
-    blocks = rank * 40
-    fourth, projected, back_wide = call(
-        grads_kernel,
-        [shaped(adapters, rank, blocks), shaped(count, width), shaped(wide, count)],
+    projected, mag = call(
+        hidden_kernel,
+        [shaped(count, width), shaped(adapters, width)],
         scalars=2,
         grid=(1,),
         in_specs=[
-            whole(size, 4 * rank, width),
             whole(count, width),
             first_block,
             first_block,
+            whole(wide, count),
+            whole(wide, width),
             whole(adapters, width),
             whole(adapters, width),
             whole(count, width),
-            whole(count, width),
-            whole(wide, width),
-            whole(own_rows, count),
-        ],
-        out_specs=[whole(adapters, rank, blocks), whole(count, width), whole(wide, count)],
-        flops=2 * count * wide * (own_rows + 2 * width),
-        moved=4 * adapters * rank * blocks,
-    )(where, seg_lengths, third, base, from_below, from_above, norms, magnitude, cotangent, scaled, up_own, turned)
-    fourth = exchange(fourth, "dp")
-    gather_c = shift(gather_a, core_pairs)
-    gather_d = shift(gather_b, core_pairs)
+        ],
+        out_specs=[whole(count, width), whole(adapters, width)],
+        flops=2 * count * wide * width,
+        moved=16 * count * width,
+    )(where, seg_lengths, base, from_below, from_above, low_wide, up_own, norms, magnitude,
+      cotangent)
 
     fifth = call(
         total_kernel,
-        shaped(adapters, rank, blocks),
-        grid=(1,),
-        in_specs=[whole(adapters, rank, blocks)],
-        out_specs=whole(adapters, rank, blocks),
+        shaped(adapters, rank, blocks + width),
+        grid=(1,),
+        in_specs=[whole(adapters, rank, blocks), whole(adapters, width)],
+        out_specs=whole(adapters, rank, blocks + width),
         moved=4 * adapters * rank * blocks,
-    )(fourth)
+    )(fourth, mag)
     fifth = exchange(fifth, "dp")
 
     per = 4
+    offsets = (0, -3, 3, -1, -4, 2, 1, -2)
 
     def column(k, x_bit, c_bit):
         def at(i, s):
-            slot = i * per + k
-            off = jnp.where(slot < 3, slot - 1, jnp.where(slot < 6, slot - 7, slot - 4))
+            off = jnp.where(i == 0, offsets[k], offsets[per + k])
             block = (s[3] + off + zs) % zs
             return (0, (s[2] ^ x_bit) * (2 * zs) + block * 2 + (s[1] ^ c_bit))
 
         return pl.BlockSpec((own_rows, width), at)
 
-    columns = [
-        column(k, x, c) for k in range(per) for x, c in ((0, 0), (1, 0), (0, 1), (1, 1))
-    ]
+    def columns(x_bit):
+        return [column(k, x_bit, c) for k in range(per) for c in range(2)]
+
     block = pl.BlockSpec((per, count, width), lambda i, s: (i, 0, 0))
+    weights = [in_hbm(base_weight)] * (2 * per)
+    part = call(
+        tokens_kernel,
+        shaped(own_rows, count, dtype=F32),
+        scalars=1,
+        grid=(zs // per,),
+        in_specs=[block] * 2 + columns(0) + [whole(wide, own_rows), whole(wide, count)],
+        out_specs=whole(own_rows, count),
+        scratch=[pltpu.VMEM((own_rows, count), F32)],
+        flops=count * own_rows * (full + 2 * wide),
+        moved=own_rows * full,
+    )(where, gather_a, gather_c, *weights, down_flat, back_wide)
     grad_tokens = call(
-        tokens_kernel,
+        tokens_rest_kernel,
         shaped(own_rows, count),
         scalars=1,
         grid=(zs // per,),
-        in_specs=[block] * 4
-        + columns
-        + [whole(wide, count), whole(wide, own_rows)],
+        in_specs=[block] * 2 + columns(1) + [whole(own_rows, count)],
         out_specs=whole(own_rows, count),
         scratch=[pltpu.VMEM((own_rows, count), F32)],
-        flops=2 * count * own_rows * (full + wide),
-        moved=2 * own_rows * full,
-    )(where, gather_a, gather_b, gather_c, gather_d, *[in_hbm(base_weight)] * (4 * per), back_wide, down_flat)
+        flops=count * own_rows * full,
+        moved=own_rows * full,
+    )(where, gather_b, gather_d, *weights, part)
 
     grad_down, grad_up, grad_magnitude = call(
         final_kernel,
@@ -508,7 +558,7 @@
             shaped(adapters, width, dtype=F32),
         ],
         grid=(1,),
-        in_specs=[whole(adapters, rank, blocks), whole(adapters, width)],
+        in_specs=[whole(adapters, rank, blocks + width), whole(adapters, width)],
         out_specs=[
             whole(adapters, rank, own_rows),
             whole(adapters, rank, width),

time: 166 us -> 138 us (0.83)
  the two profiles are of different devices: /device:TPU:8 before, /device:TPU:10 now
where the time goes in v5:
time: 138 us
  starting transfers between devices  79.6 us (58%)
  Pallas kernels  24.8 us (18%)
  waiting for transfers between devices  20.7 us (15%)
  blocking collectives  11.5 us (8%)
    ppermute x13, starting transfers between devices, shift(): return lax.ppermute(block, 'tensor', pairs)  44.4 us
    all_to_all x4, starting transfers between devices, exchange(): lax.all_to_all(blocks, axis, 0, 0, tiled=True, axis_index_groups=groups)  35.2 us
    all_to_all x4, waiting for transfers between devices, exchange(): lax.all_to_all(blocks, axis, 0, 0, tiled=True, axis_index_groups=groups)  15.4 us
    all_to_all x1, blocking collectives, exchange(): lax.all_to_all(blocks, axis, 0, 0, tiled=True, axis_index_groups=groups)  11.5 us
    pallas_call x1, Pallas kernels, local(): call(first_kernel, [shaped(size, HEAD, width), shaped(size // 2, count, w...  6.38 us
    ppermute x13, waiting for transfers between devices, shift(): return lax.ppermute(block, 'tensor', pairs)  5.31 us
    pallas_call x1, Pallas kernels, local(): call(tokens_rest_kernel, shaped(own_rows, count), scalars=1, grid=(zs //...  3.69 us
    pallas_call x1, Pallas kernels, local(): call(tokens_kernel, shaped(own_rows, count, dtype=F32), scalars=1, grid=(...  3.37 us
  transfers between devices with their start and end apart: 17, of which 6 were waited for; matrix products, arithmetic and copies ran while one was open for 0% of the time, Pallas kernels for 11%

profile of v5, /device:TPU:10, one launch (start us, length us, event | category | flops | bytes accessed | tf_op | source)
XLA Modules:
  0.0 137.5 jit_solution(6672398655496086973)
XLA Ops:
  0.7 0.1 pad_add_fusion.where
  0.8 6.4 %shard_map.110 = (bf16[32,24,128]{2,1,0:T(8,128)(2,1)}, bf16[16,256,128]{2,1,0:T(8,128)(2,1)S(1)}, bf16[16,256,128]{2,1,0:T(8,128)(2,1)}) custom-call(s32[4]{0:T(128)S(1)} %pad_add_fusion.where, bf16[448,256]{1,0:T(8,128)(2,1)} %bitcast.14, bf16[448,4096]{1,0:T(8,128)(2,1)} %rest_7_.3, bf16[16,16,448]{2,1,0:T(8,128)(2,1)} %bitcast.11), custom_call_target="tpu_custom_call" | custom-call | flops 939524096 | bytes 3670016 | tf_op jit(solution)/shard_map/pallas_call | solution.py:330
  7.1 2.0 %collective-permute-start = (bf16[16,256,128]{2,1,0:T(8,128)(2,1)}, bf16[16,256,128]{2,1,0:T(8,128)(2,1)S(1)}, u32[]{:S(2)}, u32[]{:S(2)}) collective-permute-start(bf16[16,256,128]{2,1,0:T(8,128)(2,1)} %get-tuple-element.28), channel_id=1, source_target_pairs={{0,1},{1,0},{2,3},{3,2},{4,5},{5,4},{6,7},{7,6},{8,9},{9,8},{10,11... | collective-permute-start | bytes 3145736 | tf_op jit(solution)/shard_map/ppermute | solution.py:73
  9.2 12.4 %all-to-all-start = ((bf16[32,24,128]{2,1,0:T(8,128)(2,1)}), bf16[32,24,128]{2,1,0:T(8,128)(2,1)S(1)}, u32[]{:S(2)}, u32[]{:S(2)}) async-start(bf16[32,24,128]{2,1,0:T(8,128)(2,1)} %get-tuple-element.34), calls=%async_computation | async-start | bytes 393216 | tf_op jit(solution)/shard_map/all_to_all | solution.py:305
  21.6 0.0 collective-permute-done.got_a.got_b
  21.6 2.0 %shard_map.111 = (bf16[8,256,128]{2,1,0:T(8,128)(2,1)S(1)}, bf16[8,256,128]{2,1,0:T(8,128)(2,1)}) custom-call(s32[4]{0:T(128)S(1)} %pad_add_fusion.where, bf16[16,256,128]{2,1,0:T(8,128)(2,1)S(1)} %get-tuple-element.27.keep_a.keep_b, bf16[16,256,128]{2,1,0:T(8,128)(2,1)S(1)} %collective-permute-done.got_a.got_b, ...), custom_call_target="tpu_custom_call" | custom-call | bytes 3145728 | tf_op jit(solution)/shard_map/pallas_call | solution.py:365
  23.6 5.2 %collective-permute-start.1 = (bf16[8,256,128]{2,1,0:T(8,128)(2,1)}, bf16[8,256,128]{2,1,0:T(8,128)(2,1)S(1)}, u32[]{:S(2)}, u32[]{:S(2)}) collective-permute-start(bf16[8,256,128]{2,1,0:T(8,128)(2,1)} %get-tuple-element.30), channel_id=1, source_target_pairs={{0,16},{1,17},{2,18},{3,19},{4,20},{5,21},{6,22},{7,23},{8,24},{9,... | collective-permute-start | bytes 1572872 | tf_op jit(solution)/shard_map/ppermute | solution.py:73
  28.8 6.1 %all-to-all-done.head = bf16[32,24,128]{2,1,0:T(8,128)(2,1)S(1)} async-done(((bf16[32,24,128]{2,1,0:T(8,128)(2,1)}), bf16[32,24,128]{2,1,0:T(8,128)(2,1)S(1)}, u32[]{:S(2)}, u32[]{:S(2)}) %all-to-all-start) | async-done | bytes 196640 | tf_op jit(solution)/shard_map/all_to_all | solution.py:305
  35.0 1.3 shard_map.113
  36.3 8.5 %all-to-all-start.1 = ((f32[16,2,128]{2,1,0:T(2,128)}), f32[16,2,128]{2,1,0:T(2,128)S(1)}, u32[]{:S(2)}, u32[]{:S(2)}) async-start(f32[16,2,128]{2,1,0:T(2,128)} %shard_map.113), calls=%async_computation.1 | async-start | bytes 32768 | tf_op jit(solution)/shard_map/all_to_all | solution.py:305
  44.8 0.8 shard_map.114.low
  45.6 5.5 %all-to-all-done.1.second = f32[16,2,128]{2,1,0:T(2,128)S(1)} async-done(((f32[16,2,128]{2,1,0:T(2,128)}), f32[16,2,128]{2,1,0:T(2,128)S(1)}, u32[]{:S(2)}, u32[]{:S(2)}) %all-to-all-start.1) | async-done | bytes 16416 | tf_op jit(solution)/shard_map/all_to_all | solution.py:305
  51.1 1.1 shard_map.115
  52.3 11.5 %all_to_all.25.rank_rows = bf16[8,64,128]{2,1,0:T(8,128)(2,1)S(1)} all-to-all(bf16[8,64,128]{2,1,0:T(8,128)(2,1)S(1)} %get-tuple-element.39), channel_id=1, replica_groups={{0,2,4,6,8,10,12,14},{1,3,5,7,9,11,13,15},{16,18,20,22,24,26,28,30},{17..., dimensions={0} | all-to-all | bytes 262144 | tf_op jit(solution)/shard_map/all_to_all | solution.py:305
  63.7 2.4 %collective-permute-start.8 = (bf16[64,128]{1,0:T(8,128)(2,1)S(1)}, bf16[64,128]{1,0:T(8,128)(2,1)S(1)}, u32[]{:S(2)}, u32[]{:S(2)}) collective-permute-start(bf16[64,128]{1,0:T(8,128)(2,1)S(1)} %shard_map.117), channel_id=1, source_target_pairs={{0,16},{1,17},{2,18},{3,19},{4,20},{5,21},{6,22},{7,23},{8,24},{9,... | collective-permute-start | bytes 49160 | tf_op jit(solution)/shard_map/ppermute | solution.py:73
  66.1 2.1 %collective-permute-start.4 = (bf16[256,128]{1,0:T(8,128)(2,1)S(1)}, bf16[256,128]{1,0:T(8,128)(2,1)S(1)}, u32[]{:S(2)}, u32[]{:S(2)}) collective-permute-start(bf16[256,128]{1,0:T(8,128)(2,1)S(1)} %get-tuple-element.35.scaled), channel_id=1, source_target_pairs={{0,6},{1,7},{2,8},{3,9},{4,10},{5,11},{6,12},{7,13},{8,14},{9,15},... | collective-permute-start | bytes 196616 | tf_op jit(solution)/shard_map/ppermute | solution.py:73
  68.2 6.7 %collective-permute-start.5 = (bf16[256,128]{1,0:T(8,128)(2,1)S(1)}, bf16[256,128]{1,0:T(8,128)(2,1)S(1)}, u32[]{:S(2)}, u32[]{:S(2)}) collective-permute-start(bf16[256,128]{1,0:T(8,128)(2,1)S(1)} %get-tuple-element.35.scaled), channel_id=1, source_target_pairs={{0,10},{1,11},{2,12},{3,13},{4,14},{5,15},{6,0},{7,1},{8,2},{9,3},... | collective-permute-start | bytes 196616 | tf_op jit(solution)/shard_map/ppermute | solution.py:73
  75.0 0.0 collective-permute-done.1.got
  75.0 0.7 shard_map.112
  75.7 1.9 %collective-permute-start.2 = (bf16[3,256,128]{2,1,0:T(8,128)(2,1)S(1)}, bf16[3,256,128]{2,1,0:T(8,128)(2,1)S(1)}, u32[]{:S(2)}, u32[]{:S(2)}) collective-permute-start(bf16[3,256,128]{2,1,0:T(8,128)(2,1)S(1)} %get-tuple-element.32), channel_id=1, source_target_pairs={{0,6},{1,7},{2,8},{3,9},{4,10},{5,11},{6,12},{7,13},{8,14},{9,15},... | collective-permute-start | bytes 589832 | tf_op jit(solution)/shard_map/ppermute | solution.py:73
  77.6 6.9 %collective-permute-start.3 = (bf16[2,256,128]{2,1,0:T(8,128)(2,1)S(1)}, bf16[2,256,128]{2,1,0:T(8,128)(2,1)S(1)}, u32[]{:S(2)}, u32[]{:S(2)}) collective-permute-start(bf16[2,256,128]{2,1,0:T(8,128)(2,1)S(1)} %get-tuple-element.33), channel_id=1, source_target_pairs={{0,10},{1,11},{2,12},{3,13},{4,14},{5,15},{6,0},{7,1},{8,2},{9,3},... | collective-permute-start | bytes 393224 | tf_op jit(solution)/shard_map/ppermute | solution.py:73
  84.5 0.0 collective-permute-done.8
  84.6 1.9 %collective-permute-start.9 = (bf16[64,128]{1,0:T(8,128)(2,1)S(1)}, bf16[64,128]{1,0:T(8,128)(2,1)S(1)}, u32[]{:S(2)}, u32[]{:S(2)}) collective-permute-start(bf16[64,128]{1,0:T(8,128)(2,1)S(1)} %add_convert_fusion.ranks), channel_id=1, source_target_pairs={{0,1},{1,0},{2,3},{3,2},{4,5},{5,4},{6,7},{7,6},{8,9},{9,8},{10,11... | collective-permute-start | bytes 49160 | tf_op jit(solution)/shard_map/ppermute | solution.py:73
  86.5 1.1 collective-permute-done.9.got
  87.6 1.6 %shard_map.118 = (bf16[16,16,640]{2,1,0:T(8,128)(2,1)}, bf16[256,256]{1,0:T(8,128)(2,1)S(1)}, bf16[256,256]{1,0:T(8,128)(2,1)S(1)}) custom-call(s32[4]{0:T(128)S(1)} %pad_add_fusion.where, s32[16]{0:T(128)S(1)} %copy-done.5, bf16[64,128]{1,0:T(8,128)(2,1)S(1)} %add_convert_fusion.ranks, bf16[64,128]{1,0:T(8,128)(2,1)S(1)} %collective-permute-done.9.got, ...), custom_call_target="tpu_custom_call" | custom-call | flops 75497472 | bytes 655360 | tf_op jit(solution)/shard_map/pallas_call | solution.py:464
  89.2 6.2 %all-to-all-start.3 = ((bf16[16,16,640]{2,1,0:T(8,128)(2,1)}), bf16[16,16,640]{2,1,0:T(8,128)(2,1)S(1)}, u32[]{:S(2)}, u32[]{:S(2)}) async-start(bf16[16,16,640]{2,1,0:T(8,128)(2,1)} %get-tuple-element.44), calls=%async_computation.3 | async-start | bytes 655360 | tf_op jit(solution)/shard_map/all_to_all | solution.py:305
  95.4 0.0 collective-permute-done.4.below
  95.4 0.0 collective-permute-done.5.above
  95.4 0.0 collective-permute-done.3.down
  95.5 0.0 collective-permute-done.2.up
  95.5 0.1 shard_map.116
  95.6 2.5 %collective-permute-start.6 = (bf16[4,256,128]{2,1,0:T(8,128)(2,1)S(1)}, bf16[4,256,128]{2,1,0:T(8,128)(2,1)S(1)}, u32[]{:S(2)}, u32[]{:S(2)}) collective-permute-start(bf16[4,256,128]{2,1,0:T(8,128)(2,1)S(1)} %get-tuple-element.37.after), channel_id=1, source_target_pairs={{0,2},{1,3},{2,4},{3,5},{4,6},{5,7},{6,8},{7,9},{8,10},{9,11},{10,... | collective-permute-start | bytes 786440 | tf_op jit(solution)/shard_map/ppermute | solution.py:73
  98.0 4.6 %collective-permute-start.7 = (bf16[3,256,128]{2,1,0:T(8,128)(2,1)S(1)}, bf16[3,256,128]{2,1,0:T(8,128)(2,1)S(1)}, u32[]{:S(2)}, u32[]{:S(2)}) collective-permute-start(bf16[3,256,128]{2,1,0:T(8,128)(2,1)S(1)} %get-tuple-element.38), channel_id=1, source_target_pairs={{0,14},{1,15},{2,0},{3,1},{4,2},{5,3},{6,4},{7,5},{8,6},{9,7},{10,... | collective-permute-start | bytes 589832 | tf_op jit(solution)/shard_map/ppermute | solution.py:73
  102.6 3.9 %collective-permute-done.7.base_b.from_above = bf16[3,256,128]{2,1,0:T(8,128)(2,1)S(1)} collective-permute-done((bf16[3,256,128]{2,1,0:T(8,128)(2,1)S(1)}, bf16[3,256,128]{2,1,0:T(8,128)(2,1)S(1)}, u32[]{:S(2)}, u32[]{:S(2)}) %collective-permute-start.7) | collective-permute-done | bytes 196640 | tf_op jit(solution)/shard_map/ppermute | solution.py:73
  106.5 0.2 collective-permute-done.6.base_a.from_below
  106.8 3.8 %collective-permute-start.10 = (bf16[8,256,128]{2,1,0:T(8,128)(2,1)S(1)}, bf16[8,256,128]{2,1,0:T(8,128)(2,1)S(1)}, u32[]{:S(2)}, u32[]{:S(2)}) collective-permute-start(bf16[8,256,128]{2,1,0:T(8,128)(2,1)S(1)} %shard_map.120.x0), channel_id=1, source_target_pairs={{0,16},{1,17},{2,18},{3,19},{4,20},{5,21},{6,22},{7,23},{8,24},{9,... | collective-permute-start | bytes 1572872 | tf_op jit(solution)/shard_map/ppermute | solution.py:73
  110.6 2.1 %shard_map.119 = (bf16[256,128]{1,0:T(8,128)(2,1)}, bf16[16,128]{1,0:T(8,128)(2,1)S(1)}) custom-call(s32[4]{0:T(128)S(1)} %pad_add_fusion.where, s32[16]{0:T(128)S(1)} %copy-done.5, f32[256,128]{1,0:T(8,128)S(1)} %get-tuple-element.36.base, bf16[4,256,128]{2,1,0:T(8,128)(2,1)S(1)} %collective-permute-done.6.base_a.from_below, ...), custom_call_target="tpu_custom_call" | custom-call | flops 16777216 | bytes 524288 | tf_op jit(solution)/shard_map/pallas_call | solution.py:483
  112.7 0.0 all-to-all-done.3.arrived
  112.7 0.8 shard_map.123
  113.5 8.1 %all-to-all-start.4 = ((bf16[16,16,768]{2,1,0:T(8,128)(2,1)}), bf16[16,16,768]{2,1,0:T(8,128)(2,1)S(1)}, u32[]{:S(2)}, u32[]{:S(2)}) async-start(bf16[16,16,768]{2,1,0:T(8,128)(2,1)} %shard_map.123), calls=%async_computation.4 | async-start | bytes 786432 | tf_op jit(solution)/shard_map/all_to_all | solution.py:305
  121.6 1.9 %collective-permute-start.12 = (bf16[8,256,128]{2,1,0:T(8,128)(2,1)S(1)}, bf16[8,256,128]{2,1,0:T(8,128)(2,1)S(1)}, u32[]{:S(2)}, u32[]{:S(2)}) collective-permute-start(bf16[8,256,128]{2,1,0:T(8,128)(2,1)S(1)} %shard_map.120.x0), channel_id=1, source_target_pairs={{0,1},{1,0},{2,3},{3,2},{4,5},{5,4},{6,7},{7,6},{8,9},{9,8},{10,11... | collective-permute-start | bytes 1572872 | tf_op jit(solution)/shard_map/ppermute | solution.py:73
  123.5 0.0 collective-permute-done.10.x0
  123.6 2.4 %collective-permute-start.11 = (bf16[8,256,128]{2,1,0:T(8,128)(2,1)S(1)}, bf16[8,256,128]{2,1,0:T(8,128)(2,1)S(1)}, u32[]{:S(2)}, u32[]{:S(2)}) collective-permute-start(bf16[8,256,128]{2,1,0:T(8,128)(2,1)S(1)} %collective-permute-done.10.x0), channel_id=1, source_target_pairs={{0,1},{1,0},{2,3},{3,2},{4,5},{5,4},{6,7},{7,6},{8,9},{9,8},{10,11... | collective-permute-start | bytes 1572872 | tf_op jit(solution)/shard_map/ppermute | solution.py:73
  126.0 0.0 collective-permute-done.12.x1
  126.0 3.4 %shard_map.121.rest_8_ = f32[448,256]{1,0:T(8,128)S(1)} custom-call(s32[4]{0:T(128)S(1)} %pad_add_fusion.where, bf16[8,256,128]{2,1,0:T(8,128)(2,1)S(1)} %shard_map.120.x0, bf16[8,256,128]{2,1,0:T(8,128)(2,1)S(1)} %collective-permute-done.12.x1, bf16[448,4096]{1,0:T(8,128)(2,1)} %rest_7_.3, bf16[448,4096]{1,0:T(8,128)(2,1)} %rest_7_.3, ...), custom_call_target="tpu_custom_call" | custom-call | flops 528482304 | bytes 1835008 | tf_op jit(solution)/shard_map/pallas_call | solution.py:530
  129.4 3.7 %all-to-all-done.4.fifth = bf16[16,16,768]{2,1,0:T(8,128)(2,1)S(1)} async-done(((bf16[16,16,768]{2,1,0:T(8,128)(2,1)}), bf16[16,16,768]{2,1,0:T(8,128)(2,1)S(1)}, u32[]{:S(2)}, u32[]{:S(2)}) %all-to-all-start.4) | async-done | bytes 393248 | tf_op jit(solution)/shard_map/all_to_all | solution.py:305
  133.1 0.8 shard_map.124
  133.8 3.7 %shard_map.122 = bf16[448,256]{1,0:T(8,128)(2,1)} custom-call(s32[4]{0:T(128)S(1)} %pad_add_fusion.where, bf16[8,256,128]{2,1,0:T(8,128)(2,1)S(1)} %collective-permute-done.10.x0, bf16[8,256,128]{2,1,0:T(8,128)(2,1)S(1)} %collective-permute-done.11.x1, bf16[448,4096]{1,0:T(8,128)(2,1)} %rest_7_.3, bf16[448,4096]{1,0:T(8,128)(2,1)} %rest_7_.3, ...), custom_call_target="tpu_custom_call" | custom-call | flops 469762048 | bytes 1835008 | tf_op jit(solution)/shard_map/pallas_call | solution.py:541
  (16 shorter events, 0.1 us)
Async XLA Ops:
  0.8 34.2 %copy-start.2 = (bf16[16,16,128]{2,1,0:T(8,128)(2,1)S(1)}, bf16[16,16,128]{2,1,0:T(8,128)(2,1)}, u32[]{:S(2)}) copy-start(bf16[16,16,128]{2,1,0:T(8,128)(2,1)} %up.1) | copy-start | bytes 196612
  0.8 44.0 %copy-start = (bf16[16,448,16]{1,2,0:T(8,128)(2,1)S(1)}, bf16[16,448,16]{1,2,0:T(8,128)(2,1)}, u32[]{:S(2)}) copy-start(bf16[16,448,16]{1,2,0:T(8,128)(2,1)} %param.9) | copy-start | bytes 688132
  0.8 44.0 %copy-start.1 = (bf16[256,448]{0,1:T(8,128)(2,1)S(1)}, bf16[256,448]{0,1:T(8,128)(2,1)}, u32[]{:S(2)}) copy-start(bf16[256,448]{0,1:T(8,128)(2,1)} %param.7) | copy-start | bytes 688132
  0.8 44.1 %copy-start.5 = (s32[16]{0:T(128)S(1)}, s32[16]{0:T(128)}, u32[]{:S(2)}) copy-start(s32[16]{0:T(128)} %seg.7) | copy-start | bytes 196
  7.1 44.0 %copy-start.3 = (bf16[256,128]{1,0:T(8,128)(2,1)S(1)}, bf16[256,128]{1,0:T(8,128)(2,1)}, u32[]{:S(2)}) copy-start(bf16[256,128]{1,0:T(8,128)(2,1)} %cotangent.3) | copy-start | bytes 196612
  7.1 44.0 %copy-start.4 = (bf16[16,128]{1,0:T(8,128)(2,1)S(1)}, bf16[16,128]{1,0:T(8,128)(2,1)}, u32[]{:S(2)}) copy-start(bf16[16,128]{1,0:T(8,128)(2,1)} %magnitude.3) | copy-start | bytes 12292
  7.1 14.4 %collective-permute-start = (bf16[16,256,128]{2,1,0:T(8,128)(2,1)}, bf16[16,256,128]{2,1,0:T(8,128)(2,1)S(1)}, u32[]{:S(2)}, u32[]{:S(2)}) collective-permute-start(bf16[16,256,128]{2,1,0:T(8,128)(2,1)} %get-tuple-element.28), channel_id=1, source_target_pairs={{0,1},{1,0},{2,3},{3,2},{4,5},{5,4},{6,7},{7,6},{8,9},{9,8},{10,11... | collective-permute-start | bytes 3145736 | tf_op jit(solution)/shard_map/ppermute | solution.py:73
  9.2 25.8 %all-to-all-start = ((bf16[32,24,128]{2,1,0:T(8,128)(2,1)}), bf16[32,24,128]{2,1,0:T(8,128)(2,1)S(1)}, u32[]{:S(2)}, u32[]{:S(2)}) async-start(bf16[32,24,128]{2,1,0:T(8,128)(2,1)} %get-tuple-element.34), calls=%async_computation | async-start | bytes 393216 | tf_op jit(solution)/shard_map/all_to_all | solution.py:305
  23.6 51.3 %collective-permute-start.1 = (bf16[8,256,128]{2,1,0:T(8,128)(2,1)}, bf16[8,256,128]{2,1,0:T(8,128)(2,1)S(1)}, u32[]{:S(2)}, u32[]{:S(2)}) collective-permute-start(bf16[8,256,128]{2,1,0:T(8,128)(2,1)} %get-tuple-element.30), channel_id=1, source_target_pairs={{0,16},{1,17},{2,18},{3,19},{4,20},{5,21},{6,22},{7,23},{8,24},{9,... | collective-permute-start | bytes 1572872 | tf_op jit(solution)/shard_map/ppermute | solution.py:73
  36.3 14.8 %all-to-all-start.1 = ((f32[16,2,128]{2,1,0:T(2,128)}), f32[16,2,128]{2,1,0:T(2,128)S(1)}, u32[]{:S(2)}, u32[]{:S(2)}) async-start(f32[16,2,128]{2,1,0:T(2,128)} %shard_map.113), calls=%async_computation.1 | async-start | bytes 32768 | tf_op jit(solution)/shard_map/all_to_all | solution.py:305
  63.7 20.8 %collective-permute-start.8 = (bf16[64,128]{1,0:T(8,128)(2,1)S(1)}, bf16[64,128]{1,0:T(8,128)(2,1)S(1)}, u32[]{:S(2)}, u32[]{:S(2)}) collective-permute-start(bf16[64,128]{1,0:T(8,128)(2,1)S(1)} %shard_map.117), channel_id=1, source_target_pairs={{0,16},{1,17},{2,18},{3,19},{4,20},{5,21},{6,22},{7,23},{8,24},{9,... | collective-permute-start | bytes 49160 | tf_op jit(solution)/shard_map/ppermute | solution.py:73
  66.1 29.3 %collective-permute-start.4 = (bf16[256,128]{1,0:T(8,128)(2,1)S(1)}, bf16[256,128]{1,0:T(8,128)(2,1)S(1)}, u32[]{:S(2)}, u32[]{:S(2)}) collective-permute-start(bf16[256,128]{1,0:T(8,128)(2,1)S(1)} %get-tuple-element.35.scaled), channel_id=1, source_target_pairs={{0,6},{1,7},{2,8},{3,9},{4,10},{5,11},{6,12},{7,13},{8,14},{9,15},... | collective-permute-start | bytes 196616 | tf_op jit(solution)/shard_map/ppermute | solution.py:73
  68.2 27.2 %collective-permute-start.5 = (bf16[256,128]{1,0:T(8,128)(2,1)S(1)}, bf16[256,128]{1,0:T(8,128)(2,1)S(1)}, u32[]{:S(2)}, u32[]{:S(2)}) collective-permute-start(bf16[256,128]{1,0:T(8,128)(2,1)S(1)} %get-tuple-element.35.scaled), channel_id=1, source_target_pairs={{0,10},{1,11},{2,12},{3,13},{4,14},{5,15},{6,0},{7,1},{8,2},{9,3},... | collective-permute-start | bytes 196616 | tf_op jit(solution)/shard_map/ppermute | solution.py:73
  75.7 19.8 %collective-permute-start.2 = (bf16[3,256,128]{2,1,0:T(8,128)(2,1)S(1)}, bf16[3,256,128]{2,1,0:T(8,128)(2,1)S(1)}, u32[]{:S(2)}, u32[]{:S(2)}) collective-permute-start(bf16[3,256,128]{2,1,0:T(8,128)(2,1)S(1)} %get-tuple-element.32), channel_id=1, source_target_pairs={{0,6},{1,7},{2,8},{3,9},{4,10},{5,11},{6,12},{7,13},{8,14},{9,15},... | collective-permute-start | bytes 589832 | tf_op jit(solution)/shard_map/ppermute | solution.py:73
  77.6 17.9 %collective-permute-start.3 = (bf16[2,256,128]{2,1,0:T(8,128)(2,1)S(1)}, bf16[2,256,128]{2,1,0:T(8,128)(2,1)S(1)}, u32[]{:S(2)}, u32[]{:S(2)}) collective-permute-start(bf16[2,256,128]{2,1,0:T(8,128)(2,1)S(1)} %get-tuple-element.33), channel_id=1, source_target_pairs={{0,10},{1,11},{2,12},{3,13},{4,14},{5,15},{6,0},{7,1},{8,2},{9,3},... | collective-permute-start | bytes 393224 | tf_op jit(solution)/shard_map/ppermute | solution.py:73
  84.6 3.1 %collective-permute-start.9 = (bf16[64,128]{1,0:T(8,128)(2,1)S(1)}, bf16[64,128]{1,0:T(8,128)(2,1)S(1)}, u32[]{:S(2)}, u32[]{:S(2)}) collective-permute-start(bf16[64,128]{1,0:T(8,128)(2,1)S(1)} %add_convert_fusion.ranks), channel_id=1, source_target_pairs={{0,1},{1,0},{2,3},{3,2},{4,5},{5,4},{6,7},{7,6},{8,9},{9,8},{10,11... | collective-permute-start | bytes 49160 | tf_op jit(solution)/shard_map/ppermute | solution.py:73
  89.2 23.5 %all-to-all-start.3 = ((bf16[16,16,640]{2,1,0:T(8,128)(2,1)}), bf16[16,16,640]{2,1,0:T(8,128)(2,1)S(1)}, u32[]{:S(2)}, u32[]{:S(2)}) async-start(bf16[16,16,640]{2,1,0:T(8,128)(2,1)} %get-tuple-element.44), calls=%async_computation.3 | async-start | bytes 655360 | tf_op jit(solution)/shard_map/all_to_all | solution.py:305
  95.6 11.2 %collective-permute-start.6 = (bf16[4,256,128]{2,1,0:T(8,128)(2,1)S(1)}, bf16[4,256,128]{2,1,0:T(8,128)(2,1)S(1)}, u32[]{:S(2)}, u32[]{:S(2)}) collective-permute-start(bf16[4,256,128]{2,1,0:T(8,128)(2,1)S(1)} %get-tuple-element.37.after), channel_id=1, source_target_pairs={{0,2},{1,3},{2,4},{3,5},{4,6},{5,7},{6,8},{7,9},{8,10},{9,11},{10,... | collective-permute-start | bytes 786440 | tf_op jit(solution)/shard_map/ppermute | solution.py:73
  98.0 8.5 %collective-permute-start.7 = (bf16[3,256,128]{2,1,0:T(8,128)(2,1)S(1)}, bf16[3,256,128]{2,1,0:T(8,128)(2,1)S(1)}, u32[]{:S(2)}, u32[]{:S(2)}) collective-permute-start(bf16[3,256,128]{2,1,0:T(8,128)(2,1)S(1)} %get-tuple-element.38), channel_id=1, source_target_pairs={{0,14},{1,15},{2,0},{3,1},{4,2},{5,3},{6,4},{7,5},{8,6},{9,7},{10,... | collective-permute-start | bytes 589832 | tf_op jit(solution)/shard_map/ppermute | solution.py:73
  106.8 16.7 %collective-permute-start.10 = (bf16[8,256,128]{2,1,0:T(8,128)(2,1)S(1)}, bf16[8,256,128]{2,1,0:T(8,128)(2,1)S(1)}, u32[]{:S(2)}, u32[]{:S(2)}) collective-permute-start(bf16[8,256,128]{2,1,0:T(8,128)(2,1)S(1)} %shard_map.120.x0), channel_id=1, source_target_pairs={{0,16},{1,17},{2,18},{3,19},{4,20},{5,21},{6,22},{7,23},{8,24},{9,... | collective-permute-start | bytes 1572872 | tf_op jit(solution)/shard_map/ppermute | solution.py:73
  113.5 19.6 %all-to-all-start.4 = ((bf16[16,16,768]{2,1,0:T(8,128)(2,1)}), bf16[16,16,768]{2,1,0:T(8,128)(2,1)S(1)}, u32[]{:S(2)}, u32[]{:S(2)}) async-start(bf16[16,16,768]{2,1,0:T(8,128)(2,1)} %shard_map.123), calls=%async_computation.4 | async-start | bytes 786432 | tf_op jit(solution)/shard_map/all_to_all | solution.py:305
  121.6 4.3 %collective-permute-start.12 = (bf16[8,256,128]{2,1,0:T(8,128)(2,1)S(1)}, bf16[8,256,128]{2,1,0:T(8,128)(2,1)S(1)}, u32[]{:S(2)}, u32[]{:S(2)}) collective-permute-start(bf16[8,256,128]{2,1,0:T(8,128)(2,1)S(1)} %shard_map.120.x0), channel_id=1, source_target_pairs={{0,1},{1,0},{2,3},{3,2},{4,5},{5,4},{6,7},{7,6},{8,9},{9,8},{10,11... | collective-permute-start | bytes 1572872 | tf_op jit(solution)/shard_map/ppermute | solution.py:73
  123.6 10.3 %collective-permute-start.11 = (bf16[8,256,128]{2,1,0:T(8,128)(2,1)S(1)}, bf16[8,256,128]{2,1,0:T(8,128)(2,1)S(1)}, u32[]{:S(2)}, u32[]{:S(2)}) collective-permute-start(bf16[8,256,128]{2,1,0:T(8,128)(2,1)S(1)} %collective-permute-done.10.x0), channel_id=1, source_target_pairs={{0,1},{1,0},{2,3},{3,2},{4,5},{5,4},{6,7},{7,6},{8,9},{9,8},{10,11... | collective-permute-start | bytes 1572872 | tf_op jit(solution)/shard_map/ppermute | solution.py:73

commit v6 on v5

--- a/solution.py
+++ b/solution.py
@@ -175,30 +175,13 @@
 
 def lift_kernel(where, keep, got, up, down, near):
     count = keep.shape[0]
-    for out, first in ((up, 2), (down, count - 3), (near, count - 1)):
-        for i in range(out.shape[0]):
-            at = (where[3] + first + i) % count
+    for out, steps in ((up, (1, 4, -2)), (down, (-1, 2)), (near, (0, 3, -3))):
+        for i, step in enumerate(steps):
+            at = (where[3] + step + count) % count
             out[i] = (keep[at].astype(F32) + got[at].astype(F32)).astype(BF16)
 
 
-def pack_kernel(near, up, down, scaled, below, above, before, after, own):
-    before[0] = (near[0].astype(F32) + up[0].astype(F32)).astype(BF16)
-    before[1] = scaled[...]
-    before[2] = below[...]
-    after[0] = (near[2].astype(F32) + up[2].astype(F32) + down[1].astype(F32)).astype(BF16)
-    after[1] = scaled[...]
-    after[2] = below[...]
-    after[3] = above[...]
-    own[...] = near[1].astype(F32) + up[1].astype(F32) + down[0].astype(F32)
-
-
-def join_kernel(after, from_below, from_above, out):
-    out[:3] = after[1:]
-    out[3:6] = from_below[1:]
-    out[6:] = from_above[1:]
-
-
-def scale_kernel(where, seg, second, magnitude, cotangent, up, low, third, scaled, norms):
+def scale_kernel(where, seg, second, magnitude, cotangent, up, low, share, norms):
     count = cotangent.shape[0]
     marks = bounds(seg, seg.shape[0], where[0] * count)
     parts = second[...]
@@ -207,10 +190,37 @@
     norms[...] = col_norms
     scale = token_scale_of(magnitude[...].astype(F32) / col_norms, marks, count)
     grad = (cotangent[...].astype(F32) * scale).astype(BF16)
-    scaled[...] = grad
+    share[:count] = grad
     back = packed(picked(dot(up[...], grad, 1, 1), marks)).astype(BF16)
-    every = jnp.concatenate([low[...], back], axis=0)
-    third[...] = jnp.broadcast_to(every[None], third.shape)
+    share[count:] = jnp.concatenate([low[...], back], axis=0)
+
+
+def third_kernel(share, other, third):
+    total = (share[...].astype(F32) + other[...].astype(F32)).astype(BF16)
+    third[...] = jnp.broadcast_to(total[None], third.shape)
+
+
+def far_kernel(near, up, down, share, other, to_up, to_down, own):
+    own[...] = near[0].astype(F32) + up[0].astype(F32) + down[0].astype(F32)
+    to_up[0] = (near[1].astype(F32) + up[1].astype(F32) + down[1].astype(F32)).astype(BF16)
+    to_down[0] = (near[2].astype(F32) + up[2].astype(F32)).astype(BF16)
+    for out in (to_up, to_down):
+        out[1] = share[...]
+        out[2] = other[...]
+
+
+def pack_kernel(share, other, below, above, before, after):
+    for out in (before, after):
+        out[0] = share[...]
+        out[1] = other[...]
+        out[2:4] = below[1:]
+    after[4:6] = above[1:]
+
+
+def join_kernel(after, from_below, from_above, out):
+    out[:6] = after[...]
+    out[6:12] = from_below[...]
+    out[12:] = from_above[...]
 
 
 def sums_kernel(rank_rows, ranks):
@@ -267,7 +277,7 @@
     grad_magnitude[...] = total / norms[...]
 
 
-def tokens_kernel(where, x0, x1, *rest):
+def tokens_kernel(where, blocks, *rest):
     *columns, first, second, out, total = rest
     step = pl.program_id(0)
 
@@ -275,7 +285,7 @@
     def _():
         total[...] = dot(first[...], second[...], 0, 0)
 
-    left = [block[i] for i in range(x0.shape[0]) for block in (x0, x1)]
+    left = [blocks[i] for i in range(blocks.shape[0])]
     right = [column[...] for column in columns]
     total[...] += dot(jnp.concatenate(right, axis=1), jnp.concatenate(left, axis=1), 1, 1)
 
@@ -284,7 +294,7 @@
         out[...] = total[...]
 
 
-def tokens_rest_kernel(where, x0, x1, *rest):
+def tokens_rest_kernel(where, blocks, *rest):
     *columns, part, out, total = rest
     step = pl.program_id(0)
 
@@ -292,7 +302,7 @@
     def _():
         total[...] = part[...]
 
-    left = [block[i] for i in range(x0.shape[0]) for block in (x0, x1)]
+    left = [blocks[i] for i in range(blocks.shape[0])]
     right = [column[...] for column in columns]
     total[...] += dot(jnp.concatenate(right, axis=1), jnp.concatenate(left, axis=1), 1, 1)
 
@@ -404,12 +414,12 @@
         out_specs=[whole(n, count, width) for n in (3, 2, 3)],
         moved=6 * zs * count * width,
     )(where, keep, got)
-    up3 = shift(up3, along_z(3))
-    down2 = shift(down2, along_z(-3))
-
-    third, scaled, norms = call(
+    up3 = shift(up3, along_z(1))
+    down2 = shift(down2, along_z(-1))
+
+    share, norms = call(
         scale_kernel,
-        [shaped(zs, 4 * rank, width), shaped(count, width), shaped(adapters, width, dtype=F32)],
+        [shaped(count + 4 * rank, width), shaped(adapters, width, dtype=F32)],
         scalars=2,
         grid=(1,),
         in_specs=[
@@ -419,13 +429,32 @@
             whole(wide, width),
             whole(2 * rank, width),
         ],
-        out_specs=[whole(zs, 4 * rank, width), whole(count, width), whole(adapters, width)],
+        out_specs=[whole(count + 4 * rank, width), whole(adapters, width)],
         flops=2 * count * wide * width,
         moved=8 * count * width,
     )(where, seg_lengths, second, magnitude, cotangent, up_own, low)
+    other = shift(share, hi_pairs)
+    rank_rows = pl.BlockSpec((4 * rank, width), lambda i: (count // (4 * rank), 0))
+    scaled = whole(count, width)
+    third = call(
+        third_kernel,
+        shaped(zs, 4 * rank, width),
+        grid=(1,),
+        in_specs=[rank_rows, rank_rows],
+        out_specs=whole(zs, 4 * rank, width),
+        moved=2 * zs * 4 * rank * width,
+    )(share, other)
     third = exchange(third, "tensor", z_groups)
-    below = shift(scaled, along_z(3))
-    above = shift(scaled, along_z(-3))
+    to_up, to_down, base = call(
+        far_kernel,
+        [shaped(3, count, width), shaped(3, count, width), shaped(count, width, dtype=F32)],
+        grid=(1,),
+        in_specs=[whole(n, count, width) for n in (3, 3, 2)] + [scaled] * 2,
+        out_specs=[whole(3, count, width), whole(3, count, width), whole(count, width)],
+        moved=36 * count * width,
+    )(near, up3, down2, share, other)
+    below = shift(to_up, along_z(3))
+    above = shift(to_down, along_z(-3))
     ranks = call(
         sums_kernel,
         shaped(4 * rank, width),
@@ -434,30 +463,27 @@
         out_specs=whole(4 * rank, width),
         moved=2 * zs * 4 * rank * width,
     )(third)
-    ranks = (ranks.astype(F32) + shift(ranks, hi_pairs).astype(F32)).astype(BF16)
-    other = shift(ranks, core_pairs)
-
-    before, after, base = call(
+    other_ranks = shift(ranks, core_pairs)
+
+    before, after = call(
         pack_kernel,
-        [shaped(3, count, width), shaped(4, count, width), shaped(count, width, dtype=F32)],
-        grid=(1,),
-        in_specs=[whole(n, count, width) for n in (3, 3, 2)] + [whole(count, width)] * 3,
-        out_specs=[whole(3, count, width), whole(4, count, width), whole(count, width)],
-        moved=36 * count * width,
-    )(near, up3, down2, scaled, below, above)
+        [shaped(4, count, width), shaped(6, count, width)],
+        grid=(1,),
+        in_specs=[scaled] * 2 + [whole(3, count, width)] * 2,
+        out_specs=[whole(4, count, width), whole(6, count, width)],
+        moved=32 * count * width,
+    )(share, other, below, above)
     from_below = shift(after, along_z(1))
     from_above = shift(before, along_z(-1))
     gather_a = call(
         join_kernel,
-        shaped(zs, count, width),
-        grid=(1,),
-        in_specs=[whole(n, count, width) for n in (4, 4, 3)],
-        out_specs=whole(zs, count, width),
-        moved=4 * zs * count * width,
+        shaped(2 * zs, count, width),
+        grid=(1,),
+        in_specs=[whole(n, count, width) for n in (6, 6, 4)],
+        out_specs=whole(2 * zs, count, width),
+        moved=8 * zs * count * width,
     )(after, from_below, from_above)
-    gather_b = shift(gather_a, hi_pairs)
-    gather_c = shift(gather_a, core_pairs)
-    gather_d = shift(gather_b, core_pairs)
+    gather_b = shift(gather_a, core_pairs)
 
     edge = own_rows + -own_rows % LANES
     blocks = edge + width
@@ -476,7 +502,7 @@
         out_specs=[whole(adapters, rank, blocks), whole(wide, count), whole(wide, count)],
         flops=2 * count * wide * (own_rows + width),
         moved=4 * adapters * rank * blocks,
-    )(where, seg_lengths, ranks, other, scaled, up_own, turned)
+    )(where, seg_lengths, ranks, other_ranks, share, up_own, turned)
     fourth = exchange(fourth, "dp")
 
     first_block = pl.BlockSpec((1, count, width), lambda i, *s: (0, 0, 0))
@@ -498,7 +524,7 @@
         out_specs=[whole(count, width), whole(adapters, width)],
         flops=2 * count * wide * width,
         moved=16 * count * width,
-    )(where, seg_lengths, base, from_below, from_above, low_wide, up_own, norms, magnitude,
+    )(where, seg_lengths, base, below, above, low_wide, up_own, norms, magnitude,
       cotangent)
 
     fifth = call(
@@ -522,33 +548,33 @@
 
         return pl.BlockSpec((own_rows, width), at)
 
-    def columns(x_bit):
-        return [column(k, x_bit, c) for k in range(per) for c in range(2)]
-
-    block = pl.BlockSpec((per, count, width), lambda i, s: (i, 0, 0))
+    def columns(c_bit):
+        return [column(k, x, c_bit) for k in range(per) for x in range(2)]
+
+    block = pl.BlockSpec((2 * per, count, width), lambda i, s: (i, 0, 0))
     weights = [in_hbm(base_weight)] * (2 * per)
     part = call(
         tokens_kernel,
         shaped(own_rows, count, dtype=F32),
         scalars=1,
         grid=(zs // per,),
-        in_specs=[block] * 2 + columns(0) + [whole(wide, own_rows), whole(wide, count)],
+        in_specs=[block] + columns(0) + [whole(wide, own_rows), whole(wide, count)],
         out_specs=whole(own_rows, count),
         scratch=[pltpu.VMEM((own_rows, count), F32)],
         flops=count * own_rows * (full + 2 * wide),
         moved=own_rows * full,
-    )(where, gather_a, gather_c, *weights, down_flat, back_wide)
+    )(where, gather_a, *weights, down_flat, back_wide)
     grad_tokens = call(
         tokens_rest_kernel,
         shaped(own_rows, count),
         scalars=1,
         grid=(zs // per,),
-        in_specs=[block] * 2 + columns(1) + [whole(own_rows, count)],
+        in_specs=[block] + columns(1) + [whole(own_rows, count)],
         out_specs=whole(own_rows, count),
         scratch=[pltpu.VMEM((own_rows, count), F32)],
         flops=count * own_rows * full,
         moved=own_rows * full,
-    )(where, gather_b, gather_d, *weights, part)
+    )(where, gather_b, *weights, part)
 
     grad_down, grad_up, grad_magnitude = call(
         final_kernel,

time: 138 us -> 149 us (1.080)
  the two profiles are of different devices: /device:TPU:10 before, /device:TPU:14 now
where the time goes in v6:
time: 149 us; the launch traced here: 148 us
  starting transfers between devices  84.9 us (57%)
  waiting for transfers between devices  36.3 us (24%)
  Pallas kernels  23.8 us (16%)
  local copies, waits for them, and re-layouts  2.24 us (2%)
    ppermute x11, starting transfers between devices, shift(): return lax.ppermute(block, 'tensor', pairs)  44.7 us
    all_to_all x5, starting transfers between devices, exchange(): lax.all_to_all(blocks, axis, 0, 0, tiled=True, axis_index_groups=groups)  40.1 us
    ppermute x11, waiting for transfers between devices, shift(): return lax.ppermute(block, 'tensor', pairs)  20.7 us
    all_to_all x5, waiting for transfers between devices, exchange(): lax.all_to_all(blocks, axis, 0, 0, tiled=True, axis_index_groups=groups)  15.5 us
    pallas_call x1, Pallas kernels, local(): call(first_kernel, [shaped(size, HEAD, width), shaped(size // 2, count, w...  5.78 us
    pallas_call x1, Pallas kernels, local(): call(tokens_rest_kernel, shaped(own_rows, count), scalars=1, grid=(zs //...  3.69 us
    pallas_call x1, Pallas kernels, local(): call(tokens_kernel, shaped(own_rows, count, dtype=F32), scalars=1, grid=(...  3.36 us
  transfers between devices with their start and end apart: 16, of which 8 were waited for; matrix products, arithmetic and copies ran while one was open for 0% of the time, Pallas kernels for 9%

profile of v6, /device:TPU:14, one launch (start us, length us, event | category | flops | bytes accessed | tf_op | source)
XLA Modules:
  0.0 148.1 jit_solution(11171787515500559385)
XLA Ops:
  0.7 0.1 pad_add_fusion.where
  0.8 5.8 %shard_map.110 = (bf16[32,24,128]{2,1,0:T(8,128)(2,1)}, bf16[16,256,128]{2,1,0:T(8,128)(2,1)S(1)}, bf16[16,256,128]{2,1,0:T(8,128)(2,1)S(1)}) custom-call(s32[4]{0:T(128)S(1)} %pad_add_fusion.where, bf16[448,256]{1,0:T(8,128)(2,1)} %bitcast.14, bf16[448,4096]{1,0:T(8,128)(2,1)} %rest_7_.3, bf16[16,16,448]{2,1,0:T(8,128)(2,1)} %bitcast.11), custom_call_target="tpu_custom_call" | custom-call | flops 939524096 | bytes 3670016 | tf_op jit(solution)/shard_map/pallas_call | solution.py:340
  6.5 0.0 copy-start.7
  6.6 0.0 copy-start.3
  6.6 0.0 copy-start.6
  6.6 2.1 %collective-permute-start = (bf16[16,256,128]{2,1,0:T(8,128)(2,1)S(1)}, bf16[16,256,128]{2,1,0:T(8,128)(2,1)S(1)}, u32[]{:S(2)}, u32[]{:S(2)}) collective-permute-start(bf16[16,256,128]{2,1,0:T(8,128)(2,1)S(1)} %get-tuple-element.29), channel_id=1, source_target_pairs={{0,1},{1,0},{2,3},{3,2},{4,5},{5,4},{6,7},{7,6},{8,9},{9,8},{10,11... | collective-permute-start | bytes 3145736 | tf_op jit(solution)/shard_map/ppermute | solution.py:73
  8.6 2.6 %collective-permute-done.got_a.got_b = bf16[16,256,128]{2,1,0:T(8,128)(2,1)S(1)} collective-permute-done((bf16[16,256,128]{2,1,0:T(8,128)(2,1)S(1)}, bf16[16,256,128]{2,1,0:T(8,128)(2,1)S(1)}, u32[]{:S(2)}, u32[]{:S(2)}) %collective-permute-start) | collective-permute-done | bytes 1048608 | tf_op jit(solution)/shard_map/ppermute | solution.py:73
  11.3 0.9 shard_map.111
  12.1 3.3 %collective-permute-start.1 = (bf16[8,256,128]{2,1,0:T(8,128)(2,1)S(1)}, bf16[8,256,128]{2,1,0:T(8,128)(2,1)S(1)}, u32[]{:S(2)}, u32[]{:S(2)}) collective-permute-start(bf16[8,256,128]{2,1,0:T(8,128)(2,1)S(1)} %get-tuple-element.31), channel_id=1, source_target_pairs={{0,16},{1,17},{2,18},{3,19},{4,20},{5,21},{6,22},{7,23},{8,24},{9,... | collective-permute-start | bytes 1572872 | tf_op jit(solution)/shard_map/ppermute | solution.py:73
  15.5 13.5 %all-to-all-start = ((bf16[32,24,128]{2,1,0:T(8,128)(2,1)}), bf16[32,24,128]{2,1,0:T(8,128)(2,1)S(1)}, u32[]{:S(2)}, u32[]{:S(2)}) async-start(bf16[32,24,128]{2,1,0:T(8,128)(2,1)} %get-tuple-element.35), calls=%async_computation | async-start | bytes 393216 | tf_op jit(solution)/shard_map/all_to_all | solution.py:315
  28.9 0.6 collective-permute-done.1.got
  29.5 0.7 shard_map.112
  30.2 4.3 %collective-permute-start.2 = (bf16[3,256,128]{2,1,0:T(8,128)(2,1)S(1)}, bf16[3,256,128]{2,1,0:T(8,128)(2,1)S(1)}, u32[]{:S(2)}, u32[]{:S(2)}) collective-permute-start(bf16[3,256,128]{2,1,0:T(8,128)(2,1)S(1)} %get-tuple-element.33), channel_id=1, source_target_pairs={{0,2},{1,3},{2,4},{3,5},{4,6},{5,7},{6,8},{7,9},{8,10},{9,11},{10,... | collective-permute-start | bytes 589832 | tf_op jit(solution)/shard_map/ppermute | solution.py:73
  34.5 10.6 %collective-permute-start.3 = (bf16[2,256,128]{2,1,0:T(8,128)(2,1)S(1)}, bf16[2,256,128]{2,1,0:T(8,128)(2,1)S(1)}, u32[]{:S(2)}, u32[]{:S(2)}) collective-permute-start(bf16[2,256,128]{2,1,0:T(8,128)(2,1)S(1)} %get-tuple-element.34), channel_id=1, source_target_pairs={{0,14},{1,15},{2,0},{3,1},{4,2},{5,3},{6,4},{7,5},{8,6},{9,7},{10,... | collective-permute-start | bytes 393224 | tf_op jit(solution)/shard_map/ppermute | solution.py:73
  45.1 1.3 shard_map.113
  46.4 8.5 %all-to-all-start.1 = ((f32[16,2,128]{2,1,0:T(2,128)}), f32[16,2,128]{2,1,0:T(2,128)S(1)}, u32[]{:S(2)}, u32[]{:S(2)}) async-start(f32[16,2,128]{2,1,0:T(2,128)} %shard_map.113), calls=%async_computation.1 | async-start | bytes 32768 | tf_op jit(solution)/shard_map/all_to_all | solution.py:315
  54.9 0.8 shard_map.114.low
  55.7 5.5 %all-to-all-done.1.second = f32[16,2,128]{2,1,0:T(2,128)S(1)} async-done(((f32[16,2,128]{2,1,0:T(2,128)}), f32[16,2,128]{2,1,0:T(2,128)S(1)}, u32[]{:S(2)}, u32[]{:S(2)}) %all-to-all-start.1) | async-done | bytes 16416 | tf_op jit(solution)/shard_map/all_to_all | solution.py:315
  61.2 1.1 shard_map.115
  62.3 3.2 %collective-permute-start.4 = (bf16[320,128]{1,0:T(8,128)(2,1)S(1)}, bf16[320,128]{1,0:T(8,128)(2,1)S(1)}, u32[]{:S(2)}, u32[]{:S(2)}) collective-permute-start(bf16[320,128]{1,0:T(8,128)(2,1)S(1)} %get-tuple-element.36.share.scaled), channel_id=1, source_target_pairs={{0,16},{1,17},{2,18},{3,19},{4,20},{5,21},{6,22},{7,23},{8,24},{9,... | collective-permute-start | bytes 245768 | tf_op jit(solution)/shard_map/ppermute | solution.py:73
  65.5 4.6 %collective-permute-done.4.other = bf16[320,128]{1,0:T(8,128)(2,1)S(1)} collective-permute-done((bf16[320,128]{1,0:T(8,128)(2,1)S(1)}, bf16[320,128]{1,0:T(8,128)(2,1)S(1)}, u32[]{:S(2)}, u32[]{:S(2)}) %collective-permute-start.4) | collective-permute-done | bytes 81952 | tf_op jit(solution)/shard_map/ppermute | solution.py:73
  70.2 0.1 shard_map.116
  70.2 2.4 %collective-permute-start.5 = (bf16[3,256,128]{2,1,0:T(8,128)(2,1)S(1)}, bf16[3,256,128]{2,1,0:T(8,128)(2,1)S(1)}, u32[]{:S(2)}, u32[]{:S(2)}) collective-permute-start(bf16[3,256,128]{2,1,0:T(8,128)(2,1)S(1)} %get-tuple-element.38), channel_id=1, source_target_pairs={{0,6},{1,7},{2,8},{3,9},{4,10},{5,11},{6,12},{7,13},{8,14},{9,15},... | collective-permute-start | bytes 589832 | tf_op jit(solution)/shard_map/ppermute | solution.py:73
  72.7 6.4 %collective-permute-start.6 = (bf16[3,256,128]{2,1,0:T(8,128)(2,1)S(1)}, bf16[3,256,128]{2,1,0:T(8,128)(2,1)S(1)}, u32[]{:S(2)}, u32[]{:S(2)}) collective-permute-start(bf16[3,256,128]{2,1,0:T(8,128)(2,1)S(1)} %get-tuple-element.39), channel_id=1, source_target_pairs={{0,10},{1,11},{2,12},{3,13},{4,14},{5,15},{6,0},{7,1},{8,2},{9,3},... | collective-permute-start | bytes 589832 | tf_op jit(solution)/shard_map/ppermute | solution.py:73
  79.1 0.7 shard_map.117
  79.8 4.5 %all-to-all-start.2 = ((bf16[8,64,128]{2,1,0:T(8,128)(2,1)}), bf16[8,64,128]{2,1,0:T(8,128)(2,1)S(1)}, u32[]{:S(2)}, u32[]{:S(2)}) async-start(bf16[8,64,128]{2,1,0:T(8,128)(2,1)} %shard_map.117), calls=%async_computation.2 | async-start | bytes 262144 | tf_op jit(solution)/shard_map/all_to_all | solution.py:315
  84.3 4.7 %collective-permute-done.6.base_b.above = bf16[3,256,128]{2,1,0:T(8,128)(2,1)S(1)} collective-permute-done((bf16[3,256,128]{2,1,0:T(8,128)(2,1)S(1)}, bf16[3,256,128]{2,1,0:T(8,128)(2,1)S(1)}, u32[]{:S(2)}, u32[]{:S(2)}) %collective-permute-start.6) | collective-permute-done | bytes 196640 | tf_op jit(solution)/shard_map/ppermute | solution.py:73
  89.0 0.1 shard_map.121
  89.0 5.7 %collective-permute-start.8 = (bf16[6,256,128]{2,1,0:T(8,128)(2,1)S(1)}, bf16[6,256,128]{2,1,0:T(8,128)(2,1)S(1)}, u32[]{:S(2)}, u32[]{:S(2)}) collective-permute-start(bf16[6,256,128]{2,1,0:T(8,128)(2,1)S(1)} %get-tuple-element.43.after), channel_id=1, source_target_pairs={{0,2},{1,3},{2,4},{3,5},{4,6},{5,7},{6,8},{7,9},{8,10},{9,11},{10,... | collective-permute-start | bytes 1179656 | tf_op jit(solution)/shard_map/ppermute | solution.py:73
  94.8 1.9 %collective-permute-start.7 = (bf16[64,128]{1,0:T(8,128)(2,1)S(1)}, bf16[64,128]{1,0:T(8,128)(2,1)S(1)}, u32[]{:S(2)}, u32[]{:S(2)}) collective-permute-start(bf16[64,128]{1,0:T(8,128)(2,1)S(1)} %shard_map.118.ranks), channel_id=1, source_target_pairs={{0,1},{1,0},{2,3},{3,2},{4,5},{5,4},{6,7},{7,6},{8,9},{9,8},{10,11... | collective-permute-start | bytes 49160 | tf_op jit(solution)/shard_map/ppermute | solution.py:73
  96.7 1.1 collective-permute-done.7.got
  97.9 1.5 %shard_map.119 = (bf16[16,16,640]{2,1,0:T(8,128)(2,1)}, bf16[256,256]{1,0:T(8,128)(2,1)S(1)}, bf16[256,256]{1,0:T(8,128)(2,1)S(1)}) custom-call(s32[4]{0:T(128)S(1)} %pad_add_fusion.where, s32[16]{0:T(128)S(1)} %copy-done.7, bf16[64,128]{1,0:T(8,128)(2,1)S(1)} %shard_map.118.ranks, bf16[64,128]{1,0:T(8,128)(2,1)S(1)} %collective-permute-done.7.got, ...), custom_call_target="tpu_custom_call" | custom-call | flops 75497472 | bytes 655360 | tf_op jit(solution)/shard_map/pallas_call | solution.py:490
  99.4 0.7 copy-done.4
  100.1 5.6 %all-to-all-start.3 = ((bf16[16,16,640]{2,1,0:T(8,128)(2,1)}), bf16[16,16,640]{2,1,0:T(8,128)(2,1)S(1)}, u32[]{:S(2)}, u32[]{:S(2)}) async-start(bf16[16,16,640]{2,1,0:T(8,128)(2,1)} %get-tuple-element.46), calls=%async_computation.3 | async-start | bytes 655360 | tf_op jit(solution)/shard_map/all_to_all | solution.py:315
  105.7 2.9 %collective-permute-start.9 = (bf16[4,256,128]{2,1,0:T(8,128)(2,1)S(1)}, bf16[4,256,128]{2,1,0:T(8,128)(2,1)S(1)}, u32[]{:S(2)}, u32[]{:S(2)}) collective-permute-start(bf16[4,256,128]{2,1,0:T(8,128)(2,1)S(1)} %get-tuple-element.44), channel_id=1, source_target_pairs={{0,14},{1,15},{2,0},{3,1},{4,2},{5,3},{6,4},{7,5},{8,6},{9,7},{10,... | collective-permute-start | bytes 786440 | tf_op jit(solution)/shard_map/ppermute | solution.py:73
  108.6 7.0 %collective-permute-done.9.from_above = bf16[4,256,128]{2,1,0:T(8,128)(2,1)S(1)} collective-permute-done((bf16[4,256,128]{2,1,0:T(8,128)(2,1)S(1)}, bf16[4,256,128]{2,1,0:T(8,128)(2,1)S(1)}, u32[]{:S(2)}, u32[]{:S(2)}) %collective-permute-start.9) | collective-permute-done | bytes 262176 | tf_op jit(solution)/shard_map/ppermute | solution.py:73
  115.7 0.1 shard_map.122.blocks
  115.7 1.9 %collective-permute-start.10 = (bf16[16,256,128]{2,1,0:T(8,128)(2,1)S(1)}, bf16[16,256,128]{2,1,0:T(8,128)(2,1)S(1)}, u32[]{:S(2)}, u32[]{:S(2)}) collective-permute-start(bf16[16,256,128]{2,1,0:T(8,128)(2,1)S(1)} %shard_map.122.blocks), channel_id=1, source_target_pairs={{0,1},{1,0},{2,3},{3,2},{4,5},{5,4},{6,7},{7,6},{8,9},{9,8},{10,11... | collective-permute-start | bytes 3145736 | tf_op jit(solution)/shard_map/ppermute | solution.py:73
  117.7 0.0 copy-start.5
  117.7 0.9 copy-done.5
  118.6 0.7 copy-done.8
  119.2 2.1 %shard_map.120 = (bf16[256,128]{1,0:T(8,128)(2,1)}, bf16[16,128]{1,0:T(8,128)(2,1)S(1)}) custom-call(s32[4]{0:T(128)S(1)} %pad_add_fusion.where, s32[16]{0:T(128)S(1)} %copy-done.8, f32[256,128]{1,0:T(8,128)S(1)} %get-tuple-element.37.base, bf16[3,256,128]{2,1,0:T(8,128)(2,1)S(1)} %collective-permute-done.5.base_a.below, ...), custom_call_target="tpu_custom_call" | custom-call | flops 16777216 | bytes 524288 | tf_op jit(solution)/shard_map/pallas_call | solution.py:509
  121.3 0.8 shard_map.125
  122.1 8.1 %all-to-all-start.4 = ((bf16[16,16,768]{2,1,0:T(8,128)(2,1)}), bf16[16,16,768]{2,1,0:T(8,128)(2,1)S(1)}, u32[]{:S(2)}, u32[]{:S(2)}) async-start(bf16[16,16,768]{2,1,0:T(8,128)(2,1)} %shard_map.125), calls=%async_computation.4 | async-start | bytes 786432 | tf_op jit(solution)/shard_map/all_to_all | solution.py:315
  130.3 3.4 %shard_map.123.rest_8_ = f32[448,256]{1,0:T(8,128)S(1)} custom-call(s32[4]{0:T(128)S(1)} %pad_add_fusion.where, bf16[16,256,128]{2,1,0:T(8,128)(2,1)S(1)} %shard_map.122.blocks, bf16[448,4096]{1,0:T(8,128)(2,1)} %rest_7_.3, bf16[448,4096]{1,0:T(8,128)(2,1)} %rest_7_.3, bf16[448,4096]{1,0:T(8,128)(2,1)} %rest_7_.3, bf16[448,4096]{1,0:T(8,128)(2,1)} %rest_7_.3, ...), custom_call_target="tpu_custom_call" | custom-call | flops 528482304 | bytes 1835008 | tf_op jit(solution)/shard_map/pallas_call | solution.py:556
  133.7 10.0 %all-to-all-done.4.fifth = bf16[16,16,768]{2,1,0:T(8,128)(2,1)S(1)} async-done(((bf16[16,16,768]{2,1,0:T(8,128)(2,1)}), bf16[16,16,768]{2,1,0:T(8,128)(2,1)S(1)}, u32[]{:S(2)}, u32[]{:S(2)}) %all-to-all-start.4) | async-done | bytes 393248 | tf_op jit(solution)/shard_map/all_to_all | solution.py:315
  143.7 0.8 shard_map.126
  144.4 3.7 %shard_map.124 = bf16[448,256]{1,0:T(8,128)(2,1)} custom-call(s32[4]{0:T(128)S(1)} %pad_add_fusion.where, bf16[16,256,128]{2,1,0:T(8,128)(2,1)S(1)} %collective-permute-done.10.blocks, bf16[448,4096]{1,0:T(8,128)(2,1)} %rest_7_.3, bf16[448,4096]{1,0:T(8,128)(2,1)} %rest_7_.3, bf16[448,4096]{1,0:T(8,128)(2,1)} %rest_7_.3, bf16[448,4096]{1,0:T(8,128)(2,1)} %rest_7_.3, ...), custom_call_target="tpu_custom_call" | custom-call | flops 469762048 | bytes 1835008 | tf_op jit(solution)/shard_map/pallas_call | solution.py:567
  (20 shorter events, 0.1 us)
Async XLA Ops:
  6.5 38.5 %copy-start.2 = (bf16[16,16,128]{2,1,0:T(8,128)(2,1)S(1)}, bf16[16,16,128]{2,1,0:T(8,128)(2,1)}, u32[]{:S(2)}) copy-start(bf16[16,16,128]{2,1,0:T(8,128)(2,1)} %up.1) | copy-start | bytes 196612
  6.5 48.3 %copy-start = (bf16[16,448,16]{1,2,0:T(8,128)(2,1)S(1)}, bf16[16,448,16]{1,2,0:T(8,128)(2,1)}, u32[]{:S(2)}) copy-start(bf16[16,448,16]{1,2,0:T(8,128)(2,1)} %param.9) | copy-start | bytes 688132
  6.5 48.3 %copy-start.1 = (bf16[256,448]{0,1:T(8,128)(2,1)S(1)}, bf16[256,448]{0,1:T(8,128)(2,1)}, u32[]{:S(2)}) copy-start(bf16[256,448]{0,1:T(8,128)(2,1)} %param.7) | copy-start | bytes 688132
  6.5 48.3 %copy-start.7 = (s32[16]{0:T(128)S(1)}, s32[16]{0:T(128)}, u32[]{:S(2)}) copy-start(s32[16]{0:T(128)} %seg.7) | copy-start | bytes 196
  6.6 54.6 %copy-start.3 = (bf16[256,128]{1,0:T(8,128)(2,1)S(1)}, bf16[256,128]{1,0:T(8,128)(2,1)}, u32[]{:S(2)}) copy-start(bf16[256,128]{1,0:T(8,128)(2,1)} %cotangent.3) | copy-start | bytes 196612
  6.6 54.6 %copy-start.6 = (bf16[16,128]{1,0:T(8,128)(2,1)S(1)}, bf16[16,128]{1,0:T(8,128)(2,1)}, u32[]{:S(2)}) copy-start(bf16[16,128]{1,0:T(8,128)(2,1)} %magnitude.3) | copy-start | bytes 12292
  6.6 4.7 %collective-permute-start = (bf16[16,256,128]{2,1,0:T(8,128)(2,1)S(1)}, bf16[16,256,128]{2,1,0:T(8,128)(2,1)S(1)}, u32[]{:S(2)}, u32[]{:S(2)}) collective-permute-start(bf16[16,256,128]{2,1,0:T(8,128)(2,1)S(1)} %get-tuple-element.29), channel_id=1, source_target_pairs={{0,1},{1,0},{2,3},{3,2},{4,5},{5,4},{6,7},{7,6},{8,9},{9,8},{10,11... | collective-permute-start | bytes 3145736 | tf_op jit(solution)/shard_map/ppermute | solution.py:73
  12.1 17.4 %collective-permute-start.1 = (bf16[8,256,128]{2,1,0:T(8,128)(2,1)S(1)}, bf16[8,256,128]{2,1,0:T(8,128)(2,1)S(1)}, u32[]{:S(2)}, u32[]{:S(2)}) collective-permute-start(bf16[8,256,128]{2,1,0:T(8,128)(2,1)S(1)} %get-tuple-element.31), channel_id=1, source_target_pairs={{0,16},{1,17},{2,18},{3,19},{4,20},{5,21},{6,22},{7,23},{8,24},{9,... | collective-permute-start | bytes 1572872 | tf_op jit(solution)/shard_map/ppermute | solution.py:73
  15.5 29.6 %all-to-all-start = ((bf16[32,24,128]{2,1,0:T(8,128)(2,1)}), bf16[32,24,128]{2,1,0:T(8,128)(2,1)S(1)}, u32[]{:S(2)}, u32[]{:S(2)}) async-start(bf16[32,24,128]{2,1,0:T(8,128)(2,1)} %get-tuple-element.35), calls=%async_computation | async-start | bytes 393216 | tf_op jit(solution)/shard_map/all_to_all | solution.py:315
  30.2 40.0 %collective-permute-start.2 = (bf16[3,256,128]{2,1,0:T(8,128)(2,1)S(1)}, bf16[3,256,128]{2,1,0:T(8,128)(2,1)S(1)}, u32[]{:S(2)}, u32[]{:S(2)}) collective-permute-start(bf16[3,256,128]{2,1,0:T(8,128)(2,1)S(1)} %get-tuple-element.33), channel_id=1, source_target_pairs={{0,2},{1,3},{2,4},{3,5},{4,6},{5,7},{6,8},{7,9},{8,10},{9,11},{10,... | collective-permute-start | bytes 589832 | tf_op jit(solution)/shard_map/ppermute | solution.py:73
  34.5 35.7 %collective-permute-start.3 = (bf16[2,256,128]{2,1,0:T(8,128)(2,1)S(1)}, bf16[2,256,128]{2,1,0:T(8,128)(2,1)S(1)}, u32[]{:S(2)}, u32[]{:S(2)}) collective-permute-start(bf16[2,256,128]{2,1,0:T(8,128)(2,1)S(1)} %get-tuple-element.34), channel_id=1, source_target_pairs={{0,14},{1,15},{2,0},{3,1},{4,2},{5,3},{6,4},{7,5},{8,6},{9,7},{10,... | collective-permute-start | bytes 393224 | tf_op jit(solution)/shard_map/ppermute | solution.py:73
  46.4 14.8 %all-to-all-start.1 = ((f32[16,2,128]{2,1,0:T(2,128)}), f32[16,2,128]{2,1,0:T(2,128)S(1)}, u32[]{:S(2)}, u32[]{:S(2)}) async-start(f32[16,2,128]{2,1,0:T(2,128)} %shard_map.113), calls=%async_computation.1 | async-start | bytes 32768 | tf_op jit(solution)/shard_map/all_to_all | solution.py:315
  62.3 7.8 %collective-permute-start.4 = (bf16[320,128]{1,0:T(8,128)(2,1)S(1)}, bf16[320,128]{1,0:T(8,128)(2,1)S(1)}, u32[]{:S(2)}, u32[]{:S(2)}) collective-permute-start(bf16[320,128]{1,0:T(8,128)(2,1)S(1)} %get-tuple-element.36.share.scaled), channel_id=1, source_target_pairs={{0,16},{1,17},{2,18},{3,19},{4,20},{5,21},{6,22},{7,23},{8,24},{9,... | collective-permute-start | bytes 245768 | tf_op jit(solution)/shard_map/ppermute | solution.py:73
  70.2 14.0 %collective-permute-start.5 = (bf16[3,256,128]{2,1,0:T(8,128)(2,1)S(1)}, bf16[3,256,128]{2,1,0:T(8,128)(2,1)S(1)}, u32[]{:S(2)}, u32[]{:S(2)}) collective-permute-start(bf16[3,256,128]{2,1,0:T(8,128)(2,1)S(1)} %get-tuple-element.38), channel_id=1, source_target_pairs={{0,6},{1,7},{2,8},{3,9},{4,10},{5,11},{6,12},{7,13},{8,14},{9,15},... | collective-permute-start | bytes 589832 | tf_op jit(solution)/shard_map/ppermute | solution.py:73
  72.7 16.3 %collective-permute-start.6 = (bf16[3,256,128]{2,1,0:T(8,128)(2,1)S(1)}, bf16[3,256,128]{2,1,0:T(8,128)(2,1)S(1)}, u32[]{:S(2)}, u32[]{:S(2)}) collective-permute-start(bf16[3,256,128]{2,1,0:T(8,128)(2,1)S(1)} %get-tuple-element.39), channel_id=1, source_target_pairs={{0,10},{1,11},{2,12},{3,13},{4,14},{5,15},{6,0},{7,1},{8,2},{9,3},... | collective-permute-start | bytes 589832 | tf_op jit(solution)/shard_map/ppermute | solution.py:73
  79.8 15.0 %all-to-all-start.2 = ((bf16[8,64,128]{2,1,0:T(8,128)(2,1)}), bf16[8,64,128]{2,1,0:T(8,128)(2,1)S(1)}, u32[]{:S(2)}, u32[]{:S(2)}) async-start(bf16[8,64,128]{2,1,0:T(8,128)(2,1)} %shard_map.117), calls=%async_computation.2 | async-start | bytes 262144 | tf_op jit(solution)/shard_map/all_to_all | solution.py:315
  89.0 26.6 %collective-permute-start.8 = (bf16[6,256,128]{2,1,0:T(8,128)(2,1)S(1)}, bf16[6,256,128]{2,1,0:T(8,128)(2,1)S(1)}, u32[]{:S(2)}, u32[]{:S(2)}) collective-permute-start(bf16[6,256,128]{2,1,0:T(8,128)(2,1)S(1)} %get-tuple-element.43.after), channel_id=1, source_target_pairs={{0,2},{1,3},{2,4},{3,5},{4,6},{5,7},{6,8},{7,9},{8,10},{9,11},{10,... | collective-permute-start | bytes 1179656 | tf_op jit(solution)/shard_map/ppermute | solution.py:73
  94.8 3.1 %collective-permute-start.7 = (bf16[64,128]{1,0:T(8,128)(2,1)S(1)}, bf16[64,128]{1,0:T(8,128)(2,1)S(1)}, u32[]{:S(2)}, u32[]{:S(2)}) collective-permute-start(bf16[64,128]{1,0:T(8,128)(2,1)S(1)} %shard_map.118.ranks), channel_id=1, source_target_pairs={{0,1},{1,0},{2,3},{3,2},{4,5},{5,4},{6,7},{7,6},{8,9},{9,8},{10,11... | collective-permute-start | bytes 49160 | tf_op jit(solution)/shard_map/ppermute | solution.py:73
  99.4 0.7 copy-start.4
  100.1 21.2 %all-to-all-start.3 = ((bf16[16,16,640]{2,1,0:T(8,128)(2,1)}), bf16[16,16,640]{2,1,0:T(8,128)(2,1)S(1)}, u32[]{:S(2)}, u32[]{:S(2)}) async-start(bf16[16,16,640]{2,1,0:T(8,128)(2,1)} %get-tuple-element.46), calls=%async_computation.3 | async-start | bytes 655360 | tf_op jit(solution)/shard_map/all_to_all | solution.py:315
  105.7 10.0 %collective-permute-start.9 = (bf16[4,256,128]{2,1,0:T(8,128)(2,1)S(1)}, bf16[4,256,128]{2,1,0:T(8,128)(2,1)S(1)}, u32[]{:S(2)}, u32[]{:S(2)}) collective-permute-start(bf16[4,256,128]{2,1,0:T(8,128)(2,1)S(1)} %get-tuple-element.44), channel_id=1, source_target_pairs={{0,14},{1,15},{2,0},{3,1},{4,2},{5,3},{6,4},{7,5},{8,6},{9,7},{10,... | collective-permute-start | bytes 786440 | tf_op jit(solution)/shard_map/ppermute | solution.py:73
  115.7 28.7 %collective-permute-start.10 = (bf16[16,256,128]{2,1,0:T(8,128)(2,1)S(1)}, bf16[16,256,128]{2,1,0:T(8,128)(2,1)S(1)}, u32[]{:S(2)}, u32[]{:S(2)}) collective-permute-start(bf16[16,256,128]{2,1,0:T(8,128)(2,1)S(1)} %shard_map.122.blocks), channel_id=1, source_target_pairs={{0,1},{1,0},{2,3},{3,2},{4,5},{5,4},{6,7},{7,6},{8,9},{9,8},{10,11... | collective-permute-start | bytes 3145736 | tf_op jit(solution)/shard_map/ppermute | solution.py:73
  117.7 0.9 copy-start.5
  118.6 0.7 copy-start.8
  122.1 21.5 %all-to-all-start.4 = ((bf16[16,16,768]{2,1,0:T(8,128)(2,1)}), bf16[16,16,768]{2,1,0:T(8,128)(2,1)S(1)}, u32[]{:S(2)}, u32[]{:S(2)}) async-start(bf16[16,16,768]{2,1,0:T(8,128)(2,1)} %shard_map.125), calls=%async_computation.4 | async-start | bytes 786432 | tf_op jit(solution)/shard_map/all_to_all | solution.py:315

commit v7 on v6

--- a/solution.py
+++ b/solution.py
@@ -6,7 +6,6 @@
 from jax.sharding import PartitionSpec as P
 
 
-HIGHEST_MODE = lax.Precision.HIGHEST
 EPSILON = 1e-06
 F32 = jnp.float32
 BF16 = jnp.bfloat16
@@ -108,8 +107,8 @@
         lines[:count] = tokens[...].T
         lines[count:] = mine
         square = dot(mine, mine, 1, 1)
-        tile = (iota((rank, LANES), 1) % rank == iota((rank, LANES), 0)).astype(F32)
-        spread = dot(square, tile, 1, 0, HIGHEST_MODE)
+        tile = (iota((rank, LANES), 1) % rank == iota((rank, LANES), 0)).astype(BF16)
+        spread = dot(square.astype(BF16), tile, 1, 0)
         rows, cols = iota((rank, LANES), 0), iota((rank, LANES), 1)
         spread = jnp.where(cols // rank == rows % 8, spread, 0.0)
         gram[0:1, :] = jnp.sum(spread[:8], axis=0, keepdims=True)
@@ -117,35 +116,30 @@
 
     share = 32
     pieces = weight.shape[0] // share
-    part = weight[pl.ds(pl.multiple_of(jnp.minimum(where[0], pieces - 1) * share, share), share), :]
-    part = part.astype(F32)
-    squares = jnp.sum(part * part, axis=0, keepdims=True) * (where[0] < pieces).astype(F32)
+    start = pl.multiple_of(jnp.minimum(where[0], pieces - 1) * share, share)
+    mine = (where[0] < pieces).astype(F32)
     row = iota((8, LANES), 0)
-    for block in range(0, weight.shape[1], 4 * LANES):
-        both = dot(lines[...], weight[:, block : block + 4 * LANES], 1, 0)
-        base = both[:count].astype(BF16)
-        for k in range(4):
+    swap = where[1] != 0
+    step = 8 * LANES
+    for block in range(0, weight.shape[1], step):
+        columns = slice(block, block + step)
+        both = dot(lines[...], weight[:, columns], 1, 0)
+        part = weight[pl.ds(start, share), columns].astype(F32)
+        squares = jnp.sum(part * part, axis=0, keepdims=True) * mine
+        for k in range(step // LANES):
             lanes = slice(k * LANES, (k + 1) * LANES)
             tail = jnp.where(
                 row == 0,
-                squares[:, block + k * LANES : block + (k + 1) * LANES],
+                squares[:, lanes],
                 jnp.where(row == 1, gram[0:1, :], jnp.where(row == 2, gram[1:2, :], 0.0)),
             )
             head[block // LANES + k] = jnp.concatenate([both[count:, lanes], tail], 0).astype(BF16)
-        for k in range(2):
+        for k in range(step // LANES // 2):
+            even = both[:count, 2 * k * LANES : (2 * k + 1) * LANES]
+            odd = both[:count, (2 * k + 1) * LANES : (2 * k + 2) * LANES]
             at = block // LANES // 2 + k
-            even = base[:, 2 * k * LANES : (2 * k + 1) * LANES]
-            odd = base[:, (2 * k + 1) * LANES : (2 * k + 2) * LANES]
-
-            @pl.when(where[1] == 0)
-            def _():
-                keep[at] = even
-                give[at] = odd
-
-            @pl.when(where[1] != 0)
-            def _():
-                keep[at] = odd
-                give[at] = even
+            keep[at] = jnp.where(swap, odd, even).astype(BF16)
+            give[at] = jnp.where(swap, even, odd).astype(BF16)
 
 
 def low_kernel(where, seg, tokens, down, low):
@@ -166,8 +160,10 @@
     rows, cols = iota((rank, LANES), 0), iota((rank, LANES), 1)
     spread = jnp.where(rows < 8, total[rank + 1 : rank + 2], total[rank + 2 : rank + 3])
     spread = jnp.where(cols // rank == rows % 8, spread, 0.0)
-    tiled = jnp.concatenate([factor] * (LANES // rank), axis=0)
-    gram_up = dot(spread, tiled, 1, 0, HIGHEST_MODE)
+    tiled = jnp.concatenate([up[0]] * (LANES // rank), axis=0)
+    high = spread.astype(BF16)
+    rest = (spread - high.astype(F32)).astype(BF16)
+    gram_up = dot(high, tiled, 1, 0) + dot(rest, tiled, 1, 0)
     mine = jnp.sum(factor * (2.0 * total[:rank] + gram_up), axis=0, keepdims=True)
     both = jnp.concatenate([mine, total[rank : rank + 1]], axis=0)
     second[...] = jnp.broadcast_to(both[None], second.shape)
@@ -181,7 +177,7 @@
             out[i] = (keep[at].astype(F32) + got[at].astype(F32)).astype(BF16)
 
 
-def scale_kernel(where, seg, second, magnitude, cotangent, up, low, share, norms):
+def scale_kernel(where, seg, second, magnitude, cotangent, up, low, scaled, third, norms):
     count = cotangent.shape[0]
     marks = bounds(seg, seg.shape[0], where[0] * count)
     parts = second[...]
@@ -190,14 +186,10 @@
     norms[...] = col_norms
     scale = token_scale_of(magnitude[...].astype(F32) / col_norms, marks, count)
     grad = (cotangent[...].astype(F32) * scale).astype(BF16)
-    share[:count] = grad
+    scaled[...] = grad
     back = packed(picked(dot(up[...], grad, 1, 1), marks)).astype(BF16)
-    share[count:] = jnp.concatenate([low[...], back], axis=0)
-
-
-def third_kernel(share, other, third):
-    total = (share[...].astype(F32) + other[...].astype(F32)).astype(BF16)
-    third[...] = jnp.broadcast_to(total[None], third.shape)
+    every = jnp.concatenate([low[...], back], axis=0)
+    third[...] = jnp.broadcast_to(every[None], third.shape)
 
 
 def far_kernel(near, up, down, share, other, to_up, to_down, own):
@@ -332,14 +324,18 @@
     hi_pairs = [(i, (i + size // 2) % size) for i in range(size)]
 
     turned = tokens.T
-    z_groups = [[h * 2 * zs + a * 2 + c for a in range(zs)] for h in range(2) for c in range(2)]
+    core_groups = [list(range(c, size, 2)) for c in range(2)]
     down_rows = jnp.transpose(adapter_down, (0, 2, 1))
     down_flat = down_rows.reshape(wide, own_rows)
     up_own = adapter_up.reshape(wide, width)
 
     head, keep, give = call(
         first_kernel,
-        [shaped(size, HEAD, width), shaped(size // 2, count, width), shaped(size // 2, count, width)],
+        [
+            shaped(size, HEAD, width),
+            shaped(size // 2, count, width),
+            pltpu.HBM((size // 2, count, width), BF16),
+        ],
         scalars=1,
         grid=(2,),
         in_specs=[
@@ -417,9 +413,13 @@
     up3 = shift(up3, along_z(1))
     down2 = shift(down2, along_z(-1))
 
-    share, norms = call(
+    share, third, norms = call(
         scale_kernel,
-        [shaped(count + 4 * rank, width), shaped(adapters, width, dtype=F32)],
+        [
+            shaped(count, width),
+            shaped(2 * zs, 4 * rank, width),
+            shaped(adapters, width, dtype=F32),
+        ],
         scalars=2,
         grid=(1,),
         in_specs=[
@@ -429,22 +429,17 @@
             whole(wide, width),
             whole(2 * rank, width),
         ],
-        out_specs=[whole(count + 4 * rank, width), whole(adapters, width)],
+        out_specs=[
+            whole(count, width),
+            whole(2 * zs, 4 * rank, width),
+            whole(adapters, width),
+        ],
         flops=2 * count * wide * width,
         moved=8 * count * width,
     )(where, seg_lengths, second, magnitude, cotangent, up_own, low)
+    third = exchange(third, "tensor", core_groups)
     other = shift(share, hi_pairs)
-    rank_rows = pl.BlockSpec((4 * rank, width), lambda i: (count // (4 * rank), 0))
     scaled = whole(count, width)
-    third = call(
-        third_kernel,
-        shaped(zs, 4 * rank, width),
-        grid=(1,),
-        in_specs=[rank_rows, rank_rows],
-        out_specs=whole(zs, 4 * rank, width),
-        moved=2 * zs * 4 * rank * width,
-    )(share, other)
-    third = exchange(third, "tensor", z_groups)
     to_up, to_down, base = call(
         far_kernel,
         [shaped(3, count, width), shaped(3, count, width), shaped(count, width, dtype=F32)],
@@ -459,7 +454,7 @@
         sums_kernel,
         shaped(4 * rank, width),
         grid=(1,),
-        in_specs=[whole(zs, 4 * rank, width)],
+        in_specs=[whole(2 * zs, 4 * rank, width)],
         out_specs=whole(4 * rank, width),
         moved=2 * zs * 4 * rank * width,
     )(third)

time: 149 us -> 158 us (1.060)
  blocking collectives: 0 us -> 23.7 us
  starting transfers between devices: 84.9 us -> 66.3 us
  waiting for transfers between devices: 36.3 us -> 41.1 us
    all_to_all x0 -> x1, blocking collectives: none -> 23.7 us  [exchange(): lax.all_to_all(blocks, axis, 0, 0, tiled=True, axis_index_groups=groups)]
    all_to_all x5 -> x4, starting transfers between devices: 40.1 us -> 28.8 us  [exchange(): lax.all_to_all(blocks, axis, 0, 0, tiled=True, axis_index_groups=groups)]
    ppermute x11, starting transfers between devices: 44.7 us -> 37.5 us  [shift(): return lax.ppermute(block, 'tensor', pairs)]
    ppermute x11, waiting for transfers between devices: 20.7 us -> 25.6 us  [shift(): return lax.ppermute(block, 'tensor', pairs)]
    all_to_all x5 -> x4, waiting for transfers between devices: 15.5 us -> 15.5 us  [exchange(): lax.all_to_all(blocks, axis, 0, 0, tiled=True, axis_index_groups=groups)]
  transfers between devices with their start and end apart: 16 -> 15, of which waited for: 8 -> 8; matrix products, arithmetic and copies ran while one was open for 0% -> 0% of each run, Pallas kernels for 9% -> 9%
where the time goes in v7:
time: 158 us; the launch traced here: 157 us
  starting transfers between devices  66.3 us (42%)
  waiting for transfers between devices  41.1 us (26%)
  blocking collectives  23.7 us (15%)
  Pallas kernels  23 us (15%)
  local copies, waits for them, and re-layouts  2.23 us (1%)
    ppermute x11, starting transfers between devices, shift(): return lax.ppermute(block, 'tensor', pairs)  37.5 us
    all_to_all x4, starting transfers between devices, exchange(): lax.all_to_all(blocks, axis, 0, 0, tiled=True, axis_index_groups=groups)  28.8 us
    ppermute x11, waiting for transfers between devices, shift(): return lax.ppermute(block, 'tensor', pairs)  25.6 us
    all_to_all x1, blocking collectives, exchange(): lax.all_to_all(blocks, axis, 0, 0, tiled=True, axis_index_groups=groups)  23.7 us
    all_to_all x4, waiting for transfers between devices, exchange(): lax.all_to_all(blocks, axis, 0, 0, tiled=True, axis_index_groups=groups)  15.5 us
    pallas_call x1, Pallas kernels, local(): call(first_kernel, [shaped(size, HEAD, width), shaped(size // 2, count, w...  5.03 us
    pallas_call x1, Pallas kernels, local(): call(tokens_rest_kernel, shaped(own_rows, count), scalars=1, grid=(zs //...  3.69 us
    pallas_call x1, Pallas kernels, local(): call(tokens_kernel, shaped(own_rows, count, dtype=F32), scalars=1, grid=(...  3.36 us
  transfers between devices with their start and end apart: 15, of which 8 were waited for; matrix products, arithmetic and copies ran while one was open for 0% of the time, Pallas kernels for 9%

profile of v7, /device:TPU:14, one launch (start us, length us, event | category | flops | bytes accessed | tf_op | source)
XLA Modules:
  0.0 157.3 jit_solution(7782278364811620324)
XLA Ops:
  0.7 0.1 pad_add_fusion.where
  0.8 5.0 %shard_map.110 = (bf16[32,24,128]{2,1,0:T(8,128)(2,1)S(1)}, bf16[16,256,128]{2,1,0:T(8,128)(2,1)S(1)}, bf16[16,256,128]{2,1,0:T(8,128)(2,1)}) custom-call(s32[4]{0:T(128)S(1)} %pad_add_fusion.where, bf16[448,256]{1,0:T(8,128)(2,1)} %bitcast.14, bf16[448,4096]{1,0:T(8,128)(2,1)} %rest_7_.3, bf16[16,16,448]{2,1,0:T(8,128)(2,1)} %bitcast.11), custom_call_target="tpu_custom_call" | custom-call | flops 939524096 | bytes 3670016 | tf_op jit(solution)/shard_map/pallas_call | solution.py:332
  5.8 2.0 %collective-permute-start = (bf16[16,256,128]{2,1,0:T(8,128)(2,1)}, bf16[16,256,128]{2,1,0:T(8,128)(2,1)S(1)}, u32[]{:S(2)}, u32[]{:S(2)}) collective-permute-start(bf16[16,256,128]{2,1,0:T(8,128)(2,1)} %get-tuple-element.30), channel_id=1, source_target_pairs={{0,1},{1,0},{2,3},{3,2},{4,5},{5,4},{6,7},{7,6},{8,9},{9,8},{10,11... | collective-permute-start | bytes 3145736 | tf_op jit(solution)/shard_map/ppermute | solution.py:72
  7.8 2.8 %collective-permute-done.got_a.got_b = bf16[16,256,128]{2,1,0:T(8,128)(2,1)S(1)} collective-permute-done((bf16[16,256,128]{2,1,0:T(8,128)(2,1)}, bf16[16,256,128]{2,1,0:T(8,128)(2,1)S(1)}, u32[]{:S(2)}, u32[]{:S(2)}) %collective-permute-start) | collective-permute-done | bytes 1048608 | tf_op jit(solution)/shard_map/ppermute | solution.py:72
  10.7 0.9 shard_map.111
  11.6 3.3 %collective-permute-start.1 = (bf16[8,256,128]{2,1,0:T(8,128)(2,1)S(1)}, bf16[8,256,128]{2,1,0:T(8,128)(2,1)S(1)}, u32[]{:S(2)}, u32[]{:S(2)}) collective-permute-start(bf16[8,256,128]{2,1,0:T(8,128)(2,1)S(1)} %get-tuple-element.32), channel_id=1, source_target_pairs={{0,16},{1,17},{2,18},{3,19},{4,20},{5,21},{6,22},{7,23},{8,24},{9,... | collective-permute-start | bytes 1572872 | tf_op jit(solution)/shard_map/ppermute | solution.py:72
  14.9 23.7 %all_to_all.25.head = bf16[32,24,128]{2,1,0:T(8,128)(2,1)S(1)} all-to-all(bf16[32,24,128]{2,1,0:T(8,128)(2,1)S(1)} %get-tuple-element.36), channel_id=1, replica_groups=mesh['dp'=16,'tensor'=32] {'tensor'}, dimensions={0} | all-to-all | bytes 393216 | tf_op jit(solution)/shard_map/all_to_all | solution.py:307
  38.6 1.3 shard_map.113
  39.9 8.5 %all-to-all-start.1 = ((f32[16,2,128]{2,1,0:T(2,128)}), f32[16,2,128]{2,1,0:T(2,128)S(1)}, u32[]{:S(2)}, u32[]{:S(2)}) async-start(f32[16,2,128]{2,1,0:T(2,128)} %shard_map.113), calls=%async_computation.1 | async-start | bytes 32768 | tf_op jit(solution)/shard_map/all_to_all | solution.py:307
  48.4 0.8 shard_map.114.low
  49.1 5.5 %all-to-all-done.1.second = f32[16,2,128]{2,1,0:T(2,128)S(1)} async-done(((f32[16,2,128]{2,1,0:T(2,128)}), f32[16,2,128]{2,1,0:T(2,128)S(1)}, u32[]{:S(2)}, u32[]{:S(2)}) %all-to-all-start.1) | async-done | bytes 16416 | tf_op jit(solution)/shard_map/all_to_all | solution.py:307
  54.7 1.8 %shard_map.115 = (bf16[256,128]{1,0:T(8,128)(2,1)S(1)}, bf16[16,64,128]{2,1,0:T(8,128)(2,1)}, f32[16,128]{1,0:T(8,128)S(1)}) custom-call(s32[4]{0:T(128)S(1)} %pad_add_fusion.where, s32[16]{0:T(128)S(1)} %copy-done.7, f32[16,2,128]{2,1,0:T(2,128)S(1)} %all-to-all-done.1.second, bf16[16,128]{1,0:T(8,128)(2,1)S(1)} %copy-done.6, ...), custom_call_target="tpu_custom_call" | custom-call | flops 16777216 | bytes 262144 | tf_op jit(solution)/shard_map/pallas_call | solution.py:416
  56.5 6.5 %all-to-all-start.2 = ((bf16[16,64,128]{2,1,0:T(8,128)(2,1)}), bf16[16,64,128]{2,1,0:T(8,128)(2,1)S(1)}, u32[]{:S(2)}, u32[]{:S(2)}) async-start(bf16[16,64,128]{2,1,0:T(8,128)(2,1)} %get-tuple-element.41), calls=%async_computation.2 | async-start | bytes 524288 | tf_op jit(solution)/shard_map/all_to_all | solution.py:307
  63.0 0.0 collective-permute-done.1.got
  63.0 0.7 shard_map.112
  63.6 3.4 %collective-permute-start.2 = (bf16[3,256,128]{2,1,0:T(8,128)(2,1)S(1)}, bf16[3,256,128]{2,1,0:T(8,128)(2,1)S(1)}, u32[]{:S(2)}, u32[]{:S(2)}) collective-permute-start(bf16[3,256,128]{2,1,0:T(8,128)(2,1)S(1)} %get-tuple-element.34), channel_id=1, source_target_pairs={{0,2},{1,3},{2,4},{3,5},{4,6},{5,7},{6,8},{7,9},{8,10},{9,11},{10,... | collective-permute-start | bytes 589832 | tf_op jit(solution)/shard_map/ppermute | solution.py:72
  67.0 3.7 %collective-permute-start.3 = (bf16[2,256,128]{2,1,0:T(8,128)(2,1)S(1)}, bf16[2,256,128]{2,1,0:T(8,128)(2,1)S(1)}, u32[]{:S(2)}, u32[]{:S(2)}) collective-permute-start(bf16[2,256,128]{2,1,0:T(8,128)(2,1)S(1)} %get-tuple-element.35), channel_id=1, source_target_pairs={{0,14},{1,15},{2,0},{3,1},{4,2},{5,3},{6,4},{7,5},{8,6},{9,7},{10,... | collective-permute-start | bytes 393224 | tf_op jit(solution)/shard_map/ppermute | solution.py:72
  70.7 2.1 %collective-permute-start.4 = (bf16[256,128]{1,0:T(8,128)(2,1)S(1)}, bf16[256,128]{1,0:T(8,128)(2,1)S(1)}, u32[]{:S(2)}, u32[]{:S(2)}) collective-permute-start(bf16[256,128]{1,0:T(8,128)(2,1)S(1)} %get-tuple-element.37.share.scaled), channel_id=1, source_target_pairs={{0,16},{1,17},{2,18},{3,19},{4,20},{5,21},{6,22},{7,23},{8,24},{9,... | collective-permute-start | bytes 196616 | tf_op jit(solution)/shard_map/ppermute | solution.py:72
  72.8 5.6 %collective-permute-done.4.other = bf16[256,128]{1,0:T(8,128)(2,1)S(1)} collective-permute-done((bf16[256,128]{1,0:T(8,128)(2,1)S(1)}, bf16[256,128]{1,0:T(8,128)(2,1)S(1)}, u32[]{:S(2)}, u32[]{:S(2)}) %collective-permute-start.4) | collective-permute-done | bytes 65568 | tf_op jit(solution)/shard_map/ppermute | solution.py:72
  78.4 0.0 collective-permute-done.3.down
  78.4 0.1 shard_map.116
  78.5 4.6 %collective-permute-start.5 = (bf16[3,256,128]{2,1,0:T(8,128)(2,1)S(1)}, bf16[3,256,128]{2,1,0:T(8,128)(2,1)S(1)}, u32[]{:S(2)}, u32[]{:S(2)}) collective-permute-start(bf16[3,256,128]{2,1,0:T(8,128)(2,1)S(1)} %get-tuple-element.39), channel_id=1, source_target_pairs={{0,6},{1,7},{2,8},{3,9},{4,10},{5,11},{6,12},{7,13},{8,14},{9,15},... | collective-permute-start | bytes 589832 | tf_op jit(solution)/shard_map/ppermute | solution.py:72
  83.1 4.2 %collective-permute-start.6 = (bf16[3,256,128]{2,1,0:T(8,128)(2,1)S(1)}, bf16[3,256,128]{2,1,0:T(8,128)(2,1)S(1)}, u32[]{:S(2)}, u32[]{:S(2)}) collective-permute-start(bf16[3,256,128]{2,1,0:T(8,128)(2,1)S(1)} %get-tuple-element.40), channel_id=1, source_target_pairs={{0,10},{1,11},{2,12},{3,13},{4,14},{5,15},{6,0},{7,1},{8,2},{9,3},... | collective-permute-start | bytes 589832 | tf_op jit(solution)/shard_map/ppermute | solution.py:72
  87.3 7.1 %collective-permute-done.5.base_a.below = bf16[3,256,128]{2,1,0:T(8,128)(2,1)S(1)} collective-permute-done((bf16[3,256,128]{2,1,0:T(8,128)(2,1)S(1)}, bf16[3,256,128]{2,1,0:T(8,128)(2,1)S(1)}, u32[]{:S(2)}, u32[]{:S(2)}) %collective-permute-start.5) | collective-permute-done | bytes 196640 | tf_op jit(solution)/shard_map/ppermute | solution.py:72
  94.5 0.9 collective-permute-done.6.base_b.above
  95.3 0.1 shard_map.120
  95.4 8.4 %collective-permute-start.8 = (bf16[6,256,128]{2,1,0:T(8,128)(2,1)S(1)}, bf16[6,256,128]{2,1,0:T(8,128)(2,1)S(1)}, u32[]{:S(2)}, u32[]{:S(2)}) collective-permute-start(bf16[6,256,128]{2,1,0:T(8,128)(2,1)S(1)} %get-tuple-element.45.after), channel_id=1, source_target_pairs={{0,2},{1,3},{2,4},{3,5},{4,6},{5,7},{6,8},{7,9},{8,10},{9,11},{10,... | collective-permute-start | bytes 1179656 | tf_op jit(solution)/shard_map/ppermute | solution.py:72
  103.8 0.0 all-to-all-done.2.rank_rows
  103.9 1.9 %collective-permute-start.7 = (bf16[64,128]{1,0:T(8,128)(2,1)S(1)}, bf16[64,128]{1,0:T(8,128)(2,1)S(1)}, u32[]{:S(2)}, u32[]{:S(2)}) collective-permute-start(bf16[64,128]{1,0:T(8,128)(2,1)S(1)} %shard_map.117.ranks), channel_id=1, source_target_pairs={{0,1},{1,0},{2,3},{3,2},{4,5},{5,4},{6,7},{7,6},{8,9},{9,8},{10,11... | collective-permute-start | bytes 49160 | tf_op jit(solution)/shard_map/ppermute | solution.py:72
  105.8 1.1 collective-permute-done.7.got
  107.0 1.6 shard_map.118
  108.5 0.7 copy-done.4
  109.2 5.8 %all-to-all-start.3 = ((bf16[16,16,640]{2,1,0:T(8,128)(2,1)}), bf16[16,16,640]{2,1,0:T(8,128)(2,1)S(1)}, u32[]{:S(2)}, u32[]{:S(2)}) async-start(bf16[16,16,640]{2,1,0:T(8,128)(2,1)} %get-tuple-element.48), calls=%async_computation.3 | async-start | bytes 655360 | tf_op jit(solution)/shard_map/all_to_all | solution.py:307
  114.9 1.9 %collective-permute-start.9 = (bf16[4,256,128]{2,1,0:T(8,128)(2,1)S(1)}, bf16[4,256,128]{2,1,0:T(8,128)(2,1)S(1)}, u32[]{:S(2)}, u32[]{:S(2)}) collective-permute-start(bf16[4,256,128]{2,1,0:T(8,128)(2,1)S(1)} %get-tuple-element.46), channel_id=1, source_target_pairs={{0,14},{1,15},{2,0},{3,1},{4,2},{5,3},{6,4},{7,5},{8,6},{9,7},{10,... | collective-permute-start | bytes 786440 | tf_op jit(solution)/shard_map/ppermute | solution.py:72
  116.8 8.1 %collective-permute-done.9.from_above = bf16[4,256,128]{2,1,0:T(8,128)(2,1)S(1)} collective-permute-done((bf16[4,256,128]{2,1,0:T(8,128)(2,1)S(1)}, bf16[4,256,128]{2,1,0:T(8,128)(2,1)S(1)}, u32[]{:S(2)}, u32[]{:S(2)}) %collective-permute-start.9) | collective-permute-done | bytes 262176 | tf_op jit(solution)/shard_map/ppermute | solution.py:72
  124.9 0.1 shard_map.121.blocks
  125.0 1.9 %collective-permute-start.10 = (bf16[16,256,128]{2,1,0:T(8,128)(2,1)S(1)}, bf16[16,256,128]{2,1,0:T(8,128)(2,1)S(1)}, u32[]{:S(2)}, u32[]{:S(2)}) collective-permute-start(bf16[16,256,128]{2,1,0:T(8,128)(2,1)S(1)} %shard_map.121.blocks), channel_id=1, source_target_pairs={{0,1},{1,0},{2,3},{3,2},{4,5},{5,4},{6,7},{7,6},{8,9},{9,8},{10,11... | collective-permute-start | bytes 3145736 | tf_op jit(solution)/shard_map/ppermute | solution.py:72
  126.9 0.0 copy-start.5
  126.9 0.9 copy-done.5
  127.8 0.7 copy-done.8
  128.5 2.1 %shard_map.119 = (bf16[256,128]{1,0:T(8,128)(2,1)}, bf16[16,128]{1,0:T(8,128)(2,1)S(1)}) custom-call(s32[4]{0:T(128)S(1)} %pad_add_fusion.where, s32[16]{0:T(128)S(1)} %copy-done.8, f32[256,128]{1,0:T(8,128)S(1)} %get-tuple-element.38.base, bf16[3,256,128]{2,1,0:T(8,128)(2,1)S(1)} %collective-permute-done.5.base_a.below, ...), custom_call_target="tpu_custom_call" | custom-call | flops 16777216 | bytes 524288 | tf_op jit(solution)/shard_map/pallas_call | solution.py:504
  130.6 0.8 shard_map.124
  131.4 8.1 %all-to-all-start.4 = ((bf16[16,16,768]{2,1,0:T(8,128)(2,1)}), bf16[16,16,768]{2,1,0:T(8,128)(2,1)S(1)}, u32[]{:S(2)}, u32[]{:S(2)}) async-start(bf16[16,16,768]{2,1,0:T(8,128)(2,1)} %shard_map.124), calls=%async_computation.4 | async-start | bytes 786432 | tf_op jit(solution)/shard_map/all_to_all | solution.py:307
  139.5 3.4 %shard_map.122.rest_8_ = f32[448,256]{1,0:T(8,128)S(1)} custom-call(s32[4]{0:T(128)S(1)} %pad_add_fusion.where, bf16[16,256,128]{2,1,0:T(8,128)(2,1)S(1)} %shard_map.121.blocks, bf16[448,4096]{1,0:T(8,128)(2,1)} %rest_7_.3, bf16[448,4096]{1,0:T(8,128)(2,1)} %rest_7_.3, bf16[448,4096]{1,0:T(8,128)(2,1)} %rest_7_.3, bf16[448,4096]{1,0:T(8,128)(2,1)} %rest_7_.3, ...), custom_call_target="tpu_custom_call" | custom-call | flops 528482304 | bytes 1835008 | tf_op jit(solution)/shard_map/pallas_call | solution.py:551
  142.9 10.0 %all-to-all-done.4.fifth = bf16[16,16,768]{2,1,0:T(8,128)(2,1)S(1)} async-done(((bf16[16,16,768]{2,1,0:T(8,128)(2,1)}), bf16[16,16,768]{2,1,0:T(8,128)(2,1)S(1)}, u32[]{:S(2)}, u32[]{:S(2)}) %all-to-all-start.4) | async-done | bytes 393248 | tf_op jit(solution)/shard_map/all_to_all | solution.py:307
  152.9 0.8 shard_map.125
  153.7 0.0 collective-permute-done.10.blocks
  153.7 3.7 %shard_map.123 = bf16[448,256]{1,0:T(8,128)(2,1)} custom-call(s32[4]{0:T(128)S(1)} %pad_add_fusion.where, bf16[16,256,128]{2,1,0:T(8,128)(2,1)S(1)} %collective-permute-done.10.blocks, bf16[448,4096]{1,0:T(8,128)(2,1)} %rest_7_.3, bf16[448,4096]{1,0:T(8,128)(2,1)} %rest_7_.3, bf16[448,4096]{1,0:T(8,128)(2,1)} %rest_7_.3, bf16[448,4096]{1,0:T(8,128)(2,1)} %rest_7_.3, ...), custom_call_target="tpu_custom_call" | custom-call | flops 469762048 | bytes 1835008 | tf_op jit(solution)/shard_map/pallas_call | solution.py:562
  (18 shorter events, 0.1 us)
Async XLA Ops:
  0.8 37.8 %copy-start.2 = (bf16[16,16,128]{2,1,0:T(8,128)(2,1)S(1)}, bf16[16,16,128]{2,1,0:T(8,128)(2,1)}, u32[]{:S(2)}) copy-start(bf16[16,16,128]{2,1,0:T(8,128)(2,1)} %up.1) | copy-start | bytes 196612
  0.8 47.6 %copy-start = (bf16[16,448,16]{1,2,0:T(8,128)(2,1)S(1)}, bf16[16,448,16]{1,2,0:T(8,128)(2,1)}, u32[]{:S(2)}) copy-start(bf16[16,448,16]{1,2,0:T(8,128)(2,1)} %param.9) | copy-start | bytes 688132
  0.8 47.6 %copy-start.1 = (bf16[256,448]{0,1:T(8,128)(2,1)S(1)}, bf16[256,448]{0,1:T(8,128)(2,1)}, u32[]{:S(2)}) copy-start(bf16[256,448]{0,1:T(8,128)(2,1)} %param.7) | copy-start | bytes 688132
  0.8 47.6 %copy-start.7 = (s32[16]{0:T(128)S(1)}, s32[16]{0:T(128)}, u32[]{:S(2)}) copy-start(s32[16]{0:T(128)} %seg.7) | copy-start | bytes 196
  5.8 48.9 %copy-start.3 = (bf16[256,128]{1,0:T(8,128)(2,1)S(1)}, bf16[256,128]{1,0:T(8,128)(2,1)}, u32[]{:S(2)}) copy-start(bf16[256,128]{1,0:T(8,128)(2,1)} %cotangent.3) | copy-start | bytes 196612
  5.8 48.9 %copy-start.6 = (bf16[16,128]{1,0:T(8,128)(2,1)S(1)}, bf16[16,128]{1,0:T(8,128)(2,1)}, u32[]{:S(2)}) copy-start(bf16[16,128]{1,0:T(8,128)(2,1)} %magnitude.3) | copy-start | bytes 12292
  5.8 4.9 %collective-permute-start = (bf16[16,256,128]{2,1,0:T(8,128)(2,1)}, bf16[16,256,128]{2,1,0:T(8,128)(2,1)S(1)}, u32[]{:S(2)}, u32[]{:S(2)}) collective-permute-start(bf16[16,256,128]{2,1,0:T(8,128)(2,1)} %get-tuple-element.30), channel_id=1, source_target_pairs={{0,1},{1,0},{2,3},{3,2},{4,5},{5,4},{6,7},{7,6},{8,9},{9,8},{10,11... | collective-permute-start | bytes 3145736 | tf_op jit(solution)/shard_map/ppermute | solution.py:72
  11.6 51.4 %collective-permute-start.1 = (bf16[8,256,128]{2,1,0:T(8,128)(2,1)S(1)}, bf16[8,256,128]{2,1,0:T(8,128)(2,1)S(1)}, u32[]{:S(2)}, u32[]{:S(2)}) collective-permute-start(bf16[8,256,128]{2,1,0:T(8,128)(2,1)S(1)} %get-tuple-element.32), channel_id=1, source_target_pairs={{0,16},{1,17},{2,18},{3,19},{4,20},{5,21},{6,22},{7,23},{8,24},{9,... | collective-permute-start | bytes 1572872 | tf_op jit(solution)/shard_map/ppermute | solution.py:72
  39.9 14.8 %all-to-all-start.1 = ((f32[16,2,128]{2,1,0:T(2,128)}), f32[16,2,128]{2,1,0:T(2,128)S(1)}, u32[]{:S(2)}, u32[]{:S(2)}) async-start(f32[16,2,128]{2,1,0:T(2,128)} %shard_map.113), calls=%async_computation.1 | async-start | bytes 32768 | tf_op jit(solution)/shard_map/all_to_all | solution.py:307
  56.5 47.3 %all-to-all-start.2 = ((bf16[16,64,128]{2,1,0:T(8,128)(2,1)}), bf16[16,64,128]{2,1,0:T(8,128)(2,1)S(1)}, u32[]{:S(2)}, u32[]{:S(2)}) async-start(bf16[16,64,128]{2,1,0:T(8,128)(2,1)} %get-tuple-element.41), calls=%async_computation.2 | async-start | bytes 524288 | tf_op jit(solution)/shard_map/all_to_all | solution.py:307
  63.6 14.7 %collective-permute-start.2 = (bf16[3,256,128]{2,1,0:T(8,128)(2,1)S(1)}, bf16[3,256,128]{2,1,0:T(8,128)(2,1)S(1)}, u32[]{:S(2)}, u32[]{:S(2)}) collective-permute-start(bf16[3,256,128]{2,1,0:T(8,128)(2,1)S(1)} %get-tuple-element.34), channel_id=1, source_target_pairs={{0,2},{1,3},{2,4},{3,5},{4,6},{5,7},{6,8},{7,9},{8,10},{9,11},{10,... | collective-permute-start | bytes 589832 | tf_op jit(solution)/shard_map/ppermute | solution.py:72
  67.0 11.3 %collective-permute-start.3 = (bf16[2,256,128]{2,1,0:T(8,128)(2,1)S(1)}, bf16[2,256,128]{2,1,0:T(8,128)(2,1)S(1)}, u32[]{:S(2)}, u32[]{:S(2)}) collective-permute-start(bf16[2,256,128]{2,1,0:T(8,128)(2,1)S(1)} %get-tuple-element.35), channel_id=1, source_target_pairs={{0,14},{1,15},{2,0},{3,1},{4,2},{5,3},{6,4},{7,5},{8,6},{9,7},{10,... | collective-permute-start | bytes 393224 | tf_op jit(solution)/shard_map/ppermute | solution.py:72
  70.7 7.7 %collective-permute-start.4 = (bf16[256,128]{1,0:T(8,128)(2,1)S(1)}, bf16[256,128]{1,0:T(8,128)(2,1)S(1)}, u32[]{:S(2)}, u32[]{:S(2)}) collective-permute-start(bf16[256,128]{1,0:T(8,128)(2,1)S(1)} %get-tuple-element.37.share.scaled), channel_id=1, source_target_pairs={{0,16},{1,17},{2,18},{3,19},{4,20},{5,21},{6,22},{7,23},{8,24},{9,... | collective-permute-start | bytes 196616 | tf_op jit(solution)/shard_map/ppermute | solution.py:72
  78.5 16.0 %collective-permute-start.5 = (bf16[3,256,128]{2,1,0:T(8,128)(2,1)S(1)}, bf16[3,256,128]{2,1,0:T(8,128)(2,1)S(1)}, u32[]{:S(2)}, u32[]{:S(2)}) collective-permute-start(bf16[3,256,128]{2,1,0:T(8,128)(2,1)S(1)} %get-tuple-element.39), channel_id=1, source_target_pairs={{0,6},{1,7},{2,8},{3,9},{4,10},{5,11},{6,12},{7,13},{8,14},{9,15},... | collective-permute-start | bytes 589832 | tf_op jit(solution)/shard_map/ppermute | solution.py:72
  83.1 12.2 %collective-permute-start.6 = (bf16[3,256,128]{2,1,0:T(8,128)(2,1)S(1)}, bf16[3,256,128]{2,1,0:T(8,128)(2,1)S(1)}, u32[]{:S(2)}, u32[]{:S(2)}) collective-permute-start(bf16[3,256,128]{2,1,0:T(8,128)(2,1)S(1)} %get-tuple-element.40), channel_id=1, source_target_pairs={{0,10},{1,11},{2,12},{3,13},{4,14},{5,15},{6,0},{7,1},{8,2},{9,3},... | collective-permute-start | bytes 589832 | tf_op jit(solution)/shard_map/ppermute | solution.py:72
  95.4 29.5 %collective-permute-start.8 = (bf16[6,256,128]{2,1,0:T(8,128)(2,1)S(1)}, bf16[6,256,128]{2,1,0:T(8,128)(2,1)S(1)}, u32[]{:S(2)}, u32[]{:S(2)}) collective-permute-start(bf16[6,256,128]{2,1,0:T(8,128)(2,1)S(1)} %get-tuple-element.45.after), channel_id=1, source_target_pairs={{0,2},{1,3},{2,4},{3,5},{4,6},{5,7},{6,8},{7,9},{8,10},{9,11},{10,... | collective-permute-start | bytes 1179656 | tf_op jit(solution)/shard_map/ppermute | solution.py:72
  103.9 3.1 %collective-permute-start.7 = (bf16[64,128]{1,0:T(8,128)(2,1)S(1)}, bf16[64,128]{1,0:T(8,128)(2,1)S(1)}, u32[]{:S(2)}, u32[]{:S(2)}) collective-permute-start(bf16[64,128]{1,0:T(8,128)(2,1)S(1)} %shard_map.117.ranks), channel_id=1, source_target_pairs={{0,1},{1,0},{2,3},{3,2},{4,5},{5,4},{6,7},{7,6},{8,9},{9,8},{10,11... | collective-permute-start | bytes 49160 | tf_op jit(solution)/shard_map/ppermute | solution.py:72
  108.5 0.7 copy-start.4
  109.2 21.4 %all-to-all-start.3 = ((bf16[16,16,640]{2,1,0:T(8,128)(2,1)}), bf16[16,16,640]{2,1,0:T(8,128)(2,1)S(1)}, u32[]{:S(2)}, u32[]{:S(2)}) async-start(bf16[16,16,640]{2,1,0:T(8,128)(2,1)} %get-tuple-element.48), calls=%async_computation.3 | async-start | bytes 655360 | tf_op jit(solution)/shard_map/all_to_all | solution.py:307
  114.9 10.0 %collective-permute-start.9 = (bf16[4,256,128]{2,1,0:T(8,128)(2,1)S(1)}, bf16[4,256,128]{2,1,0:T(8,128)(2,1)S(1)}, u32[]{:S(2)}, u32[]{:S(2)}) collective-permute-start(bf16[4,256,128]{2,1,0:T(8,128)(2,1)S(1)} %get-tuple-element.46), channel_id=1, source_target_pairs={{0,14},{1,15},{2,0},{3,1},{4,2},{5,3},{6,4},{7,5},{8,6},{9,7},{10,... | collective-permute-start | bytes 786440 | tf_op jit(solution)/shard_map/ppermute | solution.py:72
  125.0 28.7 %collective-permute-start.10 = (bf16[16,256,128]{2,1,0:T(8,128)(2,1)S(1)}, bf16[16,256,128]{2,1,0:T(8,128)(2,1)S(1)}, u32[]{:S(2)}, u32[]{:S(2)}) collective-permute-start(bf16[16,256,128]{2,1,0:T(8,128)(2,1)S(1)} %shard_map.121.blocks), channel_id=1, source_target_pairs={{0,1},{1,0},{2,3},{3,2},{4,5},{5,4},{6,7},{7,6},{8,9},{9,8},{10,11... | collective-permute-start | bytes 3145736 | tf_op jit(solution)/shard_map/ppermute | solution.py:72
  126.9 0.9 copy-start.5
  127.8 0.7 copy-start.8
  131.4 21.5 %all-to-all-start.4 = ((bf16[16,16,768]{2,1,0:T(8,128)(2,1)}), bf16[16,16,768]{2,1,0:T(8,128)(2,1)S(1)}, u32[]{:S(2)}, u32[]{:S(2)}) async-start(bf16[16,16,768]{2,1,0:T(8,128)(2,1)} %shard_map.124), calls=%async_computation.4 | async-start | bytes 786432 | tf_op jit(solution)/shard_map/all_to_all | solution.py:307

commit v8 on v7

--- a/solution.py
+++ b/solution.py
@@ -142,15 +142,15 @@
             give[at] = jnp.where(swap, even, odd).astype(BF16)
 
 
-def low_kernel(where, seg, tokens, down, low):
-    marks = bounds(seg, seg.shape[0], where[0] * tokens.shape[1])
-    spread = dot(down[...], tokens[...], 1, 0)
-    low[...] = packed(picked(spread, marks)).astype(BF16)
-
-
-def halves_kernel(where, keep_a, got_a, keep_b, got_b, keep, give):
+def halves_kernel(where, seg, tokens, down, keep_a, got_a, keep_b, got_b, low, keep, give):
     keep[...] = (keep_a[...].astype(F32) + got_a[...].astype(F32)).astype(BF16)
     give[...] = (keep_b[...].astype(F32) + got_b[...].astype(F32)).astype(BF16)
+
+    @pl.when(pl.program_id(0) == 0)
+    def _():
+        marks = bounds(seg, seg.shape[0], where[0] * tokens.shape[1])
+        spread = dot(down[...], tokens[...], 1, 0)
+        low[...] = packed(picked(spread, marks)).astype(BF16)
 
 
 def squares_kernel(where, head, up, second):
@@ -163,7 +163,8 @@
     tiled = jnp.concatenate([up[0]] * (LANES // rank), axis=0)
     high = spread.astype(BF16)
     rest = (spread - high.astype(F32)).astype(BF16)
-    gram_up = dot(high, tiled, 1, 0) + dot(rest, tiled, 1, 0)
+    gram_up = dot(jnp.concatenate([high, rest], axis=0), tiled, 1, 0)
+    gram_up = gram_up[:rank] + gram_up[rank:]
     mine = jnp.sum(factor * (2.0 * total[:rank] + gram_up), axis=0, keepdims=True)
     both = jnp.concatenate([mine, total[rank : rank + 1]], axis=0)
     second[...] = jnp.broadcast_to(both[None], second.shape)
@@ -354,29 +355,20 @@
     )(where, in_hbm(turned), in_hbm(base_weight), in_hbm(down_rows))
     head = exchange(head, "tensor")
     got = shift(give, core_pairs)
-    low = call(
-        low_kernel,
-        shaped(2 * rank, width),
+    half = size // 4
+    mine = pl.BlockSpec((half // 2, count, width), lambda i, s, t: (s[2] * 2 + i, 0, 0))
+    theirs = pl.BlockSpec((half // 2, count, width), lambda i, s, t: ((1 - s[2]) * 2 + i, 0, 0))
+    out = pl.BlockSpec((half // 2, count, width), lambda i, s, t: (i, 0, 0))
+    low, keep, give = call(
+        halves_kernel,
+        [shaped(2 * rank, width), shaped(zs, count, width), shaped(zs, count, width)],
         scalars=2,
-        grid=(1,),
-        in_specs=[whole(own_rows, count), whole(wide, own_rows)],
-        out_specs=whole(2 * rank, width),
+        grid=(2,),
+        in_specs=[whole(own_rows, count), whole(wide, own_rows), mine, mine, theirs, theirs],
+        out_specs=[whole(2 * rank, width), out, out],
         flops=2 * count * own_rows * wide,
-        moved=4 * count * own_rows,
-    )(where, seg_lengths, turned, down_flat)
-
-    mine = pl.BlockSpec((2, count, width), lambda i, s: (s[2] * (zs // 2) + i, 0, 0))
-    theirs = pl.BlockSpec((2, count, width), lambda i, s: ((1 - s[2]) * (zs // 2) + i, 0, 0))
-    out = pl.BlockSpec((2, count, width), lambda i, s: (i, 0, 0))
-    keep, give = call(
-        halves_kernel,
-        [shaped(zs, count, width)] * 2,
-        scalars=1,
-        grid=(zs // 2,),
-        in_specs=[mine, mine, theirs, theirs],
-        out_specs=[out, out],
         moved=12 * zs * count * width,
-    )(where, keep, got, keep, got)
+    )(where, seg_lengths, turned, down_flat, keep, got, keep, got)
     got = shift(give, hi_pairs)
 
     def along_z(step):

time: 158 us -> 158 us (level)
  blocking collectives: 23.7 us -> 38.3 us
  starting transfers between devices: 66.3 us -> 57.8 us
  waiting for transfers between devices: 41.1 us -> 35.6 us
    all_to_all x1 -> x2, blocking collectives: 23.7 us -> 38.3 us  [exchange(): lax.all_to_all(blocks, axis, 0, 0, tiled=True, axis_index_groups=groups)]
    all_to_all x4 -> x3, starting transfers between devices: 28.8 us -> 20.4 us  [exchange(): lax.all_to_all(blocks, axis, 0, 0, tiled=True, axis_index_groups=groups)]
    all_to_all x4 -> x3, waiting for transfers between devices: 15.5 us -> 9.99 us  [exchange(): lax.all_to_all(blocks, axis, 0, 0, tiled=True, axis_index_groups=groups)]
  transfers between devices with their start and end apart: 15 -> 14, of which waited for: 8 -> 7; matrix products, arithmetic and copies ran while one was open for 0% -> 0% of each run, Pallas kernels for 9% -> 8%
where the time goes in v8:
time: 158 us; the launch traced here: 157 us
  starting transfers between devices  57.8 us (37%)
  blocking collectives  38.3 us (24%)
  waiting for transfers between devices  35.6 us (23%)
  Pallas kernels  21.8 us (14%)
  local copies, waits for them, and re-layouts  2.24 us (1%)
    all_to_all x2, blocking collectives, exchange(): lax.all_to_all(blocks, axis, 0, 0, tiled=True, axis_index_groups=groups)  38.3 us
    ppermute x11, starting transfers between devices, shift(): return lax.ppermute(block, 'tensor', pairs)  37.5 us
    ppermute x11, waiting for transfers between devices, shift(): return lax.ppermute(block, 'tensor', pairs)  25.6 us
    all_to_all x3, starting transfers between devices, exchange(): lax.all_to_all(blocks, axis, 0, 0, tiled=True, axis_index_groups=groups)  20.4 us
    all_to_all x3, waiting for transfers between devices, exchange(): lax.all_to_all(blocks, axis, 0, 0, tiled=True, axis_index_groups=groups)  9.99 us
    pallas_call x1, Pallas kernels, local(): call(first_kernel, [shaped(size, HEAD, width), shaped(size // 2, count, w...  5.02 us
    pallas_call x1, Pallas kernels, local(): call(tokens_rest_kernel, shaped(own_rows, count), scalars=1, grid=(zs //...  3.7 us
    pallas_call x1, Pallas kernels, local(): call(tokens_kernel, shaped(own_rows, count, dtype=F32), scalars=1, grid=(...  3.37 us
  transfers between devices with their start and end apart: 14, of which 7 were waited for; matrix products, arithmetic and copies ran while one was open for 0% of the time, Pallas kernels for 8%

profile of v8, /device:TPU:14, one launch (start us, length us, event | category | flops | bytes accessed | tf_op | source)
XLA Modules:
  0.0 156.8 jit_solution(17109364768710279031)
XLA Ops:
  0.6 0.0 copy-start
  0.6 0.0 copy-start.1
  0.7 0.0 copy-start.7
  0.7 0.1 pad_add_fusion.where
  0.8 5.0 %shard_map.110 = (bf16[32,24,128]{2,1,0:T(8,128)(2,1)S(1)}, bf16[16,256,128]{2,1,0:T(8,128)(2,1)S(1)}, bf16[16,256,128]{2,1,0:T(8,128)(2,1)}) custom-call(s32[4]{0:T(128)S(1)} %pad_add_fusion.where, bf16[448,256]{1,0:T(8,128)(2,1)} %bitcast.14, bf16[448,4096]{1,0:T(8,128)(2,1)} %rest_7_.3, bf16[16,16,448]{2,1,0:T(8,128)(2,1)} %bitcast.11), custom_call_target="tpu_custom_call" | custom-call | flops 939524096 | bytes 3670016 | tf_op jit(solution)/shard_map/pallas_call | solution.py:333
  5.8 2.0 %collective-permute-start = (bf16[16,256,128]{2,1,0:T(8,128)(2,1)}, bf16[16,256,128]{2,1,0:T(8,128)(2,1)S(1)}, u32[]{:S(2)}, u32[]{:S(2)}) collective-permute-start(bf16[16,256,128]{2,1,0:T(8,128)(2,1)} %get-tuple-element.31), channel_id=1, source_target_pairs={{0,1},{1,0},{2,3},{3,2},{4,5},{5,4},{6,7},{7,6},{8,9},{9,8},{10,11... | collective-permute-start | bytes 3145736 | tf_op jit(solution)/shard_map/ppermute | solution.py:72
  7.9 2.8 %collective-permute-done.got_a.got_b = bf16[16,256,128]{2,1,0:T(8,128)(2,1)S(1)} collective-permute-done((bf16[16,256,128]{2,1,0:T(8,128)(2,1)}, bf16[16,256,128]{2,1,0:T(8,128)(2,1)S(1)}, u32[]{:S(2)}, u32[]{:S(2)}) %collective-permute-start) | collective-permute-done | bytes 1048608 | tf_op jit(solution)/shard_map/ppermute | solution.py:72
  10.7 1.1 shard_map.111
  11.8 3.3 %collective-permute-start.1 = (bf16[8,256,128]{2,1,0:T(8,128)(2,1)S(1)}, bf16[8,256,128]{2,1,0:T(8,128)(2,1)S(1)}, u32[]{:S(2)}, u32[]{:S(2)}) collective-permute-start(bf16[8,256,128]{2,1,0:T(8,128)(2,1)S(1)} %get-tuple-element.33), channel_id=1, source_target_pairs={{0,16},{1,17},{2,18},{3,19},{4,20},{5,21},{6,22},{7,23},{8,24},{9,... | collective-permute-start | bytes 1572872 | tf_op jit(solution)/shard_map/ppermute | solution.py:72
  15.1 23.7 %all_to_all.25.head = bf16[32,24,128]{2,1,0:T(8,128)(2,1)S(1)} all-to-all(bf16[32,24,128]{2,1,0:T(8,128)(2,1)S(1)} %get-tuple-element.37), channel_id=1, replica_groups=mesh['dp'=16,'tensor'=32] {'tensor'}, dimensions={0} | all-to-all | bytes 393216 | tf_op jit(solution)/shard_map/all_to_all | solution.py:308
  38.8 0.7 shard_map.113
  39.5 14.6 %all_to_all.26.second = f32[16,2,128]{2,1,0:T(2,128)S(1)} all-to-all(f32[16,2,128]{2,1,0:T(2,128)S(1)} %shard_map.113), channel_id=1, replica_groups=mesh['dp'=16,'tensor'=32] {'dp'}, dimensions={0} | all-to-all | bytes 32768 | tf_op jit(solution)/shard_map/all_to_all | solution.py:308
  54.1 1.8 %shard_map.114 = (bf16[256,128]{1,0:T(8,128)(2,1)S(1)}, bf16[16,64,128]{2,1,0:T(8,128)(2,1)}, f32[16,128]{1,0:T(8,128)S(1)}) custom-call(s32[4]{0:T(128)S(1)} %pad_add_fusion.where, s32[16]{0:T(128)S(1)} %copy-done.7, f32[16,2,128]{2,1,0:T(2,128)S(1)} %all_to_all.26.second, bf16[16,128]{1,0:T(8,128)(2,1)S(1)} %copy-done.6, bf16[256,128]{1,0:T(8,128)(2,1)S(1)} %copy-done.3, ...), custom_call_target="tpu_custom_call" | custom-call | flops 16777216 | bytes 262144 | tf_op jit(solution)/shard_map/pallas_call | solution.py:408
  55.9 6.4 %all-to-all-start.2 = ((bf16[16,64,128]{2,1,0:T(8,128)(2,1)}), bf16[16,64,128]{2,1,0:T(8,128)(2,1)S(1)}, u32[]{:S(2)}, u32[]{:S(2)}) async-start(bf16[16,64,128]{2,1,0:T(8,128)(2,1)} %get-tuple-element.43), calls=%async_computation.2 | async-start | bytes 524288 | tf_op jit(solution)/shard_map/all_to_all | solution.py:308
  62.4 0.0 collective-permute-done.1.got
  62.4 0.7 shard_map.112
  63.0 3.4 %collective-permute-start.2 = (bf16[3,256,128]{2,1,0:T(8,128)(2,1)S(1)}, bf16[3,256,128]{2,1,0:T(8,128)(2,1)S(1)}, u32[]{:S(2)}, u32[]{:S(2)}) collective-permute-start(bf16[3,256,128]{2,1,0:T(8,128)(2,1)S(1)} %get-tuple-element.35), channel_id=1, source_target_pairs={{0,2},{1,3},{2,4},{3,5},{4,6},{5,7},{6,8},{7,9},{8,10},{9,11},{10,... | collective-permute-start | bytes 589832 | tf_op jit(solution)/shard_map/ppermute | solution.py:72
  66.4 3.7 %collective-permute-start.3 = (bf16[2,256,128]{2,1,0:T(8,128)(2,1)S(1)}, bf16[2,256,128]{2,1,0:T(8,128)(2,1)S(1)}, u32[]{:S(2)}, u32[]{:S(2)}) collective-permute-start(bf16[2,256,128]{2,1,0:T(8,128)(2,1)S(1)} %get-tuple-element.36), channel_id=1, source_target_pairs={{0,14},{1,15},{2,0},{3,1},{4,2},{5,3},{6,4},{7,5},{8,6},{9,7},{10,... | collective-permute-start | bytes 393224 | tf_op jit(solution)/shard_map/ppermute | solution.py:72
  70.1 2.1 %collective-permute-start.4 = (bf16[256,128]{1,0:T(8,128)(2,1)S(1)}, bf16[256,128]{1,0:T(8,128)(2,1)S(1)}, u32[]{:S(2)}, u32[]{:S(2)}) collective-permute-start(bf16[256,128]{1,0:T(8,128)(2,1)S(1)} %get-tuple-element.39.share.scaled), channel_id=1, source_target_pairs={{0,16},{1,17},{2,18},{3,19},{4,20},{5,21},{6,22},{7,23},{8,24},{9,... | collective-permute-start | bytes 196616 | tf_op jit(solution)/shard_map/ppermute | solution.py:72
  72.2 5.6 %collective-permute-done.4.other = bf16[256,128]{1,0:T(8,128)(2,1)S(1)} collective-permute-done((bf16[256,128]{1,0:T(8,128)(2,1)S(1)}, bf16[256,128]{1,0:T(8,128)(2,1)S(1)}, u32[]{:S(2)}, u32[]{:S(2)}) %collective-permute-start.4) | collective-permute-done | bytes 65568 | tf_op jit(solution)/shard_map/ppermute | solution.py:72
  77.8 0.0 collective-permute-done.3.down
  77.8 0.0 collective-permute-done.2.up
  77.8 0.1 shard_map.115
  77.9 4.6 %collective-permute-start.5 = (bf16[3,256,128]{2,1,0:T(8,128)(2,1)S(1)}, bf16[3,256,128]{2,1,0:T(8,128)(2,1)S(1)}, u32[]{:S(2)}, u32[]{:S(2)}) collective-permute-start(bf16[3,256,128]{2,1,0:T(8,128)(2,1)S(1)} %get-tuple-element.41), channel_id=1, source_target_pairs={{0,6},{1,7},{2,8},{3,9},{4,10},{5,11},{6,12},{7,13},{8,14},{9,15},... | collective-permute-start | bytes 589832 | tf_op jit(solution)/shard_map/ppermute | solution.py:72
  82.5 4.2 %collective-permute-start.6 = (bf16[3,256,128]{2,1,0:T(8,128)(2,1)S(1)}, bf16[3,256,128]{2,1,0:T(8,128)(2,1)S(1)}, u32[]{:S(2)}, u32[]{:S(2)}) collective-permute-start(bf16[3,256,128]{2,1,0:T(8,128)(2,1)S(1)} %get-tuple-element.42), channel_id=1, source_target_pairs={{0,10},{1,11},{2,12},{3,13},{4,14},{5,15},{6,0},{7,1},{8,2},{9,3},... | collective-permute-start | bytes 589832 | tf_op jit(solution)/shard_map/ppermute | solution.py:72
  86.7 7.1 %collective-permute-done.5.base_a.below = bf16[3,256,128]{2,1,0:T(8,128)(2,1)S(1)} collective-permute-done((bf16[3,256,128]{2,1,0:T(8,128)(2,1)S(1)}, bf16[3,256,128]{2,1,0:T(8,128)(2,1)S(1)}, u32[]{:S(2)}, u32[]{:S(2)}) %collective-permute-start.5) | collective-permute-done | bytes 196640 | tf_op jit(solution)/shard_map/ppermute | solution.py:72
  93.9 0.9 collective-permute-done.6.base_b.above
  94.7 0.1 shard_map.119
  94.8 8.4 %collective-permute-start.8 = (bf16[6,256,128]{2,1,0:T(8,128)(2,1)S(1)}, bf16[6,256,128]{2,1,0:T(8,128)(2,1)S(1)}, u32[]{:S(2)}, u32[]{:S(2)}) collective-permute-start(bf16[6,256,128]{2,1,0:T(8,128)(2,1)S(1)} %get-tuple-element.47.after), channel_id=1, source_target_pairs={{0,2},{1,3},{2,4},{3,5},{4,6},{5,7},{6,8},{7,9},{8,10},{9,11},{10,... | collective-permute-start | bytes 1179656 | tf_op jit(solution)/shard_map/ppermute | solution.py:72
  103.3 1.9 %collective-permute-start.7 = (bf16[64,128]{1,0:T(8,128)(2,1)S(1)}, bf16[64,128]{1,0:T(8,128)(2,1)S(1)}, u32[]{:S(2)}, u32[]{:S(2)}) collective-permute-start(bf16[64,128]{1,0:T(8,128)(2,1)S(1)} %shard_map.116.ranks), channel_id=1, source_target_pairs={{0,1},{1,0},{2,3},{3,2},{4,5},{5,4},{6,7},{7,6},{8,9},{9,8},{10,11... | collective-permute-start | bytes 49160 | tf_op jit(solution)/shard_map/ppermute | solution.py:72
  105.2 1.1 collective-permute-done.7.got
  106.4 1.6 shard_map.117
  107.9 0.7 copy-done.4
  108.6 5.8 %all-to-all-start.3 = ((bf16[16,16,640]{2,1,0:T(8,128)(2,1)}), bf16[16,16,640]{2,1,0:T(8,128)(2,1)S(1)}, u32[]{:S(2)}, u32[]{:S(2)}) async-start(bf16[16,16,640]{2,1,0:T(8,128)(2,1)} %get-tuple-element.50), calls=%async_computation.3 | async-start | bytes 655360 | tf_op jit(solution)/shard_map/all_to_all | solution.py:308
  114.3 1.9 %collective-permute-start.9 = (bf16[4,256,128]{2,1,0:T(8,128)(2,1)S(1)}, bf16[4,256,128]{2,1,0:T(8,128)(2,1)S(1)}, u32[]{:S(2)}, u32[]{:S(2)}) collective-permute-start(bf16[4,256,128]{2,1,0:T(8,128)(2,1)S(1)} %get-tuple-element.48), channel_id=1, source_target_pairs={{0,14},{1,15},{2,0},{3,1},{4,2},{5,3},{6,4},{7,5},{8,6},{9,7},{10,... | collective-permute-start | bytes 786440 | tf_op jit(solution)/shard_map/ppermute | solution.py:72
  116.3 8.1 %collective-permute-done.9.from_above = bf16[4,256,128]{2,1,0:T(8,128)(2,1)S(1)} collective-permute-done((bf16[4,256,128]{2,1,0:T(8,128)(2,1)S(1)}, bf16[4,256,128]{2,1,0:T(8,128)(2,1)S(1)}, u32[]{:S(2)}, u32[]{:S(2)}) %collective-permute-start.9) | collective-permute-done | bytes 262176 | tf_op jit(solution)/shard_map/ppermute | solution.py:72
  124.3 0.1 shard_map.120.blocks
  124.4 1.9 %collective-permute-start.10 = (bf16[16,256,128]{2,1,0:T(8,128)(2,1)S(1)}, bf16[16,256,128]{2,1,0:T(8,128)(2,1)S(1)}, u32[]{:S(2)}, u32[]{:S(2)}) collective-permute-start(bf16[16,256,128]{2,1,0:T(8,128)(2,1)S(1)} %shard_map.120.blocks), channel_id=1, source_target_pairs={{0,1},{1,0},{2,3},{3,2},{4,5},{5,4},{6,7},{7,6},{8,9},{9,8},{10,11... | collective-permute-start | bytes 3145736 | tf_op jit(solution)/shard_map/ppermute | solution.py:72
  126.3 0.0 copy-start.5
  126.3 0.9 copy-done.5
  127.2 0.7 copy-done.8
  127.9 2.1 %shard_map.118 = (bf16[256,128]{1,0:T(8,128)(2,1)}, bf16[16,128]{1,0:T(8,128)(2,1)S(1)}) custom-call(s32[4]{0:T(128)S(1)} %pad_add_fusion.where, s32[16]{0:T(128)S(1)} %copy-done.8, f32[256,128]{1,0:T(8,128)S(1)} %get-tuple-element.40.base, bf16[3,256,128]{2,1,0:T(8,128)(2,1)S(1)} %collective-permute-done.5.base_a.below, ...), custom_call_target="tpu_custom_call" | custom-call | flops 16777216 | bytes 524288 | tf_op jit(solution)/shard_map/pallas_call | solution.py:496
  130.0 0.8 shard_map.123
  130.8 8.1 %all-to-all-start.4 = ((bf16[16,16,768]{2,1,0:T(8,128)(2,1)}), bf16[16,16,768]{2,1,0:T(8,128)(2,1)S(1)}, u32[]{:S(2)}, u32[]{:S(2)}) async-start(bf16[16,16,768]{2,1,0:T(8,128)(2,1)} %shard_map.123), calls=%async_computation.4 | async-start | bytes 786432 | tf_op jit(solution)/shard_map/all_to_all | solution.py:308
  138.9 3.4 %shard_map.121.rest_8_ = f32[448,256]{1,0:T(8,128)S(1)} custom-call(s32[4]{0:T(128)S(1)} %pad_add_fusion.where, bf16[16,256,128]{2,1,0:T(8,128)(2,1)S(1)} %shard_map.120.blocks, bf16[448,4096]{1,0:T(8,128)(2,1)} %rest_7_.3, bf16[448,4096]{1,0:T(8,128)(2,1)} %rest_7_.3, bf16[448,4096]{1,0:T(8,128)(2,1)} %rest_7_.3, bf16[448,4096]{1,0:T(8,128)(2,1)} %rest_7_.3, ...), custom_call_target="tpu_custom_call" | custom-call | flops 528482304 | bytes 1835008 | tf_op jit(solution)/shard_map/pallas_call | solution.py:543
  142.3 10.0 %all-to-all-done.4.fifth = bf16[16,16,768]{2,1,0:T(8,128)(2,1)S(1)} async-done(((bf16[16,16,768]{2,1,0:T(8,128)(2,1)}), bf16[16,16,768]{2,1,0:T(8,128)(2,1)S(1)}, u32[]{:S(2)}, u32[]{:S(2)}) %all-to-all-start.4) | async-done | bytes 393248 | tf_op jit(solution)/shard_map/all_to_all | solution.py:308
  152.3 0.8 shard_map.124
  153.1 3.7 %shard_map.122 = bf16[448,256]{1,0:T(8,128)(2,1)} custom-call(s32[4]{0:T(128)S(1)} %pad_add_fusion.where, bf16[16,256,128]{2,1,0:T(8,128)(2,1)S(1)} %collective-permute-done.10.blocks, bf16[448,4096]{1,0:T(8,128)(2,1)} %rest_7_.3, bf16[448,4096]{1,0:T(8,128)(2,1)} %rest_7_.3, bf16[448,4096]{1,0:T(8,128)(2,1)} %rest_7_.3, bf16[448,4096]{1,0:T(8,128)(2,1)} %rest_7_.3, ...), custom_call_target="tpu_custom_call" | custom-call | flops 469762048 | bytes 1835008 | tf_op jit(solution)/shard_map/pallas_call | solution.py:554
  (16 shorter events, 0.1 us)
Async XLA Ops:
  0.6 10.1 %copy-start = (bf16[16,448,16]{1,2,0:T(8,128)(2,1)S(1)}, bf16[16,448,16]{1,2,0:T(8,128)(2,1)}, u32[]{:S(2)}) copy-start(bf16[16,448,16]{1,2,0:T(8,128)(2,1)} %param.9) | copy-start | bytes 688132
  0.6 10.1 %copy-start.1 = (bf16[256,448]{0,1:T(8,128)(2,1)S(1)}, bf16[256,448]{0,1:T(8,128)(2,1)}, u32[]{:S(2)}) copy-start(bf16[256,448]{0,1:T(8,128)(2,1)} %param.7) | copy-start | bytes 688132
  0.7 10.0 %copy-start.7 = (s32[16]{0:T(128)S(1)}, s32[16]{0:T(128)}, u32[]{:S(2)}) copy-start(s32[16]{0:T(128)} %seg.7) | copy-start | bytes 196
  0.8 38.0 %copy-start.2 = (bf16[16,16,128]{2,1,0:T(8,128)(2,1)S(1)}, bf16[16,16,128]{2,1,0:T(8,128)(2,1)}, u32[]{:S(2)}) copy-start(bf16[16,16,128]{2,1,0:T(8,128)(2,1)} %up.1) | copy-start | bytes 196612
  5.8 48.3 %copy-start.3 = (bf16[256,128]{1,0:T(8,128)(2,1)S(1)}, bf16[256,128]{1,0:T(8,128)(2,1)}, u32[]{:S(2)}) copy-start(bf16[256,128]{1,0:T(8,128)(2,1)} %cotangent.3) | copy-start | bytes 196612
  5.8 48.3 %copy-start.6 = (bf16[16,128]{1,0:T(8,128)(2,1)S(1)}, bf16[16,128]{1,0:T(8,128)(2,1)}, u32[]{:S(2)}) copy-start(bf16[16,128]{1,0:T(8,128)(2,1)} %magnitude.3) | copy-start | bytes 12292
  5.8 4.9 %collective-permute-start = (bf16[16,256,128]{2,1,0:T(8,128)(2,1)}, bf16[16,256,128]{2,1,0:T(8,128)(2,1)S(1)}, u32[]{:S(2)}, u32[]{:S(2)}) collective-permute-start(bf16[16,256,128]{2,1,0:T(8,128)(2,1)} %get-tuple-element.31), channel_id=1, source_target_pairs={{0,1},{1,0},{2,3},{3,2},{4,5},{5,4},{6,7},{7,6},{8,9},{9,8},{10,11... | collective-permute-start | bytes 3145736 | tf_op jit(solution)/shard_map/ppermute | solution.py:72
  11.8 50.6 %collective-permute-start.1 = (bf16[8,256,128]{2,1,0:T(8,128)(2,1)S(1)}, bf16[8,256,128]{2,1,0:T(8,128)(2,1)S(1)}, u32[]{:S(2)}, u32[]{:S(2)}) collective-permute-start(bf16[8,256,128]{2,1,0:T(8,128)(2,1)S(1)} %get-tuple-element.33), channel_id=1, source_target_pairs={{0,16},{1,17},{2,18},{3,19},{4,20},{5,21},{6,22},{7,23},{8,24},{9,... | collective-permute-start | bytes 1572872 | tf_op jit(solution)/shard_map/ppermute | solution.py:72
  55.9 47.3 %all-to-all-start.2 = ((bf16[16,64,128]{2,1,0:T(8,128)(2,1)}), bf16[16,64,128]{2,1,0:T(8,128)(2,1)S(1)}, u32[]{:S(2)}, u32[]{:S(2)}) async-start(bf16[16,64,128]{2,1,0:T(8,128)(2,1)} %get-tuple-element.43), calls=%async_computation.2 | async-start | bytes 524288 | tf_op jit(solution)/shard_map/all_to_all | solution.py:308
  63.0 14.7 %collective-permute-start.2 = (bf16[3,256,128]{2,1,0:T(8,128)(2,1)S(1)}, bf16[3,256,128]{2,1,0:T(8,128)(2,1)S(1)}, u32[]{:S(2)}, u32[]{:S(2)}) collective-permute-start(bf16[3,256,128]{2,1,0:T(8,128)(2,1)S(1)} %get-tuple-element.35), channel_id=1, source_target_pairs={{0,2},{1,3},{2,4},{3,5},{4,6},{5,7},{6,8},{7,9},{8,10},{9,11},{10,... | collective-permute-start | bytes 589832 | tf_op jit(solution)/shard_map/ppermute | solution.py:72
  66.4 11.3 %collective-permute-start.3 = (bf16[2,256,128]{2,1,0:T(8,128)(2,1)S(1)}, bf16[2,256,128]{2,1,0:T(8,128)(2,1)S(1)}, u32[]{:S(2)}, u32[]{:S(2)}) collective-permute-start(bf16[2,256,128]{2,1,0:T(8,128)(2,1)S(1)} %get-tuple-element.36), channel_id=1, source_target_pairs={{0,14},{1,15},{2,0},{3,1},{4,2},{5,3},{6,4},{7,5},{8,6},{9,7},{10,... | collective-permute-start | bytes 393224 | tf_op jit(solution)/shard_map/ppermute | solution.py:72
  70.1 7.7 %collective-permute-start.4 = (bf16[256,128]{1,0:T(8,128)(2,1)S(1)}, bf16[256,128]{1,0:T(8,128)(2,1)S(1)}, u32[]{:S(2)}, u32[]{:S(2)}) collective-permute-start(bf16[256,128]{1,0:T(8,128)(2,1)S(1)} %get-tuple-element.39.share.scaled), channel_id=1, source_target_pairs={{0,16},{1,17},{2,18},{3,19},{4,20},{5,21},{6,22},{7,23},{8,24},{9,... | collective-permute-start | bytes 196616 | tf_op jit(solution)/shard_map/ppermute | solution.py:72
  77.9 16.0 %collective-permute-start.5 = (bf16[3,256,128]{2,1,0:T(8,128)(2,1)S(1)}, bf16[3,256,128]{2,1,0:T(8,128)(2,1)S(1)}, u32[]{:S(2)}, u32[]{:S(2)}) collective-permute-start(bf16[3,256,128]{2,1,0:T(8,128)(2,1)S(1)} %get-tuple-element.41), channel_id=1, source_target_pairs={{0,6},{1,7},{2,8},{3,9},{4,10},{5,11},{6,12},{7,13},{8,14},{9,15},... | collective-permute-start | bytes 589832 | tf_op jit(solution)/shard_map/ppermute | solution.py:72
  82.5 12.2 %collective-permute-start.6 = (bf16[3,256,128]{2,1,0:T(8,128)(2,1)S(1)}, bf16[3,256,128]{2,1,0:T(8,128)(2,1)S(1)}, u32[]{:S(2)}, u32[]{:S(2)}) collective-permute-start(bf16[3,256,128]{2,1,0:T(8,128)(2,1)S(1)} %get-tuple-element.42), channel_id=1, source_target_pairs={{0,10},{1,11},{2,12},{3,13},{4,14},{5,15},{6,0},{7,1},{8,2},{9,3},... | collective-permute-start | bytes 589832 | tf_op jit(solution)/shard_map/ppermute | solution.py:72
  94.8 29.5 %collective-permute-start.8 = (bf16[6,256,128]{2,1,0:T(8,128)(2,1)S(1)}, bf16[6,256,128]{2,1,0:T(8,128)(2,1)S(1)}, u32[]{:S(2)}, u32[]{:S(2)}) collective-permute-start(bf16[6,256,128]{2,1,0:T(8,128)(2,1)S(1)} %get-tuple-element.47.after), channel_id=1, source_target_pairs={{0,2},{1,3},{2,4},{3,5},{4,6},{5,7},{6,8},{7,9},{8,10},{9,11},{10,... | collective-permute-start | bytes 1179656 | tf_op jit(solution)/shard_map/ppermute | solution.py:72
  103.3 3.1 %collective-permute-start.7 = (bf16[64,128]{1,0:T(8,128)(2,1)S(1)}, bf16[64,128]{1,0:T(8,128)(2,1)S(1)}, u32[]{:S(2)}, u32[]{:S(2)}) collective-permute-start(bf16[64,128]{1,0:T(8,128)(2,1)S(1)} %shard_map.116.ranks), channel_id=1, source_target_pairs={{0,1},{1,0},{2,3},{3,2},{4,5},{5,4},{6,7},{7,6},{8,9},{9,8},{10,11... | collective-permute-start | bytes 49160 | tf_op jit(solution)/shard_map/ppermute | solution.py:72
  107.9 0.7 copy-start.4
  108.6 21.4 %all-to-all-start.3 = ((bf16[16,16,640]{2,1,0:T(8,128)(2,1)}), bf16[16,16,640]{2,1,0:T(8,128)(2,1)S(1)}, u32[]{:S(2)}, u32[]{:S(2)}) async-start(bf16[16,16,640]{2,1,0:T(8,128)(2,1)} %get-tuple-element.50), calls=%async_computation.3 | async-start | bytes 655360 | tf_op jit(solution)/shard_map/all_to_all | solution.py:308
  114.3 10.0 %collective-permute-start.9 = (bf16[4,256,128]{2,1,0:T(8,128)(2,1)S(1)}, bf16[4,256,128]{2,1,0:T(8,128)(2,1)S(1)}, u32[]{:S(2)}, u32[]{:S(2)}) collective-permute-start(bf16[4,256,128]{2,1,0:T(8,128)(2,1)S(1)} %get-tuple-element.48), channel_id=1, source_target_pairs={{0,14},{1,15},{2,0},{3,1},{4,2},{5,3},{6,4},{7,5},{8,6},{9,7},{10,... | collective-permute-start | bytes 786440 | tf_op jit(solution)/shard_map/ppermute | solution.py:72
  124.4 28.7 %collective-permute-start.10 = (bf16[16,256,128]{2,1,0:T(8,128)(2,1)S(1)}, bf16[16,256,128]{2,1,0:T(8,128)(2,1)S(1)}, u32[]{:S(2)}, u32[]{:S(2)}) collective-permute-start(bf16[16,256,128]{2,1,0:T(8,128)(2,1)S(1)} %shard_map.120.blocks), channel_id=1, source_target_pairs={{0,1},{1,0},{2,3},{3,2},{4,5},{5,4},{6,7},{7,6},{8,9},{9,8},{10,11... | collective-permute-start | bytes 3145736 | tf_op jit(solution)/shard_map/ppermute | solution.py:72
  126.3 0.9 copy-start.5
  127.2 0.7 copy-start.8
  130.8 21.5 %all-to-all-start.4 = ((bf16[16,16,768]{2,1,0:T(8,128)(2,1)}), bf16[16,16,768]{2,1,0:T(8,128)(2,1)S(1)}, u32[]{:S(2)}, u32[]{:S(2)}) async-start(bf16[16,16,768]{2,1,0:T(8,128)(2,1)} %shard_map.123), calls=%async_computation.4 | async-start | bytes 786432 | tf_op jit(solution)/shard_map/all_to_all | solution.py:308

commit v9 on v8

--- a/solution.py
+++ b/solution.py
@@ -232,10 +232,13 @@
     back_wide[...] = back
     down_part = dot(back, tokens[...], 1, 1).astype(BF16)
     up_part = dot(low, scaled[...], 1, 0).astype(BF16)
-    pad = jnp.zeros((rank, -own_rows % LANES), BF16)
     for a in range(adapters):
-        lines = slice(a * rank, (a + 1) * rank)
-        fourth[a] = jnp.concatenate([down_part[lines], pad, up_part[lines]], axis=1)
+        lines = down_part[a * rank : (a + 1) * rank]
+        pieces = [lines[:, k : k + LANES] for k in range(0, own_rows - LANES + 1, LANES)]
+        rest = lines[:, own_rows // LANES * LANES :]
+        pieces.append(up_part[a * rank : (a + 1) * rank])
+        pieces.append(jnp.concatenate([rest[: rank // 2], rest[rank // 2 :]], axis=1))
+        fourth[a] = jnp.concatenate(pieces, axis=0)
 
 
 def hidden_kernel(where, seg, base, base_a, base_b, low, up, norms, magnitude, cotangent,
@@ -257,17 +260,23 @@
 
 def total_kernel(arrived, mag, fifth):
     total = jnp.sum(arrived[...].astype(F32), axis=0).astype(BF16)
-    both = jnp.concatenate([total, mag[...]], axis=1)
+    edge = total.shape[0] - mag.shape[0] // 2
+    both = jnp.concatenate([total[:edge], mag[...], total[edge:]], axis=0)
     fifth[...] = jnp.broadcast_to(both[None], fifth.shape)
 
 
 def final_kernel(fifth, norms, grad_down, grad_up, grad_magnitude):
-    own_rows = grad_down.shape[2]
-    edge = own_rows + -own_rows % LANES
-    grad_down[...] = fifth[:, :, :own_rows]
-    grad_up[...] = fifth[:, :, edge : edge + LANES].astype(F32)
-    total = jnp.sum(fifth[:, :, edge + LANES :].astype(F32), axis=0)
+    _, rank, own_rows = grad_down.shape
+    tiles = own_rows // LANES
+    for k in range(tiles):
+        grad_down[:, :, k * LANES : (k + 1) * LANES] = fifth[:, k * rank : (k + 1) * rank]
+    up = tiles * rank
+    grad_up[...] = fifth[:, up : up + rank].astype(F32)
+    total = jnp.sum(fifth[:, up + rank : up + 2 * rank].astype(F32), axis=0)
     grad_magnitude[...] = total / norms[...]
+    rest = fifth[:, up + 2 * rank :]
+    half = own_rows - tiles * LANES
+    grad_down[:, :, tiles * LANES :] = jnp.concatenate([rest[:, :, :half], rest[:, :, half:]], 1)
 
 
 def tokens_kernel(where, blocks, *rest):
@@ -472,11 +481,10 @@
     )(after, from_below, from_above)
     gather_b = shift(gather_a, core_pairs)
 
-    edge = own_rows + -own_rows % LANES
-    blocks = edge + width
+    lines = own_rows // LANES * rank + rank + rank // 2
     fourth, low_wide, back_wide = call(
         grads_kernel,
-        [shaped(adapters, rank, blocks), shaped(wide, count), shaped(wide, count)],
+        [shaped(adapters, lines, width), shaped(wide, count), shaped(wide, count)],
         scalars=2,
         grid=(1,),
         in_specs=[
@@ -486,9 +494,9 @@
             whole(wide, width),
             whole(own_rows, count),
         ],
-        out_specs=[whole(adapters, rank, blocks), whole(wide, count), whole(wide, count)],
+        out_specs=[whole(adapters, lines, width), whole(wide, count), whole(wide, count)],
         flops=2 * count * wide * (own_rows + width),
-        moved=4 * adapters * rank * blocks,
+        moved=4 * adapters * lines * width,
     )(where, seg_lengths, ranks, other_ranks, share, up_own, turned)
     fourth = exchange(fourth, "dp")
 
@@ -516,11 +524,11 @@
 
     fifth = call(
         total_kernel,
-        shaped(adapters, rank, blocks + width),
-        grid=(1,),
-        in_specs=[whole(adapters, rank, blocks), whole(adapters, width)],
-        out_specs=whole(adapters, rank, blocks + width),
-        moved=4 * adapters * rank * blocks,
+        shaped(adapters, lines + rank, width),
+        grid=(1,),
+        in_specs=[whole(adapters, lines, width), whole(adapters, width)],
+        out_specs=whole(adapters, lines + rank, width),
+        moved=4 * adapters * lines * width,
     )(fourth, mag)
     fifth = exchange(fifth, "dp")
 
@@ -571,13 +579,13 @@
             shaped(adapters, width, dtype=F32),
         ],
         grid=(1,),
-        in_specs=[whole(adapters, rank, blocks + width), whole(adapters, width)],
+        in_specs=[whole(adapters, lines + rank, width), whole(adapters, width)],
         out_specs=[
             whole(adapters, rank, own_rows),
             whole(adapters, rank, width),
             whole(adapters, width),
         ],
-        moved=4 * adapters * rank * blocks,
+        moved=4 * adapters * lines * width,
     )(fifth, norms)
     return (projected, grad_tokens.T, jnp.transpose(grad_down, (0, 2, 1)), grad_up, grad_magnitude)
 

time: 158 us -> 148 us (0.937)
  blocking collectives: 38.3 us -> 0 us
  starting transfers between devices: 57.8 us -> 80.8 us
  waiting for transfers between devices: 35.6 us -> 40.7 us
    all_to_all x2 -> x0, blocking collectives: 38.3 us -> none  [exchange(): lax.all_to_all(blocks, axis, 0, 0, tiled=True, axis_index_groups=groups)]
    all_to_all x3 -> x5, starting transfers between devices: 20.4 us -> 41.7 us  [exchange(): lax.all_to_all(blocks, axis, 0, 0, tiled=True, axis_index_groups=groups)]
    all_to_all x3 -> x5, waiting for transfers between devices: 9.99 us -> 20.4 us  [exchange(): lax.all_to_all(blocks, axis, 0, 0, tiled=True, axis_index_groups=groups)]
    ppermute x11, waiting for transfers between devices: 25.6 us -> 20.3 us  [shift(): return lax.ppermute(block, 'tensor', pairs)]
    ppermute x11, starting transfers between devices: 37.5 us -> 39.1 us  [shift(): return lax.ppermute(block, 'tensor', pairs)]
  transfers between devices with their start and end apart: 14 -> 16, of which waited for: 7 -> 10; matrix products, arithmetic and copies ran while one was open for 0% -> 0% of each run, Pallas kernels for 8% -> 9%
where the time goes in v9:
time: 148 us; the launch traced here: 147 us
  starting transfers between devices  80.8 us (55%)
  waiting for transfers between devices  40.7 us (28%)
  Pallas kernels  22.5 us (15%)
  local copies, waits for them, and re-layouts  1.58 us (1%)
    all_to_all x5, starting transfers between devices, exchange(): lax.all_to_all(blocks, axis, 0, 0, tiled=True, axis_index_groups=groups)  41.7 us
    ppermute x11, starting transfers between devices, shift(): return lax.ppermute(block, 'tensor', pairs)  39.1 us
    all_to_all x5, waiting for transfers between devices, exchange(): lax.all_to_all(blocks, axis, 0, 0, tiled=True, axis_index_groups=groups)  20.4 us
    ppermute x11, waiting for transfers between devices, shift(): return lax.ppermute(block, 'tensor', pairs)  20.3 us
    pallas_call x1, Pallas kernels, local(): call(first_kernel, [shaped(size, HEAD, width), shaped(size // 2, count, w...  5.04 us
    pallas_call x1, Pallas kernels, local(): call(tokens_rest_kernel, shaped(own_rows, count), scalars=1, grid=(zs //...  3.69 us
    pallas_call x1, Pallas kernels, local(): call(tokens_kernel, shaped(own_rows, count, dtype=F32), scalars=1, grid=(...  3.36 us
  transfers between devices with their start and end apart: 16, of which 10 were waited for; matrix products, arithmetic and copies ran while one was open for 0% of the time, Pallas kernels for 9%

profile of v9, /device:TPU:14, one launch (start us, length us, event | category | flops | bytes accessed | tf_op | source)
XLA Modules:
  0.0 146.6 jit_solution(3330863718844926183)
XLA Ops:
  0.6 0.0 copy-start
  0.6 0.0 copy-start.1
  0.7 0.1 pad_add_fusion.where
  0.8 5.0 %shard_map.110 = (bf16[32,24,128]{2,1,0:T(8,128)(2,1)}, bf16[16,256,128]{2,1,0:T(8,128)(2,1)S(1)}, bf16[16,256,128]{2,1,0:T(8,128)(2,1)}) custom-call(s32[4]{0:T(128)S(1)} %pad_add_fusion.where, bf16[448,256]{1,0:T(8,128)(2,1)} %bitcast.14, bf16[448,4096]{1,0:T(8,128)(2,1)} %rest_7_.3, bf16[16,16,448]{2,1,0:T(8,128)(2,1)} %bitcast.11), custom_call_target="tpu_custom_call" | custom-call | flops 939524096 | bytes 3670016 | tf_op jit(solution)/shard_map/pallas_call | solution.py:342
  5.8 0.0 copy-start.6
  5.8 2.1 %collective-permute-start = (bf16[16,256,128]{2,1,0:T(8,128)(2,1)}, bf16[16,256,128]{2,1,0:T(8,128)(2,1)S(1)}, u32[]{:S(2)}, u32[]{:S(2)}) collective-permute-start(bf16[16,256,128]{2,1,0:T(8,128)(2,1)} %get-tuple-element.31), channel_id=1, source_target_pairs={{0,1},{1,0},{2,3},{3,2},{4,5},{5,4},{6,7},{7,6},{8,9},{9,8},{10,11... | collective-permute-start | bytes 3145736 | tf_op jit(solution)/shard_map/ppermute | solution.py:72
  7.9 2.8 %collective-permute-done.got_a.got_b = bf16[16,256,128]{2,1,0:T(8,128)(2,1)S(1)} collective-permute-done((bf16[16,256,128]{2,1,0:T(8,128)(2,1)}, bf16[16,256,128]{2,1,0:T(8,128)(2,1)S(1)}, u32[]{:S(2)}, u32[]{:S(2)}) %collective-permute-start) | collective-permute-done | bytes 1048608 | tf_op jit(solution)/shard_map/ppermute | solution.py:72
  10.7 1.1 shard_map.111
  11.8 3.3 %collective-permute-start.1 = (bf16[8,256,128]{2,1,0:T(8,128)(2,1)S(1)}, bf16[8,256,128]{2,1,0:T(8,128)(2,1)S(1)}, u32[]{:S(2)}, u32[]{:S(2)}) collective-permute-start(bf16[8,256,128]{2,1,0:T(8,128)(2,1)S(1)} %get-tuple-element.33), channel_id=1, source_target_pairs={{0,16},{1,17},{2,18},{3,19},{4,20},{5,21},{6,22},{7,23},{8,24},{9,... | collective-permute-start | bytes 1572872 | tf_op jit(solution)/shard_map/ppermute | solution.py:72
  15.1 13.5 %all-to-all-start = ((bf16[32,24,128]{2,1,0:T(8,128)(2,1)}), bf16[32,24,128]{2,1,0:T(8,128)(2,1)S(1)}, u32[]{:S(2)}, u32[]{:S(2)}) async-start(bf16[32,24,128]{2,1,0:T(8,128)(2,1)} %get-tuple-element.37), calls=%async_computation | async-start | bytes 393216 | tf_op jit(solution)/shard_map/all_to_all | solution.py:317
  28.6 0.6 collective-permute-done.1.got
  29.2 0.7 shard_map.112
  29.9 4.3 %collective-permute-start.2 = (bf16[3,256,128]{2,1,0:T(8,128)(2,1)S(1)}, bf16[3,256,128]{2,1,0:T(8,128)(2,1)S(1)}, u32[]{:S(2)}, u32[]{:S(2)}) collective-permute-start(bf16[3,256,128]{2,1,0:T(8,128)(2,1)S(1)} %get-tuple-element.35), channel_id=1, source_target_pairs={{0,2},{1,3},{2,4},{3,5},{4,6},{5,7},{6,8},{7,9},{8,10},{9,11},{10,... | collective-permute-start | bytes 589832 | tf_op jit(solution)/shard_map/ppermute | solution.py:72
  34.1 4.9 %all-to-all-done.head = bf16[32,24,128]{2,1,0:T(8,128)(2,1)S(1)} async-done(((bf16[32,24,128]{2,1,0:T(8,128)(2,1)}), bf16[32,24,128]{2,1,0:T(8,128)(2,1)S(1)}, u32[]{:S(2)}, u32[]{:S(2)}) %all-to-all-start) | async-done | bytes 196640 | tf_op jit(solution)/shard_map/all_to_all | solution.py:317
  39.0 1.3 shard_map.113
  40.4 8.5 %all-to-all-start.1 = ((f32[16,2,128]{2,1,0:T(2,128)}), f32[16,2,128]{2,1,0:T(2,128)S(1)}, u32[]{:S(2)}, u32[]{:S(2)}) async-start(f32[16,2,128]{2,1,0:T(2,128)} %shard_map.113), calls=%async_computation.1 | async-start | bytes 32768 | tf_op jit(solution)/shard_map/all_to_all | solution.py:317
  48.8 5.7 %collective-permute-start.3 = (bf16[2,256,128]{2,1,0:T(8,128)(2,1)S(1)}, bf16[2,256,128]{2,1,0:T(8,128)(2,1)S(1)}, u32[]{:S(2)}, u32[]{:S(2)}) collective-permute-start(bf16[2,256,128]{2,1,0:T(8,128)(2,1)S(1)} %get-tuple-element.36), channel_id=1, source_target_pairs={{0,14},{1,15},{2,0},{3,1},{4,2},{5,3},{6,4},{7,5},{8,6},{9,7},{10,... | collective-permute-start | bytes 393224 | tf_op jit(solution)/shard_map/ppermute | solution.py:72
  54.5 0.7 all-to-all-done.1.second
  55.2 1.8 %shard_map.114 = (bf16[256,128]{1,0:T(8,128)(2,1)S(1)}, bf16[16,64,128]{2,1,0:T(8,128)(2,1)}, f32[16,128]{1,0:T(8,128)S(1)}) custom-call(s32[4]{0:T(128)S(1)} %pad_add_fusion.where, s32[16]{0:T(128)S(1)} %copy-done.7, f32[16,2,128]{2,1,0:T(2,128)S(1)} %all-to-all-done.1.second, bf16[16,128]{1,0:T(8,128)(2,1)S(1)} %copy-done.6, ...), custom_call_target="tpu_custom_call" | custom-call | flops 16777216 | bytes 262144 | tf_op jit(solution)/shard_map/pallas_call | solution.py:417
  57.0 9.5 %all-to-all-start.2 = ((bf16[16,64,128]{2,1,0:T(8,128)(2,1)}), bf16[16,64,128]{2,1,0:T(8,128)(2,1)S(1)}, u32[]{:S(2)}, u32[]{:S(2)}) async-start(bf16[16,64,128]{2,1,0:T(8,128)(2,1)} %get-tuple-element.43), calls=%async_computation.2 | async-start | bytes 524288 | tf_op jit(solution)/shard_map/all_to_all | solution.py:317
  66.5 2.0 %collective-permute-start.4 = (bf16[256,128]{1,0:T(8,128)(2,1)S(1)}, bf16[256,128]{1,0:T(8,128)(2,1)S(1)}, u32[]{:S(2)}, u32[]{:S(2)}) collective-permute-start(bf16[256,128]{1,0:T(8,128)(2,1)S(1)} %get-tuple-element.39.share.scaled), channel_id=1, source_target_pairs={{0,16},{1,17},{2,18},{3,19},{4,20},{5,21},{6,22},{7,23},{8,24},{9,... | collective-permute-start | bytes 196616 | tf_op jit(solution)/shard_map/ppermute | solution.py:72
  68.5 6.0 %collective-permute-done.4.other = bf16[256,128]{1,0:T(8,128)(2,1)S(1)} collective-permute-done((bf16[256,128]{1,0:T(8,128)(2,1)S(1)}, bf16[256,128]{1,0:T(8,128)(2,1)S(1)}, u32[]{:S(2)}, u32[]{:S(2)}) %collective-permute-start.4) | collective-permute-done | bytes 65568 | tf_op jit(solution)/shard_map/ppermute | solution.py:72
  74.5 0.1 shard_map.115
  74.6 4.8 %collective-permute-start.5 = (bf16[3,256,128]{2,1,0:T(8,128)(2,1)S(1)}, bf16[3,256,128]{2,1,0:T(8,128)(2,1)S(1)}, u32[]{:S(2)}, u32[]{:S(2)}) collective-permute-start(bf16[3,256,128]{2,1,0:T(8,128)(2,1)S(1)} %get-tuple-element.41), channel_id=1, source_target_pairs={{0,6},{1,7},{2,8},{3,9},{4,10},{5,11},{6,12},{7,13},{8,14},{9,15},... | collective-permute-start | bytes 589832 | tf_op jit(solution)/shard_map/ppermute | solution.py:72
  79.4 4.0 %collective-permute-start.6 = (bf16[3,256,128]{2,1,0:T(8,128)(2,1)S(1)}, bf16[3,256,128]{2,1,0:T(8,128)(2,1)S(1)}, u32[]{:S(2)}, u32[]{:S(2)}) collective-permute-start(bf16[3,256,128]{2,1,0:T(8,128)(2,1)S(1)} %get-tuple-element.42), channel_id=1, source_target_pairs={{0,10},{1,11},{2,12},{3,13},{4,14},{5,15},{6,0},{7,1},{8,2},{9,3},... | collective-permute-start | bytes 589832 | tf_op jit(solution)/shard_map/ppermute | solution.py:72
  83.4 5.7 %collective-permute-done.5.base_a.below = bf16[3,256,128]{2,1,0:T(8,128)(2,1)S(1)} collective-permute-done((bf16[3,256,128]{2,1,0:T(8,128)(2,1)S(1)}, bf16[3,256,128]{2,1,0:T(8,128)(2,1)S(1)}, u32[]{:S(2)}, u32[]{:S(2)}) %collective-permute-start.5) | collective-permute-done | bytes 196640 | tf_op jit(solution)/shard_map/ppermute | solution.py:72
  89.1 4.1 %collective-permute-done.6.base_b.above = bf16[3,256,128]{2,1,0:T(8,128)(2,1)S(1)} collective-permute-done((bf16[3,256,128]{2,1,0:T(8,128)(2,1)S(1)}, bf16[3,256,128]{2,1,0:T(8,128)(2,1)S(1)}, u32[]{:S(2)}, u32[]{:S(2)}) %collective-permute-start.6) | collective-permute-done | bytes 196640 | tf_op jit(solution)/shard_map/ppermute | solution.py:72
  93.2 0.1 shard_map.119
  93.3 7.2 %collective-permute-start.8 = (bf16[6,256,128]{2,1,0:T(8,128)(2,1)S(1)}, bf16[6,256,128]{2,1,0:T(8,128)(2,1)S(1)}, u32[]{:S(2)}, u32[]{:S(2)}) collective-permute-start(bf16[6,256,128]{2,1,0:T(8,128)(2,1)S(1)} %get-tuple-element.47.after), channel_id=1, source_target_pairs={{0,2},{1,3},{2,4},{3,5},{4,6},{5,7},{6,8},{7,9},{8,10},{9,11},{10,... | collective-permute-start | bytes 1179656 | tf_op jit(solution)/shard_map/ppermute | solution.py:72
  100.4 1.9 %collective-permute-start.9 = (bf16[4,256,128]{2,1,0:T(8,128)(2,1)S(1)}, bf16[4,256,128]{2,1,0:T(8,128)(2,1)S(1)}, u32[]{:S(2)}, u32[]{:S(2)}) collective-permute-start(bf16[4,256,128]{2,1,0:T(8,128)(2,1)S(1)} %get-tuple-element.48), channel_id=1, source_target_pairs={{0,14},{1,15},{2,0},{3,1},{4,2},{5,3},{6,4},{7,5},{8,6},{9,7},{10,... | collective-permute-start | bytes 786440 | tf_op jit(solution)/shard_map/ppermute | solution.py:72
  102.4 0.0 all-to-all-done.2.rank_rows
  102.4 1.9 %collective-permute-start.7 = (bf16[64,128]{1,0:T(8,128)(2,1)S(1)}, bf16[64,128]{1,0:T(8,128)(2,1)S(1)}, u32[]{:S(2)}, u32[]{:S(2)}) collective-permute-start(bf16[64,128]{1,0:T(8,128)(2,1)S(1)} %shard_map.116.ranks), channel_id=1, source_target_pairs={{0,1},{1,0},{2,3},{3,2},{4,5},{5,4},{6,7},{7,6},{8,9},{9,8},{10,11... | collective-permute-start | bytes 49160 | tf_op jit(solution)/shard_map/ppermute | solution.py:72
  104.3 1.1 collective-permute-done.7.got
  105.5 1.6 %shard_map.117 = (bf16[16,72,128]{2,1,0:T(8,128)(2,1)}, bf16[256,256]{1,0:T(8,128)(2,1)S(1)}, bf16[256,256]{1,0:T(8,128)(2,1)S(1)}) custom-call(s32[4]{0:T(128)S(1)} %pad_add_fusion.where, s32[16]{0:T(128)S(1)} %copy-done.7, bf16[64,128]{1,0:T(8,128)(2,1)S(1)} %shard_map.116.ranks, bf16[64,128]{1,0:T(8,128)(2,1)S(1)} %collective-permute-done.7.got, ...), custom_call_target="tpu_custom_call" | custom-call | flops 75497472 | bytes 589824 | tf_op jit(solution)/shard_map/pallas_call | solution.py:485
  107.1 0.7 copy-done.4
  107.8 5.7 %all-to-all-start.3 = ((bf16[16,72,128]{2,1,0:T(8,128)(2,1)}), bf16[16,72,128]{2,1,0:T(8,128)(2,1)S(1)}, u32[]{:S(2)}, u32[]{:S(2)}) async-start(bf16[16,72,128]{2,1,0:T(8,128)(2,1)} %get-tuple-element.50), calls=%async_computation.3 | async-start | bytes 589824 | tf_op jit(solution)/shard_map/all_to_all | solution.py:317
  113.5 0.1 shard_map.120.blocks
  113.5 1.9 %collective-permute-start.10 = (bf16[16,256,128]{2,1,0:T(8,128)(2,1)S(1)}, bf16[16,256,128]{2,1,0:T(8,128)(2,1)S(1)}, u32[]{:S(2)}, u32[]{:S(2)}) collective-permute-start(bf16[16,256,128]{2,1,0:T(8,128)(2,1)S(1)} %shard_map.120.blocks), channel_id=1, source_target_pairs={{0,1},{1,0},{2,3},{3,2},{4,5},{5,4},{6,7},{7,6},{8,9},{9,8},{10,11... | collective-permute-start | bytes 3145736 | tf_op jit(solution)/shard_map/ppermute | solution.py:72
  115.5 0.0 copy-start.5
  115.5 0.9 copy-done.5
  116.4 2.1 %shard_map.118 = (bf16[256,128]{1,0:T(8,128)(2,1)}, bf16[16,128]{1,0:T(8,128)(2,1)S(1)}) custom-call(s32[4]{0:T(128)S(1)} %pad_add_fusion.where, s32[16]{0:T(128)S(1)} %copy-done.7, f32[256,128]{1,0:T(8,128)S(1)} %get-tuple-element.40.base, bf16[3,256,128]{2,1,0:T(8,128)(2,1)S(1)} %collective-permute-done.5.base_a.below, ...), custom_call_target="tpu_custom_call" | custom-call | flops 16777216 | bytes 524288 | tf_op jit(solution)/shard_map/pallas_call | solution.py:504
  118.5 6.2 %all-to-all-done.3.arrived = bf16[16,72,128]{2,1,0:T(8,128)(2,1)S(1)} async-done(((bf16[16,72,128]{2,1,0:T(8,128)(2,1)}), bf16[16,72,128]{2,1,0:T(8,128)(2,1)S(1)}, u32[]{:S(2)}, u32[]{:S(2)}) %all-to-all-start.3) | async-done | bytes 294944 | tf_op jit(solution)/shard_map/all_to_all | solution.py:317
  124.7 0.8 shard_map.123
  125.5 4.6 %all-to-all-start.4 = ((bf16[16,88,128]{2,1,0:T(8,128)(2,1)}), bf16[16,88,128]{2,1,0:T(8,128)(2,1)S(1)}, u32[]{:S(2)}, u32[]{:S(2)}) async-start(bf16[16,88,128]{2,1,0:T(8,128)(2,1)} %shard_map.123), calls=%async_computation.4 | async-start | bytes 720896 | tf_op jit(solution)/shard_map/all_to_all | solution.py:317
  130.1 3.4 %shard_map.121.rest_8_ = f32[448,256]{1,0:T(8,128)S(1)} custom-call(s32[4]{0:T(128)S(1)} %pad_add_fusion.where, bf16[16,256,128]{2,1,0:T(8,128)(2,1)S(1)} %shard_map.120.blocks, bf16[448,4096]{1,0:T(8,128)(2,1)} %rest_7_.3, bf16[448,4096]{1,0:T(8,128)(2,1)} %rest_7_.3, bf16[448,4096]{1,0:T(8,128)(2,1)} %rest_7_.3, bf16[448,4096]{1,0:T(8,128)(2,1)} %rest_7_.3, ...), custom_call_target="tpu_custom_call" | custom-call | flops 528482304 | bytes 1835008 | tf_op jit(solution)/shard_map/pallas_call | solution.py:551
  133.5 8.6 %all-to-all-done.4.fifth = bf16[16,88,128]{2,1,0:T(8,128)(2,1)S(1)} async-done(((bf16[16,88,128]{2,1,0:T(8,128)(2,1)}), bf16[16,88,128]{2,1,0:T(8,128)(2,1)S(1)}, u32[]{:S(2)}, u32[]{:S(2)}) %all-to-all-start.4) | async-done | bytes 360480 | tf_op jit(solution)/shard_map/all_to_all | solution.py:317
  142.1 0.8 shard_map.124
  142.9 3.7 %shard_map.122 = bf16[448,256]{1,0:T(8,128)(2,1)} custom-call(s32[4]{0:T(128)S(1)} %pad_add_fusion.where, bf16[16,256,128]{2,1,0:T(8,128)(2,1)S(1)} %collective-permute-done.10.blocks, bf16[448,4096]{1,0:T(8,128)(2,1)} %rest_7_.3, bf16[448,4096]{1,0:T(8,128)(2,1)} %rest_7_.3, bf16[448,4096]{1,0:T(8,128)(2,1)} %rest_7_.3, bf16[448,4096]{1,0:T(8,128)(2,1)} %rest_7_.3, ...), custom_call_target="tpu_custom_call" | custom-call | flops 469762048 | bytes 1835008 | tf_op jit(solution)/shard_map/pallas_call | solution.py:562
  (16 shorter events, 0.1 us)
Async XLA Ops:
  0.6 10.1 %copy-start = (bf16[16,448,16]{1,2,0:T(8,128)(2,1)S(1)}, bf16[16,448,16]{1,2,0:T(8,128)(2,1)}, u32[]{:S(2)}) copy-start(bf16[16,448,16]{1,2,0:T(8,128)(2,1)} %param.9) | copy-start | bytes 688132
  0.6 10.1 %copy-start.1 = (bf16[256,448]{0,1:T(8,128)(2,1)S(1)}, bf16[256,448]{0,1:T(8,128)(2,1)}, u32[]{:S(2)}) copy-start(bf16[256,448]{0,1:T(8,128)(2,1)} %param.7) | copy-start | bytes 688132
  0.7 10.1 %copy-start.7 = (s32[16]{0:T(128)S(1)}, s32[16]{0:T(128)}, u32[]{:S(2)}) copy-start(s32[16]{0:T(128)} %seg.7) | copy-start | bytes 196
  5.8 33.2 %copy-start.2 = (bf16[16,16,128]{2,1,0:T(8,128)(2,1)S(1)}, bf16[16,16,128]{2,1,0:T(8,128)(2,1)}, u32[]{:S(2)}) copy-start(bf16[16,16,128]{2,1,0:T(8,128)(2,1)} %up.1) | copy-start | bytes 196612
  5.8 49.3 %copy-start.3 = (bf16[256,128]{1,0:T(8,128)(2,1)S(1)}, bf16[256,128]{1,0:T(8,128)(2,1)}, u32[]{:S(2)}) copy-start(bf16[256,128]{1,0:T(8,128)(2,1)} %cotangent.3) | copy-start | bytes 196612
  5.8 49.3 %copy-start.6 = (bf16[16,128]{1,0:T(8,128)(2,1)S(1)}, bf16[16,128]{1,0:T(8,128)(2,1)}, u32[]{:S(2)}) copy-start(bf16[16,128]{1,0:T(8,128)(2,1)} %magnitude.3) | copy-start | bytes 12292
  5.8 4.9 %collective-permute-start = (bf16[16,256,128]{2,1,0:T(8,128)(2,1)}, bf16[16,256,128]{2,1,0:T(8,128)(2,1)S(1)}, u32[]{:S(2)}, u32[]{:S(2)}) collective-permute-start(bf16[16,256,128]{2,1,0:T(8,128)(2,1)} %get-tuple-element.31), channel_id=1, source_target_pairs={{0,1},{1,0},{2,3},{3,2},{4,5},{5,4},{6,7},{7,6},{8,9},{9,8},{10,11... | collective-permute-start | bytes 3145736 | tf_op jit(solution)/shard_map/ppermute | solution.py:72
  11.8 17.4 %collective-permute-start.1 = (bf16[8,256,128]{2,1,0:T(8,128)(2,1)S(1)}, bf16[8,256,128]{2,1,0:T(8,128)(2,1)S(1)}, u32[]{:S(2)}, u32[]{:S(2)}) collective-permute-start(bf16[8,256,128]{2,1,0:T(8,128)(2,1)S(1)} %get-tuple-element.33), channel_id=1, source_target_pairs={{0,16},{1,17},{2,18},{3,19},{4,20},{5,21},{6,22},{7,23},{8,24},{9,... | collective-permute-start | bytes 1572872 | tf_op jit(solution)/shard_map/ppermute | solution.py:72
  15.1 23.9 %all-to-all-start = ((bf16[32,24,128]{2,1,0:T(8,128)(2,1)}), bf16[32,24,128]{2,1,0:T(8,128)(2,1)S(1)}, u32[]{:S(2)}, u32[]{:S(2)}) async-start(bf16[32,24,128]{2,1,0:T(8,128)(2,1)} %get-tuple-element.37), calls=%async_computation | async-start | bytes 393216 | tf_op jit(solution)/shard_map/all_to_all | solution.py:317
  29.9 44.6 %collective-permute-start.2 = (bf16[3,256,128]{2,1,0:T(8,128)(2,1)S(1)}, bf16[3,256,128]{2,1,0:T(8,128)(2,1)S(1)}, u32[]{:S(2)}, u32[]{:S(2)}) collective-permute-start(bf16[3,256,128]{2,1,0:T(8,128)(2,1)S(1)} %get-tuple-element.35), channel_id=1, source_target_pairs={{0,2},{1,3},{2,4},{3,5},{4,6},{5,7},{6,8},{7,9},{8,10},{9,11},{10,... | collective-permute-start | bytes 589832 | tf_op jit(solution)/shard_map/ppermute | solution.py:72
  40.4 14.8 %all-to-all-start.1 = ((f32[16,2,128]{2,1,0:T(2,128)}), f32[16,2,128]{2,1,0:T(2,128)S(1)}, u32[]{:S(2)}, u32[]{:S(2)}) async-start(f32[16,2,128]{2,1,0:T(2,128)} %shard_map.113), calls=%async_computation.1 | async-start | bytes 32768 | tf_op jit(solution)/shard_map/all_to_all | solution.py:317
  48.8 25.6 %collective-permute-start.3 = (bf16[2,256,128]{2,1,0:T(8,128)(2,1)S(1)}, bf16[2,256,128]{2,1,0:T(8,128)(2,1)S(1)}, u32[]{:S(2)}, u32[]{:S(2)}) collective-permute-start(bf16[2,256,128]{2,1,0:T(8,128)(2,1)S(1)} %get-tuple-element.36), channel_id=1, source_target_pairs={{0,14},{1,15},{2,0},{3,1},{4,2},{5,3},{6,4},{7,5},{8,6},{9,7},{10,... | collective-permute-start | bytes 393224 | tf_op jit(solution)/shard_map/ppermute | solution.py:72
  57.0 45.4 %all-to-all-start.2 = ((bf16[16,64,128]{2,1,0:T(8,128)(2,1)}), bf16[16,64,128]{2,1,0:T(8,128)(2,1)S(1)}, u32[]{:S(2)}, u32[]{:S(2)}) async-start(bf16[16,64,128]{2,1,0:T(8,128)(2,1)} %get-tuple-element.43), calls=%async_computation.2 | async-start | bytes 524288 | tf_op jit(solution)/shard_map/all_to_all | solution.py:317
  66.5 8.0 %collective-permute-start.4 = (bf16[256,128]{1,0:T(8,128)(2,1)S(1)}, bf16[256,128]{1,0:T(8,128)(2,1)S(1)}, u32[]{:S(2)}, u32[]{:S(2)}) collective-permute-start(bf16[256,128]{1,0:T(8,128)(2,1)S(1)} %get-tuple-element.39.share.scaled), channel_id=1, source_target_pairs={{0,16},{1,17},{2,18},{3,19},{4,20},{5,21},{6,22},{7,23},{8,24},{9,... | collective-permute-start | bytes 196616 | tf_op jit(solution)/shard_map/ppermute | solution.py:72
  74.6 14.6 %collective-permute-start.5 = (bf16[3,256,128]{2,1,0:T(8,128)(2,1)S(1)}, bf16[3,256,128]{2,1,0:T(8,128)(2,1)S(1)}, u32[]{:S(2)}, u32[]{:S(2)}) collective-permute-start(bf16[3,256,128]{2,1,0:T(8,128)(2,1)S(1)} %get-tuple-element.41), channel_id=1, source_target_pairs={{0,6},{1,7},{2,8},{3,9},{4,10},{5,11},{6,12},{7,13},{8,14},{9,15},... | collective-permute-start | bytes 589832 | tf_op jit(solution)/shard_map/ppermute | solution.py:72
  79.4 13.8 %collective-permute-start.6 = (bf16[3,256,128]{2,1,0:T(8,128)(2,1)S(1)}, bf16[3,256,128]{2,1,0:T(8,128)(2,1)S(1)}, u32[]{:S(2)}, u32[]{:S(2)}) collective-permute-start(bf16[3,256,128]{2,1,0:T(8,128)(2,1)S(1)} %get-tuple-element.42), channel_id=1, source_target_pairs={{0,10},{1,11},{2,12},{3,13},{4,14},{5,15},{6,0},{7,1},{8,2},{9,3},... | collective-permute-start | bytes 589832 | tf_op jit(solution)/shard_map/ppermute | solution.py:72
  93.3 20.2 %collective-permute-start.8 = (bf16[6,256,128]{2,1,0:T(8,128)(2,1)S(1)}, bf16[6,256,128]{2,1,0:T(8,128)(2,1)S(1)}, u32[]{:S(2)}, u32[]{:S(2)}) collective-permute-start(bf16[6,256,128]{2,1,0:T(8,128)(2,1)S(1)} %get-tuple-element.47.after), channel_id=1, source_target_pairs={{0,2},{1,3},{2,4},{3,5},{4,6},{5,7},{6,8},{7,9},{8,10},{9,11},{10,... | collective-permute-start | bytes 1179656 | tf_op jit(solution)/shard_map/ppermute | solution.py:72
  100.4 13.0 %collective-permute-start.9 = (bf16[4,256,128]{2,1,0:T(8,128)(2,1)S(1)}, bf16[4,256,128]{2,1,0:T(8,128)(2,1)S(1)}, u32[]{:S(2)}, u32[]{:S(2)}) collective-permute-start(bf16[4,256,128]{2,1,0:T(8,128)(2,1)S(1)} %get-tuple-element.48), channel_id=1, source_target_pairs={{0,14},{1,15},{2,0},{3,1},{4,2},{5,3},{6,4},{7,5},{8,6},{9,7},{10,... | collective-permute-start | bytes 786440 | tf_op jit(solution)/shard_map/ppermute | solution.py:72
  102.4 3.1 %collective-permute-start.7 = (bf16[64,128]{1,0:T(8,128)(2,1)S(1)}, bf16[64,128]{1,0:T(8,128)(2,1)S(1)}, u32[]{:S(2)}, u32[]{:S(2)}) collective-permute-start(bf16[64,128]{1,0:T(8,128)(2,1)S(1)} %shard_map.116.ranks), channel_id=1, source_target_pairs={{0,1},{1,0},{2,3},{3,2},{4,5},{5,4},{6,7},{7,6},{8,9},{9,8},{10,11... | collective-permute-start | bytes 49160 | tf_op jit(solution)/shard_map/ppermute | solution.py:72
  107.1 0.7 copy-start.4
  107.8 17.0 %all-to-all-start.3 = ((bf16[16,72,128]{2,1,0:T(8,128)(2,1)}), bf16[16,72,128]{2,1,0:T(8,128)(2,1)S(1)}, u32[]{:S(2)}, u32[]{:S(2)}) async-start(bf16[16,72,128]{2,1,0:T(8,128)(2,1)} %get-tuple-element.50), calls=%async_computation.3 | async-start | bytes 589824 | tf_op jit(solution)/shard_map/all_to_all | solution.py:317
  113.5 29.3 %collective-permute-start.10 = (bf16[16,256,128]{2,1,0:T(8,128)(2,1)S(1)}, bf16[16,256,128]{2,1,0:T(8,128)(2,1)S(1)}, u32[]{:S(2)}, u32[]{:S(2)}) collective-permute-start(bf16[16,256,128]{2,1,0:T(8,128)(2,1)S(1)} %shard_map.120.blocks), channel_id=1, source_target_pairs={{0,1},{1,0},{2,3},{3,2},{4,5},{5,4},{6,7},{7,6},{8,9},{9,8},{10,11... | collective-permute-start | bytes 3145736 | tf_op jit(solution)/shard_map/ppermute | solution.py:72
  115.5 0.9 copy-start.5
  125.5 16.6 %all-to-all-start.4 = ((bf16[16,88,128]{2,1,0:T(8,128)(2,1)}), bf16[16,88,128]{2,1,0:T(8,128)(2,1)S(1)}, u32[]{:S(2)}, u32[]{:S(2)}) async-start(bf16[16,88,128]{2,1,0:T(8,128)(2,1)} %shard_map.123), calls=%async_computation.4 | async-start | bytes 720896 | tf_op jit(solution)/shard_map/all_to_all | solution.py:317

commit v10 on v9

--- a/solution.py
+++ b/solution.py
@@ -74,6 +74,10 @@
 
 def call(kernel, out_shape, scalars=0, grid=(), in_specs=None, out_specs=None, scratch=(),
          flops=0, moved=0):
+    if grid == (1,):
+        resident = pl.BlockSpec(memory_space=pltpu.VMEM)
+        grid, in_specs = (), [resident] * len(in_specs)
+        out_specs = [resident] * len(out_specs) if isinstance(out_specs, list) else resident
     return pl.pallas_call(
         kernel,
         out_shape=out_shape,
@@ -155,12 +159,13 @@
 
 def squares_kernel(where, head, up, second):
     rank = up.shape[1]
+    own_up = up[where[0]]
     total = jnp.sum(head[...].astype(F32), axis=0)
-    factor = up[0].astype(F32)
+    factor = own_up.astype(F32)
     rows, cols = iota((rank, LANES), 0), iota((rank, LANES), 1)
     spread = jnp.where(rows < 8, total[rank + 1 : rank + 2], total[rank + 2 : rank + 3])
     spread = jnp.where(cols // rank == rows % 8, spread, 0.0)
-    tiled = jnp.concatenate([up[0]] * (LANES // rank), axis=0)
+    tiled = jnp.concatenate([own_up] * (LANES // rank), axis=0)
     high = spread.astype(BF16)
     rest = (spread - high.astype(F32)).astype(BF16)
     gram_up = dot(jnp.concatenate([high, rest], axis=0), tiled, 1, 0)

time: 148 us -> 148 us (level)
  no operation moved by 1% of the time
where the time goes in v10:
time: 148 us; the launch traced here: 147 us
  starting transfers between devices  80.8 us (55%)
  waiting for transfers between devices  40.7 us (28%)
  Pallas kernels  22.5 us (15%)
  local copies, waits for them, and re-layouts  1.58 us (1%)
    all_to_all x5, starting transfers between devices, exchange(): lax.all_to_all(blocks, axis, 0, 0, tiled=True, axis_index_groups=groups)  41.7 us
    ppermute x11, starting transfers between devices, shift(): return lax.ppermute(block, 'tensor', pairs)  39.1 us
    all_to_all x5, waiting for transfers between devices, exchange(): lax.all_to_all(blocks, axis, 0, 0, tiled=True, axis_index_groups=groups)  20.4 us
    ppermute x11, waiting for transfers between devices, shift(): return lax.ppermute(block, 'tensor', pairs)  20.3 us
    pallas_call x1, Pallas kernels, local(): call(first_kernel, [shaped(size, HEAD, width), shaped(size // 2, count, w...  5.04 us
    pallas_call x1, Pallas kernels, local(): call(tokens_rest_kernel, shaped(own_rows, count), scalars=1, grid=(zs //...  3.69 us
    pallas_call x1, Pallas kernels, local(): call(tokens_kernel, shaped(own_rows, count, dtype=F32), scalars=1, grid=(...  3.36 us
  transfers between devices with their start and end apart: 16, of which 10 were waited for; matrix products, arithmetic and copies ran while one was open for 0% of the time, Pallas kernels for 9%

profile of v10, /device:TPU:14, one launch (start us, length us, event | category | flops | bytes accessed | tf_op | source)
XLA Modules:
  0.0 146.6 jit_solution(3992963372156727691)
XLA Ops:
  0.6 0.0 copy-start
  0.6 0.0 copy-start.1
  0.7 0.1 pad_add_fusion.where
  0.8 5.0 %shard_map.110 = (bf16[32,24,128]{2,1,0:T(8,128)(2,1)}, bf16[16,256,128]{2,1,0:T(8,128)(2,1)S(1)}, bf16[16,256,128]{2,1,0:T(8,128)(2,1)}) custom-call(s32[4]{0:T(128)S(1)} %pad_add_fusion.where, bf16[448,256]{1,0:T(8,128)(2,1)} %bitcast.14, bf16[448,4096]{1,0:T(8,128)(2,1)} %rest_7_.3, bf16[16,16,448]{2,1,0:T(8,128)(2,1)} %bitcast.11), custom_call_target="tpu_custom_call" | custom-call | flops 939524096 | bytes 3670016 | tf_op jit(solution)/shard_map/pallas_call | solution.py:347
  5.8 0.0 copy-start.6
  5.8 2.1 %collective-permute-start = (bf16[16,256,128]{2,1,0:T(8,128)(2,1)}, bf16[16,256,128]{2,1,0:T(8,128)(2,1)S(1)}, u32[]{:S(2)}, u32[]{:S(2)}) collective-permute-start(bf16[16,256,128]{2,1,0:T(8,128)(2,1)} %get-tuple-element.31), channel_id=1, source_target_pairs={{0,1},{1,0},{2,3},{3,2},{4,5},{5,4},{6,7},{7,6},{8,9},{9,8},{10,11... | collective-permute-start | bytes 3145736 | tf_op jit(solution)/shard_map/ppermute | solution.py:72
  7.9 2.8 %collective-permute-done.got_a.got_b = bf16[16,256,128]{2,1,0:T(8,128)(2,1)S(1)} collective-permute-done((bf16[16,256,128]{2,1,0:T(8,128)(2,1)}, bf16[16,256,128]{2,1,0:T(8,128)(2,1)S(1)}, u32[]{:S(2)}, u32[]{:S(2)}) %collective-permute-start) | collective-permute-done | bytes 1048608 | tf_op jit(solution)/shard_map/ppermute | solution.py:72
  10.7 1.1 shard_map.111
  11.8 3.3 %collective-permute-start.1 = (bf16[8,256,128]{2,1,0:T(8,128)(2,1)S(1)}, bf16[8,256,128]{2,1,0:T(8,128)(2,1)S(1)}, u32[]{:S(2)}, u32[]{:S(2)}) collective-permute-start(bf16[8,256,128]{2,1,0:T(8,128)(2,1)S(1)} %get-tuple-element.33), channel_id=1, source_target_pairs={{0,16},{1,17},{2,18},{3,19},{4,20},{5,21},{6,22},{7,23},{8,24},{9,... | collective-permute-start | bytes 1572872 | tf_op jit(solution)/shard_map/ppermute | solution.py:72
  15.1 13.5 %all-to-all-start = ((bf16[32,24,128]{2,1,0:T(8,128)(2,1)}), bf16[32,24,128]{2,1,0:T(8,128)(2,1)S(1)}, u32[]{:S(2)}, u32[]{:S(2)}) async-start(bf16[32,24,128]{2,1,0:T(8,128)(2,1)} %get-tuple-element.37), calls=%async_computation | async-start | bytes 393216 | tf_op jit(solution)/shard_map/all_to_all | solution.py:322
  28.6 0.6 collective-permute-done.1.got
  29.2 0.7 shard_map.112
  29.9 4.3 %collective-permute-start.2 = (bf16[3,256,128]{2,1,0:T(8,128)(2,1)S(1)}, bf16[3,256,128]{2,1,0:T(8,128)(2,1)S(1)}, u32[]{:S(2)}, u32[]{:S(2)}) collective-permute-start(bf16[3,256,128]{2,1,0:T(8,128)(2,1)S(1)} %get-tuple-element.35), channel_id=1, source_target_pairs={{0,2},{1,3},{2,4},{3,5},{4,6},{5,7},{6,8},{7,9},{8,10},{9,11},{10,... | collective-permute-start | bytes 589832 | tf_op jit(solution)/shard_map/ppermute | solution.py:72
  34.1 4.9 %all-to-all-done.head = bf16[32,24,128]{2,1,0:T(8,128)(2,1)S(1)} async-done(((bf16[32,24,128]{2,1,0:T(8,128)(2,1)}), bf16[32,24,128]{2,1,0:T(8,128)(2,1)S(1)}, u32[]{:S(2)}, u32[]{:S(2)}) %all-to-all-start) | async-done | bytes 196640 | tf_op jit(solution)/shard_map/all_to_all | solution.py:322
  39.0 1.3 shard_map.113
  40.4 8.5 %all-to-all-start.1 = ((f32[16,2,128]{2,1,0:T(2,128)}), f32[16,2,128]{2,1,0:T(2,128)S(1)}, u32[]{:S(2)}, u32[]{:S(2)}) async-start(f32[16,2,128]{2,1,0:T(2,128)} %shard_map.113), calls=%async_computation.1 | async-start | bytes 32768 | tf_op jit(solution)/shard_map/all_to_all | solution.py:322
  48.8 5.7 %collective-permute-start.3 = (bf16[2,256,128]{2,1,0:T(8,128)(2,1)S(1)}, bf16[2,256,128]{2,1,0:T(8,128)(2,1)S(1)}, u32[]{:S(2)}, u32[]{:S(2)}) collective-permute-start(bf16[2,256,128]{2,1,0:T(8,128)(2,1)S(1)} %get-tuple-element.36), channel_id=1, source_target_pairs={{0,14},{1,15},{2,0},{3,1},{4,2},{5,3},{6,4},{7,5},{8,6},{9,7},{10,... | collective-permute-start | bytes 393224 | tf_op jit(solution)/shard_map/ppermute | solution.py:72
  54.5 0.7 all-to-all-done.1.second
  55.2 1.8 %shard_map.114 = (bf16[256,128]{1,0:T(8,128)(2,1)S(1)}, bf16[16,64,128]{2,1,0:T(8,128)(2,1)}, f32[16,128]{1,0:T(8,128)S(1)}) custom-call(s32[4]{0:T(128)S(1)} %pad_add_fusion.where, s32[16]{0:T(128)S(1)} %copy-done.7, f32[16,2,128]{2,1,0:T(2,128)S(1)} %all-to-all-done.1.second, bf16[16,128]{1,0:T(8,128)(2,1)S(1)} %copy-done.6, ...), custom_call_target="tpu_custom_call" | custom-call | flops 16777216 | bytes 262144 | tf_op jit(solution)/shard_map/pallas_call | solution.py:422
  57.0 9.5 %all-to-all-start.2 = ((bf16[16,64,128]{2,1,0:T(8,128)(2,1)}), bf16[16,64,128]{2,1,0:T(8,128)(2,1)S(1)}, u32[]{:S(2)}, u32[]{:S(2)}) async-start(bf16[16,64,128]{2,1,0:T(8,128)(2,1)} %get-tuple-element.43), calls=%async_computation.2 | async-start | bytes 524288 | tf_op jit(solution)/shard_map/all_to_all | solution.py:322
  66.5 2.0 %collective-permute-start.4 = (bf16[256,128]{1,0:T(8,128)(2,1)S(1)}, bf16[256,128]{1,0:T(8,128)(2,1)S(1)}, u32[]{:S(2)}, u32[]{:S(2)}) collective-permute-start(bf16[256,128]{1,0:T(8,128)(2,1)S(1)} %get-tuple-element.39.share.scaled), channel_id=1, source_target_pairs={{0,16},{1,17},{2,18},{3,19},{4,20},{5,21},{6,22},{7,23},{8,24},{9,... | collective-permute-start | bytes 196616 | tf_op jit(solution)/shard_map/ppermute | solution.py:72
  68.5 6.0 %collective-permute-done.4.other = bf16[256,128]{1,0:T(8,128)(2,1)S(1)} collective-permute-done((bf16[256,128]{1,0:T(8,128)(2,1)S(1)}, bf16[256,128]{1,0:T(8,128)(2,1)S(1)}, u32[]{:S(2)}, u32[]{:S(2)}) %collective-permute-start.4) | collective-permute-done | bytes 65568 | tf_op jit(solution)/shard_map/ppermute | solution.py:72
  74.5 0.1 shard_map.115
  74.6 4.8 %collective-permute-start.5 = (bf16[3,256,128]{2,1,0:T(8,128)(2,1)S(1)}, bf16[3,256,128]{2,1,0:T(8,128)(2,1)S(1)}, u32[]{:S(2)}, u32[]{:S(2)}) collective-permute-start(bf16[3,256,128]{2,1,0:T(8,128)(2,1)S(1)} %get-tuple-element.41), channel_id=1, source_target_pairs={{0,6},{1,7},{2,8},{3,9},{4,10},{5,11},{6,12},{7,13},{8,14},{9,15},... | collective-permute-start | bytes 589832 | tf_op jit(solution)/shard_map/ppermute | solution.py:72
  79.4 4.0 %collective-permute-start.6 = (bf16[3,256,128]{2,1,0:T(8,128)(2,1)S(1)}, bf16[3,256,128]{2,1,0:T(8,128)(2,1)S(1)}, u32[]{:S(2)}, u32[]{:S(2)}) collective-permute-start(bf16[3,256,128]{2,1,0:T(8,128)(2,1)S(1)} %get-tuple-element.42), channel_id=1, source_target_pairs={{0,10},{1,11},{2,12},{3,13},{4,14},{5,15},{6,0},{7,1},{8,2},{9,3},... | collective-permute-start | bytes 589832 | tf_op jit(solution)/shard_map/ppermute | solution.py:72
  83.4 5.7 %collective-permute-done.5.base_a.below = bf16[3,256,128]{2,1,0:T(8,128)(2,1)S(1)} collective-permute-done((bf16[3,256,128]{2,1,0:T(8,128)(2,1)S(1)}, bf16[3,256,128]{2,1,0:T(8,128)(2,1)S(1)}, u32[]{:S(2)}, u32[]{:S(2)}) %collective-permute-start.5) | collective-permute-done | bytes 196640 | tf_op jit(solution)/shard_map/ppermute | solution.py:72
  89.1 4.1 %collective-permute-done.6.base_b.above = bf16[3,256,128]{2,1,0:T(8,128)(2,1)S(1)} collective-permute-done((bf16[3,256,128]{2,1,0:T(8,128)(2,1)S(1)}, bf16[3,256,128]{2,1,0:T(8,128)(2,1)S(1)}, u32[]{:S(2)}, u32[]{:S(2)}) %collective-permute-start.6) | collective-permute-done | bytes 196640 | tf_op jit(solution)/shard_map/ppermute | solution.py:72
  93.2 0.1 shard_map.119
  93.3 7.2 %collective-permute-start.8 = (bf16[6,256,128]{2,1,0:T(8,128)(2,1)S(1)}, bf16[6,256,128]{2,1,0:T(8,128)(2,1)S(1)}, u32[]{:S(2)}, u32[]{:S(2)}) collective-permute-start(bf16[6,256,128]{2,1,0:T(8,128)(2,1)S(1)} %get-tuple-element.47.after), channel_id=1, source_target_pairs={{0,2},{1,3},{2,4},{3,5},{4,6},{5,7},{6,8},{7,9},{8,10},{9,11},{10,... | collective-permute-start | bytes 1179656 | tf_op jit(solution)/shard_map/ppermute | solution.py:72
  100.4 1.9 %collective-permute-start.9 = (bf16[4,256,128]{2,1,0:T(8,128)(2,1)S(1)}, bf16[4,256,128]{2,1,0:T(8,128)(2,1)S(1)}, u32[]{:S(2)}, u32[]{:S(2)}) collective-permute-start(bf16[4,256,128]{2,1,0:T(8,128)(2,1)S(1)} %get-tuple-element.48), channel_id=1, source_target_pairs={{0,14},{1,15},{2,0},{3,1},{4,2},{5,3},{6,4},{7,5},{8,6},{9,7},{10,... | collective-permute-start | bytes 786440 | tf_op jit(solution)/shard_map/ppermute | solution.py:72
  102.4 0.0 all-to-all-done.2.rank_rows
  102.4 1.9 %collective-permute-start.7 = (bf16[64,128]{1,0:T(8,128)(2,1)S(1)}, bf16[64,128]{1,0:T(8,128)(2,1)S(1)}, u32[]{:S(2)}, u32[]{:S(2)}) collective-permute-start(bf16[64,128]{1,0:T(8,128)(2,1)S(1)} %shard_map.116.ranks), channel_id=1, source_target_pairs={{0,1},{1,0},{2,3},{3,2},{4,5},{5,4},{6,7},{7,6},{8,9},{9,8},{10,11... | collective-permute-start | bytes 49160 | tf_op jit(solution)/shard_map/ppermute | solution.py:72
  104.3 1.1 collective-permute-done.7.got
  105.5 1.6 %shard_map.117 = (bf16[16,72,128]{2,1,0:T(8,128)(2,1)}, bf16[256,256]{1,0:T(8,128)(2,1)S(1)}, bf16[256,256]{1,0:T(8,128)(2,1)S(1)}) custom-call(s32[4]{0:T(128)S(1)} %pad_add_fusion.where, s32[16]{0:T(128)S(1)} %copy-done.7, bf16[64,128]{1,0:T(8,128)(2,1)S(1)} %shard_map.116.ranks, bf16[64,128]{1,0:T(8,128)(2,1)S(1)} %collective-permute-done.7.got, ...), custom_call_target="tpu_custom_call" | custom-call | flops 75497472 | bytes 589824 | tf_op jit(solution)/shard_map/pallas_call | solution.py:490
  107.1 0.7 copy-done.4
  107.8 5.7 %all-to-all-start.3 = ((bf16[16,72,128]{2,1,0:T(8,128)(2,1)}), bf16[16,72,128]{2,1,0:T(8,128)(2,1)S(1)}, u32[]{:S(2)}, u32[]{:S(2)}) async-start(bf16[16,72,128]{2,1,0:T(8,128)(2,1)} %get-tuple-element.50), calls=%async_computation.3 | async-start | bytes 589824 | tf_op jit(solution)/shard_map/all_to_all | solution.py:322
  113.5 0.1 shard_map.120.blocks
  113.5 1.9 %collective-permute-start.10 = (bf16[16,256,128]{2,1,0:T(8,128)(2,1)S(1)}, bf16[16,256,128]{2,1,0:T(8,128)(2,1)S(1)}, u32[]{:S(2)}, u32[]{:S(2)}) collective-permute-start(bf16[16,256,128]{2,1,0:T(8,128)(2,1)S(1)} %shard_map.120.blocks), channel_id=1, source_target_pairs={{0,1},{1,0},{2,3},{3,2},{4,5},{5,4},{6,7},{7,6},{8,9},{9,8},{10,11... | collective-permute-start | bytes 3145736 | tf_op jit(solution)/shard_map/ppermute | solution.py:72
  115.5 0.0 copy-start.5
  115.5 0.9 copy-done.5
  116.4 2.1 %shard_map.118 = (bf16[256,128]{1,0:T(8,128)(2,1)}, bf16[16,128]{1,0:T(8,128)(2,1)S(1)}) custom-call(s32[4]{0:T(128)S(1)} %pad_add_fusion.where, s32[16]{0:T(128)S(1)} %copy-done.7, f32[256,128]{1,0:T(8,128)S(1)} %get-tuple-element.40.base, bf16[3,256,128]{2,1,0:T(8,128)(2,1)S(1)} %collective-permute-done.5.base_a.below, ...), custom_call_target="tpu_custom_call" | custom-call | flops 16777216 | bytes 524288 | tf_op jit(solution)/shard_map/pallas_call | solution.py:509
  118.5 6.2 %all-to-all-done.3.arrived = bf16[16,72,128]{2,1,0:T(8,128)(2,1)S(1)} async-done(((bf16[16,72,128]{2,1,0:T(8,128)(2,1)}), bf16[16,72,128]{2,1,0:T(8,128)(2,1)S(1)}, u32[]{:S(2)}, u32[]{:S(2)}) %all-to-all-start.3) | async-done | bytes 294944 | tf_op jit(solution)/shard_map/all_to_all | solution.py:322
  124.7 0.8 shard_map.123
  125.5 4.6 %all-to-all-start.4 = ((bf16[16,88,128]{2,1,0:T(8,128)(2,1)}), bf16[16,88,128]{2,1,0:T(8,128)(2,1)S(1)}, u32[]{:S(2)}, u32[]{:S(2)}) async-start(bf16[16,88,128]{2,1,0:T(8,128)(2,1)} %shard_map.123), calls=%async_computation.4 | async-start | bytes 720896 | tf_op jit(solution)/shard_map/all_to_all | solution.py:322
  130.1 3.4 %shard_map.121.rest_8_ = f32[448,256]{1,0:T(8,128)S(1)} custom-call(s32[4]{0:T(128)S(1)} %pad_add_fusion.where, bf16[16,256,128]{2,1,0:T(8,128)(2,1)S(1)} %shard_map.120.blocks, bf16[448,4096]{1,0:T(8,128)(2,1)} %rest_7_.3, bf16[448,4096]{1,0:T(8,128)(2,1)} %rest_7_.3, bf16[448,4096]{1,0:T(8,128)(2,1)} %rest_7_.3, bf16[448,4096]{1,0:T(8,128)(2,1)} %rest_7_.3, ...), custom_call_target="tpu_custom_call" | custom-call | flops 528482304 | bytes 1835008 | tf_op jit(solution)/shard_map/pallas_call | solution.py:556
  133.5 8.6 %all-to-all-done.4.fifth = bf16[16,88,128]{2,1,0:T(8,128)(2,1)S(1)} async-done(((bf16[16,88,128]{2,1,0:T(8,128)(2,1)}), bf16[16,88,128]{2,1,0:T(8,128)(2,1)S(1)}, u32[]{:S(2)}, u32[]{:S(2)}) %all-to-all-start.4) | async-done | bytes 360480 | tf_op jit(solution)/shard_map/all_to_all | solution.py:322
  142.1 0.8 shard_map.124
  142.9 3.7 %shard_map.122 = bf16[448,256]{1,0:T(8,128)(2,1)} custom-call(s32[4]{0:T(128)S(1)} %pad_add_fusion.where, bf16[16,256,128]{2,1,0:T(8,128)(2,1)S(1)} %collective-permute-done.10.blocks, bf16[448,4096]{1,0:T(8,128)(2,1)} %rest_7_.3, bf16[448,4096]{1,0:T(8,128)(2,1)} %rest_7_.3, bf16[448,4096]{1,0:T(8,128)(2,1)} %rest_7_.3, bf16[448,4096]{1,0:T(8,128)(2,1)} %rest_7_.3, ...), custom_call_target="tpu_custom_call" | custom-call | flops 469762048 | bytes 1835008 | tf_op jit(solution)/shard_map/pallas_call | solution.py:567
  (16 shorter events, 0.1 us)
Async XLA Ops:
  0.6 10.1 %copy-start = (bf16[16,448,16]{1,2,0:T(8,128)(2,1)S(1)}, bf16[16,448,16]{1,2,0:T(8,128)(2,1)}, u32[]{:S(2)}) copy-start(bf16[16,448,16]{1,2,0:T(8,128)(2,1)} %param.9) | copy-start | bytes 688132
  0.6 10.1 %copy-start.1 = (bf16[256,448]{0,1:T(8,128)(2,1)S(1)}, bf16[256,448]{0,1:T(8,128)(2,1)}, u32[]{:S(2)}) copy-start(bf16[256,448]{0,1:T(8,128)(2,1)} %param.7) | copy-start | bytes 688132
  0.7 10.1 %copy-start.7 = (s32[16]{0:T(128)S(1)}, s32[16]{0:T(128)}, u32[]{:S(2)}) copy-start(s32[16]{0:T(128)} %seg.7) | copy-start | bytes 196
  5.8 33.2 %copy-start.2 = (bf16[16,16,128]{2,1,0:T(8,128)(2,1)S(1)}, bf16[16,16,128]{2,1,0:T(8,128)(2,1)}, u32[]{:S(2)}) copy-start(bf16[16,16,128]{2,1,0:T(8,128)(2,1)} %up.1) | copy-start | bytes 196612
  5.8 49.3 %copy-start.3 = (bf16[256,128]{1,0:T(8,128)(2,1)S(1)}, bf16[256,128]{1,0:T(8,128)(2,1)}, u32[]{:S(2)}) copy-start(bf16[256,128]{1,0:T(8,128)(2,1)} %cotangent.3) | copy-start | bytes 196612
  5.8 49.3 %copy-start.6 = (bf16[16,128]{1,0:T(8,128)(2,1)S(1)}, bf16[16,128]{1,0:T(8,128)(2,1)}, u32[]{:S(2)}) copy-start(bf16[16,128]{1,0:T(8,128)(2,1)} %magnitude.3) | copy-start | bytes 12292
  5.8 4.9 %collective-permute-start = (bf16[16,256,128]{2,1,0:T(8,128)(2,1)}, bf16[16,256,128]{2,1,0:T(8,128)(2,1)S(1)}, u32[]{:S(2)}, u32[]{:S(2)}) collective-permute-start(bf16[16,256,128]{2,1,0:T(8,128)(2,1)} %get-tuple-element.31), channel_id=1, source_target_pairs={{0,1},{1,0},{2,3},{3,2},{4,5},{5,4},{6,7},{7,6},{8,9},{9,8},{10,11... | collective-permute-start | bytes 3145736 | tf_op jit(solution)/shard_map/ppermute | solution.py:72
  11.8 17.4 %collective-permute-start.1 = (bf16[8,256,128]{2,1,0:T(8,128)(2,1)S(1)}, bf16[8,256,128]{2,1,0:T(8,128)(2,1)S(1)}, u32[]{:S(2)}, u32[]{:S(2)}) collective-permute-start(bf16[8,256,128]{2,1,0:T(8,128)(2,1)S(1)} %get-tuple-element.33), channel_id=1, source_target_pairs={{0,16},{1,17},{2,18},{3,19},{4,20},{5,21},{6,22},{7,23},{8,24},{9,... | collective-permute-start | bytes 1572872 | tf_op jit(solution)/shard_map/ppermute | solution.py:72
  15.1 23.9 %all-to-all-start = ((bf16[32,24,128]{2,1,0:T(8,128)(2,1)}), bf16[32,24,128]{2,1,0:T(8,128)(2,1)S(1)}, u32[]{:S(2)}, u32[]{:S(2)}) async-start(bf16[32,24,128]{2,1,0:T(8,128)(2,1)} %get-tuple-element.37), calls=%async_computation | async-start | bytes 393216 | tf_op jit(solution)/shard_map/all_to_all | solution.py:322
  29.9 44.6 %collective-permute-start.2 = (bf16[3,256,128]{2,1,0:T(8,128)(2,1)S(1)}, bf16[3,256,128]{2,1,0:T(8,128)(2,1)S(1)}, u32[]{:S(2)}, u32[]{:S(2)}) collective-permute-start(bf16[3,256,128]{2,1,0:T(8,128)(2,1)S(1)} %get-tuple-element.35), channel_id=1, source_target_pairs={{0,2},{1,3},{2,4},{3,5},{4,6},{5,7},{6,8},{7,9},{8,10},{9,11},{10,... | collective-permute-start | bytes 589832 | tf_op jit(solution)/shard_map/ppermute | solution.py:72
  40.4 14.8 %all-to-all-start.1 = ((f32[16,2,128]{2,1,0:T(2,128)}), f32[16,2,128]{2,1,0:T(2,128)S(1)}, u32[]{:S(2)}, u32[]{:S(2)}) async-start(f32[16,2,128]{2,1,0:T(2,128)} %shard_map.113), calls=%async_computation.1 | async-start | bytes 32768 | tf_op jit(solution)/shard_map/all_to_all | solution.py:322
  48.8 25.6 %collective-permute-start.3 = (bf16[2,256,128]{2,1,0:T(8,128)(2,1)S(1)}, bf16[2,256,128]{2,1,0:T(8,128)(2,1)S(1)}, u32[]{:S(2)}, u32[]{:S(2)}) collective-permute-start(bf16[2,256,128]{2,1,0:T(8,128)(2,1)S(1)} %get-tuple-element.36), channel_id=1, source_target_pairs={{0,14},{1,15},{2,0},{3,1},{4,2},{5,3},{6,4},{7,5},{8,6},{9,7},{10,... | collective-permute-start | bytes 393224 | tf_op jit(solution)/shard_map/ppermute | solution.py:72
  57.0 45.4 %all-to-all-start.2 = ((bf16[16,64,128]{2,1,0:T(8,128)(2,1)}), bf16[16,64,128]{2,1,0:T(8,128)(2,1)S(1)}, u32[]{:S(2)}, u32[]{:S(2)}) async-start(bf16[16,64,128]{2,1,0:T(8,128)(2,1)} %get-tuple-element.43), calls=%async_computation.2 | async-start | bytes 524288 | tf_op jit(solution)/shard_map/all_to_all | solution.py:322
  66.5 8.0 %collective-permute-start.4 = (bf16[256,128]{1,0:T(8,128)(2,1)S(1)}, bf16[256,128]{1,0:T(8,128)(2,1)S(1)}, u32[]{:S(2)}, u32[]{:S(2)}) collective-permute-start(bf16[256,128]{1,0:T(8,128)(2,1)S(1)} %get-tuple-element.39.share.scaled), channel_id=1, source_target_pairs={{0,16},{1,17},{2,18},{3,19},{4,20},{5,21},{6,22},{7,23},{8,24},{9,... | collective-permute-start | bytes 196616 | tf_op jit(solution)/shard_map/ppermute | solution.py:72
  74.6 14.6 %collective-permute-start.5 = (bf16[3,256,128]{2,1,0:T(8,128)(2,1)S(1)}, bf16[3,256,128]{2,1,0:T(8,128)(2,1)S(1)}, u32[]{:S(2)}, u32[]{:S(2)}) collective-permute-start(bf16[3,256,128]{2,1,0:T(8,128)(2,1)S(1)} %get-tuple-element.41), channel_id=1, source_target_pairs={{0,6},{1,7},{2,8},{3,9},{4,10},{5,11},{6,12},{7,13},{8,14},{9,15},... | collective-permute-start | bytes 589832 | tf_op jit(solution)/shard_map/ppermute | solution.py:72
  79.4 13.8 %collective-permute-start.6 = (bf16[3,256,128]{2,1,0:T(8,128)(2,1)S(1)}, bf16[3,256,128]{2,1,0:T(8,128)(2,1)S(1)}, u32[]{:S(2)}, u32[]{:S(2)}) collective-permute-start(bf16[3,256,128]{2,1,0:T(8,128)(2,1)S(1)} %get-tuple-element.42), channel_id=1, source_target_pairs={{0,10},{1,11},{2,12},{3,13},{4,14},{5,15},{6,0},{7,1},{8,2},{9,3},... | collective-permute-start | bytes 589832 | tf_op jit(solution)/shard_map/ppermute | solution.py:72
  93.3 20.2 %collective-permute-start.8 = (bf16[6,256,128]{2,1,0:T(8,128)(2,1)S(1)}, bf16[6,256,128]{2,1,0:T(8,128)(2,1)S(1)}, u32[]{:S(2)}, u32[]{:S(2)}) collective-permute-start(bf16[6,256,128]{2,1,0:T(8,128)(2,1)S(1)} %get-tuple-element.47.after), channel_id=1, source_target_pairs={{0,2},{1,3},{2,4},{3,5},{4,6},{5,7},{6,8},{7,9},{8,10},{9,11},{10,... | collective-permute-start | bytes 1179656 | tf_op jit(solution)/shard_map/ppermute | solution.py:72
  100.4 13.0 %collective-permute-start.9 = (bf16[4,256,128]{2,1,0:T(8,128)(2,1)S(1)}, bf16[4,256,128]{2,1,0:T(8,128)(2,1)S(1)}, u32[]{:S(2)}, u32[]{:S(2)}) collective-permute-start(bf16[4,256,128]{2,1,0:T(8,128)(2,1)S(1)} %get-tuple-element.48), channel_id=1, source_target_pairs={{0,14},{1,15},{2,0},{3,1},{4,2},{5,3},{6,4},{7,5},{8,6},{9,7},{10,... | collective-permute-start | bytes 786440 | tf_op jit(solution)/shard_map/ppermute | solution.py:72
  102.4 3.1 %collective-permute-start.7 = (bf16[64,128]{1,0:T(8,128)(2,1)S(1)}, bf16[64,128]{1,0:T(8,128)(2,1)S(1)}, u32[]{:S(2)}, u32[]{:S(2)}) collective-permute-start(bf16[64,128]{1,0:T(8,128)(2,1)S(1)} %shard_map.116.ranks), channel_id=1, source_target_pairs={{0,1},{1,0},{2,3},{3,2},{4,5},{5,4},{6,7},{7,6},{8,9},{9,8},{10,11... | collective-permute-start | bytes 49160 | tf_op jit(solution)/shard_map/ppermute | solution.py:72
  107.1 0.7 copy-start.4
  107.8 17.0 %all-to-all-start.3 = ((bf16[16,72,128]{2,1,0:T(8,128)(2,1)}), bf16[16,72,128]{2,1,0:T(8,128)(2,1)S(1)}, u32[]{:S(2)}, u32[]{:S(2)}) async-start(bf16[16,72,128]{2,1,0:T(8,128)(2,1)} %get-tuple-element.50), calls=%async_computation.3 | async-start | bytes 589824 | tf_op jit(solution)/shard_map/all_to_all | solution.py:322
  113.5 29.3 %collective-permute-start.10 = (bf16[16,256,128]{2,1,0:T(8,128)(2,1)S(1)}, bf16[16,256,128]{2,1,0:T(8,128)(2,1)S(1)}, u32[]{:S(2)}, u32[]{:S(2)}) collective-permute-start(bf16[16,256,128]{2,1,0:T(8,128)(2,1)S(1)} %shard_map.120.blocks), channel_id=1, source_target_pairs={{0,1},{1,0},{2,3},{3,2},{4,5},{5,4},{6,7},{7,6},{8,9},{9,8},{10,11... | collective-permute-start | bytes 3145736 | tf_op jit(solution)/shard_map/ppermute | solution.py:72
  115.5 0.9 copy-start.5
  125.5 16.6 %all-to-all-start.4 = ((bf16[16,88,128]{2,1,0:T(8,128)(2,1)}), bf16[16,88,128]{2,1,0:T(8,128)(2,1)S(1)}, u32[]{:S(2)}, u32[]{:S(2)}) async-start(bf16[16,88,128]{2,1,0:T(8,128)(2,1)} %shard_map.123), calls=%async_computation.4 | async-start | bytes 720896 | tf_op jit(solution)/shard_map/all_to_all | solution.py:322

commit v11 on v10

--- a/solution.py
+++ b/solution.py
@@ -60,12 +60,29 @@
     return jnp.concatenate([rows[:half], rows[half:]], axis=1)
 
 
+def one_hot(marks, count):
+    at = iota((1, count), 1)
+    rows = [((at >= lo) & (at < hi)).astype(F32) for lo, hi in marks]
+    return jnp.concatenate(rows, axis=0).astype(BF16)
+
+
+def pieces(values, number):
+    parts = []
+    for _ in range(number):
+        part = values.astype(BF16)
+        parts.append(part)
+        values = values - part.astype(F32)
+    return parts
+
+
 def token_scale_of(col_scale, marks, token_count):
-    at = iota((token_count, LANES), 0)
-    total = jnp.zeros((token_count, LANES), F32)
-    for a, (lo, hi) in enumerate(marks):
-        total += jnp.where((at >= lo) & (at < hi), col_scale[a : a + 1], 0.0)
-    return total
+    member = one_hot(marks, token_count)
+    return dot(
+        jnp.concatenate([member] * 3, axis=0),
+        jnp.concatenate(pieces(col_scale, 3), axis=0),
+        0,
+        0,
+    )
 
 
 def shift(block, pairs):
@@ -255,12 +272,9 @@
     scale = token_scale_of(magnitude[...].astype(F32) / norms[...], marks, count)
     projected[...] = (hidden * scale).astype(BF16)
     weighted = cotangent[...].astype(F32) * hidden
-    at = iota((count, LANES), 0)
-    sums = [
-        jnp.sum(jnp.where((at >= lo) & (at < hi), weighted, 0.0), axis=0, keepdims=True)
-        for lo, hi in marks
-    ]
-    mag[...] = jnp.concatenate(sums, axis=0).astype(BF16)
+    member = one_hot(marks, count)
+    high, rest = pieces(weighted, 2)
+    mag[...] = (dot(member, high, 1, 0) + dot(member, rest, 1, 0)).astype(BF16)
 
 
 def total_kernel(arrived, mag, fifth):

time: 148 us -> 147 us (level)
  transfers between devices with their start and end apart: 16 -> 16, of which waited for: 10 -> 10; matrix products, arithmetic and copies ran while one was open for 0% -> 0% of each run, Pallas kernels for 9% -> 8%
where the time goes in v11:
time: 147 us; the launch traced here: 146 us
  starting transfers between devices  80.8 us (55%)
  waiting for transfers between devices  41.4 us (28%)
  Pallas kernels  21.7 us (15%)
  local copies, waits for them, and re-layouts  1.58 us (1%)
    all_to_all x5, starting transfers between devices, exchange(): lax.all_to_all(blocks, axis, 0, 0, tiled=True, axis_index_groups=groups)  41.7 us
    ppermute x11, starting transfers between devices, shift(): return lax.ppermute(block, 'tensor', pairs)  39.1 us
    all_to_all x5, waiting for transfers between devices, exchange(): lax.all_to_all(blocks, axis, 0, 0, tiled=True, axis_index_groups=groups)  21.1 us
    ppermute x11, waiting for transfers between devices, shift(): return lax.ppermute(block, 'tensor', pairs)  20.3 us
    pallas_call x1, Pallas kernels, local(): call(first_kernel, [shaped(size, HEAD, width), shaped(size // 2, count, w...  5.04 us
    pallas_call x1, Pallas kernels, local(): call(tokens_rest_kernel, shaped(own_rows, count), scalars=1, grid=(zs //...  3.69 us
    pallas_call x1, Pallas kernels, local(): call(tokens_kernel, shaped(own_rows, count, dtype=F32), scalars=1, grid=(...  3.37 us
  transfers between devices with their start and end apart: 16, of which 10 were waited for; matrix products, arithmetic and copies ran while one was open for 0% of the time, Pallas kernels for 8%

profile of v11, /device:TPU:14, one launch (start us, length us, event | category | flops | bytes accessed | tf_op | source)
XLA Modules:
  0.0 146.4 jit_solution(8307646418379834814)
XLA Ops:
  0.6 0.0 copy-start
  0.6 0.0 copy-start.1
  0.7 0.1 pad_add_fusion.where
  0.8 5.0 %shard_map.110 = (bf16[32,24,128]{2,1,0:T(8,128)(2,1)}, bf16[16,256,128]{2,1,0:T(8,128)(2,1)S(1)}, bf16[16,256,128]{2,1,0:T(8,128)(2,1)}) custom-call(s32[4]{0:T(128)S(1)} %pad_add_fusion.where, bf16[448,256]{1,0:T(8,128)(2,1)} %bitcast.14, bf16[448,4096]{1,0:T(8,128)(2,1)} %rest_7_.3, bf16[16,16,448]{2,1,0:T(8,128)(2,1)} %bitcast.11), custom_call_target="tpu_custom_call" | custom-call | flops 939524096 | bytes 3670016 | tf_op jit(solution)/shard_map/pallas_call | solution.py:361
  5.8 0.0 copy-start.6
  5.8 2.1 %collective-permute-start = (bf16[16,256,128]{2,1,0:T(8,128)(2,1)}, bf16[16,256,128]{2,1,0:T(8,128)(2,1)S(1)}, u32[]{:S(2)}, u32[]{:S(2)}) collective-permute-start(bf16[16,256,128]{2,1,0:T(8,128)(2,1)} %get-tuple-element.31), channel_id=1, source_target_pairs={{0,1},{1,0},{2,3},{3,2},{4,5},{5,4},{6,7},{7,6},{8,9},{9,8},{10,11... | collective-permute-start | bytes 3145736 | tf_op jit(solution)/shard_map/ppermute | solution.py:89
  7.9 2.8 %collective-permute-done.got_a.got_b = bf16[16,256,128]{2,1,0:T(8,128)(2,1)S(1)} collective-permute-done((bf16[16,256,128]{2,1,0:T(8,128)(2,1)}, bf16[16,256,128]{2,1,0:T(8,128)(2,1)S(1)}, u32[]{:S(2)}, u32[]{:S(2)}) %collective-permute-start) | collective-permute-done | bytes 1048608 | tf_op jit(solution)/shard_map/ppermute | solution.py:89
  10.7 1.1 shard_map.111
  11.8 3.3 %collective-permute-start.1 = (bf16[8,256,128]{2,1,0:T(8,128)(2,1)S(1)}, bf16[8,256,128]{2,1,0:T(8,128)(2,1)S(1)}, u32[]{:S(2)}, u32[]{:S(2)}) collective-permute-start(bf16[8,256,128]{2,1,0:T(8,128)(2,1)S(1)} %get-tuple-element.33), channel_id=1, source_target_pairs={{0,16},{1,17},{2,18},{3,19},{4,20},{5,21},{6,22},{7,23},{8,24},{9,... | collective-permute-start | bytes 1572872 | tf_op jit(solution)/shard_map/ppermute | solution.py:89
  15.1 13.5 %all-to-all-start = ((bf16[32,24,128]{2,1,0:T(8,128)(2,1)}), bf16[32,24,128]{2,1,0:T(8,128)(2,1)S(1)}, u32[]{:S(2)}, u32[]{:S(2)}) async-start(bf16[32,24,128]{2,1,0:T(8,128)(2,1)} %get-tuple-element.37), calls=%async_computation | async-start | bytes 393216 | tf_op jit(solution)/shard_map/all_to_all | solution.py:336
  28.6 0.6 collective-permute-done.1.got
  29.2 0.7 shard_map.112
  29.9 4.3 %collective-permute-start.2 = (bf16[3,256,128]{2,1,0:T(8,128)(2,1)S(1)}, bf16[3,256,128]{2,1,0:T(8,128)(2,1)S(1)}, u32[]{:S(2)}, u32[]{:S(2)}) collective-permute-start(bf16[3,256,128]{2,1,0:T(8,128)(2,1)S(1)} %get-tuple-element.35), channel_id=1, source_target_pairs={{0,2},{1,3},{2,4},{3,5},{4,6},{5,7},{6,8},{7,9},{8,10},{9,11},{10,... | collective-permute-start | bytes 589832 | tf_op jit(solution)/shard_map/ppermute | solution.py:89
  34.1 4.9 %all-to-all-done.head = bf16[32,24,128]{2,1,0:T(8,128)(2,1)S(1)} async-done(((bf16[32,24,128]{2,1,0:T(8,128)(2,1)}), bf16[32,24,128]{2,1,0:T(8,128)(2,1)S(1)}, u32[]{:S(2)}, u32[]{:S(2)}) %all-to-all-start) | async-done | bytes 196640 | tf_op jit(solution)/shard_map/all_to_all | solution.py:336
  39.0 1.3 shard_map.113
  40.4 8.5 %all-to-all-start.1 = ((f32[16,2,128]{2,1,0:T(2,128)}), f32[16,2,128]{2,1,0:T(2,128)S(1)}, u32[]{:S(2)}, u32[]{:S(2)}) async-start(f32[16,2,128]{2,1,0:T(2,128)} %shard_map.113), calls=%async_computation.1 | async-start | bytes 32768 | tf_op jit(solution)/shard_map/all_to_all | solution.py:336
  48.8 5.7 %collective-permute-start.3 = (bf16[2,256,128]{2,1,0:T(8,128)(2,1)S(1)}, bf16[2,256,128]{2,1,0:T(8,128)(2,1)S(1)}, u32[]{:S(2)}, u32[]{:S(2)}) collective-permute-start(bf16[2,256,128]{2,1,0:T(8,128)(2,1)S(1)} %get-tuple-element.36), channel_id=1, source_target_pairs={{0,14},{1,15},{2,0},{3,1},{4,2},{5,3},{6,4},{7,5},{8,6},{9,7},{10,... | collective-permute-start | bytes 393224 | tf_op jit(solution)/shard_map/ppermute | solution.py:89
  54.5 0.7 all-to-all-done.1.second
  55.2 1.7 %shard_map.114 = (bf16[256,128]{1,0:T(8,128)(2,1)S(1)}, bf16[16,64,128]{2,1,0:T(8,128)(2,1)}, f32[16,128]{1,0:T(8,128)S(1)}) custom-call(s32[4]{0:T(128)S(1)} %pad_add_fusion.where, s32[16]{0:T(128)S(1)} %copy-done.7, f32[16,2,128]{2,1,0:T(2,128)S(1)} %all-to-all-done.1.second, bf16[16,128]{1,0:T(8,128)(2,1)S(1)} %copy-done.6, ...), custom_call_target="tpu_custom_call" | custom-call | flops 16777216 | bytes 262144 | tf_op jit(solution)/shard_map/pallas_call | solution.py:436
  56.8 9.5 %all-to-all-start.2 = ((bf16[16,64,128]{2,1,0:T(8,128)(2,1)}), bf16[16,64,128]{2,1,0:T(8,128)(2,1)S(1)}, u32[]{:S(2)}, u32[]{:S(2)}) async-start(bf16[16,64,128]{2,1,0:T(8,128)(2,1)} %get-tuple-element.43), calls=%async_computation.2 | async-start | bytes 524288 | tf_op jit(solution)/shard_map/all_to_all | solution.py:336
  66.3 2.0 %collective-permute-start.4 = (bf16[256,128]{1,0:T(8,128)(2,1)S(1)}, bf16[256,128]{1,0:T(8,128)(2,1)S(1)}, u32[]{:S(2)}, u32[]{:S(2)}) collective-permute-start(bf16[256,128]{1,0:T(8,128)(2,1)S(1)} %get-tuple-element.39.share.scaled), channel_id=1, source_target_pairs={{0,16},{1,17},{2,18},{3,19},{4,20},{5,21},{6,22},{7,23},{8,24},{9,... | collective-permute-start | bytes 196616 | tf_op jit(solution)/shard_map/ppermute | solution.py:89
  68.3 6.0 %collective-permute-done.4.other = bf16[256,128]{1,0:T(8,128)(2,1)S(1)} collective-permute-done((bf16[256,128]{1,0:T(8,128)(2,1)S(1)}, bf16[256,128]{1,0:T(8,128)(2,1)S(1)}, u32[]{:S(2)}, u32[]{:S(2)}) %collective-permute-start.4) | collective-permute-done | bytes 65568 | tf_op jit(solution)/shard_map/ppermute | solution.py:89
  74.3 0.1 shard_map.115
  74.4 4.8 %collective-permute-start.5 = (bf16[3,256,128]{2,1,0:T(8,128)(2,1)S(1)}, bf16[3,256,128]{2,1,0:T(8,128)(2,1)S(1)}, u32[]{:S(2)}, u32[]{:S(2)}) collective-permute-start(bf16[3,256,128]{2,1,0:T(8,128)(2,1)S(1)} %get-tuple-element.41), channel_id=1, source_target_pairs={{0,6},{1,7},{2,8},{3,9},{4,10},{5,11},{6,12},{7,13},{8,14},{9,15},... | collective-permute-start | bytes 589832 | tf_op jit(solution)/shard_map/ppermute | solution.py:89
  79.2 4.0 %collective-permute-start.6 = (bf16[3,256,128]{2,1,0:T(8,128)(2,1)S(1)}, bf16[3,256,128]{2,1,0:T(8,128)(2,1)S(1)}, u32[]{:S(2)}, u32[]{:S(2)}) collective-permute-start(bf16[3,256,128]{2,1,0:T(8,128)(2,1)S(1)} %get-tuple-element.42), channel_id=1, source_target_pairs={{0,10},{1,11},{2,12},{3,13},{4,14},{5,15},{6,0},{7,1},{8,2},{9,3},... | collective-permute-start | bytes 589832 | tf_op jit(solution)/shard_map/ppermute | solution.py:89
  83.3 5.7 %collective-permute-done.5.base_a.below = bf16[3,256,128]{2,1,0:T(8,128)(2,1)S(1)} collective-permute-done((bf16[3,256,128]{2,1,0:T(8,128)(2,1)S(1)}, bf16[3,256,128]{2,1,0:T(8,128)(2,1)S(1)}, u32[]{:S(2)}, u32[]{:S(2)}) %collective-permute-start.5) | collective-permute-done | bytes 196640 | tf_op jit(solution)/shard_map/ppermute | solution.py:89
  88.9 4.1 %collective-permute-done.6.base_b.above = bf16[3,256,128]{2,1,0:T(8,128)(2,1)S(1)} collective-permute-done((bf16[3,256,128]{2,1,0:T(8,128)(2,1)S(1)}, bf16[3,256,128]{2,1,0:T(8,128)(2,1)S(1)}, u32[]{:S(2)}, u32[]{:S(2)}) %collective-permute-start.6) | collective-permute-done | bytes 196640 | tf_op jit(solution)/shard_map/ppermute | solution.py:89
  93.0 0.1 shard_map.119
  93.1 7.1 %collective-permute-start.8 = (bf16[6,256,128]{2,1,0:T(8,128)(2,1)S(1)}, bf16[6,256,128]{2,1,0:T(8,128)(2,1)S(1)}, u32[]{:S(2)}, u32[]{:S(2)}) collective-permute-start(bf16[6,256,128]{2,1,0:T(8,128)(2,1)S(1)} %get-tuple-element.47.after), channel_id=1, source_target_pairs={{0,2},{1,3},{2,4},{3,5},{4,6},{5,7},{6,8},{7,9},{8,10},{9,11},{10,... | collective-permute-start | bytes 1179656 | tf_op jit(solution)/shard_map/ppermute | solution.py:89
  100.3 1.9 %collective-permute-start.9 = (bf16[4,256,128]{2,1,0:T(8,128)(2,1)S(1)}, bf16[4,256,128]{2,1,0:T(8,128)(2,1)S(1)}, u32[]{:S(2)}, u32[]{:S(2)}) collective-permute-start(bf16[4,256,128]{2,1,0:T(8,128)(2,1)S(1)} %get-tuple-element.48), channel_id=1, source_target_pairs={{0,14},{1,15},{2,0},{3,1},{4,2},{5,3},{6,4},{7,5},{8,6},{9,7},{10,... | collective-permute-start | bytes 786440 | tf_op jit(solution)/shard_map/ppermute | solution.py:89
  102.3 1.9 %collective-permute-start.7 = (bf16[64,128]{1,0:T(8,128)(2,1)S(1)}, bf16[64,128]{1,0:T(8,128)(2,1)S(1)}, u32[]{:S(2)}, u32[]{:S(2)}) collective-permute-start(bf16[64,128]{1,0:T(8,128)(2,1)S(1)} %shard_map.116.ranks), channel_id=1, source_target_pairs={{0,1},{1,0},{2,3},{3,2},{4,5},{5,4},{6,7},{7,6},{8,9},{9,8},{10,11... | collective-permute-start | bytes 49160 | tf_op jit(solution)/shard_map/ppermute | solution.py:89
  104.2 1.1 collective-permute-done.7.got
  105.3 1.6 %shard_map.117 = (bf16[16,72,128]{2,1,0:T(8,128)(2,1)}, bf16[256,256]{1,0:T(8,128)(2,1)S(1)}, bf16[256,256]{1,0:T(8,128)(2,1)S(1)}) custom-call(s32[4]{0:T(128)S(1)} %pad_add_fusion.where, s32[16]{0:T(128)S(1)} %copy-done.7, bf16[64,128]{1,0:T(8,128)(2,1)S(1)} %shard_map.116.ranks, bf16[64,128]{1,0:T(8,128)(2,1)S(1)} %collective-permute-done.7.got, ...), custom_call_target="tpu_custom_call" | custom-call | flops 75497472 | bytes 589824 | tf_op jit(solution)/shard_map/pallas_call | solution.py:504
  106.9 0.7 copy-done.4
  107.6 5.7 %all-to-all-start.3 = ((bf16[16,72,128]{2,1,0:T(8,128)(2,1)}), bf16[16,72,128]{2,1,0:T(8,128)(2,1)S(1)}, u32[]{:S(2)}, u32[]{:S(2)}) async-start(bf16[16,72,128]{2,1,0:T(8,128)(2,1)} %get-tuple-element.50), calls=%async_computation.3 | async-start | bytes 589824 | tf_op jit(solution)/shard_map/all_to_all | solution.py:336
  113.3 0.0 collective-permute-done.9.from_above
  113.3 0.1 shard_map.120.blocks
  113.4 1.9 %collective-permute-start.10 = (bf16[16,256,128]{2,1,0:T(8,128)(2,1)S(1)}, bf16[16,256,128]{2,1,0:T(8,128)(2,1)S(1)}, u32[]{:S(2)}, u32[]{:S(2)}) collective-permute-start(bf16[16,256,128]{2,1,0:T(8,128)(2,1)S(1)} %shard_map.120.blocks), channel_id=1, source_target_pairs={{0,1},{1,0},{2,3},{3,2},{4,5},{5,4},{6,7},{7,6},{8,9},{9,8},{10,11... | collective-permute-start | bytes 3145736 | tf_op jit(solution)/shard_map/ppermute | solution.py:89
  115.3 0.0 copy-start.5
  115.3 0.9 copy-done.5
  116.2 1.4 shard_map.118
  117.6 6.9 %all-to-all-done.3.arrived = bf16[16,72,128]{2,1,0:T(8,128)(2,1)S(1)} async-done(((bf16[16,72,128]{2,1,0:T(8,128)(2,1)}), bf16[16,72,128]{2,1,0:T(8,128)(2,1)S(1)}, u32[]{:S(2)}, u32[]{:S(2)}) %all-to-all-start.3) | async-done | bytes 294944 | tf_op jit(solution)/shard_map/all_to_all | solution.py:336
  124.6 0.8 shard_map.123
  125.4 4.6 %all-to-all-start.4 = ((bf16[16,88,128]{2,1,0:T(8,128)(2,1)}), bf16[16,88,128]{2,1,0:T(8,128)(2,1)S(1)}, u32[]{:S(2)}, u32[]{:S(2)}) async-start(bf16[16,88,128]{2,1,0:T(8,128)(2,1)} %shard_map.123), calls=%async_computation.4 | async-start | bytes 720896 | tf_op jit(solution)/shard_map/all_to_all | solution.py:336
  130.0 3.4 %shard_map.121.rest_8_ = f32[448,256]{1,0:T(8,128)S(1)} custom-call(s32[4]{0:T(128)S(1)} %pad_add_fusion.where, bf16[16,256,128]{2,1,0:T(8,128)(2,1)S(1)} %shard_map.120.blocks, bf16[448,4096]{1,0:T(8,128)(2,1)} %rest_7_.3, bf16[448,4096]{1,0:T(8,128)(2,1)} %rest_7_.3, bf16[448,4096]{1,0:T(8,128)(2,1)} %rest_7_.3, bf16[448,4096]{1,0:T(8,128)(2,1)} %rest_7_.3, ...), custom_call_target="tpu_custom_call" | custom-call | flops 528482304 | bytes 1835008 | tf_op jit(solution)/shard_map/pallas_call | solution.py:570
  133.4 8.6 %all-to-all-done.4.fifth = bf16[16,88,128]{2,1,0:T(8,128)(2,1)S(1)} async-done(((bf16[16,88,128]{2,1,0:T(8,128)(2,1)}), bf16[16,88,128]{2,1,0:T(8,128)(2,1)S(1)}, u32[]{:S(2)}, u32[]{:S(2)}) %all-to-all-start.4) | async-done | bytes 360480 | tf_op jit(solution)/shard_map/all_to_all | solution.py:336
  141.9 0.8 shard_map.124
  142.7 3.7 %shard_map.122 = bf16[448,256]{1,0:T(8,128)(2,1)} custom-call(s32[4]{0:T(128)S(1)} %pad_add_fusion.where, bf16[16,256,128]{2,1,0:T(8,128)(2,1)S(1)} %collective-permute-done.10.blocks, bf16[448,4096]{1,0:T(8,128)(2,1)} %rest_7_.3, bf16[448,4096]{1,0:T(8,128)(2,1)} %rest_7_.3, bf16[448,4096]{1,0:T(8,128)(2,1)} %rest_7_.3, bf16[448,4096]{1,0:T(8,128)(2,1)} %rest_7_.3, ...), custom_call_target="tpu_custom_call" | custom-call | flops 469762048 | bytes 1835008 | tf_op jit(solution)/shard_map/pallas_call | solution.py:581
  (16 shorter events, 0.1 us)
Async XLA Ops:
  0.6 10.1 %copy-start = (bf16[16,448,16]{1,2,0:T(8,128)(2,1)S(1)}, bf16[16,448,16]{1,2,0:T(8,128)(2,1)}, u32[]{:S(2)}) copy-start(bf16[16,448,16]{1,2,0:T(8,128)(2,1)} %param.9) | copy-start | bytes 688132
  0.6 10.1 %copy-start.1 = (bf16[256,448]{0,1:T(8,128)(2,1)S(1)}, bf16[256,448]{0,1:T(8,128)(2,1)}, u32[]{:S(2)}) copy-start(bf16[256,448]{0,1:T(8,128)(2,1)} %param.7) | copy-start | bytes 688132
  0.7 10.1 %copy-start.7 = (s32[16]{0:T(128)S(1)}, s32[16]{0:T(128)}, u32[]{:S(2)}) copy-start(s32[16]{0:T(128)} %seg.7) | copy-start | bytes 196
  5.8 33.2 %copy-start.2 = (bf16[16,16,128]{2,1,0:T(8,128)(2,1)S(1)}, bf16[16,16,128]{2,1,0:T(8,128)(2,1)}, u32[]{:S(2)}) copy-start(bf16[16,16,128]{2,1,0:T(8,128)(2,1)} %up.1) | copy-start | bytes 196612
  5.8 49.3 %copy-start.3 = (bf16[256,128]{1,0:T(8,128)(2,1)S(1)}, bf16[256,128]{1,0:T(8,128)(2,1)}, u32[]{:S(2)}) copy-start(bf16[256,128]{1,0:T(8,128)(2,1)} %cotangent.3) | copy-start | bytes 196612
  5.8 49.3 %copy-start.6 = (bf16[16,128]{1,0:T(8,128)(2,1)S(1)}, bf16[16,128]{1,0:T(8,128)(2,1)}, u32[]{:S(2)}) copy-start(bf16[16,128]{1,0:T(8,128)(2,1)} %magnitude.3) | copy-start | bytes 12292
  5.8 4.9 %collective-permute-start = (bf16[16,256,128]{2,1,0:T(8,128)(2,1)}, bf16[16,256,128]{2,1,0:T(8,128)(2,1)S(1)}, u32[]{:S(2)}, u32[]{:S(2)}) collective-permute-start(bf16[16,256,128]{2,1,0:T(8,128)(2,1)} %get-tuple-element.31), channel_id=1, source_target_pairs={{0,1},{1,0},{2,3},{3,2},{4,5},{5,4},{6,7},{7,6},{8,9},{9,8},{10,11... | collective-permute-start | bytes 3145736 | tf_op jit(solution)/shard_map/ppermute | solution.py:89
  11.8 17.4 %collective-permute-start.1 = (bf16[8,256,128]{2,1,0:T(8,128)(2,1)S(1)}, bf16[8,256,128]{2,1,0:T(8,128)(2,1)S(1)}, u32[]{:S(2)}, u32[]{:S(2)}) collective-permute-start(bf16[8,256,128]{2,1,0:T(8,128)(2,1)S(1)} %get-tuple-element.33), channel_id=1, source_target_pairs={{0,16},{1,17},{2,18},{3,19},{4,20},{5,21},{6,22},{7,23},{8,24},{9,... | collective-permute-start | bytes 1572872 | tf_op jit(solution)/shard_map/ppermute | solution.py:89
  15.1 23.9 %all-to-all-start = ((bf16[32,24,128]{2,1,0:T(8,128)(2,1)}), bf16[32,24,128]{2,1,0:T(8,128)(2,1)S(1)}, u32[]{:S(2)}, u32[]{:S(2)}) async-start(bf16[32,24,128]{2,1,0:T(8,128)(2,1)} %get-tuple-element.37), calls=%async_computation | async-start | bytes 393216 | tf_op jit(solution)/shard_map/all_to_all | solution.py:336
  29.9 44.5 %collective-permute-start.2 = (bf16[3,256,128]{2,1,0:T(8,128)(2,1)S(1)}, bf16[3,256,128]{2,1,0:T(8,128)(2,1)S(1)}, u32[]{:S(2)}, u32[]{:S(2)}) collective-permute-start(bf16[3,256,128]{2,1,0:T(8,128)(2,1)S(1)} %get-tuple-element.35), channel_id=1, source_target_pairs={{0,2},{1,3},{2,4},{3,5},{4,6},{5,7},{6,8},{7,9},{8,10},{9,11},{10,... | collective-permute-start | bytes 589832 | tf_op jit(solution)/shard_map/ppermute | solution.py:89
  40.4 14.8 %all-to-all-start.1 = ((f32[16,2,128]{2,1,0:T(2,128)}), f32[16,2,128]{2,1,0:T(2,128)S(1)}, u32[]{:S(2)}, u32[]{:S(2)}) async-start(f32[16,2,128]{2,1,0:T(2,128)} %shard_map.113), calls=%async_computation.1 | async-start | bytes 32768 | tf_op jit(solution)/shard_map/all_to_all | solution.py:336
  48.8 25.5 %collective-permute-start.3 = (bf16[2,256,128]{2,1,0:T(8,128)(2,1)S(1)}, bf16[2,256,128]{2,1,0:T(8,128)(2,1)S(1)}, u32[]{:S(2)}, u32[]{:S(2)}) collective-permute-start(bf16[2,256,128]{2,1,0:T(8,128)(2,1)S(1)} %get-tuple-element.36), channel_id=1, source_target_pairs={{0,14},{1,15},{2,0},{3,1},{4,2},{5,3},{6,4},{7,5},{8,6},{9,7},{10,... | collective-permute-start | bytes 393224 | tf_op jit(solution)/shard_map/ppermute | solution.py:89
  56.8 45.4 %all-to-all-start.2 = ((bf16[16,64,128]{2,1,0:T(8,128)(2,1)}), bf16[16,64,128]{2,1,0:T(8,128)(2,1)S(1)}, u32[]{:S(2)}, u32[]{:S(2)}) async-start(bf16[16,64,128]{2,1,0:T(8,128)(2,1)} %get-tuple-element.43), calls=%async_computation.2 | async-start | bytes 524288 | tf_op jit(solution)/shard_map/all_to_all | solution.py:336
  66.3 8.0 %collective-permute-start.4 = (bf16[256,128]{1,0:T(8,128)(2,1)S(1)}, bf16[256,128]{1,0:T(8,128)(2,1)S(1)}, u32[]{:S(2)}, u32[]{:S(2)}) collective-permute-start(bf16[256,128]{1,0:T(8,128)(2,1)S(1)} %get-tuple-element.39.share.scaled), channel_id=1, source_target_pairs={{0,16},{1,17},{2,18},{3,19},{4,20},{5,21},{6,22},{7,23},{8,24},{9,... | collective-permute-start | bytes 196616 | tf_op jit(solution)/shard_map/ppermute | solution.py:89
  74.4 14.5 %collective-permute-start.5 = (bf16[3,256,128]{2,1,0:T(8,128)(2,1)S(1)}, bf16[3,256,128]{2,1,0:T(8,128)(2,1)S(1)}, u32[]{:S(2)}, u32[]{:S(2)}) collective-permute-start(bf16[3,256,128]{2,1,0:T(8,128)(2,1)S(1)} %get-tuple-element.41), channel_id=1, source_target_pairs={{0,6},{1,7},{2,8},{3,9},{4,10},{5,11},{6,12},{7,13},{8,14},{9,15},... | collective-permute-start | bytes 589832 | tf_op jit(solution)/shard_map/ppermute | solution.py:89
  79.2 13.8 %collective-permute-start.6 = (bf16[3,256,128]{2,1,0:T(8,128)(2,1)S(1)}, bf16[3,256,128]{2,1,0:T(8,128)(2,1)S(1)}, u32[]{:S(2)}, u32[]{:S(2)}) collective-permute-start(bf16[3,256,128]{2,1,0:T(8,128)(2,1)S(1)} %get-tuple-element.42), channel_id=1, source_target_pairs={{0,10},{1,11},{2,12},{3,13},{4,14},{5,15},{6,0},{7,1},{8,2},{9,3},... | collective-permute-start | bytes 589832 | tf_op jit(solution)/shard_map/ppermute | solution.py:89
  93.1 20.2 %collective-permute-start.8 = (bf16[6,256,128]{2,1,0:T(8,128)(2,1)S(1)}, bf16[6,256,128]{2,1,0:T(8,128)(2,1)S(1)}, u32[]{:S(2)}, u32[]{:S(2)}) collective-permute-start(bf16[6,256,128]{2,1,0:T(8,128)(2,1)S(1)} %get-tuple-element.47.after), channel_id=1, source_target_pairs={{0,2},{1,3},{2,4},{3,5},{4,6},{5,7},{6,8},{7,9},{8,10},{9,11},{10,... | collective-permute-start | bytes 1179656 | tf_op jit(solution)/shard_map/ppermute | solution.py:89
  100.3 13.0 %collective-permute-start.9 = (bf16[4,256,128]{2,1,0:T(8,128)(2,1)S(1)}, bf16[4,256,128]{2,1,0:T(8,128)(2,1)S(1)}, u32[]{:S(2)}, u32[]{:S(2)}) collective-permute-start(bf16[4,256,128]{2,1,0:T(8,128)(2,1)S(1)} %get-tuple-element.48), channel_id=1, source_target_pairs={{0,14},{1,15},{2,0},{3,1},{4,2},{5,3},{6,4},{7,5},{8,6},{9,7},{10,... | collective-permute-start | bytes 786440 | tf_op jit(solution)/shard_map/ppermute | solution.py:89
  102.3 3.1 %collective-permute-start.7 = (bf16[64,128]{1,0:T(8,128)(2,1)S(1)}, bf16[64,128]{1,0:T(8,128)(2,1)S(1)}, u32[]{:S(2)}, u32[]{:S(2)}) collective-permute-start(bf16[64,128]{1,0:T(8,128)(2,1)S(1)} %shard_map.116.ranks), channel_id=1, source_target_pairs={{0,1},{1,0},{2,3},{3,2},{4,5},{5,4},{6,7},{7,6},{8,9},{9,8},{10,11... | collective-permute-start | bytes 49160 | tf_op jit(solution)/shard_map/ppermute | solution.py:89
  106.9 0.7 copy-start.4
  107.6 17.0 %all-to-all-start.3 = ((bf16[16,72,128]{2,1,0:T(8,128)(2,1)}), bf16[16,72,128]{2,1,0:T(8,128)(2,1)S(1)}, u32[]{:S(2)}, u32[]{:S(2)}) async-start(bf16[16,72,128]{2,1,0:T(8,128)(2,1)} %get-tuple-element.50), calls=%async_computation.3 | async-start | bytes 589824 | tf_op jit(solution)/shard_map/all_to_all | solution.py:336
  113.4 29.3 %collective-permute-start.10 = (bf16[16,256,128]{2,1,0:T(8,128)(2,1)S(1)}, bf16[16,256,128]{2,1,0:T(8,128)(2,1)S(1)}, u32[]{:S(2)}, u32[]{:S(2)}) collective-permute-start(bf16[16,256,128]{2,1,0:T(8,128)(2,1)S(1)} %shard_map.120.blocks), channel_id=1, source_target_pairs={{0,1},{1,0},{2,3},{3,2},{4,5},{5,4},{6,7},{7,6},{8,9},{9,8},{10,11... | collective-permute-start | bytes 3145736 | tf_op jit(solution)/shard_map/ppermute | solution.py:89
  115.3 0.9 copy-start.5
  125.4 16.6 %all-to-all-start.4 = ((bf16[16,88,128]{2,1,0:T(8,128)(2,1)}), bf16[16,88,128]{2,1,0:T(8,128)(2,1)S(1)}, u32[]{:S(2)}, u32[]{:S(2)}) async-start(bf16[16,88,128]{2,1,0:T(8,128)(2,1)} %shard_map.123), calls=%async_computation.4 | async-start | bytes 720896 | tf_op jit(solution)/shard_map/all_to_all | solution.py:336
